TPU v7x, 256 devices: a whole 4x4x8 slice. The times are simulated.
256 devices in a mesh: seq: 32 (over z, y_lo, core), chan: 8 (over y_hi, x).
Axes of the slice: x: 4, y: 4 (y_hi: 2, y_lo: 2; y = y_hi * 2 + y_lo), z: 8, core: 2. Of those that a mesh axis runs over, the one named last changes fastest.
Arguments:
- projected: bfloat16 [8192, 3, 4096], P('seq', None, 'chan'), may hold values from -6 to 6
- short_weight: float32 [3, 3, 4096], P(None, None, 'chan'), may hold values from -3 to 3
- filters: float32 [512, 8192], P(('chan', 'seq')), may hold values from -1.1 to 1.1
- skip: float32 [4096], P('chan'), may hold values from -3 to 3
- out_weight: bfloat16 [4096, 4096], P('chan', 'seq'), may hold values from -0.09375 to 0.09375
- cotangent: bfloat16 [8192, 4096], P('seq', 'chan'), may hold values from -6 to 6
Outputs:
- mixed: bfloat16 [8192, 4096], P('seq', 'chan')
- projected_grad: bfloat16 [8192, 3, 4096], P('seq', None, 'chan')
- filter_grad: float32 [512, 8192], P(('chan', 'seq'))
All inputs are finite; a program needn't handle non-finite values.
Results may differ from a plain program's by a relative error of at most 0.008.
Values may be sent and summed in bfloat16 or wider, within the bound.
No kernel may reach another device: no remote copies, remote signals or barrier semaphores. Data moves between devices by JAX's collectives and lax.ppermute only.
A program may use at most 64 MiB of HBM per device.

v0:
```python
import functools
import math

import jax
import jax.numpy as jnp
from jax import lax
from jax.experimental import pallas as pl
from jax.experimental.pallas import tpu as pltpu
from jax.sharding import Mesh, PartitionSpec as P


GROUP = 8
SHORT = 3
BLOCK = 256
HALF = 128
LAGS = 4
BUILD_UNROLL = 16

SEQ = ("z", "yl", "core")
CHAN = ("yh", "x")
F32 = jnp.float32
BF16 = jnp.bfloat16


def from_behind(shard, by):
    count = lax.axis_size(SEQ)
    pairs = [(i, i + by) for i in range(count) if 0 <= i + by < count]
    return lax.ppermute(shard, SEQ, pairs)


def swap(shard, axis):
    return lax.ppermute(shard, axis, [(0, 1), (1, 0)])


def gathered(shard, axes, count):
    copies = jnp.broadcast_to(shard[None], (count,) + shard.shape)
    return lax.all_to_all(copies, axes, split_axis=0, concat_axis=0, tiled=True)


def skew_masks():
    rows = lax.broadcasted_iota(jnp.int32, (HALF, HALF), 0)
    lanes = lax.broadcasted_iota(jnp.int32, (HALF, HALF), 1)
    return rows, lanes


def toeplitz_kernel(h_ref, tile_ref):
    groups, count, _ = h_ref.shape
    rows, lanes = skew_masks()
    inside = lanes >= rows
    for g in range(groups):
        tile_ref[g, 0] = jnp.zeros((HALF, HALF), BF16)

        def step(j, before, g=g):
            row = h_ref[g, pl.ds(j, 1), :]
            turned = pltpu.roll(jnp.broadcast_to(row, (HALF, HALF)), 0, 1, stride=1, stride_axis=0)
            tile_ref[g, j + 1] = jnp.where(inside, turned, before).astype(BF16)
            return turned

        lax.fori_loop(0, count, step, jnp.zeros((HALF, HALF), F32), unroll=BUILD_UNROLL)


def toeplitz_tiles(h):
    groups, count, _ = h.shape
    return pl.pallas_call(
        toeplitz_kernel,
        name="toeplitz_tiles",
        out_shape=jax.ShapeDtypeStruct((groups, count + 1, HALF, HALF), BF16),
        cost_estimate=pl.CostEstimate(flops=4000000, bytes_accessed=4500000, transcendentals=0),
    )(h)


def toeplitz_block(tile_ref, g, d):
    same = tile_ref[g, 2 * d + 1]
    upper = jnp.concatenate([same, tile_ref[g, 2 * d + 2]], axis=1)
    lower = jnp.concatenate([tile_ref[g, 2 * d], same], axis=1)
    return jnp.concatenate([upper, lower], axis=0)


def group_rows(ref, g):
    part = ref[...].astype(F32)[:, g * GROUP : (g + 1) * GROUP, :]
    return part.reshape(part.shape[0] * GROUP, BLOCK)


def conv_kernel(x_ref, tile_ref, y_ref, wide_ref, acc_ref):
    blocks, chans, _ = x_ref.shape
    total = blocks * GROUP
    parts = []
    for g in range(chans // GROUP):
        signal = group_rows(x_ref, g)
        for k in range(LAGS):
            late = signal
            if k > 0:
                late = jnp.concatenate(
                    [jnp.zeros((k * GROUP, BLOCK), F32), signal[: total - k * GROUP]], axis=0
                )
            wide_ref[:, k * BLOCK : (k + 1) * BLOCK] = late.astype(BF16)
        for d in range(0, blocks, LAGS):
            rows = total - d * GROUP
            weights = jnp.concatenate(
                [toeplitz_block(tile_ref, g, d + k) for k in range(LAGS)], axis=0
            )
            part = jnp.dot(wide_ref[:rows, :], weights, preferred_element_type=F32)
            if d == 0:
                acc_ref[...] = part
            else:
                acc_ref[d * GROUP :, :] += part
        parts.append(acc_ref[...].reshape(blocks, GROUP, BLOCK))
    y_ref[...] = jnp.concatenate(parts, axis=1).astype(BF16)


def back_kernel(m_ref, x_ref, tile_ref, y_ref, f_ref, wide_ref, acc_ref, low_ref, high_ref, *, scale):
    blocks, chans, _ = x_ref.shape
    total = blocks * GROUP
    rows_i, lanes_i = skew_masks()
    wrapped = lanes_i <= rows_i
    flip = (
        lax.broadcasted_iota(jnp.int32, (BLOCK, BLOCK), 0)
        + lax.broadcasted_iota(jnp.int32, (BLOCK, BLOCK), 1)
        == BLOCK - 1
    )
    flip = jnp.where(flip, 1.0, 0.0).astype(BF16)
    zero = jnp.zeros((HALF, HALF), F32)
    parts = []

    def fold(v):
        return v.reshape(HALF // 8, 8, HALF).sum(axis=0)

    def turned(cross, r, l):
        return pltpu.roll(
            cross[r * HALF : (r + 1) * HALF, l * HALF : (l + 1) * HALF], 1, 1, stride=1, stride_axis=0
        )

    for g in range(chans // GROUP):
        grad = group_rows(m_ref, g)
        wide_ref[total:, :] = jnp.zeros((wide_ref.shape[0] - total, LAGS * BLOCK), BF16)
        for k in range(LAGS):
            early = grad
            if k > 0:
                early = jnp.concatenate(
                    [grad[k * GROUP :], jnp.zeros((k * GROUP, BLOCK), F32)], axis=0
                )
            wide_ref[:total, k * BLOCK : (k + 1) * BLOCK] = early.astype(BF16)
        signal = group_rows(x_ref, g).astype(BF16)
        flipped = lax.dot_general(
            flip, signal, (((1,), (1,)), ((), ())), preferred_element_type=F32
        ).astype(BF16)
        high_ref[blocks] = jnp.zeros((8, BLOCK), F32)
        for d in range(0, blocks, LAGS):
            rows = total - d * GROUP
            weights = jnp.concatenate(
                [toeplitz_block(tile_ref, g, d + k) for k in range(LAGS)], axis=1
            )
            part = lax.dot_general(
                wide_ref[d * GROUP : total, :],
                weights,
                (((1,), (1,)), ((), ())),
                preferred_element_type=F32,
            )
            if d == 0:
                acc_ref[...] = part
            else:
                acc_ref[:rows, :] += part
            depth = total if 2 * d < blocks else total // 2
            cross_all = jnp.dot(
                flipped[:, :depth],
                wide_ref[d * GROUP : d * GROUP + depth, :],
                preferred_element_type=F32,
            )
            for k in range(LAGS):
                cross = cross_all[:, k * BLOCK : (k + 1) * BLOCK]
                s00, s01, s10, s11 = (turned(cross, r, l) for r in range(2) for l in range(2))
                low0 = jnp.where(wrapped, s01 + s10, s11)
                high0 = jnp.where(wrapped, zero, s00)
                low1 = jnp.where(wrapped, s11, zero)
                high1 = jnp.where(wrapped, s00, s01 + s10)
                low_ref[d + k] = jnp.concatenate([fold(low0), fold(low1)], axis=1)
                high_ref[d + k] = jnp.concatenate([fold(high0), fold(high1)], axis=1)
        parts.append(acc_ref[...].reshape(blocks, GROUP, BLOCK))
        f_ref[g] = (low_ref[...] + high_ref[pl.ds(1, blocks)]).sum(axis=1) * scale
    y_ref[...] = jnp.concatenate(parts, axis=1).astype(BF16)


def conv_forward(x, tiles):
    blocks = x.shape[0]
    total = blocks * GROUP
    return pl.pallas_call(
        conv_kernel,
        name="conv_forward",
        out_shape=jax.ShapeDtypeStruct(x.shape, BF16),
        scratch_shapes=[
            pltpu.VMEM((total, LAGS * BLOCK), BF16),
            pltpu.VMEM((total, BLOCK), F32),
        ],
        cost_estimate=pl.CostEstimate(flops=6000000000, bytes_accessed=600000, transcendentals=0),
    )(x, tiles)


def conv_backward(m, x, tiles):
    blocks, chans, _ = x.shape
    total = blocks * GROUP
    scale = 1.0 / math.sqrt(GROUP * blocks * BLOCK)
    return pl.pallas_call(
        functools.partial(back_kernel, scale=scale),
        name="conv_backward",
        out_shape=(
            jax.ShapeDtypeStruct(x.shape, BF16),
            jax.ShapeDtypeStruct((chans // GROUP, blocks, BLOCK), F32),
        ),
        scratch_shapes=[
            pltpu.VMEM((total + total // 2, LAGS * BLOCK), BF16),
            pltpu.VMEM((total, BLOCK), F32),
            pltpu.VMEM((blocks, 8, BLOCK), F32),
            pltpu.VMEM((blocks + 1, 8, BLOCK), F32),
        ],
        cost_estimate=pl.CostEstimate(flops=10000000000, bytes_accessed=1000000, transcendentals=0),
    )(m, x, tiles)


def whole_columns(core, own_ref, other_ref):
    first = core == 0
    own, other = own_ref[0], other_ref[0]
    return jnp.concatenate(
        [jnp.where(first, own, other), jnp.where(first, other, own)], axis=1
    )


def side_columns(side, width):
    return pl.ds(pl.multiple_of(side * width, width), width)


def grad_mm_kernel(
    at_ref, query_ref, cot0, cot1, cot2, cot3, own, own_c, side, side_c, out_ref, mixed_ref, sent_ref
):
    step = pl.program_id(0)
    yl, core = at_ref[0], at_ref[1]
    near = whole_columns(core, own, own_c)
    far = whole_columns(core, side, side_c)
    width = near.shape[1]

    def product(cot_ref, weights, at):
        return lax.dot_general(
            cot_ref[0, :, side_columns(at, width)],
            weights,
            (((1,), (1,)), ((), ())),
            preferred_element_type=F32,
        )

    @pl.when(step == 0)
    def _():
        out_ref[...] = jnp.zeros_like(out_ref)

    for k, cot_ref in enumerate((cot0, cot1, cot2, cot3)):

        @pl.when(step // 2 == k)
        def _(cot_ref=cot_ref):
            out_ref[...] += product(cot_ref, near, yl) + product(cot_ref, far, 1 - yl)

    @pl.when(step == pl.num_programs(0) - 1)
    def _():
        mixed = (out_ref[...] * query_ref[...]).astype(BF16)
        mixed_ref[...] = mixed
        sent_ref[...] = mixed.astype(F32).T.astype(BF16)


def own_turn(k):
    def index(i, q):
        return jnp.clip(i - 2 * k, 0, 1), 0, 0

    return index


def grad_matmul(at, query, cots, ws):
    _, tok, cols = cots[0].shape
    count, rows, width = ws[0].shape
    return pl.pallas_call(
        grad_mm_kernel,
        name="grad_matmul",
        out_shape=(
            jax.ShapeDtypeStruct((tok, rows), F32),
            jax.ShapeDtypeStruct((tok, rows), BF16),
            jax.ShapeDtypeStruct((rows, tok), BF16),
        ),
        grid_spec=pltpu.PrefetchScalarGridSpec(
            num_scalar_prefetch=1,
            grid=(count,),
            in_specs=[pl.BlockSpec((tok, rows), lambda i, q: (0, 0))]
            + [pl.BlockSpec((1, tok, cols), own_turn(k)) for k in range(len(cots))]
            + [pl.BlockSpec((1, rows, width), lambda i, q: (q[2 + i], 0, 0))] * len(ws),
            out_specs=(
                pl.BlockSpec((tok, rows), lambda i, q: (0, 0)),
                pl.BlockSpec((tok, rows), lambda i, q: (0, 0)),
                pl.BlockSpec((rows, tok), lambda i, q: (0, 0)),
            ),
        ),
        cost_estimate=pl.CostEstimate(flops=4000000000, bytes_accessed=6500000, transcendentals=0),
    )(at, query, *cots, *ws)


def mix_mm_kernel(
    at_ref, conv_ref, query_ref, carried_ref, skip_ref, own, own_c, side, side_c,
    out0, out1, out2, out3, mixed_ref, gated_ref,
):
    step = pl.program_id(0)
    yl, core = at_ref[0], at_ref[1]

    @pl.when(step == 0)
    def _():
        conv = conv_ref[...].astype(F32).T
        mixed_in = conv + skip_ref[...] * carried_ref[...].astype(F32)
        mixed_ref[...] = mixed_in
        gated_ref[...] = (query_ref[...] * mixed_in).astype(BF16)

    gated = gated_ref[...]
    near = whole_columns(core, own, own_c)
    far = whole_columns(core, side, side_c)
    width = near.shape[1]
    near = jnp.dot(gated, near, preferred_element_type=F32).astype(BF16)
    far = jnp.dot(gated, far, preferred_element_type=F32).astype(BF16)
    for k, out_ref in enumerate((out0, out1, out2, out3)):

        @pl.when(step // 2 == k)
        def _(out_ref=out_ref):
            out_ref[0, :, side_columns(yl, width)] = near
            out_ref[0, :, side_columns(1 - yl, width)] = far


def mix_matmul(at, conv, query, carried, skip, ws):
    tok, rows = query.shape
    count, _, width = ws[0].shape
    cols = len(ws) * width
    whole = pl.BlockSpec((tok, rows), lambda i, q: (0, 0))
    *parts, mixed_in = pl.pallas_call(
        mix_mm_kernel,
        name="mix_matmul",
        out_shape=(jax.ShapeDtypeStruct((2, tok, cols), BF16),) * (count // 2)
        + (jax.ShapeDtypeStruct((tok, rows), F32),),
        grid_spec=pltpu.PrefetchScalarGridSpec(
            num_scalar_prefetch=1,
            grid=(count,),
            in_specs=[
                pl.BlockSpec((rows, tok), lambda i, q: (0, 0)),
                whole,
                whole,
                pl.BlockSpec((1, rows), lambda i, q: (0, 0)),
            ]
            + [pl.BlockSpec((1, rows, width), lambda i, q: (q[2 + i], 0, 0))] * len(ws),
            out_specs=[pl.BlockSpec((1, tok, cols), own_turn(k)) for k in range(count // 2)]
            + [whole],
            scratch_shapes=[pltpu.VMEM((tok, rows), BF16)],
        ),
        cost_estimate=pl.CostEstimate(flops=4000000000, bytes_accessed=6500000, transcendentals=0),
    )(at, conv, query, carried, skip[None, :], *ws)
    return parts, mixed_in


def shift_x(shard, by):
    count = lax.axis_size("x")
    return lax.ppermute(shard, "x", [(i, (i + by) % count) for i in range(count)])


def pre_kernel(proj_ref, before_ref, taps_ref, query_ref, key_ref, value_ref, carried_ref, sent_ref):
    row = lax.broadcasted_iota(jnp.int32, proj_ref.shape[1:], 0)
    sides = []
    for i in range(3):
        now = proj_ref[i].astype(F32)
        before = before_ref[i].astype(F32)
        total = taps_ref[i, SHORT - 1 : SHORT, :] * now
        for j in range(1, SHORT):
            late = pltpu.roll(now, j, 0)
            for r in range(j):
                late = jnp.where(row == r, before[SHORT - 1 - j + r][None, :], late)
            total = total + taps_ref[i, SHORT - 1 - j : SHORT - j, :] * late
        sides.append(total)
    query_ref[...], key_ref[...], value_ref[...] = sides
    carried = (sides[1] * sides[2]).astype(BF16)
    carried_ref[...] = carried
    sent_ref[...] = carried.astype(F32).T.astype(BF16)


def short_forward(projected, before, taps):
    tok, _, cols = projected.shape
    side = jax.ShapeDtypeStruct((tok, cols), F32)
    return pl.pallas_call(
        pre_kernel,
        name="short_forward",
        out_shape=(
            side,
            side,
            side,
            jax.ShapeDtypeStruct((tok, cols), BF16),
            jax.ShapeDtypeStruct((cols, tok), BF16),
        ),
        cost_estimate=pl.CostEstimate(flops=5000000, bytes_accessed=3500000, transcendentals=0),
    )(projected.transpose(1, 0, 2), before.transpose(1, 0, 2), taps)


def channel_major(sent):
    count = lax.axis_size(SEQ)
    sent = sent.reshape(count, sent.shape[0] // count, sent.shape[1])
    return lax.all_to_all(sent, SEQ, split_axis=0, concat_axis=0, tiled=True)


def token_major(block):
    got = lax.all_to_all(block, SEQ, split_axis=0, concat_axis=0, tiled=True)
    return got.reshape(got.shape[0] * got.shape[1], got.shape[2])


def on_device(projected, short_weight, filters, skip, out_weight, cotangent):
    tok_rows, _ = cotangent.shape
    groups_dev, seq_length = filters.shape
    rim = SHORT - 1
    wide = lax.axis_size("x")
    yl, core = lax.axis_index("yl"), lax.axis_index("core")
    yh, x = lax.axis_index("yh"), lax.axis_index("x")
    steps = [(k, e) for k in range(wide) for e in range(2)]

    def scalars(sign):
        met = [((yh + e) % 2) * wide + (x + sign * k + wide) % wide for k, e in steps]
        return jnp.stack([yl, core] + met).astype(jnp.int32)

    before = from_behind(projected[tok_rows - rim :], 1)
    w_own = gathered(out_weight, "z", lax.axis_size("z"))
    cot_pair = jnp.stack([cotangent, swap(cotangent, "yh")])
    cots = [cot_pair] + [shift_x(cot_pair, k) for k in range(1, wide)]
    w_side = swap(w_own, "yl")
    w_own_other = swap(w_own, "core")
    w_side_other = swap(w_side, "core")
    ws = (w_own, w_own_other, w_side, w_side_other)

    tiles = toeplitz_tiles(filters.reshape(groups_dev, seq_length // HALF, HALF))
    query_side, key_side, value_side, carried, carried_sent = short_forward(
        projected, before, short_weight
    )
    carried_seq = channel_major(carried_sent)
    conv_seq = conv_forward(carried_seq, tiles)
    conv = token_major(conv_seq)

    gated_grad, mixed_grad, grad_sent = grad_matmul(scalars(-1), query_side, cots, ws)
    grad_seq = channel_major(grad_sent)

    parts, mixed_in = mix_matmul(scalars(1), conv, query_side, carried, skip, ws)
    shares = [parts[0]] + [shift_x(parts[k], k) for k in range(1, wide)]
    theirs = sum(p[1].astype(F32) for p in shares).astype(BF16)
    got = swap(theirs, "yh")
    mixed = (sum(p[0].astype(F32) for p in shares) + got.astype(F32)).astype(BF16)

    back_seq, filter_grad = conv_backward(grad_seq, carried_seq, tiles)
    back = token_major(back_seq).T
    query_grad = gated_grad * mixed_in
    carried_grad = back.astype(F32) + skip * mixed_grad.astype(F32)
    short_grad = jnp.stack([query_grad, carried_grad * value_side, carried_grad * key_side], axis=1)
    after = from_behind(short_grad[:rim], -1)
    extended_grad = jnp.concatenate([short_grad, after], axis=0)
    projected_grad = short_weight[:, 0, :] * extended_grad[rim : rim + tok_rows]
    for j in range(1, SHORT):
        projected_grad = (
            projected_grad
            + short_weight[:, j, :] * extended_grad[rim - j : rim - j + tok_rows]
        )
    return (mixed, projected_grad.astype(BF16), filter_grad.reshape(groups_dev, seq_length))


def solution(mesh):
    fine = Mesh(mesh.devices.reshape(8, 2, 2, 2, 4), ("z", "yl", "core", "yh", "x"))
    placed = (
        P(SEQ, None, CHAN),
        P(None, None, CHAN),
        P(CHAN + SEQ, None),
        P(CHAN),
        P(CHAN, SEQ),
        P(SEQ, CHAN),
    )
    return jax.shard_map(
        on_device,
        mesh=fine,
        in_specs=placed,
        out_specs=(P(SEQ, CHAN), P(SEQ, None, CHAN), P(CHAN + SEQ, None)),
        check_vma=False,
    )
```

profile of v0, /device:TPU:2, one launch (start us, length us, event | category | flops | bytes accessed | tf_op | source)
XLA Modules:
  0.0 178.6 jit_solution(15289578245249319821)
XLA Ops:
  0.6 1.0 broadcast_in_dim.5
  1.7 37.1 %all_to_all.25.own = bf16[8,512,128]{2,1,0:T(8,128)(2,1)S(1)} all-to-all(bf16[8,512,128]{2,1,0:T(8,128)(2,1)S(1)} %broadcast_in_dim.5), channel_id=1, replica_groups=mesh['z'=8,'yl'=2,'core'=2,'yh'=2,'x'=4] {'z'}, dimensions={0} | all-to-all | bytes 2097152 | tf_op jit(solution)/shard_map/all_to_all | solution.py:37
  38.8 1.6 collective-permute-start.2
  40.4 0.7 slice.45
  41.2 1.3 collective-permute-start
  42.4 0.8 collective-permute-done
  43.3 0.6 copy-done.18
  43.9 3.0 %short_forward.1 = (f32[256,512]{1,0:T(8,128)}, f32[256,512]{1,0:T(8,128)}, f32[256,512]{1,0:T(8,128)}, bf16[256,512]{1,0:T(8,128)(2,1)}, bf16[512,256]{1,0:T(8,128)(2,1)}) custom-call(bf16[3,256,512]{2,1,0:T(8,128)(2,1)} %bitcast.58, bf16[3,2,512]{2,1,0:T(2,128)(2,1)} %bitcast.69, f32[3,3,512]{2,1,0:T(4,128)} %taps_ref.1), custom_call_target="tpu_custom_call" | custom-call | flops 5000000 | bytes 3500000 | tf_op jit(solution)/shard_map/short_forward/pallas_call | solution.py:383
  46.8 21.7 %all-to-all-start = ((bf16[32,16,256]{2,1,0:T(8,128)(2,1)}), bf16[32,16,256]{2,1,0:T(8,128)(2,1)S(1)}, u32[]{:S(2)}, u32[]{:S(2)}) async-start(bf16[32,16,256]{2,1,0:T(8,128)(2,1)} %bitcast.60), calls=%async_computation | async-start | bytes 524288 | tf_op jit(solution)/shard_map/all_to_all | solution.py:400
  68.6 3.0 %collective-permute-start.8 = (bf16[256,512]{1,0:T(8,128)(2,1)S(1)}, bf16[256,512]{1,0:T(8,128)(2,1)S(1)}, u32[]{:S(2)}, u32[]{:S(2)}) collective-permute-start(bf16[256,512]{1,0:T(8,128)(2,1)S(1)} %copy-done.14), channel_id=1, source_target_pairs={{0,4},{4,0},{1,5},{5,1},{2,6},{6,2},{3,7},{7,3},{8,12},{12,8},{9,1... | collective-permute-start | bytes 786440 | tf_op jit(solution)/shard_map/ppermute | solution.py:32
  71.6 0.5 collective-permute-start.3
  72.1 0.6 copy.20
  72.7 4.6 %toeplitz_tiles.1.tile_ref = bf16[2,65,128,128]{3,2,1,0:T(8,128)(2,1)} custom-call(f32[2,64,128]{2,1,0:T(8,128)} %bitcast.59), custom_call_target="tpu_custom_call" | custom-call | flops 4000000 | bytes 4500000 | tf_op jit(solution)/shard_map/toeplitz_tiles/pallas_call | solution.py:64
  77.3 3.9 %collective-permute-done.8 = bf16[256,512]{1,0:T(8,128)(2,1)S(1)} collective-permute-done((bf16[256,512]{1,0:T(8,128)(2,1)S(1)}, bf16[256,512]{1,0:T(8,128)(2,1)S(1)}, u32[]{:S(2)}, u32[]{:S(2)}) %collective-permute-start.8) | collective-permute-done | bytes 262176 | tf_op jit(solution)/shard_map/ppermute | solution.py:32
  81.2 0.1 pad_maximum_fusion.2.cot0
  81.3 0.6 collective-permute-start.11
  81.9 2.4 %collective-permute-start.10 = (bf16[2,256,512]{2,1,0:T(8,128)(2,1)S(1)}, bf16[2,256,512]{2,1,0:T(8,128)(2,1)}, u32[]{:S(2)}, u32[]{:S(2)}) collective-permute-start(bf16[2,256,512]{2,1,0:T(8,128)(2,1)S(1)} %pad_maximum_fusion.2.cot0), channel_id=1, source_target_pairs={{0,2},{1,3},{2,0},{3,1},{4,6},{5,7},{6,4},{7,5},{8,10},{9,11},{10,... | collective-permute-start | bytes 1572872 | tf_op jit(solution)/shard_map/ppermute | solution.py:358
  84.3 1.8 %collective-permute-start.9 = (bf16[2,256,512]{2,1,0:T(8,128)(2,1)S(1)}, bf16[2,256,512]{2,1,0:T(8,128)(2,1)}, u32[]{:S(2)}, u32[]{:S(2)}) collective-permute-start(bf16[2,256,512]{2,1,0:T(8,128)(2,1)S(1)} %pad_maximum_fusion.2.cot0), channel_id=1, source_target_pairs={{0,1},{1,2},{2,3},{3,0},{4,5},{5,6},{6,7},{7,4},{8,9},{9,10},{10,1... | collective-permute-start | bytes 1572872 | tf_op jit(solution)/shard_map/ppermute | solution.py:358
  86.1 0.7 copy-done.11
  86.8 4.7 %conv_forward.1 = bf16[32,16,256]{2,1,0:T(8,128)(2,1)} custom-call(bf16[32,16,256]{2,1,0:T(8,128)(2,1)} %copy-done.11, bf16[2,65,128,128]{3,2,1,0:T(8,128)(2,1)} %toeplitz_tiles.1.tile_ref), custom_call_target="tpu_custom_call" | custom-call | flops 6000000000 | bytes 600000 | tf_op jit(solution)/shard_map/conv_forward/pallas_call | solution.py:186
  91.5 7.7 %all-to-all-start.1 = ((bf16[32,16,256]{2,1,0:T(8,128)(2,1)}), bf16[32,16,256]{2,1,0:T(8,128)(2,1)S(1)}, u32[]{:S(2)}, u32[]{:S(2)}) async-start(bf16[32,16,256]{2,1,0:T(8,128)(2,1)} %conv_forward.1), calls=%async_computation.1 | async-start | bytes 524288 | tf_op jit(solution)/shard_map/all_to_all | solution.py:404
  99.2 0.7 stack.96.at_ref
  99.9 0.6 stack.89.at_ref
  100.5 6.4 %collective-permute-done.10.cot2 = bf16[2,256,512]{2,1,0:T(8,128)(2,1)} collective-permute-done((bf16[2,256,512]{2,1,0:T(8,128)(2,1)S(1)}, bf16[2,256,512]{2,1,0:T(8,128)(2,1)}, u32[]{:S(2)}, u32[]{:S(2)}) %collective-permute-start.10) | collective-permute-done | bytes 524320 | tf_op jit(solution)/shard_map/ppermute | solution.py:358
  107.0 0.9 collective-permute-done.9.cot1
  107.9 9.7 %grad_matmul.1 = (f32[256,512]{1,0:T(8,128)}, bf16[256,512]{1,0:T(8,128)(2,1)}, bf16[512,256]{1,0:T(8,128)(2,1)}) custom-call(s32[10]{0:T(128)} %stack.96.at_ref, f32[256,512]{1,0:T(8,128)} %get-tuple-element.19.query_ref, bf16[2,256,512]{2,1,0:T(8,128)(2,1)} %copy-done.10, bf16[2,256,512]{2,1,0:T(8,128)(2,1)} %collective-permute-done.9.cot1, ...), custom_call_target="tpu_custom_call" | custom-call | flops 4000000000 | bytes 6500000 | tf_op jit(solution)/shard_map/grad_matmul/pallas_call | solution.py:275
  117.5 7.9 %all-to-all-start.3 = ((bf16[32,16,256]{2,1,0:T(8,128)(2,1)}), bf16[32,16,256]{2,1,0:T(8,128)(2,1)S(1)}, u32[]{:S(2)}, u32[]{:S(2)}) async-start(bf16[32,16,256]{2,1,0:T(8,128)(2,1)} %bitcast.62), calls=%async_computation.3 | async-start | bytes 524288 | tf_op jit(solution)/shard_map/all_to_all | solution.py:400
  125.5 9.1 %mix_matmul.1 = (bf16[2,256,512]{2,1,0:T(8,128)(2,1)}, bf16[2,256,512]{2,1,0:T(8,128)(2,1)}, bf16[2,256,512]{2,1,0:T(8,128)(2,1)}, bf16[2,256,512]{2,1,0:T(8,128)(2,1)}, f32[256,512]{1,0:T(8,128)}) custom-call(s32[10]{0:T(128)} %stack.89.at_ref, bf16[512,256]{1,0:T(8,128)(2,1)} %bitcast.61, f32[256,512]{1,0:T(8,128)} %get-tuple-element.19.query_ref, ...), custom_call_target="tpu_custom_call" | custom-call | flops 4000000000 | bytes 6500000 | tf_op jit(solution)/shard_map/mix_matmul/pallas_call | solution.py:332
  134.6 1.5 collective-permute-start.4
  136.1 3.3 %collective-permute-start.5 = (bf16[2,256,512]{2,1,0:T(8,128)(2,1)}, bf16[2,256,512]{2,1,0:T(8,128)(2,1)S(1)}, u32[]{:S(2)}, u32[]{:S(2)}) collective-permute-start(bf16[2,256,512]{2,1,0:T(8,128)(2,1)} %get-tuple-element.23), channel_id=1, source_target_pairs={{0,2},{1,3},{2,0},{3,1},{4,6},{5,7},{6,4},{7,5},{8,10},{9,11},{10,... | collective-permute-start | bytes 1572872 | tf_op jit(solution)/shard_map/ppermute | solution.py:358
  139.5 0.7 copy-done.13
  140.2 8.0 %conv_backward.1 = (bf16[32,16,256]{2,1,0:T(8,128)(2,1)}, f32[2,32,256]{2,1,0:T(8,128)}) custom-call(bf16[32,16,256]{2,1,0:T(8,128)(2,1)} %copy-done.13, bf16[32,16,256]{2,1,0:T(8,128)(2,1)} %copy-done.11, bf16[2,65,128,128]{3,2,1,0:T(8,128)(2,1)} %toeplitz_tiles.1.tile_ref), custom_call_target="tpu_custom_call" | custom-call | flops 10000000000 | bytes 1000000 | tf_op jit(solution)/shard_map/conv_backward/pallas_call | solution.py:202
  148.1 8.4 %all-to-all-start.4 = ((bf16[32,16,256]{2,1,0:T(8,128)(2,1)}), bf16[32,16,256]{2,1,0:T(8,128)(2,1)S(1)}, u32[]{:S(2)}, u32[]{:S(2)}) async-start(bf16[32,16,256]{2,1,0:T(8,128)(2,1)} %get-tuple-element.28), calls=%async_computation.4 | async-start | bytes 524288 | tf_op jit(solution)/shard_map/all_to_all | solution.py:404
  156.6 0.1 multiply_bitcast_fusion.2
  156.6 0.7 copy.15
  157.4 5.7 %collective-permute-done.6 = bf16[2,256,512]{2,1,0:T(8,128)(2,1)} collective-permute-done((bf16[2,256,512]{2,1,0:T(8,128)(2,1)}, bf16[2,256,512]{2,1,0:T(8,128)(2,1)}, u32[]{:S(2)}, u32[]{:S(2)}) %collective-permute-start.6) | collective-permute-done | bytes 524320 | tf_op jit(solution)/shard_map/ppermute | solution.py:358
  163.1 1.9 %fusion.4 = bf16[256,512]{1,0:T(8,128)(2,1)} fusion(bf16[2,256,512]{2,1,0:T(8,128)(2,1)} %collective-permute-done.6, bf16[2,256,512]{2,1,0:T(8,128)(2,1)S(1)} %collective-permute-done.5, bf16[2,256,512]{2,1,0:T(8,128)(2,1)S(1)} %collective-permute-done.4, bf16[2,256,512]{2,1,0:T(8,128)(2,1)S(1)} %copy-done.5), kind=kLoop, calls=%fused_computation.15 | loop fusion | flops 1048576 | bytes 1310720 | tf_op jit(solution)/shard_map/add | solution.py:443
  165.0 2.1 %collective-permute-start.7 = (bf16[256,512]{1,0:T(8,128)(2,1)}, bf16[256,512]{1,0:T(8,128)(2,1)}, u32[]{:S(2)}, u32[]{:S(2)}) collective-permute-start(bf16[256,512]{1,0:T(8,128)(2,1)} %fusion.4), channel_id=1, source_target_pairs={{0,4},{4,0},{1,5},{5,1},{2,6},{6,2},{3,7},{7,3},{8,12},{12,8},{9,1... | collective-permute-start | bytes 786440 | tf_op jit(solution)/shard_map/ppermute | solution.py:32
  167.1 1.8 %all-to-all-done.4 = bf16[32,16,256]{2,1,0:T(8,128)(2,1)S(1)} async-done(((bf16[32,16,256]{2,1,0:T(8,128)(2,1)}), bf16[32,16,256]{2,1,0:T(8,128)(2,1)S(1)}, u32[]{:S(2)}, u32[]{:S(2)}) %all-to-all-start.4) | async-done | bytes 262176 | tf_op jit(solution)/shard_map/all_to_all | solution.py:404
  168.9 0.1 bitcast_convert_fusion
  169.0 0.2 copy.10
  169.2 1.1 multiply_bitcast_fusion.1
  170.4 0.1 pad_maximum_fusion.1
  170.5 1.4 collective-permute-start.12
  171.9 3.1 %collective-permute-done.7 = bf16[256,512]{1,0:T(8,128)(2,1)} collective-permute-done((bf16[256,512]{1,0:T(8,128)(2,1)}, bf16[256,512]{1,0:T(8,128)(2,1)}, u32[]{:S(2)}, u32[]{:S(2)}) %collective-permute-start.7) | collective-permute-done | bytes 262176 | tf_op jit(solution)/shard_map/ppermute | solution.py:32
  175.1 1.9 %fusion.3 = bf16[256,512]{1,0:T(8,128)(2,1)} fusion(bf16[256,512]{1,0:T(8,128)(2,1)} %collective-permute-done.7, bf16[2,256,512]{2,1,0:T(8,128)(2,1)} %collective-permute-done.6, bf16[2,256,512]{2,1,0:T(8,128)(2,1)S(1)} %copy-done.9, bf16[2,256,512]{2,1,0:T(8,128)(2,1)S(1)} %copy-done.7, bf16[2,256,512]{2,1,0:T(8,128)(2,1)S(1)} %copy-done.5), kind=kLoop, calls=%fused_computation.10 | loop fusion | flops 1310720 | bytes 1572864 | tf_op jit(solution)/shard_map/convert_element_type | solution.py:445
  177.0 0.2 pad_maximum_fusion
  177.2 1.4 fusion.2
  (55 shorter events, 0.2 us)
Async XLA Ops:
  1.7 66.9 %copy-start.14 = (bf16[256,512]{1,0:T(8,128)(2,1)S(1)}, bf16[256,512]{1,0:T(8,128)(2,1)}, u32[]{:S(2)}) copy-start(bf16[256,512]{1,0:T(8,128)(2,1)} %param.11) | copy-start | bytes 786436
  1.7 70.4 %copy-start.16 = (f32[2,8192]{1,0:T(2,128)S(1)}, f32[2,8192]{1,0:T(2,128)}, u32[]{:S(2)}) copy-start(f32[2,8192]{1,0:T(2,128)} %param.8) | copy-start | bytes 196612
  38.8 38.5 %copy-start = (bf16[8,512,128]{2,1,0:T(8,128)(2,1)}, bf16[8,512,128]{2,1,0:T(8,128)(2,1)S(1)}, u32[]{:S(2)}) copy-start(bf16[8,512,128]{2,1,0:T(8,128)(2,1)S(1)} %all_to_all.25.own) | copy-start | bytes 3145732
  38.8 32.7 %collective-permute-start.2 = (bf16[8,512,128]{2,1,0:T(8,128)(2,1)S(1)}, bf16[8,512,128]{2,1,0:T(8,128)(2,1)S(1)}, u32[]{:S(2)}, u32[]{:S(2)}) collective-permute-start(bf16[8,512,128]{2,1,0:T(8,128)(2,1)S(1)} %all_to_all.25.own), channel_id=1, source_target_pairs={{0,16},{16,0},{1,17},{17,1},{2,18},{18,2},{3,19},{19,3},{4,20},{20... | collective-permute-start | bytes 3145736 | tf_op jit(solution)/shard_map/ppermute | solution.py:32
  41.2 2.1 %collective-permute-start = (bf16[2,3,512]{2,0,1:T(2,128)(2,1)S(1)}, bf16[2,3,512]{2,0,1:T(2,128)(2,1)S(1)}, u32[]{:S(2)}, u32[]{:S(2)}) collective-permute-start(bf16[2,3,512]{2,0,1:T(2,128)(2,1)S(1)} %slice.45), channel_id=1, source_target_pairs={{0,8},{8,16},{16,24},{24,32},{32,40},{40,48},{48,56},{56,64},{64,7... | collective-permute-start | bytes 18440 | tf_op jit(solution)/shard_map/ppermute | solution.py:28
  43.3 0.6 copy-start.18
  46.8 39.3 %all-to-all-start = ((bf16[32,16,256]{2,1,0:T(8,128)(2,1)}), bf16[32,16,256]{2,1,0:T(8,128)(2,1)S(1)}, u32[]{:S(2)}, u32[]{:S(2)}) async-start(bf16[32,16,256]{2,1,0:T(8,128)(2,1)} %bitcast.60), calls=%async_computation | async-start | bytes 524288 | tf_op jit(solution)/shard_map/all_to_all | solution.py:400
  68.6 12.6 %collective-permute-start.8 = (bf16[256,512]{1,0:T(8,128)(2,1)S(1)}, bf16[256,512]{1,0:T(8,128)(2,1)S(1)}, u32[]{:S(2)}, u32[]{:S(2)}) collective-permute-start(bf16[256,512]{1,0:T(8,128)(2,1)S(1)} %copy-done.14), channel_id=1, source_target_pairs={{0,4},{4,0},{1,5},{5,1},{2,6},{6,2},{3,7},{7,3},{8,12},{12,8},{9,1... | collective-permute-start | bytes 786440 | tf_op jit(solution)/shard_map/ppermute | solution.py:32
  71.5 36.3 %collective-permute-start.1 = (bf16[8,512,128]{2,1,0:T(8,128)(2,1)S(1)}, bf16[8,512,128]{2,1,0:T(8,128)(2,1)}, u32[]{:S(2)}, u32[]{:S(2)}) collective-permute-start(bf16[8,512,128]{2,1,0:T(8,128)(2,1)S(1)} %all_to_all.25.own), channel_id=1, source_target_pairs={{0,8},{8,0},{1,9},{9,1},{2,10},{10,2},{3,11},{11,3},{4,12},{12,4},... | collective-permute-start | bytes 3145736 | tf_op jit(solution)/shard_map/ppermute | solution.py:32
  71.6 5.7 %copy-start.20 = (bf16[8,512,128]{2,1,0:T(8,128)(2,1)}, bf16[8,512,128]{2,1,0:T(8,128)(2,1)S(1)}, u32[]{:S(2)}) copy-start(bf16[8,512,128]{2,1,0:T(8,128)(2,1)S(1)} %collective-permute-done.2.side) | copy-start | bytes 3145732
  71.6 36.3 %collective-permute-start.3 = (bf16[8,512,128]{2,1,0:T(8,128)(2,1)S(1)}, bf16[8,512,128]{2,1,0:T(8,128)(2,1)}, u32[]{:S(2)}, u32[]{:S(2)}) collective-permute-start(bf16[8,512,128]{2,1,0:T(8,128)(2,1)S(1)} %collective-permute-done.2.side), channel_id=1, source_target_pairs={{0,8},{8,0},{1,9},{9,1},{2,10},{10,2},{3,11},{11,3},{4,12},{12,4},... | collective-permute-start | bytes 3145736 | tf_op jit(solution)/shard_map/ppermute | solution.py:32
  81.2 10.2 %copy-start.10 = (bf16[2,256,512]{2,1,0:T(8,128)(2,1)}, bf16[2,256,512]{2,1,0:T(8,128)(2,1)S(1)}, u32[]{:S(2)}) copy-start(bf16[2,256,512]{2,1,0:T(8,128)(2,1)S(1)} %pad_maximum_fusion.2.cot0) | copy-start | bytes 1572868
  81.2 17.9 %copy-start.15 = (f32[3,3,512]{2,1,0:T(4,128)S(1)}, f32[3,3,512]{2,1,0:T(4,128)}, u32[]{:S(2)}) copy-start(f32[3,3,512]{2,1,0:T(4,128)} %taps_ref.1) | copy-start | bytes 55300
  81.3 19.3 %collective-permute-start.11 = (bf16[2,256,512]{2,1,0:T(8,128)(2,1)S(1)}, bf16[2,256,512]{2,1,0:T(8,128)(2,1)}, u32[]{:S(2)}, u32[]{:S(2)}) collective-permute-start(bf16[2,256,512]{2,1,0:T(8,128)(2,1)S(1)} %pad_maximum_fusion.2.cot0), channel_id=1, source_target_pairs={{0,3},{1,0},{2,1},{3,2},{4,7},{5,4},{6,5},{7,6},{8,11},{9,8},{10,9... | collective-permute-start | bytes 1572872 | tf_op jit(solution)/shard_map/ppermute | solution.py:358
  81.9 25.1 %collective-permute-start.10 = (bf16[2,256,512]{2,1,0:T(8,128)(2,1)S(1)}, bf16[2,256,512]{2,1,0:T(8,128)(2,1)}, u32[]{:S(2)}, u32[]{:S(2)}) collective-permute-start(bf16[2,256,512]{2,1,0:T(8,128)(2,1)S(1)} %pad_maximum_fusion.2.cot0), channel_id=1, source_target_pairs={{0,2},{1,3},{2,0},{3,1},{4,6},{5,7},{6,4},{7,5},{8,10},{9,11},{10,... | collective-permute-start | bytes 1572872 | tf_op jit(solution)/shard_map/ppermute | solution.py:358
  84.3 23.6 %collective-permute-start.9 = (bf16[2,256,512]{2,1,0:T(8,128)(2,1)S(1)}, bf16[2,256,512]{2,1,0:T(8,128)(2,1)}, u32[]{:S(2)}, u32[]{:S(2)}) collective-permute-start(bf16[2,256,512]{2,1,0:T(8,128)(2,1)S(1)} %pad_maximum_fusion.2.cot0), channel_id=1, source_target_pairs={{0,1},{1,2},{2,3},{3,0},{4,5},{5,6},{6,7},{7,4},{8,9},{9,10},{10,1... | collective-permute-start | bytes 1572872 | tf_op jit(solution)/shard_map/ppermute | solution.py:358
  86.1 0.7 copy-start.11
  91.5 26.0 %all-to-all-start.1 = ((bf16[32,16,256]{2,1,0:T(8,128)(2,1)}), bf16[32,16,256]{2,1,0:T(8,128)(2,1)S(1)}, u32[]{:S(2)}, u32[]{:S(2)}) async-start(bf16[32,16,256]{2,1,0:T(8,128)(2,1)} %conv_forward.1), calls=%async_computation.1 | async-start | bytes 524288 | tf_op jit(solution)/shard_map/all_to_all | solution.py:404
  117.5 8.0 %copy-start.12 = (bf16[32,16,256]{2,1,0:T(8,128)(2,1)}, bf16[32,16,256]{2,1,0:T(8,128)(2,1)S(1)}, u32[]{:S(2)}) copy-start(bf16[32,16,256]{2,1,0:T(8,128)(2,1)S(1)} %all-to-all-done.1) | copy-start | bytes 786436
  117.5 21.9 %all-to-all-start.3 = ((bf16[32,16,256]{2,1,0:T(8,128)(2,1)}), bf16[32,16,256]{2,1,0:T(8,128)(2,1)S(1)}, u32[]{:S(2)}, u32[]{:S(2)}) async-start(bf16[32,16,256]{2,1,0:T(8,128)(2,1)} %bitcast.62), calls=%async_computation.3 | async-start | bytes 524288 | tf_op jit(solution)/shard_map/all_to_all | solution.py:400
  134.6 22.8 %collective-permute-start.4 = (bf16[2,256,512]{2,1,0:T(8,128)(2,1)}, bf16[2,256,512]{2,1,0:T(8,128)(2,1)S(1)}, u32[]{:S(2)}, u32[]{:S(2)}) collective-permute-start(bf16[2,256,512]{2,1,0:T(8,128)(2,1)} %get-tuple-element.22), channel_id=1, source_target_pairs={{0,1},{1,2},{2,3},{3,0},{4,5},{5,6},{6,7},{7,4},{8,9},{9,10},{10,1... | collective-permute-start | bytes 1572872 | tf_op jit(solution)/shard_map/ppermute | solution.py:358
  136.1 21.2 %collective-permute-start.5 = (bf16[2,256,512]{2,1,0:T(8,128)(2,1)}, bf16[2,256,512]{2,1,0:T(8,128)(2,1)S(1)}, u32[]{:S(2)}, u32[]{:S(2)}) collective-permute-start(bf16[2,256,512]{2,1,0:T(8,128)(2,1)} %get-tuple-element.23), channel_id=1, source_target_pairs={{0,2},{1,3},{2,0},{3,1},{4,6},{5,7},{6,4},{7,5},{8,10},{9,11},{10,... | collective-permute-start | bytes 1572872 | tf_op jit(solution)/shard_map/ppermute | solution.py:358
  139.4 17.1 %copy-start.3 = (f32[256,512]{1,0:T(8,128)S(1)}, f32[256,512]{1,0:T(8,128)}, u32[]{:S(2)}) copy-start(f32[256,512]{1,0:T(8,128)} %get-tuple-element.25) | copy-start | bytes 1572868
  139.4 17.1 %copy-start.4 = (f32[256,512]{1,0:T(8,128)S(1)}, f32[256,512]{1,0:T(8,128)}, u32[]{:S(2)}) copy-start(f32[256,512]{1,0:T(8,128)} %get-tuple-element.26) | copy-start | bytes 1572868
  139.4 23.6 %collective-permute-start.6 = (bf16[2,256,512]{2,1,0:T(8,128)(2,1)}, bf16[2,256,512]{2,1,0:T(8,128)(2,1)}, u32[]{:S(2)}, u32[]{:S(2)}) collective-permute-start(bf16[2,256,512]{2,1,0:T(8,128)(2,1)} %get-tuple-element.24), channel_id=1, source_target_pairs={{0,3},{1,0},{2,1},{3,2},{4,7},{5,4},{6,5},{7,6},{8,11},{9,8},{10,9... | collective-permute-start | bytes 1572872 | tf_op jit(solution)/shard_map/ppermute | solution.py:358
  139.5 0.7 copy-start.13
  148.1 8.5 %copy-start.17 = (f32[2,32,256]{2,1,0:T(8,128)S(1)}, f32[2,32,256]{2,1,0:T(8,128)}, u32[]{:S(2)}) copy-start(f32[2,32,256]{2,1,0:T(8,128)} %get-tuple-element.32) | copy-start | bytes 196612
  148.1 15.0 %copy-start.5 = (bf16[2,256,512]{2,1,0:T(8,128)(2,1)S(1)}, bf16[2,256,512]{2,1,0:T(8,128)(2,1)}, u32[]{:S(2)}) copy-start(bf16[2,256,512]{2,1,0:T(8,128)(2,1)} %get-tuple-element.21) | copy-start | bytes 1572868
  148.1 20.8 %all-to-all-start.4 = ((bf16[32,16,256]{2,1,0:T(8,128)(2,1)}), bf16[32,16,256]{2,1,0:T(8,128)(2,1)S(1)}, u32[]{:S(2)}, u32[]{:S(2)}) async-start(bf16[32,16,256]{2,1,0:T(8,128)(2,1)} %get-tuple-element.28), calls=%async_computation.4 | async-start | bytes 524288 | tf_op jit(solution)/shard_map/all_to_all | solution.py:404
  157.3 11.6 %copy-start.6 = (bf16[2,256,512]{2,1,0:T(8,128)(2,1)}, bf16[2,256,512]{2,1,0:T(8,128)(2,1)S(1)}, u32[]{:S(2)}) copy-start(bf16[2,256,512]{2,1,0:T(8,128)(2,1)S(1)} %collective-permute-done.4) | copy-start | bytes 1572868
  157.3 9.8 %copy-start.8 = (bf16[2,256,512]{2,1,0:T(8,128)(2,1)}, bf16[2,256,512]{2,1,0:T(8,128)(2,1)S(1)}, u32[]{:S(2)}) copy-start(bf16[2,256,512]{2,1,0:T(8,128)(2,1)S(1)} %collective-permute-done.5) | copy-start | bytes 1572868
  163.1 6.1 %copy-start.1 = (f32[256,512]{1,0:T(8,128)S(1)}, f32[256,512]{1,0:T(8,128)}, u32[]{:S(2)}) copy-start(f32[256,512]{1,0:T(8,128)} %get-tuple-element.31) | copy-start | bytes 1572868
  163.1 6.1 %copy-start.2 = (f32[256,512]{1,0:T(8,128)S(1)}, f32[256,512]{1,0:T(8,128)}, u32[]{:S(2)}) copy-start(f32[256,512]{1,0:T(8,128)} %get-tuple-element.30) | copy-start | bytes 1572868
  163.1 6.1 %copy-start.19 = (f32[512]{0:T(512)S(1)}, f32[512]{0:T(512)}, u32[]{:S(2)}) copy-start(f32[512]{0:T(512)} %param.9) | copy-start | bytes 6148
  165.0 10.1 %collective-permute-start.7 = (bf16[256,512]{1,0:T(8,128)(2,1)}, bf16[256,512]{1,0:T(8,128)(2,1)}, u32[]{:S(2)}, u32[]{:S(2)}) collective-permute-start(bf16[256,512]{1,0:T(8,128)(2,1)} %fusion.4), channel_id=1, source_target_pairs={{0,4},{4,0},{1,5},{5,1},{2,6},{6,2},{3,7},{7,3},{8,12},{12,8},{9,1... | collective-permute-start | bytes 786440 | tf_op jit(solution)/shard_map/ppermute | solution.py:32
  170.4 4.7 %copy-start.7 = (bf16[2,256,512]{2,1,0:T(8,128)(2,1)S(1)}, bf16[2,256,512]{2,1,0:T(8,128)(2,1)}, u32[]{:S(2)}) copy-start(bf16[2,256,512]{2,1,0:T(8,128)(2,1)} %copy-done.6) | copy-start | bytes 1572868
  170.4 4.7 %copy-start.9 = (bf16[2,256,512]{2,1,0:T(8,128)(2,1)S(1)}, bf16[2,256,512]{2,1,0:T(8,128)(2,1)}, u32[]{:S(2)}) copy-start(bf16[2,256,512]{2,1,0:T(8,128)(2,1)} %copy-done.8) | copy-start | bytes 1572868
  170.5 6.5 %collective-permute-start.12 = (f32[2,3,512]{2,0,1:T(2,128)S(1)}, f32[2,3,512]{2,0,1:T(2,128)S(1)}, u32[]{:S(2)}, u32[]{:S(2)}) collective-permute-start(f32[2,3,512]{2,0,1:T(2,128)S(1)} %slice.66), channel_id=1, source_target_pairs={{8,0},{16,8},{24,16},{32,24},{40,32},{48,40},{56,48},{64,56},{72,6... | collective-permute-start | bytes 36872 | tf_op jit(solution)/shard_map/ppermute | solution.py:28
where the time goes:
time: 180 us; the launch traced here: 179 us
  starting transfers between devices  65.3 us (36%)
  Pallas kernels  39 us (22%)
  blocking collectives  37.1 us (21%)
  waiting for transfers between devices  22.7 us (13%)
  other arithmetic  6.78 us (4%)
  local copies, waits for them, and re-layouts  6.67 us (4%)
    all_to_all x1, blocking collectives, gathered(): return lax.all_to_all(copies, axes, split_axis=0, concat_axis=0, tiled=True)  37.1 us
    all_to_all x2, starting transfers between devices, channel_major(): return lax.all_to_all(sent, SEQ, split_axis=0, concat_axis=0, tiled=True)  29.6 us
    all_to_all x2, starting transfers between devices, token_major(): got = lax.all_to_all(block, SEQ, split_axis=0, concat_axis=0, tiled=True)  16.1 us
    ppermute x6, waiting for transfers between devices, shift_x(): lax.ppermute(shard, 'x', [(i, (i + by) % count) for i in range(count)])  13.1 us
    ppermute x6, starting transfers between devices, shift_x(): lax.ppermute(shard, 'x', [(i, (i + by) % count) for i in range(count)])  9.69 us
    pallas_call x1, Pallas kernels, grad_matmul(): pl.pallas_call(grad_mm_kernel, name='grad_matmul', out_shape=(jax.ShapeDt...  9.65 us
    pallas_call x1, Pallas kernels, mix_matmul(): pl.pallas_call(mix_mm_kernel, name='mix_matmul', out_shape=(jax.ShapeDtyp...  9.09 us
    pallas_call x1, Pallas kernels, conv_backward(): pl.pallas_call(functools.partial(back_kernel, scale=scale), name='conv_ba...  7.95 us
  transfers between devices with their start and end apart: 17, of which 7 were waited for; matrix products, arithmetic and copies ran while one was open for 5% of the time, Pallas kernels for 22%

commit v1 on v0

--- a/solution.py
+++ b/solution.py
@@ -14,6 +14,7 @@
 BLOCK = 256
 HALF = 128
 LAGS = 4
+WHALF = 4
 BUILD_UNROLL = 16
 
 SEQ = ("z", "yl", "core")
@@ -30,11 +31,6 @@
 
 def swap(shard, axis):
     return lax.ppermute(shard, axis, [(0, 1), (1, 0)])
-
-
-def gathered(shard, axes, count):
-    copies = jnp.broadcast_to(shard[None], (count,) + shard.shape)
-    return lax.all_to_all(copies, axes, split_axis=0, concat_axis=0, tiled=True)
 
 
 def skew_masks():
@@ -216,62 +212,61 @@
     )(m, x, tiles)
 
 
-def whole_columns(core, own_ref, other_ref):
-    first = core == 0
-    own, other = own_ref[0], other_ref[0]
-    return jnp.concatenate(
-        [jnp.where(first, own, other), jnp.where(first, other, own)], axis=1
-    )
+def whole_columns(at_ref, sign, step, refs):
+    own, own_c, side, side_c, own2, own_c2, side2, side_c2 = refs
+    first = at_ref[1] == 0
+    met = ((at_ref[2] + step) & 1) * 4 + ((at_ref[3] + sign * (step // 2) + 4) & 3)
+    place = (at_ref[4] - met + 9) & 7
+    early = place < WHALF
+    lo = jnp.minimum(place, WHALF - 1)
+    hi = jnp.maximum(place - WHALF, 0)
+
+    def pick(a, b):
+        return jnp.where(early, a[lo], b[hi])
+
+    parts = []
+    for a, b, c, d in ((own, own2, own_c, own_c2), (side, side2, side_c, side_c2)):
+        mine, other = pick(a, b), pick(c, d)
+        parts += [jnp.where(first, mine, other), jnp.where(first, other, mine)]
+    return jnp.concatenate(parts, axis=1)
 
 
 def side_columns(side, width):
     return pl.ds(pl.multiple_of(side * width, width), width)
 
 
-def grad_mm_kernel(
-    at_ref, query_ref, cot0, cot1, cot2, cot3, own, own_c, side, side_c, out_ref, mixed_ref, sent_ref
-):
-    step = pl.program_id(0)
-    yl, core = at_ref[0], at_ref[1]
-    near = whole_columns(core, own, own_c)
-    far = whole_columns(core, side, side_c)
-    width = near.shape[1]
-
-    def product(cot_ref, weights, at):
-        return lax.dot_general(
-            cot_ref[0, :, side_columns(at, width)],
-            weights,
+def grad_mm_kernel(at_ref, query_ref, cot0, cot1, cot2, cot3, *refs):
+    *w_refs, out_ref, mixed_ref, sent_ref = refs
+    yl = at_ref[0]
+    width = cot0.shape[2] // 2
+    for step in range(8):
+        cot_ref = (cot0, cot1, cot2, cot3)[step // 2]
+        e = step % 2
+        lhs = jnp.concatenate(
+            [cot_ref[e, :, side_columns(yl, width)], cot_ref[e, :, side_columns(1 - yl, width)]],
+            axis=1,
+        )
+        part = lax.dot_general(
+            lhs,
+            whole_columns(at_ref, -1, step, w_refs),
             (((1,), (1,)), ((), ())),
             preferred_element_type=F32,
         )
-
-    @pl.when(step == 0)
-    def _():
-        out_ref[...] = jnp.zeros_like(out_ref)
-
-    for k, cot_ref in enumerate((cot0, cot1, cot2, cot3)):
-
-        @pl.when(step // 2 == k)
-        def _(cot_ref=cot_ref):
-            out_ref[...] += product(cot_ref, near, yl) + product(cot_ref, far, 1 - yl)
-
-    @pl.when(step == pl.num_programs(0) - 1)
-    def _():
-        mixed = (out_ref[...] * query_ref[...]).astype(BF16)
-        mixed_ref[...] = mixed
-        sent_ref[...] = mixed.astype(F32).T.astype(BF16)
-
-
-def own_turn(k):
-    def index(i, q):
-        return jnp.clip(i - 2 * k, 0, 1), 0, 0
-
-    return index
+        if step == 0:
+            out_ref[...] = part
+        else:
+            out_ref[...] += part
+    mixed = (out_ref[...] * query_ref[...]).astype(BF16)
+    mixed_ref[...] = mixed
+    sent_ref[...] = mixed.astype(F32).T.astype(BF16)
+
+
+SCALARS = pl.BlockSpec(memory_space=pltpu.SMEM)
+WHOLE = pl.BlockSpec(memory_space=pltpu.VMEM)
 
 
 def grad_matmul(at, query, cots, ws):
-    _, tok, cols = cots[0].shape
-    count, rows, width = ws[0].shape
+    tok, rows = query.shape
     return pl.pallas_call(
         grad_mm_kernel,
         name="grad_matmul",
@@ -280,77 +275,48 @@
             jax.ShapeDtypeStruct((tok, rows), BF16),
             jax.ShapeDtypeStruct((rows, tok), BF16),
         ),
-        grid_spec=pltpu.PrefetchScalarGridSpec(
-            num_scalar_prefetch=1,
-            grid=(count,),
-            in_specs=[pl.BlockSpec((tok, rows), lambda i, q: (0, 0))]
-            + [pl.BlockSpec((1, tok, cols), own_turn(k)) for k in range(len(cots))]
-            + [pl.BlockSpec((1, rows, width), lambda i, q: (q[2 + i], 0, 0))] * len(ws),
-            out_specs=(
-                pl.BlockSpec((tok, rows), lambda i, q: (0, 0)),
-                pl.BlockSpec((tok, rows), lambda i, q: (0, 0)),
-                pl.BlockSpec((rows, tok), lambda i, q: (0, 0)),
-            ),
-        ),
+        in_specs=[SCALARS] + [WHOLE] * (1 + len(cots) + len(ws)),
+        out_specs=(WHOLE,) * 3,
         cost_estimate=pl.CostEstimate(flops=4000000000, bytes_accessed=6500000, transcendentals=0),
     )(at, query, *cots, *ws)
 
 
-def mix_mm_kernel(
-    at_ref, conv_ref, query_ref, carried_ref, skip_ref, own, own_c, side, side_c,
-    out0, out1, out2, out3, mixed_ref, gated_ref,
-):
-    step = pl.program_id(0)
-    yl, core = at_ref[0], at_ref[1]
-
-    @pl.when(step == 0)
-    def _():
-        conv = conv_ref[...].astype(F32).T
-        mixed_in = conv + skip_ref[...] * carried_ref[...].astype(F32)
-        mixed_ref[...] = mixed_in
-        gated_ref[...] = (query_ref[...] * mixed_in).astype(BF16)
-
-    gated = gated_ref[...]
-    near = whole_columns(core, own, own_c)
-    far = whole_columns(core, side, side_c)
-    width = near.shape[1]
-    near = jnp.dot(gated, near, preferred_element_type=F32).astype(BF16)
-    far = jnp.dot(gated, far, preferred_element_type=F32).astype(BF16)
-    for k, out_ref in enumerate((out0, out1, out2, out3)):
-
-        @pl.when(step // 2 == k)
-        def _(out_ref=out_ref):
-            out_ref[0, :, side_columns(yl, width)] = near
-            out_ref[0, :, side_columns(1 - yl, width)] = far
+def mix_mm_kernel(at_ref, conv_ref, query_ref, carried_ref, skip_ref, *refs):
+    *w_refs, out0, out1, out2, out3, mixed_ref = refs
+    yl = at_ref[0]
+    conv = conv_ref[...].astype(F32).T
+    mixed_in = conv + skip_ref[...] * carried_ref[...].astype(F32)
+    mixed_ref[...] = mixed_in
+    gated = (query_ref[...] * mixed_in).astype(BF16)
+    width = out0.shape[2] // 2
+    for step in range(8):
+        out_ref = (out0, out1, out2, out3)[step // 2]
+        e = step % 2
+        part = jnp.dot(
+            gated, whole_columns(at_ref, 1, step, w_refs), preferred_element_type=F32
+        ).astype(BF16)
+        out_ref[e, :, side_columns(yl, width)] = part[:, :width]
+        out_ref[e, :, side_columns(1 - yl, width)] = part[:, width:]
 
 
 def mix_matmul(at, conv, query, carried, skip, ws):
     tok, rows = query.shape
-    count, _, width = ws[0].shape
-    cols = len(ws) * width
-    whole = pl.BlockSpec((tok, rows), lambda i, q: (0, 0))
+    cols = 4 * ws[0].shape[2]
     *parts, mixed_in = pl.pallas_call(
         mix_mm_kernel,
         name="mix_matmul",
-        out_shape=(jax.ShapeDtypeStruct((2, tok, cols), BF16),) * (count // 2)
+        out_shape=(jax.ShapeDtypeStruct((2, tok, cols), BF16),) * 4
         + (jax.ShapeDtypeStruct((tok, rows), F32),),
-        grid_spec=pltpu.PrefetchScalarGridSpec(
-            num_scalar_prefetch=1,
-            grid=(count,),
-            in_specs=[
-                pl.BlockSpec((rows, tok), lambda i, q: (0, 0)),
-                whole,
-                whole,
-                pl.BlockSpec((1, rows), lambda i, q: (0, 0)),
-            ]
-            + [pl.BlockSpec((1, rows, width), lambda i, q: (q[2 + i], 0, 0))] * len(ws),
-            out_specs=[pl.BlockSpec((1, tok, cols), own_turn(k)) for k in range(count // 2)]
-            + [whole],
-            scratch_shapes=[pltpu.VMEM((tok, rows), BF16)],
-        ),
+        in_specs=[SCALARS] + [WHOLE] * (4 + len(ws)),
+        out_specs=(WHOLE,) * 5,
         cost_estimate=pl.CostEstimate(flops=4000000000, bytes_accessed=6500000, transcendentals=0),
     )(at, conv, query, carried, skip[None, :], *ws)
     return parts, mixed_in
+
+
+def shift_z(shard, by):
+    count = lax.axis_size("z")
+    return lax.ppermute(shard, "z", [(i, (i + by) % count) for i in range(count)])
 
 
 def shift_x(shard, by):
@@ -409,23 +375,25 @@
     tok_rows, _ = cotangent.shape
     groups_dev, seq_length = filters.shape
     rim = SHORT - 1
-    wide = lax.axis_size("x")
+    wide, deep = lax.axis_size("x"), lax.axis_size("z")
     yl, core = lax.axis_index("yl"), lax.axis_index("core")
-    yh, x = lax.axis_index("yh"), lax.axis_index("x")
-    steps = [(k, e) for k in range(wide) for e in range(2)]
-
-    def scalars(sign):
-        met = [((yh + e) % 2) * wide + (x + sign * k + wide) % wide for k, e in steps]
-        return jnp.stack([yl, core] + met).astype(jnp.int32)
-
+    yh, x, z = lax.axis_index("yh"), lax.axis_index("x"), lax.axis_index("z")
+
+    at = jnp.stack([yl, core, yh, x, z]).astype(jnp.int32)
     before = from_behind(projected[tok_rows - rim :], 1)
-    w_own = gathered(out_weight, "z", lax.axis_size("z"))
     cot_pair = jnp.stack([cotangent, swap(cotangent, "yh")])
     cots = [cot_pair] + [shift_x(cot_pair, k) for k in range(1, wide)]
+    w_own = jnp.stack(
+        [shift_z(out_weight, deep - 1), out_weight, shift_z(out_weight, 1), shift_z(out_weight, 2)]
+    )
+    w_own2 = jnp.stack([shift_z(out_weight, r) for r in range(3, deep - 1)])
     w_side = swap(w_own, "yl")
-    w_own_other = swap(w_own, "core")
-    w_side_other = swap(w_side, "core")
-    ws = (w_own, w_own_other, w_side, w_side_other)
+    w_side2 = swap(w_own2, "yl")
+    w_own_c = swap(w_own, "core")
+    w_side_c = swap(w_side, "core")
+    w_own_c2 = swap(w_own2, "core")
+    w_side_c2 = swap(w_side2, "core")
+    ws = (w_own, w_own_c, w_side, w_side_c, w_own2, w_own_c2, w_side2, w_side_c2)
 
     tiles = toeplitz_tiles(filters.reshape(groups_dev, seq_length // HALF, HALF))
     query_side, key_side, value_side, carried, carried_sent = short_forward(
@@ -435,10 +403,10 @@
     conv_seq = conv_forward(carried_seq, tiles)
     conv = token_major(conv_seq)
 
-    gated_grad, mixed_grad, grad_sent = grad_matmul(scalars(-1), query_side, cots, ws)
+    gated_grad, mixed_grad, grad_sent = grad_matmul(at, query_side, cots, ws)
     grad_seq = channel_major(grad_sent)
 
-    parts, mixed_in = mix_matmul(scalars(1), conv, query_side, carried, skip, ws)
+    parts, mixed_in = mix_matmul(at, conv, query_side, carried, skip, ws)
     shares = [parts[0]] + [shift_x(parts[k], k) for k in range(1, wide)]
     theirs = sum(p[1].astype(F32) for p in shares).astype(BF16)
     got = swap(theirs, "yh")

time: 180 us -> 167 us (0.928)
  blocking collectives: 37.1 us -> 0 us
  starting transfers between devices: 65.3 us -> 83.9 us
  waiting for transfers between devices: 22.7 us -> 36.7 us
  Pallas kernels: 39 us -> 30.6 us
    all_to_all x1 -> x0, blocking collectives: 37.1 us -> none  [gathered(): return lax.all_to_all(copies, axes, split_axis=0, concat_axis=0, tiled=True)]
    ppermute x0 -> x7, starting transfers between devices: none -> 18.8 us  [shift_z(): lax.ppermute(shard, 'z', [(i, (i + by) % count) for i in range(count)])]
    ppermute x0 -> x7, waiting for transfers between devices: none -> 10.9 us  [shift_z(): lax.ppermute(shard, 'z', [(i, (i + by) % count) for i in range(count)])]
    pallas_call x1, Pallas kernels: 9.65 us -> 5.27 us  [grad_matmul(): pl.pallas_call(grad_mm_kernel, name='grad_matmul', out_shape=(jax.ShapeDt...]
    pallas_call x1, Pallas kernels: 9.09 us -> 5.09 us  [mix_matmul(): pl.pallas_call(mix_mm_kernel, name='mix_matmul', out_shape=(jax.ShapeDtyp...]
    all_to_all x2, waiting for transfers between devices: 0.01 us -> 2.51 us  [channel_major(): return lax.all_to_all(sent, SEQ, split_axis=0, concat_axis=0, tiled=True)]
    all_to_all x2, starting transfers between devices: 16.1 us -> 13.6 us  [token_major(): got = lax.all_to_all(block, SEQ, split_axis=0, concat_axis=0, tiled=True)]
    ppermute x5 -> x8, starting transfers between devices: 7.21 us -> 8.99 us  [swap(): return lax.ppermute(shard, axis, [(0, 1), (1, 0)])]
  transfers between devices with their start and end apart: 17 -> 27, of which waited for: 7 -> 12; matrix products, arithmetic and copies ran while one was open for 5% -> 6% of each run, Pallas kernels for 22% -> 18%
where the time goes in v1:
time: 167 us; the launch traced here: 166 us
  starting transfers between devices  83.9 us (50%)
  waiting for transfers between devices  36.7 us (22%)
  Pallas kernels  30.6 us (18%)
  other arithmetic  7.83 us (5%)
  local copies, waits for them, and re-layouts  5.78 us (3%)
    all_to_all x2, starting transfers between devices, channel_major(): return lax.all_to_all(sent, SEQ, split_axis=0, concat_axis=0, tiled=True)  29.1 us
    ppermute x7, starting transfers between devices, shift_z(): lax.ppermute(shard, 'z', [(i, (i + by) % count) for i in range(count)])  18.8 us
    all_to_all x2, starting transfers between devices, token_major(): got = lax.all_to_all(block, SEQ, split_axis=0, concat_axis=0, tiled=True)  13.6 us
    ppermute x6, waiting for transfers between devices, shift_x(): lax.ppermute(shard, 'x', [(i, (i + by) % count) for i in range(count)])  13.2 us
    ppermute x7, waiting for transfers between devices, shift_z(): lax.ppermute(shard, 'z', [(i, (i + by) % count) for i in range(count)])  10.9 us
    ppermute x6, starting transfers between devices, shift_x(): lax.ppermute(shard, 'x', [(i, (i + by) % count) for i in range(count)])  9.59 us
    ppermute x8, starting transfers between devices, swap(): return lax.ppermute(shard, axis, [(0, 1), (1, 0)])  8.99 us
    pallas_call x1, Pallas kernels, conv_backward(): pl.pallas_call(functools.partial(back_kernel, scale=scale), name='conv_ba...  7.96 us
  transfers between devices with their start and end apart: 27, of which 12 were waited for; matrix products, arithmetic and copies ran while one was open for 6% of the time, Pallas kernels for 18%

profile of v1, /device:TPU:2, one launch (start us, length us, event | category | flops | bytes accessed | tf_op | source)
XLA Modules:
  0.0 165.8 jit_solution(5121806332076939199)
XLA Ops:
  0.6 7.3 %collective-permute-start.8 = (bf16[512,128]{1,0:T(8,128)(2,1)}, bf16[512,128]{1,0:T(8,128)(2,1)S(1)}, u32[]{:S(2)}, u32[]{:S(2)}) collective-permute-start(bf16[512,128]{1,0:T(8,128)(2,1)} %param.10), channel_id=1, source_target_pairs={{0,128},{32,160},{64,192},{96,224},{128,0},{160,32},{192,64},{224,... | collective-permute-start | bytes 393224 | tf_op jit(solution)/shard_map/ppermute | solution.py:319
  7.9 1.9 %collective-permute-start.7 = (bf16[512,128]{1,0:T(8,128)(2,1)}, bf16[512,128]{1,0:T(8,128)(2,1)S(1)}, u32[]{:S(2)}, u32[]{:S(2)}) collective-permute-start(bf16[512,128]{1,0:T(8,128)(2,1)} %param.10), channel_id=1, source_target_pairs={{0,96},{32,128},{64,160},{96,192},{128,224},{160,0},{192,32},{224,... | collective-permute-start | bytes 393224 | tf_op jit(solution)/shard_map/ppermute | solution.py:319
  9.8 2.7 %collective-permute-start.10 = (bf16[512,128]{1,0:T(8,128)(2,1)}, bf16[512,128]{1,0:T(8,128)(2,1)S(1)}, u32[]{:S(2)}, u32[]{:S(2)}) collective-permute-start(bf16[512,128]{1,0:T(8,128)(2,1)} %param.10), channel_id=1, source_target_pairs={{0,192},{32,224},{64,0},{96,32},{128,64},{160,96},{192,128},{224,1... | collective-permute-start | bytes 393224 | tf_op jit(solution)/shard_map/ppermute | solution.py:319
  12.9 2.9 %collective-permute-start.3 = (bf16[512,128]{1,0:T(8,128)(2,1)}, bf16[512,128]{1,0:T(8,128)(2,1)S(1)}, u32[]{:S(2)}, u32[]{:S(2)}) collective-permute-start(bf16[512,128]{1,0:T(8,128)(2,1)} %param.10), channel_id=1, source_target_pairs={{0,64},{32,96},{64,128},{96,160},{128,192},{160,224},{192,0},{224,... | collective-permute-start | bytes 393224 | tf_op jit(solution)/shard_map/ppermute | solution.py:319
  15.9 1.0 collective-permute-start.2
  16.9 5.9 %collective-permute-done.7 = bf16[512,128]{1,0:T(8,128)(2,1)S(1)} collective-permute-done((bf16[512,128]{1,0:T(8,128)(2,1)}, bf16[512,128]{1,0:T(8,128)(2,1)S(1)}, u32[]{:S(2)}, u32[]{:S(2)}) %collective-permute-start.7) | collective-permute-done | bytes 131104 | tf_op jit(solution)/shard_map/ppermute | solution.py:319
  22.8 2.5 %collective-permute-start.1 = (bf16[512,128]{1,0:T(8,128)(2,1)}, bf16[512,128]{1,0:T(8,128)(2,1)S(1)}, u32[]{:S(2)}, u32[]{:S(2)}) collective-permute-start(bf16[512,128]{1,0:T(8,128)(2,1)} %param.10), channel_id=1, source_target_pairs={{0,224},{32,0},{64,32},{96,64},{128,96},{160,128},{192,160},{224,1... | collective-permute-start | bytes 393224 | tf_op jit(solution)/shard_map/ppermute | solution.py:319
  25.3 3.8 %collective-permute-done.9 = bf16[512,128]{1,0:T(8,128)(2,1)S(1)} collective-permute-done((bf16[512,128]{1,0:T(8,128)(2,1)}, bf16[512,128]{1,0:T(8,128)(2,1)S(1)}, u32[]{:S(2)}, u32[]{:S(2)}) %collective-permute-start.9) | collective-permute-done | bytes 131104 | tf_op jit(solution)/shard_map/ppermute | solution.py:319
  29.2 1.7 %collective-permute-start.12 = (bf16[4,512,128]{2,1,0:T(8,128)(2,1)S(1)}, bf16[4,512,128]{2,1,0:T(8,128)(2,1)S(1)}, u32[]{:S(2)}, u32[]{:S(2)}) collective-permute-start(bf16[4,512,128]{2,1,0:T(8,128)(2,1)S(1)} %pad_maximum_fusion.3.refs_4_), channel_id=1, source_target_pairs={{0,16},{16,0},{1,17},{17,1},{2,18},{18,2},{3,19},{19,3},{4,20},{20... | collective-permute-start | bytes 1572872 | tf_op jit(solution)/shard_map/ppermute | solution.py:33
  31.3 0.7 collective-permute-done.1
  32.1 1.0 pad_maximum_fusion.2.refs_0_
  33.0 1.7 %collective-permute-start.5 = (bf16[4,512,128]{2,1,0:T(8,128)(2,1)S(1)}, bf16[4,512,128]{2,1,0:T(8,128)(2,1)}, u32[]{:S(2)}, u32[]{:S(2)}) collective-permute-start(bf16[4,512,128]{2,1,0:T(8,128)(2,1)S(1)} %pad_maximum_fusion.2.refs_0_), channel_id=1, source_target_pairs={{0,16},{16,0},{1,17},{17,1},{2,18},{18,2},{3,19},{19,3},{4,20},{20... | collective-permute-start | bytes 1572872 | tf_op jit(solution)/shard_map/ppermute | solution.py:33
  34.7 0.7 slice.45
  35.5 2.4 %collective-permute-start = (bf16[2,3,512]{2,0,1:T(2,128)(2,1)S(1)}, bf16[2,3,512]{2,0,1:T(2,128)(2,1)S(1)}, u32[]{:S(2)}, u32[]{:S(2)}) collective-permute-start(bf16[2,3,512]{2,0,1:T(2,128)(2,1)S(1)} %slice.45), channel_id=1, source_target_pairs={{0,8},{8,16},{16,24},{24,32},{32,40},{40,48},{48,56},{56,64},{64,7... | collective-permute-start | bytes 18440 | tf_op jit(solution)/shard_map/ppermute | solution.py:29
  37.9 0.8 collective-permute-done
  39.3 3.0 %short_forward.1 = (f32[256,512]{1,0:T(8,128)}, f32[256,512]{1,0:T(8,128)}, f32[256,512]{1,0:T(8,128)}, bf16[256,512]{1,0:T(8,128)(2,1)}, bf16[512,256]{1,0:T(8,128)(2,1)}) custom-call(bf16[3,256,512]{2,1,0:T(8,128)(2,1)} %bitcast.55, bf16[3,2,512]{2,1,0:T(2,128)(2,1)} %bitcast.74, f32[3,3,512]{2,1,0:T(4,128)} %taps_ref.1), custom_call_target="tpu_custom_call" | custom-call | flops 5000000 | bytes 3500000 | tf_op jit(solution)/shard_map/short_forward/pallas_call | solution.py:349
  42.3 21.2 %all-to-all-start = ((bf16[32,16,256]{2,1,0:T(8,128)(2,1)}), bf16[32,16,256]{2,1,0:T(8,128)(2,1)S(1)}, u32[]{:S(2)}, u32[]{:S(2)}) async-start(bf16[32,16,256]{2,1,0:T(8,128)(2,1)} %bitcast.57), calls=%async_computation | async-start | bytes 524288 | tf_op jit(solution)/shard_map/all_to_all | solution.py:366
  63.5 3.0 %collective-permute-start.18 = (bf16[256,512]{1,0:T(8,128)(2,1)S(1)}, bf16[256,512]{1,0:T(8,128)(2,1)S(1)}, u32[]{:S(2)}, u32[]{:S(2)}) collective-permute-start(bf16[256,512]{1,0:T(8,128)(2,1)S(1)} %copy-done.15), channel_id=1, source_target_pairs={{0,4},{4,0},{1,5},{5,1},{2,6},{6,2},{3,7},{7,3},{8,12},{12,8},{9,1... | collective-permute-start | bytes 786440 | tf_op jit(solution)/shard_map/ppermute | solution.py:33
  66.5 0.6 copy.20
  67.1 4.6 %toeplitz_tiles.1.tile_ref = bf16[2,65,128,128]{3,2,1,0:T(8,128)(2,1)} custom-call(f32[2,64,128]{2,1,0:T(8,128)} %bitcast.56), custom_call_target="tpu_custom_call" | custom-call | flops 4000000 | bytes 4500000 | tf_op jit(solution)/shard_map/toeplitz_tiles/pallas_call | solution.py:60
  71.7 4.4 %collective-permute-done.18 = bf16[256,512]{1,0:T(8,128)(2,1)S(1)} collective-permute-done((bf16[256,512]{1,0:T(8,128)(2,1)S(1)}, bf16[256,512]{1,0:T(8,128)(2,1)S(1)}, u32[]{:S(2)}, u32[]{:S(2)}) %collective-permute-start.18) | collective-permute-done | bytes 262176 | tf_op jit(solution)/shard_map/ppermute | solution.py:33
  76.8 2.4 %collective-permute-start.20 = (bf16[2,256,512]{2,1,0:T(8,128)(2,1)S(1)}, bf16[2,256,512]{2,1,0:T(8,128)(2,1)}, u32[]{:S(2)}, u32[]{:S(2)}) collective-permute-start(bf16[2,256,512]{2,1,0:T(8,128)(2,1)S(1)} %pad_maximum_fusion.4.cot0), channel_id=1, source_target_pairs={{0,2},{1,3},{2,0},{3,1},{4,6},{5,7},{6,4},{7,5},{8,10},{9,11},{10,... | collective-permute-start | bytes 1572872 | tf_op jit(solution)/shard_map/ppermute | solution.py:324
  79.2 1.8 %collective-permute-start.19 = (bf16[2,256,512]{2,1,0:T(8,128)(2,1)S(1)}, bf16[2,256,512]{2,1,0:T(8,128)(2,1)}, u32[]{:S(2)}, u32[]{:S(2)}) collective-permute-start(bf16[2,256,512]{2,1,0:T(8,128)(2,1)S(1)} %pad_maximum_fusion.4.cot0), channel_id=1, source_target_pairs={{0,1},{1,2},{2,3},{3,0},{4,5},{5,6},{6,7},{7,4},{8,9},{9,10},{10,1... | collective-permute-start | bytes 1572872 | tf_op jit(solution)/shard_map/ppermute | solution.py:324
  81.5 0.7 copy-done.12
  82.2 4.7 %conv_forward.1 = bf16[32,16,256]{2,1,0:T(8,128)(2,1)} custom-call(bf16[32,16,256]{2,1,0:T(8,128)(2,1)} %copy-done.12, bf16[2,65,128,128]{3,2,1,0:T(8,128)(2,1)} %toeplitz_tiles.1.tile_ref), custom_call_target="tpu_custom_call" | custom-call | flops 6000000000 | bytes 600000 | tf_op jit(solution)/shard_map/conv_forward/pallas_call | solution.py:182
  86.9 7.7 %all-to-all-start.1 = ((bf16[32,16,256]{2,1,0:T(8,128)(2,1)}), bf16[32,16,256]{2,1,0:T(8,128)(2,1)S(1)}, u32[]{:S(2)}, u32[]{:S(2)}) async-start(bf16[32,16,256]{2,1,0:T(8,128)(2,1)} %conv_forward.1), calls=%async_computation.1 | async-start | bytes 524288 | tf_op jit(solution)/shard_map/all_to_all | solution.py:370
  95.3 6.6 %collective-permute-done.20.cot2 = bf16[2,256,512]{2,1,0:T(8,128)(2,1)} collective-permute-done((bf16[2,256,512]{2,1,0:T(8,128)(2,1)S(1)}, bf16[2,256,512]{2,1,0:T(8,128)(2,1)}, u32[]{:S(2)}, u32[]{:S(2)}) %collective-permute-start.20) | collective-permute-done | bytes 524320 | tf_op jit(solution)/shard_map/ppermute | solution.py:324
  101.9 0.9 collective-permute-done.19.cot1
  102.8 0.8 copy-done.23
  103.6 5.3 %grad_matmul.1 = (f32[256,512]{1,0:T(8,128)}, bf16[256,512]{1,0:T(8,128)(2,1)}, bf16[512,256]{1,0:T(8,128)(2,1)}) custom-call(s32[5]{0:T(128)} %stack.74.at_ref, f32[256,512]{1,0:T(8,128)} %get-tuple-element.19.query_ref, bf16[2,256,512]{2,1,0:T(8,128)(2,1)} %copy-done.11, bf16[2,256,512]{2,1,0:T(8,128)(2,1)} %collective-permute-done.19.cot1, ...), custom_call_target="tpu_custom_call" | custom-call | flops 4000000000 | bytes 6500000 | tf_op jit(solution)/shard_map/grad_matmul/pallas_call | solution.py:270
  108.9 7.9 %all-to-all-start.2 = ((bf16[32,16,256]{2,1,0:T(8,128)(2,1)}), bf16[32,16,256]{2,1,0:T(8,128)(2,1)S(1)}, u32[]{:S(2)}, u32[]{:S(2)}) async-start(bf16[32,16,256]{2,1,0:T(8,128)(2,1)} %bitcast.59), calls=%async_computation.2 | async-start | bytes 524288 | tf_op jit(solution)/shard_map/all_to_all | solution.py:366
  116.8 5.1 %mix_matmul.1 = (bf16[2,256,512]{2,1,0:T(8,128)(2,1)}, bf16[2,256,512]{2,1,0:T(8,128)(2,1)}, bf16[2,256,512]{2,1,0:T(8,128)(2,1)}, bf16[2,256,512]{2,1,0:T(8,128)(2,1)}, f32[256,512]{1,0:T(8,128)}) custom-call(s32[5]{0:T(128)} %stack.74.at_ref, bf16[512,256]{1,0:T(8,128)(2,1)} %bitcast.58, f32[256,512]{1,0:T(8,128)} %get-tuple-element.19.query_ref, ...), custom_call_target="tpu_custom_call" | custom-call | flops 4000000000 | bytes 6500000 | tf_op jit(solution)/shard_map/mix_matmul/pallas_call | solution.py:305
  121.9 1.4 collective-permute-start.14
  123.4 3.3 %collective-permute-start.15 = (bf16[2,256,512]{2,1,0:T(8,128)(2,1)}, bf16[2,256,512]{2,1,0:T(8,128)(2,1)S(1)}, u32[]{:S(2)}, u32[]{:S(2)}) collective-permute-start(bf16[2,256,512]{2,1,0:T(8,128)(2,1)} %get-tuple-element.23), channel_id=1, source_target_pairs={{0,2},{1,3},{2,0},{3,1},{4,6},{5,7},{6,4},{7,5},{8,10},{9,11},{10,... | collective-permute-start | bytes 1572872 | tf_op jit(solution)/shard_map/ppermute | solution.py:324
  126.7 2.5 %all-to-all-done.2.m_ref = bf16[32,16,256]{2,1,0:T(8,128)(2,1)S(1)} async-done(((bf16[32,16,256]{2,1,0:T(8,128)(2,1)}), bf16[32,16,256]{2,1,0:T(8,128)(2,1)S(1)}, u32[]{:S(2)}, u32[]{:S(2)}) %all-to-all-start.2) | async-done | bytes 262176 | tf_op jit(solution)/shard_map/all_to_all | solution.py:366
  129.2 0.7 copy-done.14
  129.9 8.0 %conv_backward.1 = (bf16[32,16,256]{2,1,0:T(8,128)(2,1)}, f32[2,32,256]{2,1,0:T(8,128)}) custom-call(bf16[32,16,256]{2,1,0:T(8,128)(2,1)} %copy-done.14, bf16[32,16,256]{2,1,0:T(8,128)(2,1)} %copy-done.12, bf16[2,65,128,128]{3,2,1,0:T(8,128)(2,1)} %toeplitz_tiles.1.tile_ref), custom_call_target="tpu_custom_call" | custom-call | flops 10000000000 | bytes 1000000 | tf_op jit(solution)/shard_map/conv_backward/pallas_call | solution.py:198
  137.9 5.9 %all-to-all-start.3 = ((bf16[32,16,256]{2,1,0:T(8,128)(2,1)}), bf16[32,16,256]{2,1,0:T(8,128)(2,1)S(1)}, u32[]{:S(2)}, u32[]{:S(2)}) async-start(bf16[32,16,256]{2,1,0:T(8,128)(2,1)} %get-tuple-element.28), calls=%async_computation.3 | async-start | bytes 524288 | tf_op jit(solution)/shard_map/all_to_all | solution.py:370
  143.9 0.7 copy.15
  144.6 5.7 %collective-permute-done.16 = bf16[2,256,512]{2,1,0:T(8,128)(2,1)} collective-permute-done((bf16[2,256,512]{2,1,0:T(8,128)(2,1)}, bf16[2,256,512]{2,1,0:T(8,128)(2,1)}, u32[]{:S(2)}, u32[]{:S(2)}) %collective-permute-start.16) | collective-permute-done | bytes 524320 | tf_op jit(solution)/shard_map/ppermute | solution.py:324
  150.3 1.9 %fusion.4 = bf16[256,512]{1,0:T(8,128)(2,1)} fusion(bf16[2,256,512]{2,1,0:T(8,128)(2,1)} %collective-permute-done.16, bf16[2,256,512]{2,1,0:T(8,128)(2,1)S(1)} %collective-permute-done.15, bf16[2,256,512]{2,1,0:T(8,128)(2,1)S(1)} %collective-permute-done.14, bf16[2,256,512]{2,1,0:T(8,128)(2,1)S(1)} %copy-done.6), kind=kLoop, calls=%fused_computation.17 | loop fusion | flops 1048576 | bytes 1310720 | tf_op jit(solution)/shard_map/add | solution.py:411
  152.2 2.2 %collective-permute-start.17 = (bf16[256,512]{1,0:T(8,128)(2,1)}, bf16[256,512]{1,0:T(8,128)(2,1)}, u32[]{:S(2)}, u32[]{:S(2)}) collective-permute-start(bf16[256,512]{1,0:T(8,128)(2,1)} %fusion.4), channel_id=1, source_target_pairs={{0,4},{4,0},{1,5},{5,1},{2,6},{6,2},{3,7},{7,3},{8,12},{12,8},{9,1... | collective-permute-start | bytes 786440 | tf_op jit(solution)/shard_map/ppermute | solution.py:33
  154.4 1.8 %all-to-all-done.3 = bf16[32,16,256]{2,1,0:T(8,128)(2,1)S(1)} async-done(((bf16[32,16,256]{2,1,0:T(8,128)(2,1)}), bf16[32,16,256]{2,1,0:T(8,128)(2,1)S(1)}, u32[]{:S(2)}, u32[]{:S(2)}) %all-to-all-start.3) | async-done | bytes 262176 | tf_op jit(solution)/shard_map/all_to_all | solution.py:370
  156.5 1.1 multiply_bitcast_fusion.1
  157.8 1.4 collective-permute-start.22
  159.2 3.1 %collective-permute-done.17 = bf16[256,512]{1,0:T(8,128)(2,1)} collective-permute-done((bf16[256,512]{1,0:T(8,128)(2,1)}, bf16[256,512]{1,0:T(8,128)(2,1)}, u32[]{:S(2)}, u32[]{:S(2)}) %collective-permute-start.17) | collective-permute-done | bytes 262176 | tf_op jit(solution)/shard_map/ppermute | solution.py:33
  162.4 1.9 %fusion.3 = bf16[256,512]{1,0:T(8,128)(2,1)} fusion(bf16[256,512]{1,0:T(8,128)(2,1)} %collective-permute-done.17, bf16[2,256,512]{2,1,0:T(8,128)(2,1)} %collective-permute-done.16, bf16[2,256,512]{2,1,0:T(8,128)(2,1)S(1)} %copy-done.10, bf16[2,256,512]{2,1,0:T(8,128)(2,1)S(1)} %copy-done.8, bf16[2,256,512]{2,1,0:T(8,128)(2,1)S(1)} %copy-done.6), kind=kLoop, calls=%fused_computation.12 | loop fusion | flops 1310720 | bytes 1572864 | tf_op jit(solution)/shard_map/convert_element_type | solution.py:413
  164.4 1.4 fusion.2
  (80 shorter events, 4.1 us)
Async XLA Ops:
  0.6 15.2 %collective-permute-start.8 = (bf16[512,128]{1,0:T(8,128)(2,1)}, bf16[512,128]{1,0:T(8,128)(2,1)S(1)}, u32[]{:S(2)}, u32[]{:S(2)}) collective-permute-start(bf16[512,128]{1,0:T(8,128)(2,1)} %param.10), channel_id=1, source_target_pairs={{0,128},{32,160},{64,192},{96,224},{128,0},{160,32},{192,64},{224,... | collective-permute-start | bytes 393224 | tf_op jit(solution)/shard_map/ppermute | solution.py:319
  7.9 14.9 %collective-permute-start.7 = (bf16[512,128]{1,0:T(8,128)(2,1)}, bf16[512,128]{1,0:T(8,128)(2,1)S(1)}, u32[]{:S(2)}, u32[]{:S(2)}) collective-permute-start(bf16[512,128]{1,0:T(8,128)(2,1)} %param.10), channel_id=1, source_target_pairs={{0,96},{32,128},{64,160},{96,192},{128,224},{160,0},{192,32},{224,... | collective-permute-start | bytes 393224 | tf_op jit(solution)/shard_map/ppermute | solution.py:319
  9.8 15.5 %collective-permute-start.10 = (bf16[512,128]{1,0:T(8,128)(2,1)}, bf16[512,128]{1,0:T(8,128)(2,1)S(1)}, u32[]{:S(2)}, u32[]{:S(2)}) collective-permute-start(bf16[512,128]{1,0:T(8,128)(2,1)} %param.10), channel_id=1, source_target_pairs={{0,192},{32,224},{64,0},{96,32},{128,64},{160,96},{192,128},{224,1... | collective-permute-start | bytes 393224 | tf_op jit(solution)/shard_map/ppermute | solution.py:319
  12.5 16.6 %collective-permute-start.9 = (bf16[512,128]{1,0:T(8,128)(2,1)}, bf16[512,128]{1,0:T(8,128)(2,1)S(1)}, u32[]{:S(2)}, u32[]{:S(2)}) collective-permute-start(bf16[512,128]{1,0:T(8,128)(2,1)} %param.10), channel_id=1, source_target_pairs={{0,160},{32,192},{64,224},{96,0},{128,32},{160,64},{192,96},{224,1... | collective-permute-start | bytes 393224 | tf_op jit(solution)/shard_map/ppermute | solution.py:319
  12.9 17.9 %collective-permute-start.3 = (bf16[512,128]{1,0:T(8,128)(2,1)}, bf16[512,128]{1,0:T(8,128)(2,1)S(1)}, u32[]{:S(2)}, u32[]{:S(2)}) collective-permute-start(bf16[512,128]{1,0:T(8,128)(2,1)} %param.10), channel_id=1, source_target_pairs={{0,64},{32,96},{64,128},{96,160},{128,192},{160,224},{192,0},{224,... | collective-permute-start | bytes 393224 | tf_op jit(solution)/shard_map/ppermute | solution.py:319
  15.9 15.4 %collective-permute-start.2 = (bf16[512,128]{1,0:T(8,128)(2,1)}, bf16[512,128]{1,0:T(8,128)(2,1)S(1)}, u32[]{:S(2)}, u32[]{:S(2)}) collective-permute-start(bf16[512,128]{1,0:T(8,128)(2,1)} %param.10), channel_id=1, source_target_pairs={{0,32},{32,64},{64,96},{96,128},{128,160},{160,192},{192,224},{224... | collective-permute-start | bytes 393224 | tf_op jit(solution)/shard_map/ppermute | solution.py:319
  22.8 9.2 %collective-permute-start.1 = (bf16[512,128]{1,0:T(8,128)(2,1)}, bf16[512,128]{1,0:T(8,128)(2,1)S(1)}, u32[]{:S(2)}, u32[]{:S(2)}) collective-permute-start(bf16[512,128]{1,0:T(8,128)(2,1)} %param.10), channel_id=1, source_target_pairs={{0,224},{32,0},{64,32},{96,64},{128,96},{160,128},{192,160},{224,1... | collective-permute-start | bytes 393224 | tf_op jit(solution)/shard_map/ppermute | solution.py:319
  29.1 34.3 %copy-start.15 = (bf16[256,512]{1,0:T(8,128)(2,1)S(1)}, bf16[256,512]{1,0:T(8,128)(2,1)}, u32[]{:S(2)}) copy-start(bf16[256,512]{1,0:T(8,128)(2,1)} %param.11) | copy-start | bytes 786436
  29.1 37.3 %copy-start.17 = (f32[2,8192]{1,0:T(2,128)S(1)}, f32[2,8192]{1,0:T(2,128)}, u32[]{:S(2)}) copy-start(f32[2,8192]{1,0:T(2,128)} %param.8) | copy-start | bytes 196612
  29.2 42.5 %copy-start.4 = (bf16[4,512,128]{2,1,0:T(8,128)(2,1)}, bf16[4,512,128]{2,1,0:T(8,128)(2,1)S(1)}, u32[]{:S(2)}) copy-start(bf16[4,512,128]{2,1,0:T(8,128)(2,1)S(1)} %pad_maximum_fusion.3.refs_4_) | copy-start | bytes 1572868
  29.2 47.6 %collective-permute-start.12 = (bf16[4,512,128]{2,1,0:T(8,128)(2,1)S(1)}, bf16[4,512,128]{2,1,0:T(8,128)(2,1)S(1)}, u32[]{:S(2)}, u32[]{:S(2)}) collective-permute-start(bf16[4,512,128]{2,1,0:T(8,128)(2,1)S(1)} %pad_maximum_fusion.3.refs_4_), channel_id=1, source_target_pairs={{0,16},{16,0},{1,17},{17,1},{2,18},{18,2},{3,19},{19,3},{4,20},{20... | collective-permute-start | bytes 1572872 | tf_op jit(solution)/shard_map/ppermute | solution.py:33
  30.9 48.3 %collective-permute-start.11 = (bf16[4,512,128]{2,1,0:T(8,128)(2,1)S(1)}, bf16[4,512,128]{2,1,0:T(8,128)(2,1)S(1)}, u32[]{:S(2)}, u32[]{:S(2)}) collective-permute-start(bf16[4,512,128]{2,1,0:T(8,128)(2,1)S(1)} %pad_maximum_fusion.3.refs_4_), channel_id=1, source_target_pairs={{0,8},{8,0},{1,9},{9,1},{2,10},{10,2},{3,11},{11,3},{4,12},{12,4},... | collective-permute-start | bytes 1572872 | tf_op jit(solution)/shard_map/ppermute | solution.py:33
  33.0 38.7 %copy-start.5 = (bf16[4,512,128]{2,1,0:T(8,128)(2,1)}, bf16[4,512,128]{2,1,0:T(8,128)(2,1)S(1)}, u32[]{:S(2)}) copy-start(bf16[4,512,128]{2,1,0:T(8,128)(2,1)S(1)} %pad_maximum_fusion.2.refs_0_) | copy-start | bytes 1572868
  33.0 48.0 %collective-permute-start.5 = (bf16[4,512,128]{2,1,0:T(8,128)(2,1)S(1)}, bf16[4,512,128]{2,1,0:T(8,128)(2,1)}, u32[]{:S(2)}, u32[]{:S(2)}) collective-permute-start(bf16[4,512,128]{2,1,0:T(8,128)(2,1)S(1)} %pad_maximum_fusion.2.refs_0_), channel_id=1, source_target_pairs={{0,16},{16,0},{1,17},{17,1},{2,18},{18,2},{3,19},{19,3},{4,20},{20... | collective-permute-start | bytes 1572872 | tf_op jit(solution)/shard_map/ppermute | solution.py:33
  34.7 46.3 %collective-permute-start.4 = (bf16[4,512,128]{2,1,0:T(8,128)(2,1)S(1)}, bf16[4,512,128]{2,1,0:T(8,128)(2,1)}, u32[]{:S(2)}, u32[]{:S(2)}) collective-permute-start(bf16[4,512,128]{2,1,0:T(8,128)(2,1)S(1)} %pad_maximum_fusion.2.refs_0_), channel_id=1, source_target_pairs={{0,8},{8,0},{1,9},{9,1},{2,10},{10,2},{3,11},{11,3},{4,12},{12,4},... | collective-permute-start | bytes 1572872 | tf_op jit(solution)/shard_map/ppermute | solution.py:33
  35.5 3.2 %collective-permute-start = (bf16[2,3,512]{2,0,1:T(2,128)(2,1)S(1)}, bf16[2,3,512]{2,0,1:T(2,128)(2,1)S(1)}, u32[]{:S(2)}, u32[]{:S(2)}) collective-permute-start(bf16[2,3,512]{2,0,1:T(2,128)(2,1)S(1)} %slice.45), channel_id=1, source_target_pairs={{0,8},{8,16},{16,24},{24,32},{32,40},{40,48},{48,56},{56,64},{64,7... | collective-permute-start | bytes 18440 | tf_op jit(solution)/shard_map/ppermute | solution.py:29
  42.3 39.2 %all-to-all-start = ((bf16[32,16,256]{2,1,0:T(8,128)(2,1)}), bf16[32,16,256]{2,1,0:T(8,128)(2,1)S(1)}, u32[]{:S(2)}, u32[]{:S(2)}) async-start(bf16[32,16,256]{2,1,0:T(8,128)(2,1)} %bitcast.57), calls=%async_computation | async-start | bytes 524288 | tf_op jit(solution)/shard_map/all_to_all | solution.py:366
  63.5 12.6 %collective-permute-start.18 = (bf16[256,512]{1,0:T(8,128)(2,1)S(1)}, bf16[256,512]{1,0:T(8,128)(2,1)S(1)}, u32[]{:S(2)}, u32[]{:S(2)}) collective-permute-start(bf16[256,512]{1,0:T(8,128)(2,1)S(1)} %copy-done.15), channel_id=1, source_target_pairs={{0,4},{4,0},{1,5},{5,1},{2,6},{6,2},{3,7},{7,3},{8,12},{12,8},{9,1... | collective-permute-start | bytes 786440 | tf_op jit(solution)/shard_map/ppermute | solution.py:33
  76.1 10.8 %copy-start.11 = (bf16[2,256,512]{2,1,0:T(8,128)(2,1)}, bf16[2,256,512]{2,1,0:T(8,128)(2,1)S(1)}, u32[]{:S(2)}) copy-start(bf16[2,256,512]{2,1,0:T(8,128)(2,1)S(1)} %pad_maximum_fusion.4.cot0) | copy-start | bytes 1572868
  76.1 18.5 %copy-start.16 = (f32[3,3,512]{2,1,0:T(4,128)S(1)}, f32[3,3,512]{2,1,0:T(4,128)}, u32[]{:S(2)}) copy-start(f32[3,3,512]{2,1,0:T(4,128)} %taps_ref.1) | copy-start | bytes 55300
  76.2 19.1 %collective-permute-start.21 = (bf16[2,256,512]{2,1,0:T(8,128)(2,1)S(1)}, bf16[2,256,512]{2,1,0:T(8,128)(2,1)}, u32[]{:S(2)}, u32[]{:S(2)}) collective-permute-start(bf16[2,256,512]{2,1,0:T(8,128)(2,1)S(1)} %pad_maximum_fusion.4.cot0), channel_id=1, source_target_pairs={{0,3},{1,0},{2,1},{3,2},{4,7},{5,4},{6,5},{7,6},{8,11},{9,8},{10,9... | collective-permute-start | bytes 1572872 | tf_op jit(solution)/shard_map/ppermute | solution.py:324
  76.8 10.1 %copy-start.21 = (bf16[4,512,128]{2,1,0:T(8,128)(2,1)}, bf16[4,512,128]{2,1,0:T(8,128)(2,1)S(1)}, u32[]{:S(2)}) copy-start(bf16[4,512,128]{2,1,0:T(8,128)(2,1)S(1)} %collective-permute-done.12.refs_6_) | copy-start | bytes 1572868
  76.8 25.1 %collective-permute-start.20 = (bf16[2,256,512]{2,1,0:T(8,128)(2,1)S(1)}, bf16[2,256,512]{2,1,0:T(8,128)(2,1)}, u32[]{:S(2)}, u32[]{:S(2)}) collective-permute-start(bf16[2,256,512]{2,1,0:T(8,128)(2,1)S(1)} %pad_maximum_fusion.4.cot0), channel_id=1, source_target_pairs={{0,2},{1,3},{2,0},{3,1},{4,6},{5,7},{6,4},{7,5},{8,10},{9,11},{10,... | collective-permute-start | bytes 1572872 | tf_op jit(solution)/shard_map/ppermute | solution.py:324
  79.2 7.7 %copy-start.22 = (bf16[4,512,128]{2,1,0:T(8,128)(2,1)}, bf16[4,512,128]{2,1,0:T(8,128)(2,1)S(1)}, u32[]{:S(2)}) copy-start(bf16[4,512,128]{2,1,0:T(8,128)(2,1)S(1)} %collective-permute-done.11.refs_5_) | copy-start | bytes 1572868
  79.2 23.6 %collective-permute-start.19 = (bf16[2,256,512]{2,1,0:T(8,128)(2,1)S(1)}, bf16[2,256,512]{2,1,0:T(8,128)(2,1)}, u32[]{:S(2)}, u32[]{:S(2)}) collective-permute-start(bf16[2,256,512]{2,1,0:T(8,128)(2,1)S(1)} %pad_maximum_fusion.4.cot0), channel_id=1, source_target_pairs={{0,1},{1,2},{2,3},{3,0},{4,5},{5,6},{6,7},{7,4},{8,9},{9,10},{10,1... | collective-permute-start | bytes 1572872 | tf_op jit(solution)/shard_map/ppermute | solution.py:324
  81.0 21.8 %collective-permute-start.13 = (bf16[4,512,128]{2,1,0:T(8,128)(2,1)S(1)}, bf16[4,512,128]{2,1,0:T(8,128)(2,1)}, u32[]{:S(2)}, u32[]{:S(2)}) collective-permute-start(bf16[4,512,128]{2,1,0:T(8,128)(2,1)S(1)} %collective-permute-done.12.refs_6_), channel_id=1, source_target_pairs={{0,8},{8,0},{1,9},{9,1},{2,10},{10,2},{3,11},{11,3},{4,12},{12,4},... | collective-permute-start | bytes 1572872 | tf_op jit(solution)/shard_map/ppermute | solution.py:33
  81.0 21.8 %collective-permute-start.6 = (bf16[4,512,128]{2,1,0:T(8,128)(2,1)}, bf16[4,512,128]{2,1,0:T(8,128)(2,1)S(1)}, u32[]{:S(2)}, u32[]{:S(2)}) collective-permute-start(bf16[4,512,128]{2,1,0:T(8,128)(2,1)} %collective-permute-done.5.refs_2_), channel_id=1, source_target_pairs={{0,8},{8,0},{1,9},{9,1},{2,10},{10,2},{3,11},{11,3},{4,12},{12,4},... | collective-permute-start | bytes 1572872 | tf_op jit(solution)/shard_map/ppermute | solution.py:33
  86.9 22.0 %all-to-all-start.1 = ((bf16[32,16,256]{2,1,0:T(8,128)(2,1)}), bf16[32,16,256]{2,1,0:T(8,128)(2,1)S(1)}, u32[]{:S(2)}, u32[]{:S(2)}) async-start(bf16[32,16,256]{2,1,0:T(8,128)(2,1)} %conv_forward.1), calls=%async_computation.1 | async-start | bytes 524288 | tf_op jit(solution)/shard_map/all_to_all | solution.py:370
  102.8 0.8 copy-start.23
  108.9 8.0 %copy-start.13 = (bf16[32,16,256]{2,1,0:T(8,128)(2,1)}, bf16[32,16,256]{2,1,0:T(8,128)(2,1)S(1)}, u32[]{:S(2)}) copy-start(bf16[32,16,256]{2,1,0:T(8,128)(2,1)S(1)} %all-to-all-done.1) | copy-start | bytes 786436
  108.9 20.3 %all-to-all-start.2 = ((bf16[32,16,256]{2,1,0:T(8,128)(2,1)}), bf16[32,16,256]{2,1,0:T(8,128)(2,1)S(1)}, u32[]{:S(2)}, u32[]{:S(2)}) async-start(bf16[32,16,256]{2,1,0:T(8,128)(2,1)} %bitcast.59), calls=%async_computation.2 | async-start | bytes 524288 | tf_op jit(solution)/shard_map/all_to_all | solution.py:366
  121.9 22.7 %collective-permute-start.14 = (bf16[2,256,512]{2,1,0:T(8,128)(2,1)}, bf16[2,256,512]{2,1,0:T(8,128)(2,1)S(1)}, u32[]{:S(2)}, u32[]{:S(2)}) collective-permute-start(bf16[2,256,512]{2,1,0:T(8,128)(2,1)} %get-tuple-element.22), channel_id=1, source_target_pairs={{0,1},{1,2},{2,3},{3,0},{4,5},{5,6},{6,7},{7,4},{8,9},{9,10},{10,1... | collective-permute-start | bytes 1572872 | tf_op jit(solution)/shard_map/ppermute | solution.py:324
  123.4 21.2 %collective-permute-start.15 = (bf16[2,256,512]{2,1,0:T(8,128)(2,1)}, bf16[2,256,512]{2,1,0:T(8,128)(2,1)S(1)}, u32[]{:S(2)}, u32[]{:S(2)}) collective-permute-start(bf16[2,256,512]{2,1,0:T(8,128)(2,1)} %get-tuple-element.23), channel_id=1, source_target_pairs={{0,2},{1,3},{2,0},{3,1},{4,6},{5,7},{6,4},{7,5},{8,10},{9,11},{10,... | collective-permute-start | bytes 1572872 | tf_op jit(solution)/shard_map/ppermute | solution.py:324
  126.7 17.1 %copy-start.2 = (f32[256,512]{1,0:T(8,128)S(1)}, f32[256,512]{1,0:T(8,128)}, u32[]{:S(2)}) copy-start(f32[256,512]{1,0:T(8,128)} %get-tuple-element.25) | copy-start | bytes 1572868
  126.7 17.1 %copy-start.3 = (f32[256,512]{1,0:T(8,128)S(1)}, f32[256,512]{1,0:T(8,128)}, u32[]{:S(2)}) copy-start(f32[256,512]{1,0:T(8,128)} %get-tuple-element.26) | copy-start | bytes 1572868
  126.7 23.6 %collective-permute-start.16 = (bf16[2,256,512]{2,1,0:T(8,128)(2,1)}, bf16[2,256,512]{2,1,0:T(8,128)(2,1)}, u32[]{:S(2)}, u32[]{:S(2)}) collective-permute-start(bf16[2,256,512]{2,1,0:T(8,128)(2,1)} %get-tuple-element.24), channel_id=1, source_target_pairs={{0,3},{1,0},{2,1},{3,2},{4,7},{5,4},{6,5},{7,6},{8,11},{9,8},{10,9... | collective-permute-start | bytes 1572872 | tf_op jit(solution)/shard_map/ppermute | solution.py:324
  137.9 6.0 %copy-start.18 = (f32[2,32,256]{2,1,0:T(8,128)S(1)}, f32[2,32,256]{2,1,0:T(8,128)}, u32[]{:S(2)}) copy-start(f32[2,32,256]{2,1,0:T(8,128)} %get-tuple-element.32) | copy-start | bytes 196612
  137.9 12.5 %copy-start.6 = (bf16[2,256,512]{2,1,0:T(8,128)(2,1)S(1)}, bf16[2,256,512]{2,1,0:T(8,128)(2,1)}, u32[]{:S(2)}) copy-start(bf16[2,256,512]{2,1,0:T(8,128)(2,1)} %get-tuple-element.21) | copy-start | bytes 1572868
  137.9 18.3 %all-to-all-start.3 = ((bf16[32,16,256]{2,1,0:T(8,128)(2,1)}), bf16[32,16,256]{2,1,0:T(8,128)(2,1)S(1)}, u32[]{:S(2)}, u32[]{:S(2)}) async-start(bf16[32,16,256]{2,1,0:T(8,128)(2,1)} %get-tuple-element.28), calls=%async_computation.3 | async-start | bytes 524288 | tf_op jit(solution)/shard_map/all_to_all | solution.py:370
  144.6 11.6 %copy-start.7 = (bf16[2,256,512]{2,1,0:T(8,128)(2,1)}, bf16[2,256,512]{2,1,0:T(8,128)(2,1)S(1)}, u32[]{:S(2)}) copy-start(bf16[2,256,512]{2,1,0:T(8,128)(2,1)S(1)} %collective-permute-done.14) | copy-start | bytes 1572868
  144.6 9.8 %copy-start.9 = (bf16[2,256,512]{2,1,0:T(8,128)(2,1)}, bf16[2,256,512]{2,1,0:T(8,128)(2,1)S(1)}, u32[]{:S(2)}) copy-start(bf16[2,256,512]{2,1,0:T(8,128)(2,1)S(1)} %collective-permute-done.15) | copy-start | bytes 1572868
  150.3 6.1 %copy-start = (f32[256,512]{1,0:T(8,128)S(1)}, f32[256,512]{1,0:T(8,128)}, u32[]{:S(2)}) copy-start(f32[256,512]{1,0:T(8,128)} %get-tuple-element.31) | copy-start | bytes 1572868
  150.3 6.1 %copy-start.1 = (f32[256,512]{1,0:T(8,128)S(1)}, f32[256,512]{1,0:T(8,128)}, u32[]{:S(2)}) copy-start(f32[256,512]{1,0:T(8,128)} %get-tuple-element.30) | copy-start | bytes 1572868
  150.3 6.1 %copy-start.20 = (f32[512]{0:T(512)S(1)}, f32[512]{0:T(512)}, u32[]{:S(2)}) copy-start(f32[512]{0:T(512)} %param.9) | copy-start | bytes 6148
  152.2 10.1 %collective-permute-start.17 = (bf16[256,512]{1,0:T(8,128)(2,1)}, bf16[256,512]{1,0:T(8,128)(2,1)}, u32[]{:S(2)}, u32[]{:S(2)}) collective-permute-start(bf16[256,512]{1,0:T(8,128)(2,1)} %fusion.4), channel_id=1, source_target_pairs={{0,4},{4,0},{1,5},{5,1},{2,6},{6,2},{3,7},{7,3},{8,12},{12,8},{9,1... | collective-permute-start | bytes 786440 | tf_op jit(solution)/shard_map/ppermute | solution.py:33
  157.6 4.7 %copy-start.8 = (bf16[2,256,512]{2,1,0:T(8,128)(2,1)S(1)}, bf16[2,256,512]{2,1,0:T(8,128)(2,1)}, u32[]{:S(2)}) copy-start(bf16[2,256,512]{2,1,0:T(8,128)(2,1)} %copy-done.7) | copy-start | bytes 1572868
  157.6 4.7 %copy-start.10 = (bf16[2,256,512]{2,1,0:T(8,128)(2,1)S(1)}, bf16[2,256,512]{2,1,0:T(8,128)(2,1)}, u32[]{:S(2)}) copy-start(bf16[2,256,512]{2,1,0:T(8,128)(2,1)} %copy-done.9) | copy-start | bytes 1572868
  157.8 6.5 %collective-permute-start.22 = (f32[2,3,512]{2,0,1:T(2,128)S(1)}, f32[2,3,512]{2,0,1:T(2,128)S(1)}, u32[]{:S(2)}, u32[]{:S(2)}) collective-permute-start(f32[2,3,512]{2,0,1:T(2,128)S(1)} %slice.66), channel_id=1, source_target_pairs={{8,0},{16,8},{24,16},{32,24},{40,32},{48,40},{56,48},{64,56},{72,6... | collective-permute-start | bytes 36872 | tf_op jit(solution)/shard_map/ppermute | solution.py:29
  (3 other events, 2.0 us)

commit v2 on v1

--- a/solution.py
+++ b/solution.py
@@ -15,6 +15,7 @@
 HALF = 128
 LAGS = 4
 WHALF = 4
+SCRATCH = pltpu.CompilerParams(vmem_limit_bytes=24 << 20)
 BUILD_UNROLL = 16
 
 SEQ = ("z", "yl", "core")
@@ -40,27 +41,32 @@
 
 
 def toeplitz_kernel(h_ref, tile_ref):
-    groups, count, _ = h_ref.shape
+    groups, count = tile_ref.shape[0], tile_ref.shape[1] - 1
     rows, lanes = skew_masks()
     inside = lanes >= rows
+    zero = jnp.zeros((HALF, HALF), F32)
     for g in range(groups):
-        tile_ref[g, 0] = jnp.zeros((HALF, HALF), BF16)
-
-        def step(j, before, g=g):
-            row = h_ref[g, pl.ds(j, 1), :]
+        tile_ref[g, 0] = zero.astype(BF16)
+
+    def step(j, before):
+        turns = []
+        for g in range(groups):
+            row = h_ref[g : g + 1, pl.ds(pl.multiple_of(j * HALF, HALF), HALF)]
             turned = pltpu.roll(jnp.broadcast_to(row, (HALF, HALF)), 0, 1, stride=1, stride_axis=0)
-            tile_ref[g, j + 1] = jnp.where(inside, turned, before).astype(BF16)
-            return turned
-
-        lax.fori_loop(0, count, step, jnp.zeros((HALF, HALF), F32), unroll=BUILD_UNROLL)
+            tile_ref[g, j + 1] = jnp.where(inside, turned, before[g]).astype(BF16)
+            turns.append(turned)
+        return tuple(turns)
+
+    lax.fori_loop(0, count, step, (zero,) * groups, unroll=BUILD_UNROLL)
 
 
 def toeplitz_tiles(h):
-    groups, count, _ = h.shape
+    groups, length = h.shape
     return pl.pallas_call(
         toeplitz_kernel,
         name="toeplitz_tiles",
-        out_shape=jax.ShapeDtypeStruct((groups, count + 1, HALF, HALF), BF16),
+        out_shape=pltpu.VMEM((groups, length // HALF + 1, HALF, HALF), BF16),
+        compiler_params=SCRATCH,
         cost_estimate=pl.CostEstimate(flops=4000000, bytes_accessed=4500000, transcendentals=0),
     )(h)
 
@@ -187,8 +193,9 @@
             pltpu.VMEM((total, LAGS * BLOCK), BF16),
             pltpu.VMEM((total, BLOCK), F32),
         ],
+        compiler_params=SCRATCH,
         cost_estimate=pl.CostEstimate(flops=6000000000, bytes_accessed=600000, transcendentals=0),
-    )(x, tiles)
+    )(x, pltpu.with_memory_space_constraint(tiles, pltpu.VMEM))
 
 
 def conv_backward(m, x, tiles):
@@ -208,8 +215,9 @@
             pltpu.VMEM((blocks, 8, BLOCK), F32),
             pltpu.VMEM((blocks + 1, 8, BLOCK), F32),
         ],
+        compiler_params=SCRATCH,
         cost_estimate=pl.CostEstimate(flops=10000000000, bytes_accessed=1000000, transcendentals=0),
-    )(m, x, tiles)
+    )(m, x, pltpu.with_memory_space_constraint(tiles, pltpu.VMEM))
 
 
 def whole_columns(at_ref, sign, step, refs):
@@ -277,6 +285,7 @@
         ),
         in_specs=[SCALARS] + [WHOLE] * (1 + len(cots) + len(ws)),
         out_specs=(WHOLE,) * 3,
+        compiler_params=SCRATCH,
         cost_estimate=pl.CostEstimate(flops=4000000000, bytes_accessed=6500000, transcendentals=0),
     )(at, query, *cots, *ws)
 
@@ -309,6 +318,7 @@
         + (jax.ShapeDtypeStruct((tok, rows), F32),),
         in_specs=[SCALARS] + [WHOLE] * (4 + len(ws)),
         out_specs=(WHOLE,) * 5,
+        compiler_params=SCRATCH,
         cost_estimate=pl.CostEstimate(flops=4000000000, bytes_accessed=6500000, transcendentals=0),
     )(at, conv, query, carried, skip[None, :], *ws)
     return parts, mixed_in
@@ -356,6 +366,7 @@
             jax.ShapeDtypeStruct((tok, cols), BF16),
             jax.ShapeDtypeStruct((cols, tok), BF16),
         ),
+        compiler_params=SCRATCH,
         cost_estimate=pl.CostEstimate(flops=5000000, bytes_accessed=3500000, transcendentals=0),
     )(projected.transpose(1, 0, 2), before.transpose(1, 0, 2), taps)
 
@@ -395,7 +406,7 @@
     w_side_c2 = swap(w_side2, "core")
     ws = (w_own, w_own_c, w_side, w_side_c, w_own2, w_own_c2, w_side2, w_side_c2)
 
-    tiles = toeplitz_tiles(filters.reshape(groups_dev, seq_length // HALF, HALF))
+    tiles = toeplitz_tiles(filters)
     query_side, key_side, value_side, carried, carried_sent = short_forward(
         projected, before, short_weight
     )

time: 167 us -> 171 us (1.024)
  local copies, waits for them, and re-layouts: 5.78 us -> 17.4 us
  Pallas kernels: 30.6 us -> 19.4 us
  starting transfers between devices: 83.9 us -> 87.1 us
    unnamed x52 -> x49, local copies, waits for them, and re-layouts: 4.21 us -> 17.1 us
    pallas_call x1, Pallas kernels: 4.62 us -> 1.45 us  [toeplitz_tiles(): pl.pallas_call(toeplitz_kernel, name='toeplitz_tiles', out_shape=pltpu.VM...]
    all_to_all x2, starting transfers between devices: 13.6 us -> 16.2 us  [token_major(): got = lax.all_to_all(block, SEQ, split_axis=0, concat_axis=0, tiled=True)]
    all_to_all x2, waiting for transfers between devices: 2.51 us -> 0.01 us  [channel_major(): return lax.all_to_all(sent, SEQ, split_axis=0, concat_axis=0, tiled=True)]
    pallas_call x1, Pallas kernels: 4.68 us -> 2.37 us  [conv_forward(): pl.pallas_call(conv_kernel, name='conv_forward', out_shape=jax.ShapeDtype...]
  transfers between devices with their start and end apart: 27 -> 27, of which waited for: 12 -> 11; matrix products, arithmetic and copies ran while one was open for 6% -> 5% of each run, Pallas kernels for 18% -> 11%
where the time goes in v2:
time: 171 us; the launch traced here: 170 us
  starting transfers between devices  87.1 us (51%)
  waiting for transfers between devices  36 us (21%)
  Pallas kernels  19.4 us (11%)
  local copies, waits for them, and re-layouts  17.4 us (10%)
  other arithmetic  8.83 us (5%)
    all_to_all x2, starting transfers between devices, channel_major(): return lax.all_to_all(sent, SEQ, split_axis=0, concat_axis=0, tiled=True)  29.9 us
    ppermute x7, starting transfers between devices, shift_z(): lax.ppermute(shard, 'z', [(i, (i + by) % count) for i in range(count)])  18.8 us
    unnamed x49, local copies, waits for them, and re-layouts  17.1 us
    all_to_all x2, starting transfers between devices, token_major(): got = lax.all_to_all(block, SEQ, split_axis=0, concat_axis=0, tiled=True)  16.2 us
    ppermute x6, waiting for transfers between devices, shift_x(): lax.ppermute(shard, 'x', [(i, (i + by) % count) for i in range(count)])  12.7 us
    ppermute x7, waiting for transfers between devices, shift_z(): lax.ppermute(shard, 'z', [(i, (i + by) % count) for i in range(count)])  10.9 us
    ppermute x6, starting transfers between devices, shift_x(): lax.ppermute(shard, 'x', [(i, (i + by) % count) for i in range(count)])  9.59 us
    ppermute x8, starting transfers between devices, swap(): return lax.ppermute(shard, axis, [(0, 1), (1, 0)])  8.99 us
  transfers between devices with their start and end apart: 27, of which 11 were waited for; matrix products, arithmetic and copies ran while one was open for 5% of the time, Pallas kernels for 11%

profile of v2, /device:TPU:2, one launch (start us, length us, event | category | flops | bytes accessed | tf_op | source)
XLA Modules:
  0.0 169.6 jit_solution(16695273453400638819)
XLA Ops:
  0.7 7.3 %collective-permute-start.8 = (bf16[512,128]{1,0:T(8,128)(2,1)}, bf16[512,128]{1,0:T(8,128)(2,1)S(1)}, u32[]{:S(2)}, u32[]{:S(2)}) collective-permute-start(bf16[512,128]{1,0:T(8,128)(2,1)} %param.10), channel_id=1, source_target_pairs={{0,128},{32,160},{64,192},{96,224},{128,0},{160,32},{192,64},{224,... | collective-permute-start | bytes 393224 | tf_op jit(solution)/shard_map/ppermute | solution.py:329
  7.9 1.9 %collective-permute-start.7 = (bf16[512,128]{1,0:T(8,128)(2,1)}, bf16[512,128]{1,0:T(8,128)(2,1)S(1)}, u32[]{:S(2)}, u32[]{:S(2)}) collective-permute-start(bf16[512,128]{1,0:T(8,128)(2,1)} %param.10), channel_id=1, source_target_pairs={{0,96},{32,128},{64,160},{96,192},{128,224},{160,0},{192,32},{224,... | collective-permute-start | bytes 393224 | tf_op jit(solution)/shard_map/ppermute | solution.py:329
  9.9 2.7 %collective-permute-start.10 = (bf16[512,128]{1,0:T(8,128)(2,1)}, bf16[512,128]{1,0:T(8,128)(2,1)S(1)}, u32[]{:S(2)}, u32[]{:S(2)}) collective-permute-start(bf16[512,128]{1,0:T(8,128)(2,1)} %param.10), channel_id=1, source_target_pairs={{0,192},{32,224},{64,0},{96,32},{128,64},{160,96},{192,128},{224,1... | collective-permute-start | bytes 393224 | tf_op jit(solution)/shard_map/ppermute | solution.py:329
  13.0 2.9 %collective-permute-start.3 = (bf16[512,128]{1,0:T(8,128)(2,1)}, bf16[512,128]{1,0:T(8,128)(2,1)S(1)}, u32[]{:S(2)}, u32[]{:S(2)}) collective-permute-start(bf16[512,128]{1,0:T(8,128)(2,1)} %param.10), channel_id=1, source_target_pairs={{0,64},{32,96},{64,128},{96,160},{128,192},{160,224},{192,0},{224,... | collective-permute-start | bytes 393224 | tf_op jit(solution)/shard_map/ppermute | solution.py:329
  15.9 1.0 collective-permute-start.2
  16.9 5.9 %collective-permute-done.7 = bf16[512,128]{1,0:T(8,128)(2,1)S(1)} collective-permute-done((bf16[512,128]{1,0:T(8,128)(2,1)}, bf16[512,128]{1,0:T(8,128)(2,1)S(1)}, u32[]{:S(2)}, u32[]{:S(2)}) %collective-permute-start.7) | collective-permute-done | bytes 131104 | tf_op jit(solution)/shard_map/ppermute | solution.py:329
  22.8 2.5 %collective-permute-start.1 = (bf16[512,128]{1,0:T(8,128)(2,1)}, bf16[512,128]{1,0:T(8,128)(2,1)S(1)}, u32[]{:S(2)}, u32[]{:S(2)}) collective-permute-start(bf16[512,128]{1,0:T(8,128)(2,1)} %param.10), channel_id=1, source_target_pairs={{0,224},{32,0},{64,32},{96,64},{128,96},{160,128},{192,160},{224,1... | collective-permute-start | bytes 393224 | tf_op jit(solution)/shard_map/ppermute | solution.py:329
  25.3 3.8 %collective-permute-done.9 = bf16[512,128]{1,0:T(8,128)(2,1)S(1)} collective-permute-done((bf16[512,128]{1,0:T(8,128)(2,1)}, bf16[512,128]{1,0:T(8,128)(2,1)S(1)}, u32[]{:S(2)}, u32[]{:S(2)}) %collective-permute-start.9) | collective-permute-done | bytes 131104 | tf_op jit(solution)/shard_map/ppermute | solution.py:329
  29.2 1.7 collective-permute-start.12
  32.1 1.0 pad_maximum_fusion.2.refs_0_
  33.0 1.7 collective-permute-start.5
  34.7 2.4 %collective-permute-start = (bf16[2,3,512]{2,0,1:T(2,128)(2,1)S(1)}, bf16[2,3,512]{2,0,1:T(2,128)(2,1)S(1)}, u32[]{:S(2)}, u32[]{:S(2)}) collective-permute-start(bf16[2,3,512]{2,0,1:T(2,128)(2,1)S(1)} %slice.45), channel_id=1, source_target_pairs={{0,8},{8,16},{16,24},{24,32},{32,40},{40,48},{48,56},{56,64},{64,7... | collective-permute-start | bytes 18440 | tf_op jit(solution)/shard_map/ppermute | solution.py:30
  38.0 1.5 short_forward.1
  41.0 21.9 %all-to-all-start = ((bf16[32,16,256]{2,1,0:T(8,128)(2,1)}), bf16[32,16,256]{2,1,0:T(8,128)(2,1)S(1)}, u32[]{:S(2)}, u32[]{:S(2)}) async-start(bf16[32,16,256]{2,1,0:T(8,128)(2,1)} %bitcast.7), calls=%async_computation | async-start | bytes 524288 | tf_op jit(solution)/shard_map/all_to_all | solution.py:377
  62.9 3.0 %collective-permute-start.18 = (bf16[256,512]{1,0:T(8,128)(2,1)S(1)}, bf16[256,512]{1,0:T(8,128)(2,1)}, u32[]{:S(2)}, u32[]{:S(2)}) collective-permute-start(bf16[256,512]{1,0:T(8,128)(2,1)S(1)} %copy-done.21), channel_id=1, source_target_pairs={{0,4},{4,0},{1,5},{5,1},{2,6},{6,2},{3,7},{7,3},{8,12},{12,8},{9,1... | collective-permute-start | bytes 786440 | tf_op jit(solution)/shard_map/ppermute | solution.py:34
  65.8 1.4 toeplitz_tiles.1.tile_ref
  67.3 2.0 %copy-done = bf16[2,65,128,128]{3,2,1,0:T(8,128)(2,1)} copy-done((bf16[2,65,128,128]{3,2,1,0:T(8,128)(2,1)}, bf16[2,65,128,128]{3,2,1,0:T(8,128)(2,1)S(1)}, u32[]{:S(2)}) %copy-start) | copy-done | bytes 4259864
  69.3 6.3 %collective-permute-done.18 = bf16[256,512]{1,0:T(8,128)(2,1)} collective-permute-done((bf16[256,512]{1,0:T(8,128)(2,1)S(1)}, bf16[256,512]{1,0:T(8,128)(2,1)}, u32[]{:S(2)}, u32[]{:S(2)}) %collective-permute-start.18) | collective-permute-done | bytes 262176 | tf_op jit(solution)/shard_map/ppermute | solution.py:34
  75.6 1.0 pad_maximum_fusion.4.cot0
  77.2 2.4 %collective-permute-start.20 = (bf16[2,256,512]{2,1,0:T(8,128)(2,1)S(1)}, bf16[2,256,512]{2,1,0:T(8,128)(2,1)}, u32[]{:S(2)}, u32[]{:S(2)}) collective-permute-start(bf16[2,256,512]{2,1,0:T(8,128)(2,1)S(1)} %pad_maximum_fusion.4.cot0), channel_id=1, source_target_pairs={{0,2},{1,3},{2,0},{3,1},{4,6},{5,7},{6,4},{7,5},{8,10},{9,11},{10,... | collective-permute-start | bytes 1572872 | tf_op jit(solution)/shard_map/ppermute | solution.py:334
  79.6 1.8 %collective-permute-start.19 = (bf16[2,256,512]{2,1,0:T(8,128)(2,1)S(1)}, bf16[2,256,512]{2,1,0:T(8,128)(2,1)}, u32[]{:S(2)}, u32[]{:S(2)}) collective-permute-start(bf16[2,256,512]{2,1,0:T(8,128)(2,1)S(1)} %pad_maximum_fusion.4.cot0), channel_id=1, source_target_pairs={{0,1},{1,2},{2,3},{3,0},{4,5},{5,6},{6,7},{7,4},{8,9},{9,10},{10,1... | collective-permute-start | bytes 1572872 | tf_op jit(solution)/shard_map/ppermute | solution.py:334
  82.0 2.2 %copy-done.1 = bf16[2,65,128,128]{3,2,1,0:T(8,128)(2,1)S(1)} copy-done((bf16[2,65,128,128]{3,2,1,0:T(8,128)(2,1)S(1)}, bf16[2,65,128,128]{3,2,1,0:T(8,128)(2,1)}, u32[]{:S(2)}) %copy-start.1) | copy-done | bytes 4259864
  84.2 2.4 %conv_forward.1 = bf16[32,16,256]{2,1,0:T(8,128)(2,1)} custom-call(bf16[32,16,256]{2,1,0:T(8,128)(2,1)S(1)} %all-to-all-done.x_ref, bf16[2,65,128,128]{3,2,1,0:T(8,128)(2,1)S(1)} %copy-done.1), custom_call_target="tpu_custom_call" | custom-call | flops 6000000000 | bytes 600000 | tf_op jit(solution)/shard_map/conv_forward/pallas_call | solution.py:188
  86.5 7.8 %all-to-all-start.1 = ((bf16[32,16,256]{2,1,0:T(8,128)(2,1)}), bf16[32,16,256]{2,1,0:T(8,128)(2,1)}, u32[]{:S(2)}, u32[]{:S(2)}) async-start(bf16[32,16,256]{2,1,0:T(8,128)(2,1)} %conv_forward.1), calls=%async_computation.1 | async-start | bytes 524288 | tf_op jit(solution)/shard_map/all_to_all | solution.py:381
  94.5 7.8 %collective-permute-done.20.cot2 = bf16[2,256,512]{2,1,0:T(8,128)(2,1)} collective-permute-done((bf16[2,256,512]{2,1,0:T(8,128)(2,1)S(1)}, bf16[2,256,512]{2,1,0:T(8,128)(2,1)}, u32[]{:S(2)}, u32[]{:S(2)}) %collective-permute-start.20) | collective-permute-done | bytes 524320 | tf_op jit(solution)/shard_map/ppermute | solution.py:334
  102.3 0.9 collective-permute-done.19.cot1
  103.2 1.0 copy-done.13
  104.2 1.0 copy-done.16
  105.3 3.6 %grad_matmul.1 = (f32[256,512]{1,0:T(8,128)S(1)}, bf16[256,512]{1,0:T(8,128)(2,1)S(1)}, bf16[512,256]{1,0:T(8,128)(2,1)S(1)}) custom-call(s32[5]{0:T(128)S(1)} %stack.74.at_ref, f32[256,512]{1,0:T(8,128)S(1)} %copy-done.16, bf16[2,256,512]{2,1,0:T(8,128)(2,1)S(1)} %pad_maximum_fusion.4.cot0, bf16[2,256,512]{2,1,0:T(8,128)(2,1)} %collective-permute-done.19.cot1, ...), custom_call_target="tpu_custom_call" | custom-call | flops 4000000000 | bytes 6500000 | tf_op jit(solution)/shard_map/grad_matmul/pallas_call | solution.py:278
  109.6 8.1 %all-to-all-start.2 = ((bf16[32,16,256]{2,1,0:T(8,128)(2,1)}), bf16[32,16,256]{2,1,0:T(8,128)(2,1)}, u32[]{:S(2)}, u32[]{:S(2)}) async-start(bf16[32,16,256]{2,1,0:T(8,128)(2,1)} %bitcast.52), calls=%async_computation.2 | async-start | bytes 524288 | tf_op jit(solution)/shard_map/all_to_all | solution.py:377
  117.7 1.0 copy-done.14
  118.8 1.0 copy-done.17
  119.8 0.9 copy-done.19
  120.8 4.0 %mix_matmul.1 = (bf16[2,256,512]{2,1,0:T(8,128)(2,1)S(1)}, bf16[2,256,512]{2,1,0:T(8,128)(2,1)}, bf16[2,256,512]{2,1,0:T(8,128)(2,1)}, bf16[2,256,512]{2,1,0:T(8,128)(2,1)}, f32[256,512]{1,0:T(8,128)S(1)}) custom-call(s32[5]{0:T(128)S(1)} %stack.74.at_ref, bf16[512,256]{1,0:T(8,128)(2,1)} %bitcast.8.conv_ref, f32[256,512]{1,0:T(8,128)S(1)} %copy-done.17, ...), custom_call_target="tpu_custom_call" | custom-call | flops 4000000000 | bytes 6500000 | tf_op jit(solution)/shard_map/mix_matmul/pallas_call | solution.py:314
  125.6 1.4 collective-permute-start.14
  127.0 3.3 %collective-permute-start.15 = (bf16[2,256,512]{2,1,0:T(8,128)(2,1)}, bf16[2,256,512]{2,1,0:T(8,128)(2,1)}, u32[]{:S(2)}, u32[]{:S(2)}) collective-permute-start(bf16[2,256,512]{2,1,0:T(8,128)(2,1)} %get-tuple-element.23), channel_id=1, source_target_pairs={{0,2},{1,3},{2,0},{3,1},{4,6},{5,7},{6,4},{7,5},{8,10},{9,11},{10,... | collective-permute-start | bytes 1572872 | tf_op jit(solution)/shard_map/ppermute | solution.py:334
  130.3 2.2 %copy-done.2 = bf16[2,65,128,128]{3,2,1,0:T(8,128)(2,1)S(1)} copy-done((bf16[2,65,128,128]{3,2,1,0:T(8,128)(2,1)S(1)}, bf16[2,65,128,128]{3,2,1,0:T(8,128)(2,1)}, u32[]{:S(2)}) %copy-start.2) | copy-done | bytes 4259864
  132.5 0.9 copy-done.7
  133.5 6.5 %conv_backward.1 = (bf16[32,16,256]{2,1,0:T(8,128)(2,1)}, f32[2,32,256]{2,1,0:T(8,128)S(1)}) custom-call(bf16[32,16,256]{2,1,0:T(8,128)(2,1)} %all-to-all-done.2.m_ref, bf16[32,16,256]{2,1,0:T(8,128)(2,1)S(1)} %copy-done.7, bf16[2,65,128,128]{3,2,1,0:T(8,128)(2,1)S(1)} %copy-done.2), custom_call_target="tpu_custom_call" | custom-call | flops 10000000000 | bytes 1000000 | tf_op jit(solution)/shard_map/conv_backward/pallas_call | solution.py:205
  140.0 8.3 %all-to-all-start.3 = ((bf16[32,16,256]{2,1,0:T(8,128)(2,1)}), bf16[32,16,256]{2,1,0:T(8,128)(2,1)S(1)}, u32[]{:S(2)}, u32[]{:S(2)}) async-start(bf16[32,16,256]{2,1,0:T(8,128)(2,1)} %get-tuple-element.28), calls=%async_computation.3 | async-start | bytes 524288 | tf_op jit(solution)/shard_map/all_to_all | solution.py:381
  149.9 4.0 %collective-permute-done.16 = bf16[2,256,512]{2,1,0:T(8,128)(2,1)} collective-permute-done((bf16[2,256,512]{2,1,0:T(8,128)(2,1)}, bf16[2,256,512]{2,1,0:T(8,128)(2,1)}, u32[]{:S(2)}, u32[]{:S(2)}) %collective-permute-start.16) | collective-permute-done | bytes 524320 | tf_op jit(solution)/shard_map/ppermute | solution.py:334
  153.9 1.9 %fusion.4 = bf16[256,512]{1,0:T(8,128)(2,1)} fusion(bf16[2,256,512]{2,1,0:T(8,128)(2,1)} %collective-permute-done.16, bf16[2,256,512]{2,1,0:T(8,128)(2,1)} %collective-permute-done.15, bf16[2,256,512]{2,1,0:T(8,128)(2,1)} %collective-permute-done.14, bf16[2,256,512]{2,1,0:T(8,128)(2,1)S(1)} %copy-done.5), kind=kLoop, calls=%fused_computation.17 | loop fusion | flops 1048576 | bytes 1310720 | tf_op jit(solution)/shard_map/add | solution.py:422
  155.8 2.2 %collective-permute-start.17 = (bf16[256,512]{1,0:T(8,128)(2,1)}, bf16[256,512]{1,0:T(8,128)(2,1)}, u32[]{:S(2)}, u32[]{:S(2)}) collective-permute-start(bf16[256,512]{1,0:T(8,128)(2,1)} %fusion.4), channel_id=1, source_target_pairs={{0,4},{4,0},{1,5},{5,1},{2,6},{6,2},{3,7},{7,3},{8,12},{12,8},{9,1... | collective-permute-start | bytes 786440 | tf_op jit(solution)/shard_map/ppermute | solution.py:34
  158.0 2.7 %all-to-all-done.3 = bf16[32,16,256]{2,1,0:T(8,128)(2,1)S(1)} async-done(((bf16[32,16,256]{2,1,0:T(8,128)(2,1)}), bf16[32,16,256]{2,1,0:T(8,128)(2,1)S(1)}, u32[]{:S(2)}, u32[]{:S(2)}) %all-to-all-start.3) | async-done | bytes 262176 | tf_op jit(solution)/shard_map/all_to_all | solution.py:381
  162.1 1.3 collective-permute-start.22
  163.4 2.5 %collective-permute-done.17 = bf16[256,512]{1,0:T(8,128)(2,1)} collective-permute-done((bf16[256,512]{1,0:T(8,128)(2,1)}, bf16[256,512]{1,0:T(8,128)(2,1)}, u32[]{:S(2)}, u32[]{:S(2)}) %collective-permute-start.17) | collective-permute-done | bytes 262176 | tf_op jit(solution)/shard_map/ppermute | solution.py:34
  166.0 2.1 %fusion.3 = bf16[256,512]{1,0:T(8,128)(2,1)} fusion(bf16[256,512]{1,0:T(8,128)(2,1)} %collective-permute-done.17, bf16[2,256,512]{2,1,0:T(8,128)(2,1)} %collective-permute-done.16, bf16[2,256,512]{2,1,0:T(8,128)(2,1)} %collective-permute-done.15, bf16[2,256,512]{2,1,0:T(8,128)(2,1)} %collective-permute-done.14, bf16[2,256,512]{2,1,0:T(8,128)(2,1)S(1)} %copy-done.5), kind=kLoop, calls=%fused_computation.12 | loop fusion | flops 1310720 | bytes 1572864 | tf_op jit(solution)/shard_map/convert_element_type | solution.py:424
  168.2 1.4 fusion.2
  (77 shorter events, 10.0 us)
Async XLA Ops:
  0.6 34.1 %copy-start.3 = (bf16[256,3,512]{2,0,1:T(8,128)(2,1)S(1)}, bf16[256,3,512]{2,0,1:T(8,128)(2,1)}, u32[]{:S(2)}) copy-start(bf16[256,3,512]{2,0,1:T(8,128)(2,1)} %param.6) | copy-start | bytes 2359300
  0.6 37.3 %copy-start.9 = (f32[3,3,512]{2,1,0:T(4,128)S(1)}, f32[3,3,512]{2,1,0:T(4,128)}, u32[]{:S(2)}) copy-start(f32[3,3,512]{2,1,0:T(4,128)} %taps_ref.1) | copy-start | bytes 55300
  0.7 15.2 %collective-permute-start.8 = (bf16[512,128]{1,0:T(8,128)(2,1)}, bf16[512,128]{1,0:T(8,128)(2,1)S(1)}, u32[]{:S(2)}, u32[]{:S(2)}) collective-permute-start(bf16[512,128]{1,0:T(8,128)(2,1)} %param.10), channel_id=1, source_target_pairs={{0,128},{32,160},{64,192},{96,224},{128,0},{160,32},{192,64},{224,... | collective-permute-start | bytes 393224 | tf_op jit(solution)/shard_map/ppermute | solution.py:329
  7.9 14.9 %collective-permute-start.7 = (bf16[512,128]{1,0:T(8,128)(2,1)}, bf16[512,128]{1,0:T(8,128)(2,1)S(1)}, u32[]{:S(2)}, u32[]{:S(2)}) collective-permute-start(bf16[512,128]{1,0:T(8,128)(2,1)} %param.10), channel_id=1, source_target_pairs={{0,96},{32,128},{64,160},{96,192},{128,224},{160,0},{192,32},{224,... | collective-permute-start | bytes 393224 | tf_op jit(solution)/shard_map/ppermute | solution.py:329
  9.9 15.5 %collective-permute-start.10 = (bf16[512,128]{1,0:T(8,128)(2,1)}, bf16[512,128]{1,0:T(8,128)(2,1)S(1)}, u32[]{:S(2)}, u32[]{:S(2)}) collective-permute-start(bf16[512,128]{1,0:T(8,128)(2,1)} %param.10), channel_id=1, source_target_pairs={{0,192},{32,224},{64,0},{96,32},{128,64},{160,96},{192,128},{224,1... | collective-permute-start | bytes 393224 | tf_op jit(solution)/shard_map/ppermute | solution.py:329
  12.5 16.6 %collective-permute-start.9 = (bf16[512,128]{1,0:T(8,128)(2,1)}, bf16[512,128]{1,0:T(8,128)(2,1)S(1)}, u32[]{:S(2)}, u32[]{:S(2)}) collective-permute-start(bf16[512,128]{1,0:T(8,128)(2,1)} %param.10), channel_id=1, source_target_pairs={{0,160},{32,192},{64,224},{96,0},{128,32},{160,64},{192,96},{224,1... | collective-permute-start | bytes 393224 | tf_op jit(solution)/shard_map/ppermute | solution.py:329
  13.0 17.9 %collective-permute-start.3 = (bf16[512,128]{1,0:T(8,128)(2,1)}, bf16[512,128]{1,0:T(8,128)(2,1)S(1)}, u32[]{:S(2)}, u32[]{:S(2)}) collective-permute-start(bf16[512,128]{1,0:T(8,128)(2,1)} %param.10), channel_id=1, source_target_pairs={{0,64},{32,96},{64,128},{96,160},{128,192},{160,224},{192,0},{224,... | collective-permute-start | bytes 393224 | tf_op jit(solution)/shard_map/ppermute | solution.py:329
  15.9 15.4 %collective-permute-start.2 = (bf16[512,128]{1,0:T(8,128)(2,1)}, bf16[512,128]{1,0:T(8,128)(2,1)S(1)}, u32[]{:S(2)}, u32[]{:S(2)}) collective-permute-start(bf16[512,128]{1,0:T(8,128)(2,1)} %param.10), channel_id=1, source_target_pairs={{0,32},{32,64},{64,96},{96,128},{128,160},{160,192},{192,224},{224... | collective-permute-start | bytes 393224 | tf_op jit(solution)/shard_map/ppermute | solution.py:329
  22.8 9.2 %collective-permute-start.1 = (bf16[512,128]{1,0:T(8,128)(2,1)}, bf16[512,128]{1,0:T(8,128)(2,1)S(1)}, u32[]{:S(2)}, u32[]{:S(2)}) collective-permute-start(bf16[512,128]{1,0:T(8,128)(2,1)} %param.10), channel_id=1, source_target_pairs={{0,224},{32,0},{64,32},{96,64},{128,96},{160,128},{192,160},{224,1... | collective-permute-start | bytes 393224 | tf_op jit(solution)/shard_map/ppermute | solution.py:329
  29.1 33.7 %copy-start.21 = (bf16[256,512]{1,0:T(8,128)(2,1)S(1)}, bf16[256,512]{1,0:T(8,128)(2,1)}, u32[]{:S(2)}) copy-start(bf16[256,512]{1,0:T(8,128)(2,1)} %param.11) | copy-start | bytes 786436
  29.1 36.7 %copy-start.10 = (f32[2,8192]{1,0:T(2,128)S(1)}, f32[2,8192]{1,0:T(2,128)}, u32[]{:S(2)}) copy-start(f32[2,8192]{1,0:T(2,128)} %h_ref.1) | copy-start | bytes 196612
  29.2 48.0 %collective-permute-start.12 = (bf16[4,512,128]{2,1,0:T(8,128)(2,1)S(1)}, bf16[4,512,128]{2,1,0:T(8,128)(2,1)}, u32[]{:S(2)}, u32[]{:S(2)}) collective-permute-start(bf16[4,512,128]{2,1,0:T(8,128)(2,1)S(1)} %pad_maximum_fusion.3.refs_4_), channel_id=1, source_target_pairs={{0,16},{16,0},{1,17},{17,1},{2,18},{18,2},{3,19},{19,3},{4,20},{20... | collective-permute-start | bytes 1572872 | tf_op jit(solution)/shard_map/ppermute | solution.py:34
  30.9 48.7 %collective-permute-start.11 = (bf16[4,512,128]{2,1,0:T(8,128)(2,1)S(1)}, bf16[4,512,128]{2,1,0:T(8,128)(2,1)S(1)}, u32[]{:S(2)}, u32[]{:S(2)}) collective-permute-start(bf16[4,512,128]{2,1,0:T(8,128)(2,1)S(1)} %pad_maximum_fusion.3.refs_4_), channel_id=1, source_target_pairs={{0,8},{8,0},{1,9},{9,1},{2,10},{10,2},{3,11},{11,3},{4,12},{12,4},... | collective-permute-start | bytes 1572872 | tf_op jit(solution)/shard_map/ppermute | solution.py:34
  33.0 48.4 %collective-permute-start.5 = (bf16[4,512,128]{2,1,0:T(8,128)(2,1)S(1)}, bf16[4,512,128]{2,1,0:T(8,128)(2,1)}, u32[]{:S(2)}, u32[]{:S(2)}) collective-permute-start(bf16[4,512,128]{2,1,0:T(8,128)(2,1)S(1)} %pad_maximum_fusion.2.refs_0_), channel_id=1, source_target_pairs={{0,16},{16,0},{1,17},{17,1},{2,18},{18,2},{3,19},{19,3},{4,20},{20... | collective-permute-start | bytes 1572872 | tf_op jit(solution)/shard_map/ppermute | solution.py:34
  34.7 46.7 %collective-permute-start.4 = (bf16[4,512,128]{2,1,0:T(8,128)(2,1)S(1)}, bf16[4,512,128]{2,1,0:T(8,128)(2,1)}, u32[]{:S(2)}, u32[]{:S(2)}) collective-permute-start(bf16[4,512,128]{2,1,0:T(8,128)(2,1)S(1)} %pad_maximum_fusion.2.refs_0_), channel_id=1, source_target_pairs={{0,8},{8,0},{1,9},{9,1},{2,10},{10,2},{3,11},{11,3},{4,12},{12,4},... | collective-permute-start | bytes 1572872 | tf_op jit(solution)/shard_map/ppermute | solution.py:34
  34.7 3.2 %collective-permute-start = (bf16[2,3,512]{2,0,1:T(2,128)(2,1)S(1)}, bf16[2,3,512]{2,0,1:T(2,128)(2,1)S(1)}, u32[]{:S(2)}, u32[]{:S(2)}) collective-permute-start(bf16[2,3,512]{2,0,1:T(2,128)(2,1)S(1)} %slice.45), channel_id=1, source_target_pairs={{0,8},{8,16},{16,24},{24,32},{32,40},{40,48},{48,56},{56,64},{64,7... | collective-permute-start | bytes 18440 | tf_op jit(solution)/shard_map/ppermute | solution.py:30
  39.4 0.8 copy-start.15
  41.0 41.0 %all-to-all-start = ((bf16[32,16,256]{2,1,0:T(8,128)(2,1)}), bf16[32,16,256]{2,1,0:T(8,128)(2,1)S(1)}, u32[]{:S(2)}, u32[]{:S(2)}) async-start(bf16[32,16,256]{2,1,0:T(8,128)(2,1)} %bitcast.7), calls=%async_computation | async-start | bytes 524288 | tf_op jit(solution)/shard_map/all_to_all | solution.py:377
  62.9 12.7 %collective-permute-start.18 = (bf16[256,512]{1,0:T(8,128)(2,1)S(1)}, bf16[256,512]{1,0:T(8,128)(2,1)}, u32[]{:S(2)}, u32[]{:S(2)}) collective-permute-start(bf16[256,512]{1,0:T(8,128)(2,1)S(1)} %copy-done.21), channel_id=1, source_target_pairs={{0,4},{4,0},{1,5},{5,1},{2,6},{6,2},{3,7},{7,3},{8,12},{12,8},{9,1... | collective-permute-start | bytes 786440 | tf_op jit(solution)/shard_map/ppermute | solution.py:34
  65.8 9.7 %copy-start.22 = (bf16[256,512]{1,0:T(8,128)(2,1)S(1)}, bf16[256,512]{1,0:T(8,128)(2,1)}, u32[]{:S(2)}) copy-start(bf16[256,512]{1,0:T(8,128)(2,1)} %param.11) | copy-start | bytes 786436
  67.3 2.0 %copy-start = (bf16[2,65,128,128]{3,2,1,0:T(8,128)(2,1)}, bf16[2,65,128,128]{3,2,1,0:T(8,128)(2,1)S(1)}, u32[]{:S(2)}) copy-start(bf16[2,65,128,128]{3,2,1,0:T(8,128)(2,1)S(1)} %toeplitz_tiles.1.tile_ref) | copy-start | bytes 12779524
  76.6 17.9 %collective-permute-start.21 = (bf16[2,256,512]{2,1,0:T(8,128)(2,1)S(1)}, bf16[2,256,512]{2,1,0:T(8,128)(2,1)}, u32[]{:S(2)}, u32[]{:S(2)}) collective-permute-start(bf16[2,256,512]{2,1,0:T(8,128)(2,1)S(1)} %pad_maximum_fusion.4.cot0), channel_id=1, source_target_pairs={{0,3},{1,0},{2,1},{3,2},{4,7},{5,4},{6,5},{7,6},{8,11},{9,8},{10,9... | collective-permute-start | bytes 1572872 | tf_op jit(solution)/shard_map/ppermute | solution.py:334
  77.2 25.1 %collective-permute-start.20 = (bf16[2,256,512]{2,1,0:T(8,128)(2,1)S(1)}, bf16[2,256,512]{2,1,0:T(8,128)(2,1)}, u32[]{:S(2)}, u32[]{:S(2)}) collective-permute-start(bf16[2,256,512]{2,1,0:T(8,128)(2,1)S(1)} %pad_maximum_fusion.4.cot0), channel_id=1, source_target_pairs={{0,2},{1,3},{2,0},{3,1},{4,6},{5,7},{6,4},{7,5},{8,10},{9,11},{10,... | collective-permute-start | bytes 1572872 | tf_op jit(solution)/shard_map/ppermute | solution.py:334
  79.6 6.9 %copy-start.12 = (bf16[4,512,128]{2,1,0:T(8,128)(2,1)}, bf16[4,512,128]{2,1,0:T(8,128)(2,1)S(1)}, u32[]{:S(2)}) copy-start(bf16[4,512,128]{2,1,0:T(8,128)(2,1)S(1)} %collective-permute-done.11.refs_5_) | copy-start | bytes 1572868
  79.6 23.6 %collective-permute-start.19 = (bf16[2,256,512]{2,1,0:T(8,128)(2,1)S(1)}, bf16[2,256,512]{2,1,0:T(8,128)(2,1)}, u32[]{:S(2)}, u32[]{:S(2)}) collective-permute-start(bf16[2,256,512]{2,1,0:T(8,128)(2,1)S(1)} %pad_maximum_fusion.4.cot0), channel_id=1, source_target_pairs={{0,1},{1,2},{2,3},{3,0},{4,5},{5,6},{6,7},{7,4},{8,9},{9,10},{10,1... | collective-permute-start | bytes 1572872 | tf_op jit(solution)/shard_map/ppermute | solution.py:334
  81.4 21.8 %collective-permute-start.13 = (bf16[4,512,128]{2,1,0:T(8,128)(2,1)}, bf16[4,512,128]{2,1,0:T(8,128)(2,1)}, u32[]{:S(2)}, u32[]{:S(2)}) collective-permute-start(bf16[4,512,128]{2,1,0:T(8,128)(2,1)} %collective-permute-done.12.refs_6_), channel_id=1, source_target_pairs={{0,8},{8,0},{1,9},{9,1},{2,10},{10,2},{3,11},{11,3},{4,12},{12,4},... | collective-permute-start | bytes 1572872 | tf_op jit(solution)/shard_map/ppermute | solution.py:34
  81.4 21.8 %collective-permute-start.6 = (bf16[4,512,128]{2,1,0:T(8,128)(2,1)}, bf16[4,512,128]{2,1,0:T(8,128)(2,1)}, u32[]{:S(2)}, u32[]{:S(2)}) collective-permute-start(bf16[4,512,128]{2,1,0:T(8,128)(2,1)} %collective-permute-done.5.refs_2_), channel_id=1, source_target_pairs={{0,8},{8,0},{1,9},{9,1},{2,10},{10,2},{3,11},{11,3},{4,12},{12,4},... | collective-permute-start | bytes 1572872 | tf_op jit(solution)/shard_map/ppermute | solution.py:34
  82.0 2.2 %copy-start.1 = (bf16[2,65,128,128]{3,2,1,0:T(8,128)(2,1)S(1)}, bf16[2,65,128,128]{3,2,1,0:T(8,128)(2,1)}, u32[]{:S(2)}) copy-start(bf16[2,65,128,128]{3,2,1,0:T(8,128)(2,1)} %copy-done) | copy-start | bytes 12779524
  84.2 2.4 %copy-start.6 = (bf16[32,16,256]{2,1,0:T(8,128)(2,1)}, bf16[32,16,256]{2,1,0:T(8,128)(2,1)S(1)}, u32[]{:S(2)}) copy-start(bf16[32,16,256]{2,1,0:T(8,128)(2,1)S(1)} %all-to-all-done.x_ref) | copy-start | bytes 786436
  86.5 23.1 %all-to-all-start.1 = ((bf16[32,16,256]{2,1,0:T(8,128)(2,1)}), bf16[32,16,256]{2,1,0:T(8,128)(2,1)}, u32[]{:S(2)}, u32[]{:S(2)}) async-start(bf16[32,16,256]{2,1,0:T(8,128)(2,1)} %conv_forward.1), calls=%async_computation.1 | async-start | bytes 524288 | tf_op jit(solution)/shard_map/all_to_all | solution.py:381
  103.2 1.0 copy-start.13
  104.2 1.0 copy-start.16
  105.3 12.4 %copy-start.11 = (f32[512]{0:T(512)S(1)}, f32[512]{0:T(512)}, u32[]{:S(2)}) copy-start(f32[512]{0:T(512)} %param.9) | copy-start | bytes 6148
  109.6 20.7 %all-to-all-start.2 = ((bf16[32,16,256]{2,1,0:T(8,128)(2,1)}), bf16[32,16,256]{2,1,0:T(8,128)(2,1)}, u32[]{:S(2)}, u32[]{:S(2)}) async-start(bf16[32,16,256]{2,1,0:T(8,128)(2,1)} %bitcast.52), calls=%async_computation.2 | async-start | bytes 524288 | tf_op jit(solution)/shard_map/all_to_all | solution.py:377
  117.7 1.0 copy-start.14
  118.8 1.0 copy-start.17
  119.8 0.9 copy-start.19
  124.8 0.8 copy-start.4
  125.6 24.3 %collective-permute-start.14 = (bf16[2,256,512]{2,1,0:T(8,128)(2,1)}, bf16[2,256,512]{2,1,0:T(8,128)(2,1)}, u32[]{:S(2)}, u32[]{:S(2)}) collective-permute-start(bf16[2,256,512]{2,1,0:T(8,128)(2,1)} %get-tuple-element.22), channel_id=1, source_target_pairs={{0,1},{1,2},{2,3},{3,0},{4,5},{5,6},{6,7},{7,4},{8,9},{9,10},{10,1... | collective-permute-start | bytes 1572872 | tf_op jit(solution)/shard_map/ppermute | solution.py:334
  127.0 22.9 %collective-permute-start.15 = (bf16[2,256,512]{2,1,0:T(8,128)(2,1)}, bf16[2,256,512]{2,1,0:T(8,128)(2,1)}, u32[]{:S(2)}, u32[]{:S(2)}) collective-permute-start(bf16[2,256,512]{2,1,0:T(8,128)(2,1)} %get-tuple-element.23), channel_id=1, source_target_pairs={{0,2},{1,3},{2,0},{3,1},{4,6},{5,7},{6,4},{7,5},{8,10},{9,11},{10,... | collective-permute-start | bytes 1572872 | tf_op jit(solution)/shard_map/ppermute | solution.py:334
  130.3 23.6 %collective-permute-start.16 = (bf16[2,256,512]{2,1,0:T(8,128)(2,1)}, bf16[2,256,512]{2,1,0:T(8,128)(2,1)}, u32[]{:S(2)}, u32[]{:S(2)}) collective-permute-start(bf16[2,256,512]{2,1,0:T(8,128)(2,1)} %get-tuple-element.24), channel_id=1, source_target_pairs={{0,3},{1,0},{2,1},{3,2},{4,7},{5,4},{6,5},{7,6},{8,11},{9,8},{10,9... | collective-permute-start | bytes 1572872 | tf_op jit(solution)/shard_map/ppermute | solution.py:334
  130.3 2.2 %copy-start.2 = (bf16[2,65,128,128]{3,2,1,0:T(8,128)(2,1)S(1)}, bf16[2,65,128,128]{3,2,1,0:T(8,128)(2,1)}, u32[]{:S(2)}) copy-start(bf16[2,65,128,128]{3,2,1,0:T(8,128)(2,1)} %copy-done) | copy-start | bytes 12779524
  132.5 0.9 copy-start.7
  140.0 13.9 %copy-start.5 = (bf16[2,256,512]{2,1,0:T(8,128)(2,1)S(1)}, bf16[2,256,512]{2,1,0:T(8,128)(2,1)}, u32[]{:S(2)}) copy-start(bf16[2,256,512]{2,1,0:T(8,128)(2,1)} %copy-done.4) | copy-start | bytes 1572868
  140.0 20.7 %all-to-all-start.3 = ((bf16[32,16,256]{2,1,0:T(8,128)(2,1)}), bf16[32,16,256]{2,1,0:T(8,128)(2,1)S(1)}, u32[]{:S(2)}, u32[]{:S(2)}) async-start(bf16[32,16,256]{2,1,0:T(8,128)(2,1)} %get-tuple-element.28), calls=%async_computation.3 | async-start | bytes 524288 | tf_op jit(solution)/shard_map/all_to_all | solution.py:381
  155.8 10.1 %collective-permute-start.17 = (bf16[256,512]{1,0:T(8,128)(2,1)}, bf16[256,512]{1,0:T(8,128)(2,1)}, u32[]{:S(2)}, u32[]{:S(2)}) collective-permute-start(bf16[256,512]{1,0:T(8,128)(2,1)} %fusion.4), channel_id=1, source_target_pairs={{0,4},{4,0},{1,5},{5,1},{2,6},{6,2},{3,7},{7,3},{8,12},{12,8},{9,1... | collective-permute-start | bytes 786440 | tf_op jit(solution)/shard_map/ppermute | solution.py:34
  161.0 1.0 copy-start.20
  162.1 5.9 %collective-permute-start.22 = (f32[2,3,512]{2,0,1:T(2,128)S(1)}, f32[2,3,512]{2,0,1:T(2,128)S(1)}, u32[]{:S(2)}, u32[]{:S(2)}) collective-permute-start(f32[2,3,512]{2,0,1:T(2,128)S(1)} %slice.66), channel_id=1, source_target_pairs={{8,0},{16,8},{24,16},{32,24},{40,32},{48,40},{56,48},{64,56},{72,6... | collective-permute-start | bytes 36872 | tf_op jit(solution)/shard_map/ppermute | solution.py:30
  (2 other events, 1.4 us)

commit v3 on v2

--- a/solution.py
+++ b/solution.py
@@ -14,9 +14,10 @@
 BLOCK = 256
 HALF = 128
 LAGS = 4
-WHALF = 4
 SCRATCH = pltpu.CompilerParams(vmem_limit_bytes=24 << 20)
 BUILD_UNROLL = 16
+EDGE = 16
+OUTSIDE = pltpu.HBM
 
 SEQ = ("z", "yl", "core")
 CHAN = ("yh", "x")
@@ -40,7 +41,7 @@
     return rows, lanes
 
 
-def toeplitz_kernel(h_ref, tile_ref):
+def build_tiles(h_ref, tile_ref):
     groups, count = tile_ref.shape[0], tile_ref.shape[1] - 1
     rows, lanes = skew_masks()
     inside = lanes >= rows
@@ -60,17 +61,6 @@
     lax.fori_loop(0, count, step, (zero,) * groups, unroll=BUILD_UNROLL)
 
 
-def toeplitz_tiles(h):
-    groups, length = h.shape
-    return pl.pallas_call(
-        toeplitz_kernel,
-        name="toeplitz_tiles",
-        out_shape=pltpu.VMEM((groups, length // HALF + 1, HALF, HALF), BF16),
-        compiler_params=SCRATCH,
-        cost_estimate=pl.CostEstimate(flops=4000000, bytes_accessed=4500000, transcendentals=0),
-    )(h)
-
-
 def toeplitz_block(tile_ref, g, d):
     same = tile_ref[g, 2 * d + 1]
     upper = jnp.concatenate([same, tile_ref[g, 2 * d + 2]], axis=1)
@@ -83,10 +73,11 @@
     return part.reshape(part.shape[0] * GROUP, BLOCK)
 
 
-def conv_kernel(x_ref, tile_ref, y_ref, wide_ref, acc_ref):
+def conv_kernel(x_ref, h_ref, y_ref, tile_ref, wide_ref, acc_ref):
     blocks, chans, _ = x_ref.shape
     total = blocks * GROUP
     parts = []
+    build_tiles(h_ref, tile_ref)
     for g in range(chans // GROUP):
         signal = group_rows(x_ref, g)
         for k in range(LAGS):
@@ -110,7 +101,7 @@
     y_ref[...] = jnp.concatenate(parts, axis=1).astype(BF16)
 
 
-def back_kernel(m_ref, x_ref, tile_ref, y_ref, f_ref, wide_ref, acc_ref, low_ref, high_ref, *, scale):
+def back_kernel(m_ref, x_ref, h_ref, y_ref, f_ref, tile_ref, wide_ref, acc_ref, low_ref, high_ref, *, scale):
     blocks, chans, _ = x_ref.shape
     total = blocks * GROUP
     rows_i, lanes_i = skew_masks()
@@ -122,6 +113,7 @@
     )
     flip = jnp.where(flip, 1.0, 0.0).astype(BF16)
     zero = jnp.zeros((HALF, HALF), F32)
+    build_tiles(h_ref, tile_ref)
     parts = []
 
     def fold(v):
@@ -182,7 +174,7 @@
     y_ref[...] = jnp.concatenate(parts, axis=1).astype(BF16)
 
 
-def conv_forward(x, tiles):
+def conv_forward(x, h):
     blocks = x.shape[0]
     total = blocks * GROUP
     return pl.pallas_call(
@@ -190,15 +182,16 @@
         name="conv_forward",
         out_shape=jax.ShapeDtypeStruct(x.shape, BF16),
         scratch_shapes=[
+            pltpu.VMEM((h.shape[0], h.shape[1] // HALF + 1, HALF, HALF), BF16),
             pltpu.VMEM((total, LAGS * BLOCK), BF16),
             pltpu.VMEM((total, BLOCK), F32),
         ],
         compiler_params=SCRATCH,
         cost_estimate=pl.CostEstimate(flops=6000000000, bytes_accessed=600000, transcendentals=0),
-    )(x, pltpu.with_memory_space_constraint(tiles, pltpu.VMEM))
-
-
-def conv_backward(m, x, tiles):
+    )(x, h)
+
+
+def conv_backward(m, x, h):
     blocks, chans, _ = x.shape
     total = blocks * GROUP
     scale = 1.0 / math.sqrt(GROUP * blocks * BLOCK)
@@ -210,6 +203,7 @@
             jax.ShapeDtypeStruct((chans // GROUP, blocks, BLOCK), F32),
         ),
         scratch_shapes=[
+            pltpu.VMEM((h.shape[0], h.shape[1] // HALF + 1, HALF, HALF), BF16),
             pltpu.VMEM((total + total // 2, LAGS * BLOCK), BF16),
             pltpu.VMEM((total, BLOCK), F32),
             pltpu.VMEM((blocks, 8, BLOCK), F32),
@@ -217,20 +211,19 @@
         ],
         compiler_params=SCRATCH,
         cost_estimate=pl.CostEstimate(flops=10000000000, bytes_accessed=1000000, transcendentals=0),
-    )(m, x, pltpu.with_memory_space_constraint(tiles, pltpu.VMEM))
+    )(m, x, h)
 
 
 def whole_columns(at_ref, sign, step, refs):
     own, own_c, side, side_c, own2, own_c2, side2, side_c2 = refs
     first = at_ref[1] == 0
     met = ((at_ref[2] + step) & 1) * 4 + ((at_ref[3] + sign * (step // 2) + 4) & 3)
-    place = (at_ref[4] - met + 9) & 7
-    early = place < WHALF
-    lo = jnp.minimum(place, WHALF - 1)
-    hi = jnp.maximum(place - WHALF, 0)
+    apart = at_ref[4] ^ met
+    early = (apart & 1) == 0
+    place = (apart & 2) + (apart >> 2)
 
     def pick(a, b):
-        return jnp.where(early, a[lo], b[hi])
+        return jnp.where(early, a[place], b[place])
 
     parts = []
     for a, b, c, d in ((own, own2, own_c, own_c2), (side, side2, side_c, side_c2)):
@@ -243,7 +236,20 @@
     return pl.ds(pl.multiple_of(side * width, width), width)
 
 
-def grad_mm_kernel(at_ref, query_ref, cot0, cot1, cot2, cot3, *refs):
+def short_side(i, proj_ref, before_ref, taps_ref):
+    now = proj_ref[i].astype(F32)
+    before = before_ref[i].astype(F32)
+    row = lax.broadcasted_iota(jnp.int32, now.shape, 0)
+    total = taps_ref[i, SHORT - 1 : SHORT, :] * now
+    for j in range(1, SHORT):
+        late = pltpu.roll(now, j, 0)
+        for r in range(j):
+            late = jnp.where(row == r, before[SHORT - 1 - j + r][None, :], late)
+        total = total + taps_ref[i, SHORT - 1 - j : SHORT - j, :] * late
+    return total
+
+
+def grad_mm_kernel(at_ref, proj_ref, before_ref, taps_ref, cot0, cot1, cot2, cot3, *refs):
     *w_refs, out_ref, mixed_ref, sent_ref = refs
     yl = at_ref[0]
     width = cot0.shape[2] // 2
@@ -264,7 +270,7 @@
             out_ref[...] = part
         else:
             out_ref[...] += part
-    mixed = (out_ref[...] * query_ref[...]).astype(BF16)
+    mixed = (out_ref[...] * short_side(0, proj_ref, before_ref, taps_ref)).astype(BF16)
     mixed_ref[...] = mixed
     sent_ref[...] = mixed.astype(F32).T.astype(BF16)
 
@@ -273,30 +279,31 @@
 WHOLE = pl.BlockSpec(memory_space=pltpu.VMEM)
 
 
-def grad_matmul(at, query, cots, ws):
-    tok, rows = query.shape
+def grad_matmul(at, side_args, cots, ws):
+    _, tok, rows = side_args[0].shape
     return pl.pallas_call(
         grad_mm_kernel,
         name="grad_matmul",
         out_shape=(
-            jax.ShapeDtypeStruct((tok, rows), F32),
-            jax.ShapeDtypeStruct((tok, rows), BF16),
-            jax.ShapeDtypeStruct((rows, tok), BF16),
+            OUTSIDE((tok, rows), F32),
+            OUTSIDE((tok, rows), BF16),
+            OUTSIDE((rows, tok), BF16),
         ),
-        in_specs=[SCALARS] + [WHOLE] * (1 + len(cots) + len(ws)),
+        in_specs=[SCALARS] + [WHOLE] * (len(side_args) + len(cots) + len(ws)),
         out_specs=(WHOLE,) * 3,
         compiler_params=SCRATCH,
         cost_estimate=pl.CostEstimate(flops=4000000000, bytes_accessed=6500000, transcendentals=0),
-    )(at, query, *cots, *ws)
-
-
-def mix_mm_kernel(at_ref, conv_ref, query_ref, carried_ref, skip_ref, *refs):
-    *w_refs, out0, out1, out2, out3, mixed_ref = refs
+    )(at, *side_args, *cots, *ws)
+
+
+def mix_mm_kernel(at_ref, conv_ref, proj_ref, before_ref, taps_ref, skip_ref, grad_ref, *refs):
+    *w_refs, out0, out1, out2, out3, query_grad_ref = refs
     yl = at_ref[0]
     conv = conv_ref[...].astype(F32).T
-    mixed_in = conv + skip_ref[...] * carried_ref[...].astype(F32)
-    mixed_ref[...] = mixed_in
-    gated = (query_ref[...] * mixed_in).astype(BF16)
+    query, key, value = (short_side(i, proj_ref, before_ref, taps_ref) for i in range(3))
+    mixed_in = conv + skip_ref[...] * (key * value).astype(BF16).astype(F32)
+    query_grad_ref[...] = grad_ref[...] * mixed_in
+    gated = (query * mixed_in).astype(BF16)
     width = out0.shape[2] // 2
     for step in range(8):
         out_ref = (out0, out1, out2, out3)[step // 2]
@@ -308,25 +315,23 @@
         out_ref[e, :, side_columns(1 - yl, width)] = part[:, width:]
 
 
-def mix_matmul(at, conv, query, carried, skip, ws):
-    tok, rows = query.shape
+def mix_matmul(at, conv, side_args, skip, grad, ws):
+    tok, rows = grad.shape
     cols = 4 * ws[0].shape[2]
-    *parts, mixed_in = pl.pallas_call(
+    *parts, query_grad = pl.pallas_call(
         mix_mm_kernel,
         name="mix_matmul",
-        out_shape=(jax.ShapeDtypeStruct((2, tok, cols), BF16),) * 4
-        + (jax.ShapeDtypeStruct((tok, rows), F32),),
-        in_specs=[SCALARS] + [WHOLE] * (4 + len(ws)),
+        out_shape=(OUTSIDE((2, tok, cols), BF16),) * 4 + (OUTSIDE((tok, rows), F32),),
+        in_specs=[SCALARS] + [WHOLE] * (3 + len(side_args) + len(ws)),
         out_specs=(WHOLE,) * 5,
         compiler_params=SCRATCH,
         cost_estimate=pl.CostEstimate(flops=4000000000, bytes_accessed=6500000, transcendentals=0),
-    )(at, conv, query, carried, skip[None, :], *ws)
-    return parts, mixed_in
-
-
-def shift_z(shard, by):
-    count = lax.axis_size("z")
-    return lax.ppermute(shard, "z", [(i, (i + by) % count) for i in range(count)])
+    )(at, conv, *side_args, skip, grad, *ws)
+    return parts, query_grad
+
+
+def cross_z(shard, by):
+    return lax.ppermute(shard, "z", [(i, i ^ by) for i in range(lax.axis_size("z"))])
 
 
 def shift_x(shard, by):
@@ -334,41 +339,87 @@
     return lax.ppermute(shard, "x", [(i, (i + by) % count) for i in range(count)])
 
 
-def pre_kernel(proj_ref, before_ref, taps_ref, query_ref, key_ref, value_ref, carried_ref, sent_ref):
-    row = lax.broadcasted_iota(jnp.int32, proj_ref.shape[1:], 0)
-    sides = []
-    for i in range(3):
-        now = proj_ref[i].astype(F32)
-        before = before_ref[i].astype(F32)
-        total = taps_ref[i, SHORT - 1 : SHORT, :] * now
-        for j in range(1, SHORT):
-            late = pltpu.roll(now, j, 0)
-            for r in range(j):
-                late = jnp.where(row == r, before[SHORT - 1 - j + r][None, :], late)
-            total = total + taps_ref[i, SHORT - 1 - j : SHORT - j, :] * late
-        sides.append(total)
-    query_ref[...], key_ref[...], value_ref[...] = sides
-    carried = (sides[1] * sides[2]).astype(BF16)
-    carried_ref[...] = carried
-    sent_ref[...] = carried.astype(F32).T.astype(BF16)
-
-
-def short_forward(projected, before, taps):
-    tok, _, cols = projected.shape
-    side = jax.ShapeDtypeStruct((tok, cols), F32)
+def pre_kernel(proj_ref, before_ref, taps_ref, sent_ref):
+    key, value = (short_side(i, proj_ref, before_ref, taps_ref) for i in (1, 2))
+    sent_ref[...] = (key * value).T.astype(BF16)
+
+
+def carried_columns(side_args):
+    _, tok, cols = side_args[0].shape
     return pl.pallas_call(
         pre_kernel,
-        name="short_forward",
+        name="carried_columns",
+        out_shape=OUTSIDE((cols, tok), BF16),
+        compiler_params=SCRATCH,
+        cost_estimate=pl.CostEstimate(flops=5000000, bytes_accessed=1500000, transcendentals=0),
+    )(*side_args)
+
+
+def final_kernel(
+    back_ref, mixed_ref, query_grad_ref, proj_ref, before_ref, taps_ref, skip_ref, out_ref, head_ref, tail_ref
+):
+    tok = mixed_ref.shape[0]
+    row = lax.broadcasted_iota(jnp.int32, mixed_ref.shape, 0)
+    carried_grad = back_ref[...].astype(F32).T + skip_ref[...] * mixed_ref[...].astype(F32)
+    key, value = (short_side(i, proj_ref, before_ref, taps_ref) for i in (1, 2))
+    grads = (query_grad_ref[...], carried_grad * value, carried_grad * key)
+    for i, grad in enumerate(grads):
+        head_ref[i] = grad[: head_ref.shape[1]]
+        total = taps_ref[i, SHORT - 1 : SHORT, :] * grad
+        for j in range(1, SHORT):
+            early = jnp.where(row < tok - j, pltpu.roll(grad, tok - j, 0), 0.0)
+            total = total + taps_ref[i, SHORT - 1 - j : SHORT - j, :] * early
+        out_ref[i] = total.astype(BF16)
+        tail_ref[i] = total[tok - EDGE :]
+
+
+def final_short(back, mixed_grad, query_grad, side_args, skip):
+    tok, cols = mixed_grad.shape
+    return pl.pallas_call(
+        final_kernel,
+        name="final_short",
         out_shape=(
-            side,
-            side,
-            side,
-            jax.ShapeDtypeStruct((tok, cols), BF16),
-            jax.ShapeDtypeStruct((cols, tok), BF16),
+            jax.ShapeDtypeStruct((3, tok, cols), BF16),
+            OUTSIDE((3, 8, cols), F32),
+            jax.ShapeDtypeStruct((3, EDGE, cols), F32),
         ),
         compiler_params=SCRATCH,
         cost_estimate=pl.CostEstimate(flops=5000000, bytes_accessed=3500000, transcendentals=0),
-    )(projected.transpose(1, 0, 2), before.transpose(1, 0, 2), taps)
+    )(back, mixed_grad, query_grad, *side_args, skip)
+
+
+def edge_kernel(tail_ref, after_ref, taps_ref, whole_ref, out_ref):
+    row = lax.broadcasted_iota(jnp.int32, tail_ref.shape[1:], 0)
+    for i in range(3):
+        after = after_ref[i]
+        total = tail_ref[i]
+        for s in range(SHORT - 1):
+            missing = sum(
+                taps_ref[i, SHORT - 2 - s - r : SHORT - 1 - s - r, :] * after[r : r + 1]
+                for r in range(SHORT - 1 - s)
+            )
+            total = total + jnp.where(row == EDGE - 1 - s, 1.0, 0.0) * missing
+        out_ref[i] = total.astype(BF16)
+
+
+def edge_rows(tail, after, taps, whole):
+    _, tok, cols = whole.shape
+    return pl.pallas_call(
+        edge_kernel,
+        name="edge_rows",
+        out_shape=jax.ShapeDtypeStruct(whole.shape, BF16),
+        grid=(1,),
+        in_specs=[
+            pl.BlockSpec(tail.shape, lambda i: (0, 0, 0)),
+            pl.BlockSpec(after.shape, lambda i: (0, 0, 0)),
+            pl.BlockSpec(taps.shape, lambda i: (0, 0, 0)),
+            pl.BlockSpec(memory_space=pl.ANY),
+        ],
+        out_specs=pl.BlockSpec((3, EDGE, cols), lambda i: (0, tok // EDGE - 1, 0)),
+        input_output_aliases={3: 0},
+        compiler_params=SCRATCH,
+        cost_estimate=pl.CostEstimate(flops=500000, bytes_accessed=200000, transcendentals=0),
+    )(tail, after, taps, whole)
 
 
 def channel_major(sent):
@@ -386,7 +437,7 @@
     tok_rows, _ = cotangent.shape
     groups_dev, seq_length = filters.shape
     rim = SHORT - 1
-    wide, deep = lax.axis_size("x"), lax.axis_size("z")
+    wide = lax.axis_size("x")
     yl, core = lax.axis_index("yl"), lax.axis_index("core")
     yh, x, z = lax.axis_index("yh"), lax.axis_index("x"), lax.axis_index("z")
 
@@ -394,10 +445,9 @@
     before = from_behind(projected[tok_rows - rim :], 1)
     cot_pair = jnp.stack([cotangent, swap(cotangent, "yh")])
     cots = [cot_pair] + [shift_x(cot_pair, k) for k in range(1, wide)]
-    w_own = jnp.stack(
-        [shift_z(out_weight, deep - 1), out_weight, shift_z(out_weight, 1), shift_z(out_weight, 2)]
-    )
-    w_own2 = jnp.stack([shift_z(out_weight, r) for r in range(3, deep - 1)])
+    w_pair = jnp.stack([out_weight, cross_z(out_weight, 4)])
+    w_own = jnp.concatenate([w_pair, cross_z(w_pair, 2)])
+    w_own2 = cross_z(w_own, 1)
     w_side = swap(w_own, "yl")
     w_side2 = swap(w_own2, "yl")
     w_own_c = swap(w_own, "core")
@@ -406,37 +456,31 @@
     w_side_c2 = swap(w_side2, "core")
     ws = (w_own, w_own_c, w_side, w_side_c, w_own2, w_own_c2, w_side2, w_side_c2)
 
-    tiles = toeplitz_tiles(filters)
-    query_side, key_side, value_side, carried, carried_sent = short_forward(
-        projected, before, short_weight
-    )
+    side_args = (projected.transpose(1, 0, 2), before.transpose(1, 0, 2), short_weight)
+    carried_sent = carried_columns(side_args)
     carried_seq = channel_major(carried_sent)
-    conv_seq = conv_forward(carried_seq, tiles)
+    conv_seq = conv_forward(carried_seq, filters)
     conv = token_major(conv_seq)
 
-    gated_grad, mixed_grad, grad_sent = grad_matmul(at, query_side, cots, ws)
+    gated_grad, mixed_grad, grad_sent = grad_matmul(at, side_args, cots, ws)
     grad_seq = channel_major(grad_sent)
 
-    parts, mixed_in = mix_matmul(at, conv, query_side, carried, skip, ws)
+    parts, query_grad = mix_matmul(at, conv, side_args, skip[None, :], gated_grad, ws)
     shares = [parts[0]] + [shift_x(parts[k], k) for k in range(1, wide)]
     theirs = sum(p[1].astype(F32) for p in shares).astype(BF16)
     got = swap(theirs, "yh")
     mixed = (sum(p[0].astype(F32) for p in shares) + got.astype(F32)).astype(BF16)
 
-    back_seq, filter_grad = conv_backward(grad_seq, carried_seq, tiles)
-    back = token_major(back_seq).T
-    query_grad = gated_grad * mixed_in
-    carried_grad = back.astype(F32) + skip * mixed_grad.astype(F32)
-    short_grad = jnp.stack([query_grad, carried_grad * value_side, carried_grad * key_side], axis=1)
-    after = from_behind(short_grad[:rim], -1)
-    extended_grad = jnp.concatenate([short_grad, after], axis=0)
-    projected_grad = short_weight[:, 0, :] * extended_grad[rim : rim + tok_rows]
-    for j in range(1, SHORT):
-        projected_grad = (
-            projected_grad
-            + short_weight[:, j, :] * extended_grad[rim - j : rim - j + tok_rows]
-        )
-    return (mixed, projected_grad.astype(BF16), filter_grad.reshape(groups_dev, seq_length))
+    back_seq, filter_grad = conv_backward(grad_seq, carried_seq, filters)
+    back = token_major(back_seq)
+    whole, head, tail = final_short(back, mixed_grad, query_grad, side_args, skip[None, :])
+    after = from_behind(head, -1)
+    projected_grad = edge_rows(tail, after, short_weight, whole)
+    return (
+        mixed,
+        projected_grad.transpose(1, 0, 2),
+        filter_grad.reshape(groups_dev, seq_length),
+    )
 
 
 def solution(mesh):

time: 171 us -> 158 us (0.924)
  waiting for transfers between devices: 36 us -> 51 us
  local copies, waits for them, and re-layouts: 17.4 us -> 2.54 us
  starting transfers between devices: 87.1 us -> 73.5 us
  Pallas kernels: 19.4 us -> 24.2 us
  other arithmetic: 8.83 us -> 4.24 us
    unnamed x49 -> x25, local copies, waits for them, and re-layouts: 17.1 us -> 2.44 us
    all_to_all x2, waiting for transfers between devices: 0.01 us -> 11.4 us  [channel_major(): return lax.all_to_all(sent, SEQ, split_axis=0, concat_axis=0, tiled=True)]
    ppermute x7 -> x3, starting transfers between devices: 18.8 us -> 12 us  [cross_z(): lax.ppermute(shard, 'z', [(i, i ^ by) for i in range(lax.axis_size('z'))])]
    all_to_all x2, starting transfers between devices: 16.2 us -> 10.6 us  [token_major(): got = lax.all_to_all(block, SEQ, split_axis=0, concat_axis=0, tiled=True)]
    all_to_all x2, waiting for transfers between devices: 2.71 us -> 7.52 us  [token_major(): got = lax.all_to_all(block, SEQ, split_axis=0, concat_axis=0, tiled=True)]
    ppermute x6, waiting for transfers between devices: 12.7 us -> 8.91 us  [shift_x(): lax.ppermute(shard, 'x', [(i, (i + by) % count) for i in range(count)])]
    pallas_call x4 -> x5, Pallas kernels: 10.5 us -> 13.4 us  [the longest x1 4.84 us: mix_matmul(): pl.pallas_call(mix_mm_kernel, name='mix_matmul', out_shape=(OUTSIDE((2, t...]
    ppermute x7 -> x3, waiting for transfers between devices: 10.9 us -> 13.6 us  [cross_z(): lax.ppermute(shard, 'z', [(i, i ^ by) for i in range(lax.axis_size('z'))])]
  transfers between devices with their start and end apart: 27 -> 23, of which waited for: 11 -> 10; matrix products, arithmetic and copies ran while one was open for 5% -> 3% of each run, Pallas kernels for 11% -> 15%
where the time goes in v3:
time: 158 us; the launch traced here: 156 us
  starting transfers between devices  73.5 us (47%)
  waiting for transfers between devices  51 us (32%)
  Pallas kernels  24.2 us (15%)
  other arithmetic  4.24 us (3%)
  local copies, waits for them, and re-layouts  2.54 us (2%)
    all_to_all x2, starting transfers between devices, channel_major(): return lax.all_to_all(sent, SEQ, split_axis=0, concat_axis=0, tiled=True)  29.8 us
    ppermute x3, waiting for transfers between devices, cross_z(): lax.ppermute(shard, 'z', [(i, i ^ by) for i in range(lax.axis_size('z'))])  13.6 us
    ppermute x3, starting transfers between devices, cross_z(): lax.ppermute(shard, 'z', [(i, i ^ by) for i in range(lax.axis_size('z'))])  12 us
    all_to_all x2, waiting for transfers between devices, channel_major(): return lax.all_to_all(sent, SEQ, split_axis=0, concat_axis=0, tiled=True)  11.4 us
    all_to_all x2, starting transfers between devices, token_major(): got = lax.all_to_all(block, SEQ, split_axis=0, concat_axis=0, tiled=True)  10.6 us
    ppermute x8, starting transfers between devices, swap(): return lax.ppermute(shard, axis, [(0, 1), (1, 0)])  9.76 us
    ppermute x6, waiting for transfers between devices, shift_x(): lax.ppermute(shard, 'x', [(i, (i + by) % count) for i in range(count)])  8.91 us
    ppermute x8, waiting for transfers between devices, swap(): return lax.ppermute(shard, axis, [(0, 1), (1, 0)])  8.85 us
  transfers between devices with their start and end apart: 23, of which 10 were waited for; matrix products, arithmetic and copies ran while one was open for 3% of the time, Pallas kernels for 15%

profile of v3, /device:TPU:2, one launch (start us, length us, event | category | flops | bytes accessed | tf_op | source)
XLA Modules:
  0.0 156.3 jit_solution(18376478906973308182)
XLA Ops:
  0.6 7.3 %collective-permute-start.5 = (bf16[512,128]{1,0:T(8,128)(2,1)}, bf16[512,128]{1,0:T(8,128)(2,1)S(1)}, u32[]{:S(2)}, u32[]{:S(2)}) collective-permute-start(bf16[512,128]{1,0:T(8,128)(2,1)} %param.10), channel_id=1, source_target_pairs={{0,128},{32,160},{64,192},{96,224},{128,0},{160,32},{192,64},{224,... | collective-permute-start | bytes 393224 | tf_op jit(solution)/shard_map/ppermute | solution.py:334
  7.9 3.8 %collective-permute-done.5 = bf16[512,128]{1,0:T(8,128)(2,1)S(1)} collective-permute-done((bf16[512,128]{1,0:T(8,128)(2,1)}, bf16[512,128]{1,0:T(8,128)(2,1)S(1)}, u32[]{:S(2)}, u32[]{:S(2)}) %collective-permute-start.5) | collective-permute-done | bytes 131104 | tf_op jit(solution)/shard_map/ppermute | solution.py:334
  11.7 1.0 pad_maximum_fusion.2
  12.7 4.7 %collective-permute-start.6 = (bf16[2,512,128]{2,1,0:T(8,128)(2,1)S(1)}, bf16[2,512,128]{2,1,0:T(8,128)(2,1)S(1)}, u32[]{:S(2)}, u32[]{:S(2)}) collective-permute-start(bf16[2,512,128]{2,1,0:T(8,128)(2,1)S(1)} %pad_maximum_fusion.2), channel_id=1, source_target_pairs={{0,64},{32,96},{64,0},{96,32},{128,192},{160,224},{192,128},{224,1... | collective-permute-start | bytes 786440 | tf_op jit(solution)/shard_map/ppermute | solution.py:334
  17.4 9.8 %collective-permute-done.6 = bf16[2,512,128]{2,1,0:T(8,128)(2,1)S(1)} collective-permute-done((bf16[2,512,128]{2,1,0:T(8,128)(2,1)S(1)}, bf16[2,512,128]{2,1,0:T(8,128)(2,1)S(1)}, u32[]{:S(2)}, u32[]{:S(2)}) %collective-permute-start.6) | collective-permute-done | bytes 262176 | tf_op jit(solution)/shard_map/ppermute | solution.py:334
  27.2 0.1 pad_maximum_fusion.1.refs_0_
  27.2 0.1 collective-permute-start.10
  27.3 3.3 %collective-permute-start.1 = (bf16[256,512]{1,0:T(8,128)(2,1)S(1)}, bf16[256,512]{1,0:T(8,128)(2,1)S(1)}, u32[]{:S(2)}, u32[]{:S(2)}) collective-permute-start(bf16[256,512]{1,0:T(8,128)(2,1)S(1)} %copy-done.11), channel_id=1, source_target_pairs={{0,4},{4,0},{1,5},{5,1},{2,6},{6,2},{3,7},{7,3},{8,12},{12,8},{9,1... | collective-permute-start | bytes 786440 | tf_op jit(solution)/shard_map/ppermute | solution.py:35
  30.6 6.4 %collective-permute-done.1 = bf16[256,512]{1,0:T(8,128)(2,1)S(1)} collective-permute-done((bf16[256,512]{1,0:T(8,128)(2,1)S(1)}, bf16[256,512]{1,0:T(8,128)(2,1)S(1)}, u32[]{:S(2)}, u32[]{:S(2)}) %collective-permute-start.1) | collective-permute-done | bytes 262176 | tf_op jit(solution)/shard_map/ppermute | solution.py:35
  37.0 0.1 pad_maximum_fusion.cot0
  37.1 0.6 collective-permute-start.4
  37.7 2.4 %collective-permute-start.3 = (bf16[2,256,512]{2,1,0:T(8,128)(2,1)S(1)}, bf16[2,256,512]{2,1,0:T(8,128)(2,1)}, u32[]{:S(2)}, u32[]{:S(2)}) collective-permute-start(bf16[2,256,512]{2,1,0:T(8,128)(2,1)S(1)} %pad_maximum_fusion.cot0), channel_id=1, source_target_pairs={{0,2},{1,3},{2,0},{3,1},{4,6},{5,7},{6,4},{7,5},{8,10},{9,11},{10,... | collective-permute-start | bytes 1572872 | tf_op jit(solution)/shard_map/ppermute | solution.py:339
  40.1 1.6 %collective-permute-start.8 = (bf16[4,512,128]{2,1,0:T(8,128)(2,1)S(1)}, bf16[4,512,128]{2,1,0:T(8,128)(2,1)S(1)}, u32[]{:S(2)}, u32[]{:S(2)}) collective-permute-start(bf16[4,512,128]{2,1,0:T(8,128)(2,1)S(1)} %pad_maximum_fusion.1.refs_0_), channel_id=1, source_target_pairs={{0,16},{16,0},{1,17},{17,1},{2,18},{18,2},{3,19},{19,3},{4,20},{20... | collective-permute-start | bytes 1572872 | tf_op jit(solution)/shard_map/ppermute | solution.py:35
  41.7 0.9 collective-permute-start.12
  42.6 1.3 collective-permute-start
  43.9 0.8 collective-permute-done
  44.8 1.2 carried_columns.1
  46.0 25.9 %all-to-all-start = ((bf16[32,16,256]{2,1,0:T(8,128)(2,1)}), bf16[32,16,256]{2,1,0:T(8,128)(2,1)S(1)}, u32[]{:S(2)}, u32[]{:S(2)}) async-start(bf16[32,16,256]{2,1,0:T(8,128)(2,1)} %bitcast.38), calls=%async_computation | async-start | bytes 524288 | tf_op jit(solution)/shard_map/all_to_all | solution.py:428
  71.9 1.9 %collective-permute-start.2 = (bf16[2,256,512]{2,1,0:T(8,128)(2,1)S(1)}, bf16[2,256,512]{2,1,0:T(8,128)(2,1)}, u32[]{:S(2)}, u32[]{:S(2)}) collective-permute-start(bf16[2,256,512]{2,1,0:T(8,128)(2,1)S(1)} %pad_maximum_fusion.cot0), channel_id=1, source_target_pairs={{0,1},{1,2},{2,3},{3,0},{4,5},{5,6},{6,7},{7,4},{8,9},{9,10},{10,1... | collective-permute-start | bytes 1572872 | tf_op jit(solution)/shard_map/ppermute | solution.py:339
  73.8 0.5 collective-permute-start.11
  74.3 0.1 collective-permute-start.9
  74.4 0.4 collective-permute-start.13
  74.8 9.5 %all-to-all-done.x_ref = bf16[32,16,256]{2,1,0:T(8,128)(2,1)S(1)} async-done(((bf16[32,16,256]{2,1,0:T(8,128)(2,1)}), bf16[32,16,256]{2,1,0:T(8,128)(2,1)S(1)}, u32[]{:S(2)}, u32[]{:S(2)}) %all-to-all-start) | async-done | bytes 262176 | tf_op jit(solution)/shard_map/all_to_all | solution.py:428
  84.2 3.8 %conv_forward.1 = bf16[32,16,256]{2,1,0:T(8,128)(2,1)} custom-call(bf16[32,16,256]{2,1,0:T(8,128)(2,1)S(1)} %all-to-all-done.x_ref, f32[2,8192]{1,0:T(2,128)S(1)} %copy-done.5), custom_call_target="tpu_custom_call" | custom-call | flops 6000000000 | bytes 600000 | tf_op jit(solution)/shard_map/conv_forward/pallas_call | solution.py:180
  88.1 4.1 %all-to-all-start.1 = ((bf16[32,16,256]{2,1,0:T(8,128)(2,1)}), bf16[32,16,256]{2,1,0:T(8,128)(2,1)S(1)}, u32[]{:S(2)}, u32[]{:S(2)}) async-start(bf16[32,16,256]{2,1,0:T(8,128)(2,1)} %conv_forward.1), calls=%async_computation.1 | async-start | bytes 524288 | tf_op jit(solution)/shard_map/all_to_all | solution.py:432
  92.1 0.1 stack.41.at_ref
  92.3 4.5 %grad_matmul.1 = (f32[256,512]{1,0:T(8,128)}, bf16[256,512]{1,0:T(8,128)(2,1)}, bf16[512,256]{1,0:T(8,128)(2,1)}) custom-call(s32[5]{0:T(128)S(1)} %stack.41.at_ref, bf16[3,256,512]{2,1,0:T(8,128)(2,1)S(1)} %bitcast.26, bf16[3,2,512]{2,1,0:T(2,128)(2,1)S(1)} %bitcast.33, f32[3,3,512]{2,1,0:T(4,128)S(1)} %copy-done.3, ...), custom_call_target="tpu_custom_call" | custom-call | flops 4000000000 | bytes 6500000 | tf_op jit(solution)/shard_map/grad_matmul/pallas_call | solution.py:284
  96.8 7.5 %all-to-all-done.1 = bf16[32,16,256]{2,1,0:T(8,128)(2,1)S(1)} async-done(((bf16[32,16,256]{2,1,0:T(8,128)(2,1)}), bf16[32,16,256]{2,1,0:T(8,128)(2,1)S(1)}, u32[]{:S(2)}, u32[]{:S(2)}) %all-to-all-start.1) | async-done | bytes 262176 | tf_op jit(solution)/shard_map/all_to_all | solution.py:432
  104.3 3.9 %all-to-all-start.2 = ((bf16[32,16,256]{2,1,0:T(8,128)(2,1)}), bf16[32,16,256]{2,1,0:T(8,128)(2,1)S(1)}, u32[]{:S(2)}, u32[]{:S(2)}) async-start(bf16[32,16,256]{2,1,0:T(8,128)(2,1)} %bitcast.44), calls=%async_computation.2 | async-start | bytes 524288 | tf_op jit(solution)/shard_map/all_to_all | solution.py:428
  108.2 0.7 copy-done.4
  108.9 1.0 copy-done.6
  109.9 4.8 %mix_matmul.1 = (bf16[2,256,512]{2,1,0:T(8,128)(2,1)}, bf16[2,256,512]{2,1,0:T(8,128)(2,1)}, bf16[2,256,512]{2,1,0:T(8,128)(2,1)}, bf16[2,256,512]{2,1,0:T(8,128)(2,1)}, f32[256,512]{1,0:T(8,128)}) custom-call(s32[5]{0:T(128)S(1)} %stack.41.at_ref, bf16[512,256]{1,0:T(8,128)(2,1)S(1)} %bitcast.30, bf16[3,256,512]{2,1,0:T(8,128)(2,1)S(1)} %bitcast.27, ...), custom_call_target="tpu_custom_call" | custom-call | flops 4000000000 | bytes 6500000 | tf_op jit(solution)/shard_map/mix_matmul/pallas_call | solution.py:321
  114.7 1.8 %collective-permute-start.14 = (bf16[2,256,512]{2,1,0:T(8,128)(2,1)}, bf16[2,256,512]{2,1,0:T(8,128)(2,1)S(1)}, u32[]{:S(2)}, u32[]{:S(2)}) collective-permute-start(bf16[2,256,512]{2,1,0:T(8,128)(2,1)} %get-tuple-element.18), channel_id=1, source_target_pairs={{0,1},{1,2},{2,3},{3,0},{4,5},{5,6},{6,7},{7,4},{8,9},{9,10},{10,1... | collective-permute-start | bytes 1572872 | tf_op jit(solution)/shard_map/ppermute | solution.py:339
  116.6 1.4 collective-permute-start.15
  118.0 0.7 collective-permute-start.16
  118.6 1.9 %all-to-all-done.2.m_ref = bf16[32,16,256]{2,1,0:T(8,128)(2,1)S(1)} async-done(((bf16[32,16,256]{2,1,0:T(8,128)(2,1)}), bf16[32,16,256]{2,1,0:T(8,128)(2,1)S(1)}, u32[]{:S(2)}, u32[]{:S(2)}) %all-to-all-start.2) | async-done | bytes 262176 | tf_op jit(solution)/shard_map/all_to_all | solution.py:428
  120.5 7.0 %conv_backward.1 = (bf16[32,16,256]{2,1,0:T(8,128)(2,1)}, f32[2,32,256]{2,1,0:T(8,128)S(1)}) custom-call(bf16[32,16,256]{2,1,0:T(8,128)(2,1)S(1)} %all-to-all-done.2.m_ref, bf16[32,16,256]{2,1,0:T(8,128)(2,1)S(1)} %all-to-all-done.x_ref, f32[2,8192]{1,0:T(2,128)S(1)} %copy-done.5), custom_call_target="tpu_custom_call" | custom-call | flops 10000000000 | bytes 1000000 | tf_op jit(solution)/shard_map/conv_backward/pallas_call | solution.py:198
  127.5 6.5 %all-to-all-start.3 = ((bf16[32,16,256]{2,1,0:T(8,128)(2,1)}), bf16[32,16,256]{2,1,0:T(8,128)(2,1)S(1)}, u32[]{:S(2)}, u32[]{:S(2)}) async-start(bf16[32,16,256]{2,1,0:T(8,128)(2,1)} %get-tuple-element.22), calls=%async_computation.3 | async-start | bytes 524288 | tf_op jit(solution)/shard_map/all_to_all | solution.py:432
  134.0 5.6 %collective-permute-done.14 = bf16[2,256,512]{2,1,0:T(8,128)(2,1)S(1)} collective-permute-done((bf16[2,256,512]{2,1,0:T(8,128)(2,1)}, bf16[2,256,512]{2,1,0:T(8,128)(2,1)S(1)}, u32[]{:S(2)}, u32[]{:S(2)}) %collective-permute-start.14) | collective-permute-done | bytes 524320 | tf_op jit(solution)/shard_map/ppermute | solution.py:339
  139.6 3.3 %collective-permute-done.16 = bf16[2,256,512]{2,1,0:T(8,128)(2,1)} collective-permute-done((bf16[2,256,512]{2,1,0:T(8,128)(2,1)}, bf16[2,256,512]{2,1,0:T(8,128)(2,1)}, u32[]{:S(2)}, u32[]{:S(2)}) %collective-permute-start.16) | collective-permute-done | bytes 524320 | tf_op jit(solution)/shard_map/ppermute | solution.py:339
  143.0 1.2 fusion.1
  144.2 3.0 %collective-permute-start.17 = (bf16[256,512]{1,0:T(8,128)(2,1)S(1)}, bf16[256,512]{1,0:T(8,128)(2,1)}, u32[]{:S(2)}, u32[]{:S(2)}) collective-permute-start(bf16[256,512]{1,0:T(8,128)(2,1)S(1)} %fusion.1), channel_id=1, source_target_pairs={{0,4},{4,0},{1,5},{5,1},{2,6},{6,2},{3,7},{7,3},{8,12},{12,8},{9,1... | collective-permute-start | bytes 786440 | tf_op jit(solution)/shard_map/ppermute | solution.py:35
  147.2 0.7 copy.10
  147.9 2.2 %final_short.1 = (bf16[3,256,512]{2,1,0:T(8,128)(2,1)}, f32[3,8,512]{2,1,0:T(8,128)}, f32[3,16,512]{2,1,0:T(8,128)S(1)}) custom-call(bf16[512,256]{1,0:T(8,128)(2,1)S(1)} %bitcast.29, bf16[256,512]{1,0:T(8,128)(2,1)S(1)} %copy-done.2, f32[256,512]{1,0:T(8,128)S(1)} %copy-done.1, bf16[3,256,512]{2,1,0:T(8,128)(2,1)S(1)} %bitcast.28, ...), custom_call_target="tpu_custom_call" | custom-call | flops 5000000 | bytes 3500000 | tf_op jit(solution)/shard_map/final_short/pallas_call | solution.py:378
  150.0 1.3 collective-permute-start.18
  151.3 2.4 %collective-permute-done.17 = bf16[256,512]{1,0:T(8,128)(2,1)} collective-permute-done((bf16[256,512]{1,0:T(8,128)(2,1)S(1)}, bf16[256,512]{1,0:T(8,128)(2,1)}, u32[]{:S(2)}, u32[]{:S(2)}) %collective-permute-start.17) | collective-permute-done | bytes 262176 | tf_op jit(solution)/shard_map/ppermute | solution.py:35
  153.8 1.9 %fusion = bf16[256,512]{1,0:T(8,128)(2,1)} fusion(bf16[256,512]{1,0:T(8,128)(2,1)} %collective-permute-done.17, bf16[2,256,512]{2,1,0:T(8,128)(2,1)} %collective-permute-done.16, bf16[2,256,512]{2,1,0:T(8,128)(2,1)S(1)} %copy-done.9, bf16[2,256,512]{2,1,0:T(8,128)(2,1)S(1)} %collective-permute-done.14, bf16[2,256,512]{2,1,0:T(8,128)(2,1)S(1)} %copy-done.7), kind=kLoop, calls=%fused_computation.3 | loop fusion | flops 1310720 | bytes 1572864 | tf_op jit(solution)/shard_map/convert_element_type | solution.py:472
  155.7 0.7 edge_rows.1
  (37 shorter events, 0.1 us)
Async XLA Ops:
  0.6 11.1 %collective-permute-start.5 = (bf16[512,128]{1,0:T(8,128)(2,1)}, bf16[512,128]{1,0:T(8,128)(2,1)S(1)}, u32[]{:S(2)}, u32[]{:S(2)}) collective-permute-start(bf16[512,128]{1,0:T(8,128)(2,1)} %param.10), channel_id=1, source_target_pairs={{0,128},{32,160},{64,192},{96,224},{128,0},{160,32},{192,64},{224,... | collective-permute-start | bytes 393224 | tf_op jit(solution)/shard_map/ppermute | solution.py:334
  11.7 15.4 %copy-start.10 = (bf16[512,128]{1,0:T(8,128)(2,1)S(1)}, bf16[512,128]{1,0:T(8,128)(2,1)}, u32[]{:S(2)}) copy-start(bf16[512,128]{1,0:T(8,128)(2,1)} %param.10) | copy-start | bytes 393220
  12.7 14.6 %copy-start.11 = (bf16[256,512]{1,0:T(8,128)(2,1)S(1)}, bf16[256,512]{1,0:T(8,128)(2,1)}, u32[]{:S(2)}) copy-start(bf16[256,512]{1,0:T(8,128)(2,1)} %param.11) | copy-start | bytes 786436
  12.7 14.4 %collective-permute-start.6 = (bf16[2,512,128]{2,1,0:T(8,128)(2,1)S(1)}, bf16[2,512,128]{2,1,0:T(8,128)(2,1)S(1)}, u32[]{:S(2)}, u32[]{:S(2)}) collective-permute-start(bf16[2,512,128]{2,1,0:T(8,128)(2,1)S(1)} %pad_maximum_fusion.2), channel_id=1, source_target_pairs={{0,64},{32,96},{64,0},{96,32},{128,192},{160,224},{192,128},{224,1... | collective-permute-start | bytes 786440 | tf_op jit(solution)/shard_map/ppermute | solution.py:334
  27.2 15.4 %copy-start = (bf16[256,3,512]{2,0,1:T(8,128)(2,1)S(1)}, bf16[256,3,512]{2,0,1:T(8,128)(2,1)}, u32[]{:S(2)}) copy-start(bf16[256,3,512]{2,0,1:T(8,128)(2,1)} %param.6) | copy-start | bytes 2359300
  27.2 14.5 %collective-permute-start.10 = (bf16[4,512,128]{2,1,0:T(8,128)(2,1)S(1)}, bf16[4,512,128]{2,1,0:T(8,128)(2,1)S(1)}, u32[]{:S(2)}, u32[]{:S(2)}) collective-permute-start(bf16[4,512,128]{2,1,0:T(8,128)(2,1)S(1)} %pad_maximum_fusion.1.refs_0_), channel_id=1, source_target_pairs={{0,32},{32,0},{64,96},{96,64},{128,160},{160,128},{192,224},{224,1... | collective-permute-start | bytes 1572872 | tf_op jit(solution)/shard_map/ppermute | solution.py:334
  27.3 9.7 %collective-permute-start.1 = (bf16[256,512]{1,0:T(8,128)(2,1)S(1)}, bf16[256,512]{1,0:T(8,128)(2,1)S(1)}, u32[]{:S(2)}, u32[]{:S(2)}) collective-permute-start(bf16[256,512]{1,0:T(8,128)(2,1)S(1)} %copy-done.11), channel_id=1, source_target_pairs={{0,4},{4,0},{1,5},{5,1},{2,6},{6,2},{3,7},{7,3},{8,12},{12,8},{9,1... | collective-permute-start | bytes 786440 | tf_op jit(solution)/shard_map/ppermute | solution.py:35
  37.0 7.7 %copy-start.3 = (f32[3,3,512]{2,1,0:T(4,128)S(1)}, f32[3,3,512]{2,1,0:T(4,128)}, u32[]{:S(2)}) copy-start(f32[3,3,512]{2,1,0:T(4,128)} %taps_ref.9) | copy-start | bytes 55300
  37.1 36.6 %collective-permute-start.4 = (bf16[2,256,512]{2,1,0:T(8,128)(2,1)S(1)}, bf16[2,256,512]{2,1,0:T(8,128)(2,1)}, u32[]{:S(2)}, u32[]{:S(2)}) collective-permute-start(bf16[2,256,512]{2,1,0:T(8,128)(2,1)S(1)} %pad_maximum_fusion.cot0), channel_id=1, source_target_pairs={{0,3},{1,0},{2,1},{3,2},{4,7},{5,4},{6,5},{7,6},{8,11},{9,8},{10,9... | collective-permute-start | bytes 1572872 | tf_op jit(solution)/shard_map/ppermute | solution.py:339
  37.7 36.0 %collective-permute-start.3 = (bf16[2,256,512]{2,1,0:T(8,128)(2,1)S(1)}, bf16[2,256,512]{2,1,0:T(8,128)(2,1)}, u32[]{:S(2)}, u32[]{:S(2)}) collective-permute-start(bf16[2,256,512]{2,1,0:T(8,128)(2,1)S(1)} %pad_maximum_fusion.cot0), channel_id=1, source_target_pairs={{0,2},{1,3},{2,0},{3,1},{4,6},{5,7},{6,4},{7,5},{8,10},{9,11},{10,... | collective-permute-start | bytes 1572872 | tf_op jit(solution)/shard_map/ppermute | solution.py:339
  40.1 34.1 %collective-permute-start.8 = (bf16[4,512,128]{2,1,0:T(8,128)(2,1)S(1)}, bf16[4,512,128]{2,1,0:T(8,128)(2,1)S(1)}, u32[]{:S(2)}, u32[]{:S(2)}) collective-permute-start(bf16[4,512,128]{2,1,0:T(8,128)(2,1)S(1)} %pad_maximum_fusion.1.refs_0_), channel_id=1, source_target_pairs={{0,16},{16,0},{1,17},{17,1},{2,18},{18,2},{3,19},{19,3},{4,20},{20... | collective-permute-start | bytes 1572872 | tf_op jit(solution)/shard_map/ppermute | solution.py:35
  41.7 32.6 %collective-permute-start.12 = (bf16[4,512,128]{2,1,0:T(8,128)(2,1)S(1)}, bf16[4,512,128]{2,1,0:T(8,128)(2,1)}, u32[]{:S(2)}, u32[]{:S(2)}) collective-permute-start(bf16[4,512,128]{2,1,0:T(8,128)(2,1)S(1)} %collective-permute-done.10.refs_4_), channel_id=1, source_target_pairs={{0,16},{16,0},{1,17},{17,1},{2,18},{18,2},{3,19},{19,3},{4,20},{20... | collective-permute-start | bytes 1572872 | tf_op jit(solution)/shard_map/ppermute | solution.py:35
  42.6 2.1 %collective-permute-start = (bf16[2,3,512]{2,0,1:T(2,128)(2,1)S(1)}, bf16[2,3,512]{2,0,1:T(2,128)(2,1)S(1)}, u32[]{:S(2)}, u32[]{:S(2)}) collective-permute-start(bf16[2,3,512]{2,0,1:T(2,128)(2,1)S(1)} %slice.27), channel_id=1, source_target_pairs={{0,8},{8,16},{16,24},{24,32},{32,40},{40,48},{48,56},{56,64},{64,7... | collective-permute-start | bytes 18440 | tf_op jit(solution)/shard_map/ppermute | solution.py:31
  46.0 38.3 %copy-start.5 = (f32[2,8192]{1,0:T(2,128)S(1)}, f32[2,8192]{1,0:T(2,128)}, u32[]{:S(2)}) copy-start(f32[2,8192]{1,0:T(2,128)} %h_ref.3) | copy-start | bytes 196612
  46.0 38.3 %all-to-all-start = ((bf16[32,16,256]{2,1,0:T(8,128)(2,1)}), bf16[32,16,256]{2,1,0:T(8,128)(2,1)S(1)}, u32[]{:S(2)}, u32[]{:S(2)}) async-start(bf16[32,16,256]{2,1,0:T(8,128)(2,1)} %bitcast.38), calls=%async_computation | async-start | bytes 524288 | tf_op jit(solution)/shard_map/all_to_all | solution.py:428
  71.9 20.4 %collective-permute-start.2 = (bf16[2,256,512]{2,1,0:T(8,128)(2,1)S(1)}, bf16[2,256,512]{2,1,0:T(8,128)(2,1)}, u32[]{:S(2)}, u32[]{:S(2)}) collective-permute-start(bf16[2,256,512]{2,1,0:T(8,128)(2,1)S(1)} %pad_maximum_fusion.cot0), channel_id=1, source_target_pairs={{0,1},{1,2},{2,3},{3,0},{4,5},{5,6},{6,7},{7,4},{8,9},{9,10},{10,1... | collective-permute-start | bytes 1572872 | tf_op jit(solution)/shard_map/ppermute | solution.py:339
  73.7 18.5 %collective-permute-start.7 = (bf16[4,512,128]{2,1,0:T(8,128)(2,1)S(1)}, bf16[4,512,128]{2,1,0:T(8,128)(2,1)}, u32[]{:S(2)}, u32[]{:S(2)}) collective-permute-start(bf16[4,512,128]{2,1,0:T(8,128)(2,1)S(1)} %pad_maximum_fusion.1.refs_0_), channel_id=1, source_target_pairs={{0,8},{8,0},{1,9},{9,1},{2,10},{10,2},{3,11},{11,3},{4,12},{12,4},... | collective-permute-start | bytes 1572872 | tf_op jit(solution)/shard_map/ppermute | solution.py:35
  73.8 18.5 %collective-permute-start.11 = (bf16[4,512,128]{2,1,0:T(8,128)(2,1)S(1)}, bf16[4,512,128]{2,1,0:T(8,128)(2,1)}, u32[]{:S(2)}, u32[]{:S(2)}) collective-permute-start(bf16[4,512,128]{2,1,0:T(8,128)(2,1)S(1)} %collective-permute-done.10.refs_4_), channel_id=1, source_target_pairs={{0,8},{8,0},{1,9},{9,1},{2,10},{10,2},{3,11},{11,3},{4,12},{12,4},... | collective-permute-start | bytes 1572872 | tf_op jit(solution)/shard_map/ppermute | solution.py:35
  74.3 18.0 %collective-permute-start.9 = (bf16[4,512,128]{2,1,0:T(8,128)(2,1)S(1)}, bf16[4,512,128]{2,1,0:T(8,128)(2,1)}, u32[]{:S(2)}, u32[]{:S(2)}) collective-permute-start(bf16[4,512,128]{2,1,0:T(8,128)(2,1)S(1)} %collective-permute-done.8.refs_2_), channel_id=1, source_target_pairs={{0,8},{8,0},{1,9},{9,1},{2,10},{10,2},{3,11},{11,3},{4,12},{12,4},... | collective-permute-start | bytes 1572872 | tf_op jit(solution)/shard_map/ppermute | solution.py:35
  74.4 17.9 %collective-permute-start.13 = (bf16[4,512,128]{2,1,0:T(8,128)(2,1)}, bf16[4,512,128]{2,1,0:T(8,128)(2,1)}, u32[]{:S(2)}, u32[]{:S(2)}) collective-permute-start(bf16[4,512,128]{2,1,0:T(8,128)(2,1)} %collective-permute-done.12.refs_6_), channel_id=1, source_target_pairs={{0,8},{8,0},{1,9},{9,1},{2,10},{10,2},{3,11},{11,3},{4,12},{12,4},... | collective-permute-start | bytes 1572872 | tf_op jit(solution)/shard_map/ppermute | solution.py:35
  88.1 16.2 %all-to-all-start.1 = ((bf16[32,16,256]{2,1,0:T(8,128)(2,1)}), bf16[32,16,256]{2,1,0:T(8,128)(2,1)S(1)}, u32[]{:S(2)}, u32[]{:S(2)}) async-start(bf16[32,16,256]{2,1,0:T(8,128)(2,1)} %conv_forward.1), calls=%async_computation.1 | async-start | bytes 524288 | tf_op jit(solution)/shard_map/all_to_all | solution.py:432
  104.3 16.2 %all-to-all-start.2 = ((bf16[32,16,256]{2,1,0:T(8,128)(2,1)}), bf16[32,16,256]{2,1,0:T(8,128)(2,1)S(1)}, u32[]{:S(2)}, u32[]{:S(2)}) async-start(bf16[32,16,256]{2,1,0:T(8,128)(2,1)} %bitcast.44), calls=%async_computation.2 | async-start | bytes 524288 | tf_op jit(solution)/shard_map/all_to_all | solution.py:428
  108.2 0.7 copy-start.4
  108.9 1.0 copy-start.6
  114.7 24.9 %collective-permute-start.14 = (bf16[2,256,512]{2,1,0:T(8,128)(2,1)}, bf16[2,256,512]{2,1,0:T(8,128)(2,1)S(1)}, u32[]{:S(2)}, u32[]{:S(2)}) collective-permute-start(bf16[2,256,512]{2,1,0:T(8,128)(2,1)} %get-tuple-element.18), channel_id=1, source_target_pairs={{0,1},{1,2},{2,3},{3,0},{4,5},{5,6},{6,7},{7,4},{8,9},{9,10},{10,1... | collective-permute-start | bytes 1572872 | tf_op jit(solution)/shard_map/ppermute | solution.py:339
  116.6 23.1 %collective-permute-start.15 = (bf16[2,256,512]{2,1,0:T(8,128)(2,1)}, bf16[2,256,512]{2,1,0:T(8,128)(2,1)S(1)}, u32[]{:S(2)}, u32[]{:S(2)}) collective-permute-start(bf16[2,256,512]{2,1,0:T(8,128)(2,1)} %get-tuple-element.19), channel_id=1, source_target_pairs={{0,2},{1,3},{2,0},{3,1},{4,6},{5,7},{6,4},{7,5},{8,10},{9,11},{10,... | collective-permute-start | bytes 1572872 | tf_op jit(solution)/shard_map/ppermute | solution.py:339
  118.0 25.0 %collective-permute-start.16 = (bf16[2,256,512]{2,1,0:T(8,128)(2,1)}, bf16[2,256,512]{2,1,0:T(8,128)(2,1)}, u32[]{:S(2)}, u32[]{:S(2)}) collective-permute-start(bf16[2,256,512]{2,1,0:T(8,128)(2,1)} %get-tuple-element.20), channel_id=1, source_target_pairs={{0,3},{1,0},{2,1},{3,2},{4,7},{5,4},{6,5},{7,6},{8,11},{9,8},{10,9... | collective-permute-start | bytes 1572872 | tf_op jit(solution)/shard_map/ppermute | solution.py:339
  127.5 15.4 %copy-start.7 = (bf16[2,256,512]{2,1,0:T(8,128)(2,1)S(1)}, bf16[2,256,512]{2,1,0:T(8,128)(2,1)}, u32[]{:S(2)}) copy-start(bf16[2,256,512]{2,1,0:T(8,128)(2,1)} %get-tuple-element.17) | copy-start | bytes 1572868
  127.5 20.3 %all-to-all-start.3 = ((bf16[32,16,256]{2,1,0:T(8,128)(2,1)}), bf16[32,16,256]{2,1,0:T(8,128)(2,1)S(1)}, u32[]{:S(2)}, u32[]{:S(2)}) async-start(bf16[32,16,256]{2,1,0:T(8,128)(2,1)} %get-tuple-element.22), calls=%async_computation.3 | async-start | bytes 524288 | tf_op jit(solution)/shard_map/all_to_all | solution.py:432
  139.6 3.3 %copy-start.8 = (bf16[2,256,512]{2,1,0:T(8,128)(2,1)}, bf16[2,256,512]{2,1,0:T(8,128)(2,1)S(1)}, u32[]{:S(2)}) copy-start(bf16[2,256,512]{2,1,0:T(8,128)(2,1)S(1)} %collective-permute-done.15) | copy-start | bytes 1572868
  142.9 4.9 %copy-start.1 = (f32[256,512]{1,0:T(8,128)S(1)}, f32[256,512]{1,0:T(8,128)}, u32[]{:S(2)}) copy-start(f32[256,512]{1,0:T(8,128)} %get-tuple-element.24.query_grad_ref) | copy-start | bytes 1572868
  142.9 4.9 %copy-start.2 = (bf16[256,512]{1,0:T(8,128)(2,1)S(1)}, bf16[256,512]{1,0:T(8,128)(2,1)}, u32[]{:S(2)}) copy-start(bf16[256,512]{1,0:T(8,128)(2,1)} %get-tuple-element.23.mixed_ref) | copy-start | bytes 786436
  144.2 9.6 %collective-permute-start.17 = (bf16[256,512]{1,0:T(8,128)(2,1)S(1)}, bf16[256,512]{1,0:T(8,128)(2,1)}, u32[]{:S(2)}, u32[]{:S(2)}) collective-permute-start(bf16[256,512]{1,0:T(8,128)(2,1)S(1)} %fusion.1), channel_id=1, source_target_pairs={{0,4},{4,0},{1,5},{5,1},{2,6},{6,2},{3,7},{7,3},{8,12},{12,8},{9,1... | collective-permute-start | bytes 786440 | tf_op jit(solution)/shard_map/ppermute | solution.py:35
  147.9 5.9 %copy-start.9 = (bf16[2,256,512]{2,1,0:T(8,128)(2,1)S(1)}, bf16[2,256,512]{2,1,0:T(8,128)(2,1)}, u32[]{:S(2)}) copy-start(bf16[2,256,512]{2,1,0:T(8,128)(2,1)} %copy-done.8) | copy-start | bytes 1572868
  150.0 5.6 %collective-permute-start.18 = (f32[3,8,512]{2,1,0:T(8,128)}, f32[3,8,512]{2,1,0:T(8,128)S(1)}, u32[]{:S(2)}, u32[]{:S(2)}) collective-permute-start(f32[3,8,512]{2,1,0:T(8,128)} %get-tuple-element.26), channel_id=1, source_target_pairs={{8,0},{16,8},{24,16},{32,24},{40,32},{48,40},{56,48},{64,56},{72,6... | collective-permute-start | bytes 147464 | tf_op jit(solution)/shard_map/ppermute | solution.py:31

commit v4 on v3

--- a/solution.py
+++ b/solution.py
@@ -214,20 +214,18 @@
     )(m, x, h)
 
 
-def whole_columns(at_ref, sign, step, refs):
-    own, own_c, side, side_c, own2, own_c2, side2, side_c2 = refs
+def met_places(at_ref, sign):
+    z = at_ref[4]
+    for first in (z, (z + 1) & 7, (z + 7) & 7, z ^ 2):
+        for chan in (first, first ^ 4):
+            yield (sign * ((chan & 3) - at_ref[3])) & 3, (chan >> 2) ^ at_ref[2]
+
+
+def whole_columns(at_ref, place, refs):
     first = at_ref[1] == 0
-    met = ((at_ref[2] + step) & 1) * 4 + ((at_ref[3] + sign * (step // 2) + 4) & 3)
-    apart = at_ref[4] ^ met
-    early = (apart & 1) == 0
-    place = (apart & 2) + (apart >> 2)
-
-    def pick(a, b):
-        return jnp.where(early, a[place], b[place])
-
+    own, own_c, side, side_c = (ref[place % 2] for ref in refs[place // 2 * 4 : place // 2 * 4 + 4])
     parts = []
-    for a, b, c, d in ((own, own2, own_c, own_c2), (side, side2, side_c, side_c2)):
-        mine, other = pick(a, b), pick(c, d)
+    for mine, other in ((own, own_c), (side, side_c)):
         parts += [jnp.where(first, mine, other), jnp.where(first, other, mine)]
     return jnp.concatenate(parts, axis=1)
 
@@ -253,16 +251,17 @@
     *w_refs, out_ref, mixed_ref, sent_ref = refs
     yl = at_ref[0]
     width = cot0.shape[2] // 2
-    for step in range(8):
-        cot_ref = (cot0, cot1, cot2, cot3)[step // 2]
-        e = step % 2
-        lhs = jnp.concatenate(
-            [cot_ref[e, :, side_columns(yl, width)], cot_ref[e, :, side_columns(1 - yl, width)]],
-            axis=1,
-        )
+    for step, (k, e) in enumerate(met_places(at_ref, -1)):
+        halves = []
+        for at in (yl, 1 - yl):
+            c0, c1, c2, c3 = (
+                cot_ref[e, :, side_columns(at, width)] for cot_ref in (cot0, cot1, cot2, cot3)
+            )
+            halves.append(jnp.where(k < 2, jnp.where(k == 0, c0, c1), jnp.where(k == 2, c2, c3)))
+        lhs = jnp.concatenate(halves, axis=1)
         part = lax.dot_general(
             lhs,
-            whole_columns(at_ref, -1, step, w_refs),
+            whole_columns(at_ref, step, w_refs),
             (((1,), (1,)), ((), ())),
             preferred_element_type=F32,
         )
@@ -305,19 +304,21 @@
     query_grad_ref[...] = grad_ref[...] * mixed_in
     gated = (query * mixed_in).astype(BF16)
     width = out0.shape[2] // 2
-    for step in range(8):
-        out_ref = (out0, out1, out2, out3)[step // 2]
-        e = step % 2
+    for step, (k, e) in enumerate(met_places(at_ref, 1)):
         part = jnp.dot(
-            gated, whole_columns(at_ref, 1, step, w_refs), preferred_element_type=F32
+            gated, whole_columns(at_ref, step, w_refs), preferred_element_type=F32
         ).astype(BF16)
-        out_ref[e, :, side_columns(yl, width)] = part[:, :width]
-        out_ref[e, :, side_columns(1 - yl, width)] = part[:, width:]
+        for turn, out_ref in enumerate((out0, out1, out2, out3)):
+
+            @pl.when(k == turn)
+            def _(out_ref=out_ref, part=part, e=e):
+                out_ref[e, :, side_columns(yl, width)] = part[:, :width]
+                out_ref[e, :, side_columns(1 - yl, width)] = part[:, width:]
 
 
 def mix_matmul(at, conv, side_args, skip, grad, ws):
     tok, rows = grad.shape
-    cols = 4 * ws[0].shape[2]
+    cols = 4 * ws[0].shape[-1]
     *parts, query_grad = pl.pallas_call(
         mix_mm_kernel,
         name="mix_matmul",
@@ -328,6 +329,11 @@
         cost_estimate=pl.CostEstimate(flops=4000000000, bytes_accessed=6500000, transcendentals=0),
     )(at, conv, *side_args, skip, grad, *ws)
     return parts, query_grad
+
+
+def shift_z(shard, by):
+    count = lax.axis_size("z")
+    return lax.ppermute(shard, "z", [(i, (i + by) % count) for i in range(count)])
 
 
 def cross_z(shard, by):
@@ -437,7 +443,7 @@
     tok_rows, _ = cotangent.shape
     groups_dev, seq_length = filters.shape
     rim = SHORT - 1
-    wide = lax.axis_size("x")
+    wide, deep = lax.axis_size("x"), lax.axis_size("z")
     yl, core = lax.axis_index("yl"), lax.axis_index("core")
     yh, x, z = lax.axis_index("yh"), lax.axis_index("x"), lax.axis_index("z")
 
@@ -446,15 +452,13 @@
     cot_pair = jnp.stack([cotangent, swap(cotangent, "yh")])
     cots = [cot_pair] + [shift_x(cot_pair, k) for k in range(1, wide)]
     w_pair = jnp.stack([out_weight, cross_z(out_weight, 4)])
-    w_own = jnp.concatenate([w_pair, cross_z(w_pair, 2)])
-    w_own2 = cross_z(w_own, 1)
-    w_side = swap(w_own, "yl")
-    w_side2 = swap(w_own2, "yl")
-    w_own_c = swap(w_own, "core")
-    w_side_c = swap(w_side, "core")
-    w_own_c2 = swap(w_own2, "core")
-    w_side_c2 = swap(w_side2, "core")
-    ws = (w_own, w_own_c, w_side, w_side_c, w_own2, w_own_c2, w_side2, w_side_c2)
+    pairs = [shift_z(w_pair, deep - 1), shift_z(w_pair, 1), cross_z(w_pair, 2)]
+    sides = [swap(w_pair, "yl")]
+    sides += [swap(p, "yl") for p in pairs]
+    pairs = [w_pair] + pairs
+    pairs_c = [swap(p, "core") for p in pairs]
+    sides_c = [swap(p, "core") for p in sides]
+    ws = tuple(w for group in zip(pairs, pairs_c, sides, sides_c) for w in group)
 
     side_args = (projected.transpose(1, 0, 2), before.transpose(1, 0, 2), short_weight)
     carried_sent = carried_columns(side_args)

time: 158 us -> 156 us (0.987)
  waiting for transfers between devices: 51 us -> 26.6 us
  local copies, waits for them, and re-layouts: 2.54 us -> 15.6 us
  starting transfers between devices: 73.5 us -> 79.7 us
    ppermute x3 -> x2, waiting for transfers between devices: 13.6 us -> 0.62 us  [cross_z(): lax.ppermute(shard, 'z', [(i, i ^ by) for i in range(lax.axis_size('z'))])]
    unnamed x25 -> x53, local copies, waits for them, and re-layouts: 2.44 us -> 14.8 us
    all_to_all x2, waiting for transfers between devices: 11.4 us -> 0.01 us  [channel_major(): return lax.all_to_all(sent, SEQ, split_axis=0, concat_axis=0, tiled=True)]
    all_to_all x2, starting transfers between devices: 29.8 us -> 21 us  [channel_major(): return lax.all_to_all(sent, SEQ, split_axis=0, concat_axis=0, tiled=True)]
    all_to_all x2, waiting for transfers between devices: 7.52 us -> 0.01 us  [token_major(): got = lax.all_to_all(block, SEQ, split_axis=0, concat_axis=0, tiled=True)]
    ppermute x8 -> x14, starting transfers between devices: 9.76 us -> 15.6 us  [swap(): return lax.ppermute(shard, axis, [(0, 1), (1, 0)])]
    all_to_all x2, starting transfers between devices: 10.6 us -> 15.5 us  [token_major(): got = lax.all_to_all(block, SEQ, split_axis=0, concat_axis=0, tiled=True)]
    ppermute x0 -> x2, starting transfers between devices: none -> 3.89 us  [shift_z(): lax.ppermute(shard, 'z', [(i, (i + by) % count) for i in range(count)])]
  transfers between devices with their start and end apart: 23 -> 30, of which waited for: 10 -> 8; matrix products, arithmetic and copies ran while one was open for 3% -> 5% of each run, Pallas kernels for 15% -> 16%
where the time goes in v4:
time: 156 us; the launch traced here: 154 us
  starting transfers between devices  79.7 us (51%)
  waiting for transfers between devices  26.6 us (17%)
  Pallas kernels  25.2 us (16%)
  local copies, waits for them, and re-layouts  15.6 us (10%)
  other arithmetic  5.77 us (4%)
    all_to_all x2, starting transfers between devices, channel_major(): return lax.all_to_all(sent, SEQ, split_axis=0, concat_axis=0, tiled=True)  21 us
    ppermute x14, starting transfers between devices, swap(): return lax.ppermute(shard, axis, [(0, 1), (1, 0)])  15.6 us
    all_to_all x2, starting transfers between devices, token_major(): got = lax.all_to_all(block, SEQ, split_axis=0, concat_axis=0, tiled=True)  15.5 us
    unnamed x53, local copies, waits for them, and re-layouts  14.8 us
    ppermute x6, waiting for transfers between devices, shift_x(): lax.ppermute(shard, 'x', [(i, (i + by) % count) for i in range(count)])  12.2 us
    ppermute x14, waiting for transfers between devices, swap(): return lax.ppermute(shard, axis, [(0, 1), (1, 0)])  12.2 us
    ppermute x2, starting transfers between devices, cross_z(): lax.ppermute(shard, 'z', [(i, i ^ by) for i in range(lax.axis_size('z'))])  11.9 us
    ppermute x6, starting transfers between devices, shift_x(): lax.ppermute(shard, 'x', [(i, (i + by) % count) for i in range(count)])  9.21 us
  transfers between devices with their start and end apart: 30, of which 8 were waited for; matrix products, arithmetic and copies ran while one was open for 5% of the time, Pallas kernels for 16%

profile of v4, /device:TPU:2, one launch (start us, length us, event | category | flops | bytes accessed | tf_op | source)
XLA Modules:
  0.0 153.8 jit_solution(14185411928875441199)
XLA Ops:
  0.6 7.3 %collective-permute-start.5 = (bf16[512,128]{1,0:T(8,128)(2,1)}, bf16[512,128]{1,0:T(8,128)(2,1)S(1)}, u32[]{:S(2)}, u32[]{:S(2)}) collective-permute-start(bf16[512,128]{1,0:T(8,128)(2,1)} %param.10), channel_id=1, source_target_pairs={{0,128},{32,160},{64,192},{96,224},{128,0},{160,32},{192,64},{224,... | collective-permute-start | bytes 393224 | tf_op jit(solution)/shard_map/ppermute | solution.py:340
  7.9 3.2 %collective-permute-start.1 = (bf16[256,512]{1,0:T(8,128)(2,1)}, bf16[256,512]{1,0:T(8,128)(2,1)S(1)}, u32[]{:S(2)}, u32[]{:S(2)}) collective-permute-start(bf16[256,512]{1,0:T(8,128)(2,1)} %param.11), channel_id=1, source_target_pairs={{0,4},{4,0},{1,5},{5,1},{2,6},{6,2},{3,7},{7,3},{8,12},{12,8},{9,1... | collective-permute-start | bytes 786440 | tf_op jit(solution)/shard_map/ppermute | solution.py:35
  11.7 1.0 pad_maximum_fusion.1.refs_0_
  12.7 4.7 %collective-permute-start.17 = (bf16[2,512,128]{2,1,0:T(8,128)(2,1)S(1)}, bf16[2,512,128]{2,1,0:T(8,128)(2,1)S(1)}, u32[]{:S(2)}, u32[]{:S(2)}) collective-permute-start(bf16[2,512,128]{2,1,0:T(8,128)(2,1)S(1)} %pad_maximum_fusion.1.refs_0_), channel_id=1, source_target_pairs={{0,64},{32,96},{64,0},{96,32},{128,192},{160,224},{192,128},{224,1... | collective-permute-start | bytes 786440 | tf_op jit(solution)/shard_map/ppermute | solution.py:340
  17.4 3.9 %collective-permute-start.9 = (bf16[2,512,128]{2,1,0:T(8,128)(2,1)S(1)}, bf16[2,512,128]{2,1,0:T(8,128)(2,1)}, u32[]{:S(2)}, u32[]{:S(2)}) collective-permute-start(bf16[2,512,128]{2,1,0:T(8,128)(2,1)S(1)} %pad_maximum_fusion.1.refs_0_), channel_id=1, source_target_pairs={{0,224},{32,0},{64,32},{96,64},{128,96},{160,128},{192,160},{224,1... | collective-permute-start | bytes 786440 | tf_op jit(solution)/shard_map/ppermute | solution.py:336
  21.3 0.7 slice.27
  22.0 1.3 collective-permute-start
  23.3 0.8 collective-permute-done
  24.1 4.4 %collective-permute-start.7 = (bf16[2,512,128]{2,1,0:T(8,128)(2,1)S(1)}, bf16[2,512,128]{2,1,0:T(8,128)(2,1)}, u32[]{:S(2)}, u32[]{:S(2)}) collective-permute-start(bf16[2,512,128]{2,1,0:T(8,128)(2,1)S(1)} %pad_maximum_fusion.1.refs_0_), channel_id=1, source_target_pairs={{0,16},{16,0},{1,17},{17,1},{2,18},{18,2},{3,19},{19,3},{4,20},{20... | collective-permute-start | bytes 786440 | tf_op jit(solution)/shard_map/ppermute | solution.py:35
  29.2 0.9 collective-permute-done.9.refs_4_
  30.1 1.6 %collective-permute-start.15 = (bf16[2,512,128]{2,1,0:T(8,128)(2,1)S(1)}, bf16[2,512,128]{2,1,0:T(8,128)(2,1)}, u32[]{:S(2)}, u32[]{:S(2)}) collective-permute-start(bf16[2,512,128]{2,1,0:T(8,128)(2,1)S(1)} %collective-permute-done.13.refs_8_), channel_id=1, source_target_pairs={{0,16},{16,0},{1,17},{17,1},{2,18},{18,2},{3,19},{19,3},{4,20},{20... | collective-permute-start | bytes 786440 | tf_op jit(solution)/shard_map/ppermute | solution.py:35
  31.6 1.0 pad_maximum_fusion.cot0
  32.7 3.2 %collective-permute-done.7.refs_2_ = bf16[2,512,128]{2,1,0:T(8,128)(2,1)} collective-permute-done((bf16[2,512,128]{2,1,0:T(8,128)(2,1)S(1)}, bf16[2,512,128]{2,1,0:T(8,128)(2,1)}, u32[]{:S(2)}, u32[]{:S(2)}) %collective-permute-start.7) | collective-permute-done | bytes 262176 | tf_op jit(solution)/shard_map/ppermute | solution.py:35
  36.4 1.2 carried_columns.1
  37.6 13.4 %all-to-all-start = ((bf16[32,16,256]{2,1,0:T(8,128)(2,1)}), bf16[32,16,256]{2,1,0:T(8,128)(2,1)S(1)}, u32[]{:S(2)}, u32[]{:S(2)}) async-start(bf16[32,16,256]{2,1,0:T(8,128)(2,1)} %bitcast.38), calls=%async_computation | async-start | bytes 524288 | tf_op jit(solution)/shard_map/all_to_all | solution.py:434
  52.0 1.6 %collective-permute-start.11 = (bf16[2,512,128]{2,1,0:T(8,128)(2,1)}, bf16[2,512,128]{2,1,0:T(8,128)(2,1)}, u32[]{:S(2)}, u32[]{:S(2)}) collective-permute-start(bf16[2,512,128]{2,1,0:T(8,128)(2,1)} %collective-permute-done.9.refs_4_), channel_id=1, source_target_pairs={{0,16},{16,0},{1,17},{17,1},{2,18},{18,2},{3,19},{19,3},{4,20},{20... | collective-permute-start | bytes 786440 | tf_op jit(solution)/shard_map/ppermute | solution.py:35
  54.2 0.7 copy-done.14
  54.9 2.4 %collective-permute-start.3 = (bf16[2,256,512]{2,1,0:T(8,128)(2,1)S(1)}, bf16[2,256,512]{2,1,0:T(8,128)(2,1)S(1)}, u32[]{:S(2)}, u32[]{:S(2)}) collective-permute-start(bf16[2,256,512]{2,1,0:T(8,128)(2,1)S(1)} %pad_maximum_fusion.cot0), channel_id=1, source_target_pairs={{0,2},{1,3},{2,0},{3,1},{4,6},{5,7},{6,4},{7,5},{8,10},{9,11},{10,... | collective-permute-start | bytes 1572872 | tf_op jit(solution)/shard_map/ppermute | solution.py:345
  57.3 6.0 %collective-permute-done.11.refs_6_ = bf16[2,512,128]{2,1,0:T(8,128)(2,1)} collective-permute-done((bf16[2,512,128]{2,1,0:T(8,128)(2,1)}, bf16[2,512,128]{2,1,0:T(8,128)(2,1)}, u32[]{:S(2)}, u32[]{:S(2)}) %collective-permute-start.11) | collective-permute-done | bytes 262176 | tf_op jit(solution)/shard_map/ppermute | solution.py:35
  63.3 1.5 collective-permute-start.2
  66.7 3.8 %conv_forward.1 = bf16[32,16,256]{2,1,0:T(8,128)(2,1)} custom-call(bf16[32,16,256]{2,1,0:T(8,128)(2,1)S(1)} %all-to-all-done.x_ref, f32[2,8192]{1,0:T(2,128)S(1)} %copy-done.23), custom_call_target="tpu_custom_call" | custom-call | flops 6000000000 | bytes 600000 | tf_op jit(solution)/shard_map/conv_forward/pallas_call | solution.py:180
  70.6 7.1 %all-to-all-start.1 = ((bf16[32,16,256]{2,1,0:T(8,128)(2,1)}), bf16[32,16,256]{2,1,0:T(8,128)(2,1)S(1)}, u32[]{:S(2)}, u32[]{:S(2)}) async-start(bf16[32,16,256]{2,1,0:T(8,128)(2,1)} %conv_forward.1), calls=%async_computation.1 | async-start | bytes 524288 | tf_op jit(solution)/shard_map/all_to_all | solution.py:438
  77.8 4.0 %collective-permute-done.2.cot1 = bf16[2,256,512]{2,1,0:T(8,128)(2,1)} collective-permute-done((bf16[2,256,512]{2,1,0:T(8,128)(2,1)S(1)}, bf16[2,256,512]{2,1,0:T(8,128)(2,1)}, u32[]{:S(2)}, u32[]{:S(2)}) %collective-permute-start.2) | collective-permute-done | bytes 524320 | tf_op jit(solution)/shard_map/ppermute | solution.py:345
  81.8 0.9 copy-done.6
  82.7 0.9 copy-done.9
  83.7 0.9 copy-done.12
  84.6 0.9 copy-done.15
  85.6 0.9 copy-done.18
  86.5 0.9 copy-done.21
  87.5 4.0 %grad_matmul.1 = (f32[256,512]{1,0:T(8,128)}, bf16[256,512]{1,0:T(8,128)(2,1)}, bf16[512,256]{1,0:T(8,128)(2,1)}) custom-call(s32[5]{0:T(128)S(1)} %stack.41.at_ref, bf16[3,256,512]{2,1,0:T(8,128)(2,1)S(1)} %bitcast.26, bf16[3,2,512]{2,1,0:T(2,128)(2,1)S(1)} %bitcast.33, f32[3,3,512]{2,1,0:T(4,128)S(1)} %copy-done.3, ...), custom_call_target="tpu_custom_call" | custom-call | flops 4000000000 | bytes 6500000 | tf_op jit(solution)/shard_map/grad_matmul/pallas_call | solution.py:283
  91.5 7.5 %all-to-all-start.2 = ((bf16[32,16,256]{2,1,0:T(8,128)(2,1)}), bf16[32,16,256]{2,1,0:T(8,128)(2,1)S(1)}, u32[]{:S(2)}, u32[]{:S(2)}) async-start(bf16[32,16,256]{2,1,0:T(8,128)(2,1)} %bitcast.40), calls=%async_computation.2 | async-start | bytes 524288 | tf_op jit(solution)/shard_map/all_to_all | solution.py:434
  99.8 0.9 copy-done.13
  100.7 0.9 copy-done.16
  101.7 0.9 copy-done.19
  102.6 0.9 copy-done.22
  103.6 1.0 copy-done.24
  104.6 6.3 %mix_matmul.1 = (bf16[2,256,512]{2,1,0:T(8,128)(2,1)}, bf16[2,256,512]{2,1,0:T(8,128)(2,1)}, bf16[2,256,512]{2,1,0:T(8,128)(2,1)}, bf16[2,256,512]{2,1,0:T(8,128)(2,1)}, f32[256,512]{1,0:T(8,128)}) custom-call(s32[5]{0:T(128)S(1)} %stack.41.at_ref, bf16[512,256]{1,0:T(8,128)(2,1)S(1)} %bitcast.30, bf16[3,256,512]{2,1,0:T(8,128)(2,1)S(1)} %bitcast.27, ...), custom_call_target="tpu_custom_call" | custom-call | flops 4000000000 | bytes 6500000 | tf_op jit(solution)/shard_map/mix_matmul/pallas_call | solution.py:322
  111.0 1.4 collective-permute-start.21
  112.4 3.3 %collective-permute-start.22 = (bf16[2,256,512]{2,1,0:T(8,128)(2,1)}, bf16[2,256,512]{2,1,0:T(8,128)(2,1)S(1)}, u32[]{:S(2)}, u32[]{:S(2)}) collective-permute-start(bf16[2,256,512]{2,1,0:T(8,128)(2,1)} %get-tuple-element.19), channel_id=1, source_target_pairs={{0,2},{1,3},{2,0},{3,1},{4,6},{5,7},{6,4},{7,5},{8,10},{9,11},{10,... | collective-permute-start | bytes 1572872 | tf_op jit(solution)/shard_map/ppermute | solution.py:345
  115.7 7.0 %conv_backward.1 = (bf16[32,16,256]{2,1,0:T(8,128)(2,1)}, f32[2,32,256]{2,1,0:T(8,128)S(1)}) custom-call(bf16[32,16,256]{2,1,0:T(8,128)(2,1)S(1)} %all-to-all-done.2.m_ref, bf16[32,16,256]{2,1,0:T(8,128)(2,1)S(1)} %all-to-all-done.x_ref, f32[2,8192]{1,0:T(2,128)S(1)} %copy-done.23), custom_call_target="tpu_custom_call" | custom-call | flops 10000000000 | bytes 1000000 | tf_op jit(solution)/shard_map/conv_backward/pallas_call | solution.py:198
  122.7 8.4 %all-to-all-start.3 = ((bf16[32,16,256]{2,1,0:T(8,128)(2,1)}), bf16[32,16,256]{2,1,0:T(8,128)(2,1)S(1)}, u32[]{:S(2)}, u32[]{:S(2)}) async-start(bf16[32,16,256]{2,1,0:T(8,128)(2,1)} %get-tuple-element.22), calls=%async_computation.3 | async-start | bytes 524288 | tf_op jit(solution)/shard_map/all_to_all | solution.py:438
  131.2 8.2 %collective-permute-done.23 = bf16[2,256,512]{2,1,0:T(8,128)(2,1)} collective-permute-done((bf16[2,256,512]{2,1,0:T(8,128)(2,1)}, bf16[2,256,512]{2,1,0:T(8,128)(2,1)}, u32[]{:S(2)}, u32[]{:S(2)}) %collective-permute-start.23) | collective-permute-done | bytes 524320 | tf_op jit(solution)/shard_map/ppermute | solution.py:345
  139.4 1.9 %fusion.1 = bf16[256,512]{1,0:T(8,128)(2,1)} fusion(bf16[2,256,512]{2,1,0:T(8,128)(2,1)} %collective-permute-done.23, bf16[2,256,512]{2,1,0:T(8,128)(2,1)S(1)} %collective-permute-done.22, bf16[2,256,512]{2,1,0:T(8,128)(2,1)S(1)} %collective-permute-done.21, bf16[2,256,512]{2,1,0:T(8,128)(2,1)S(1)} %copy-done.25), kind=kLoop, calls=%fused_computation.4 | loop fusion | flops 1048576 | bytes 1310720 | tf_op jit(solution)/shard_map/add | solution.py:474
  141.2 2.9 %collective-permute-start.24 = (bf16[256,512]{1,0:T(8,128)(2,1)}, bf16[256,512]{1,0:T(8,128)(2,1)}, u32[]{:S(2)}, u32[]{:S(2)}) collective-permute-start(bf16[256,512]{1,0:T(8,128)(2,1)} %fusion.1), channel_id=1, source_target_pairs={{0,4},{4,0},{1,5},{5,1},{2,6},{6,2},{3,7},{7,3},{8,12},{12,8},{9,1... | collective-permute-start | bytes 786440 | tf_op jit(solution)/shard_map/ppermute | solution.py:35
  144.8 2.2 %final_short.1 = (bf16[3,256,512]{2,1,0:T(8,128)(2,1)}, f32[3,8,512]{2,1,0:T(8,128)}, f32[3,16,512]{2,1,0:T(8,128)S(1)}) custom-call(bf16[512,256]{1,0:T(8,128)(2,1)S(1)} %bitcast.29, bf16[256,512]{1,0:T(8,128)(2,1)S(1)} %copy-done.2, f32[256,512]{1,0:T(8,128)S(1)} %copy-done.1, bf16[3,256,512]{2,1,0:T(8,128)(2,1)S(1)} %bitcast.28, ...), custom_call_target="tpu_custom_call" | custom-call | flops 5000000 | bytes 3500000 | tf_op jit(solution)/shard_map/final_short/pallas_call | solution.py:384
  147.0 1.3 collective-permute-start.25
  148.3 3.0 %collective-permute-done.24 = bf16[256,512]{1,0:T(8,128)(2,1)} collective-permute-done((bf16[256,512]{1,0:T(8,128)(2,1)}, bf16[256,512]{1,0:T(8,128)(2,1)}, u32[]{:S(2)}, u32[]{:S(2)}) %collective-permute-start.24) | collective-permute-done | bytes 262176 | tf_op jit(solution)/shard_map/ppermute | solution.py:35
  151.3 1.9 %fusion = bf16[256,512]{1,0:T(8,128)(2,1)} fusion(bf16[256,512]{1,0:T(8,128)(2,1)} %collective-permute-done.24, bf16[2,256,512]{2,1,0:T(8,128)(2,1)} %collective-permute-done.23, bf16[2,256,512]{2,1,0:T(8,128)(2,1)S(1)} %collective-permute-done.22, bf16[2,256,512]{2,1,0:T(8,128)(2,1)S(1)} %collective-permute-done.21, bf16[2,256,512]{2,1,0:T(8,128)(2,1)S(1)} %copy-done.25), kind=kLoop, calls=%fused_computation.2 | loop fusion | flops 1310720 | bytes 1572864 | tf_op jit(solution)/shard_map/convert_element_type | solution.py:476
  (78 shorter events, 7.4 us)
Async XLA Ops:
  0.6 11.1 %collective-permute-start.5 = (bf16[512,128]{1,0:T(8,128)(2,1)}, bf16[512,128]{1,0:T(8,128)(2,1)S(1)}, u32[]{:S(2)}, u32[]{:S(2)}) collective-permute-start(bf16[512,128]{1,0:T(8,128)(2,1)} %param.10), channel_id=1, source_target_pairs={{0,128},{32,160},{64,192},{96,224},{128,0},{160,32},{192,64},{224,... | collective-permute-start | bytes 393224 | tf_op jit(solution)/shard_map/ppermute | solution.py:340
  7.9 20.7 %collective-permute-start.1 = (bf16[256,512]{1,0:T(8,128)(2,1)}, bf16[256,512]{1,0:T(8,128)(2,1)S(1)}, u32[]{:S(2)}, u32[]{:S(2)}) collective-permute-start(bf16[256,512]{1,0:T(8,128)(2,1)} %param.11), channel_id=1, source_target_pairs={{0,4},{4,0},{1,5},{5,1},{2,6},{6,2},{3,7},{7,3},{8,12},{12,8},{9,1... | collective-permute-start | bytes 786440 | tf_op jit(solution)/shard_map/ppermute | solution.py:35
  11.7 24.6 %copy-start = (bf16[256,3,512]{2,0,1:T(8,128)(2,1)S(1)}, bf16[256,3,512]{2,0,1:T(8,128)(2,1)}, u32[]{:S(2)}) copy-start(bf16[256,3,512]{2,0,1:T(8,128)(2,1)} %param.6) | copy-start | bytes 2359300
  12.7 15.8 %collective-permute-start.17 = (bf16[2,512,128]{2,1,0:T(8,128)(2,1)S(1)}, bf16[2,512,128]{2,1,0:T(8,128)(2,1)S(1)}, u32[]{:S(2)}, u32[]{:S(2)}) collective-permute-start(bf16[2,512,128]{2,1,0:T(8,128)(2,1)S(1)} %pad_maximum_fusion.1.refs_0_), channel_id=1, source_target_pairs={{0,64},{32,96},{64,0},{96,32},{128,192},{160,224},{192,128},{224,1... | collective-permute-start | bytes 786440 | tf_op jit(solution)/shard_map/ppermute | solution.py:340
  17.4 11.6 %collective-permute-start.13 = (bf16[2,512,128]{2,1,0:T(8,128)(2,1)S(1)}, bf16[2,512,128]{2,1,0:T(8,128)(2,1)S(1)}, u32[]{:S(2)}, u32[]{:S(2)}) collective-permute-start(bf16[2,512,128]{2,1,0:T(8,128)(2,1)S(1)} %pad_maximum_fusion.1.refs_0_), channel_id=1, source_target_pairs={{0,32},{32,64},{64,96},{96,128},{128,160},{160,192},{192,224},{224... | collective-permute-start | bytes 786440 | tf_op jit(solution)/shard_map/ppermute | solution.py:336
  17.4 12.7 %collective-permute-start.9 = (bf16[2,512,128]{2,1,0:T(8,128)(2,1)S(1)}, bf16[2,512,128]{2,1,0:T(8,128)(2,1)}, u32[]{:S(2)}, u32[]{:S(2)}) collective-permute-start(bf16[2,512,128]{2,1,0:T(8,128)(2,1)S(1)} %pad_maximum_fusion.1.refs_0_), channel_id=1, source_target_pairs={{0,224},{32,0},{64,32},{96,64},{128,96},{160,128},{192,160},{224,1... | collective-permute-start | bytes 786440 | tf_op jit(solution)/shard_map/ppermute | solution.py:336
  22.0 2.1 %collective-permute-start = (bf16[2,3,512]{2,0,1:T(2,128)(2,1)S(1)}, bf16[2,3,512]{2,0,1:T(2,128)(2,1)S(1)}, u32[]{:S(2)}, u32[]{:S(2)}) collective-permute-start(bf16[2,3,512]{2,0,1:T(2,128)(2,1)S(1)} %slice.27), channel_id=1, source_target_pairs={{0,8},{8,16},{16,24},{24,32},{32,40},{40,48},{48,56},{56,64},{64,7... | collective-permute-start | bytes 18440 | tf_op jit(solution)/shard_map/ppermute | solution.py:31
  24.1 11.7 %collective-permute-start.7 = (bf16[2,512,128]{2,1,0:T(8,128)(2,1)S(1)}, bf16[2,512,128]{2,1,0:T(8,128)(2,1)}, u32[]{:S(2)}, u32[]{:S(2)}) collective-permute-start(bf16[2,512,128]{2,1,0:T(8,128)(2,1)S(1)} %pad_maximum_fusion.1.refs_0_), channel_id=1, source_target_pairs={{0,16},{16,0},{1,17},{17,1},{2,18},{18,2},{3,19},{19,3},{4,20},{20... | collective-permute-start | bytes 786440 | tf_op jit(solution)/shard_map/ppermute | solution.py:35
  28.6 22.4 %collective-permute-start.6 = (bf16[2,512,128]{2,1,0:T(8,128)(2,1)S(1)}, bf16[2,512,128]{2,1,0:T(8,128)(2,1)S(1)}, u32[]{:S(2)}, u32[]{:S(2)}) collective-permute-start(bf16[2,512,128]{2,1,0:T(8,128)(2,1)S(1)} %pad_maximum_fusion.1.refs_0_), channel_id=1, source_target_pairs={{0,8},{8,0},{1,9},{9,1},{2,10},{10,2},{3,11},{11,3},{4,12},{12,4},... | collective-permute-start | bytes 786440 | tf_op jit(solution)/shard_map/ppermute | solution.py:35
  28.6 23.4 %collective-permute-start.19 = (bf16[2,512,128]{2,1,0:T(8,128)(2,1)S(1)}, bf16[2,512,128]{2,1,0:T(8,128)(2,1)}, u32[]{:S(2)}, u32[]{:S(2)}) collective-permute-start(bf16[2,512,128]{2,1,0:T(8,128)(2,1)S(1)} %collective-permute-done.17.refs_12_), channel_id=1, source_target_pairs={{0,16},{16,0},{1,17},{17,1},{2,18},{18,2},{3,19},{19,3},{4,20},{20... | collective-permute-start | bytes 786440 | tf_op jit(solution)/shard_map/ppermute | solution.py:35
  29.0 22.0 %copy-start.5 = (bf16[2,512,128]{2,1,0:T(8,128)(2,1)}, bf16[2,512,128]{2,1,0:T(8,128)(2,1)S(1)}, u32[]{:S(2)}) copy-start(bf16[2,512,128]{2,1,0:T(8,128)(2,1)S(1)} %collective-permute-done.13.refs_8_) | copy-start | bytes 786436
  29.0 24.7 %collective-permute-start.18 = (bf16[2,512,128]{2,1,0:T(8,128)(2,1)S(1)}, bf16[2,512,128]{2,1,0:T(8,128)(2,1)S(1)}, u32[]{:S(2)}, u32[]{:S(2)}) collective-permute-start(bf16[2,512,128]{2,1,0:T(8,128)(2,1)S(1)} %collective-permute-done.17.refs_12_), channel_id=1, source_target_pairs={{0,8},{8,0},{1,9},{9,1},{2,10},{10,2},{3,11},{11,3},{4,12},{12,4},... | collective-permute-start | bytes 786440 | tf_op jit(solution)/shard_map/ppermute | solution.py:35
  30.1 23.7 %collective-permute-start.15 = (bf16[2,512,128]{2,1,0:T(8,128)(2,1)S(1)}, bf16[2,512,128]{2,1,0:T(8,128)(2,1)}, u32[]{:S(2)}, u32[]{:S(2)}) collective-permute-start(bf16[2,512,128]{2,1,0:T(8,128)(2,1)S(1)} %collective-permute-done.13.refs_8_), channel_id=1, source_target_pairs={{0,16},{16,0},{1,17},{17,1},{2,18},{18,2},{3,19},{19,3},{4,20},{20... | collective-permute-start | bytes 786440 | tf_op jit(solution)/shard_map/ppermute | solution.py:35
  31.6 4.7 %copy-start.3 = (f32[3,3,512]{2,1,0:T(4,128)S(1)}, f32[3,3,512]{2,1,0:T(4,128)}, u32[]{:S(2)}) copy-start(f32[3,3,512]{2,1,0:T(4,128)} %taps_ref.9) | copy-start | bytes 55300
  35.8 30.9 %collective-permute-start.4 = (bf16[2,256,512]{2,1,0:T(8,128)(2,1)S(1)}, bf16[2,256,512]{2,1,0:T(8,128)(2,1)S(1)}, u32[]{:S(2)}, u32[]{:S(2)}) collective-permute-start(bf16[2,256,512]{2,1,0:T(8,128)(2,1)S(1)} %pad_maximum_fusion.cot0), channel_id=1, source_target_pairs={{0,3},{1,0},{2,1},{3,2},{4,7},{5,4},{6,5},{7,6},{8,11},{9,8},{10,9... | collective-permute-start | bytes 1572872 | tf_op jit(solution)/shard_map/ppermute | solution.py:345
  37.6 29.2 %copy-start.23 = (f32[2,8192]{1,0:T(2,128)S(1)}, f32[2,8192]{1,0:T(2,128)}, u32[]{:S(2)}) copy-start(f32[2,8192]{1,0:T(2,128)} %h_ref.3) | copy-start | bytes 196612
  37.6 29.2 %all-to-all-start = ((bf16[32,16,256]{2,1,0:T(8,128)(2,1)}), bf16[32,16,256]{2,1,0:T(8,128)(2,1)S(1)}, u32[]{:S(2)}, u32[]{:S(2)}) async-start(bf16[32,16,256]{2,1,0:T(8,128)(2,1)} %bitcast.38), calls=%async_computation | async-start | bytes 524288 | tf_op jit(solution)/shard_map/all_to_all | solution.py:434
  51.7 2.4 %collective-permute-start.14 = (bf16[2,512,128]{2,1,0:T(8,128)(2,1)S(1)}, bf16[2,512,128]{2,1,0:T(8,128)(2,1)S(1)}, u32[]{:S(2)}, u32[]{:S(2)}) collective-permute-start(bf16[2,512,128]{2,1,0:T(8,128)(2,1)S(1)} %collective-permute-done.13.refs_8_), channel_id=1, source_target_pairs={{0,8},{8,0},{1,9},{9,1},{2,10},{10,2},{3,11},{11,3},{4,12},{12,4},... | collective-permute-start | bytes 786440 | tf_op jit(solution)/shard_map/ppermute | solution.py:35
  52.0 11.3 %collective-permute-start.11 = (bf16[2,512,128]{2,1,0:T(8,128)(2,1)}, bf16[2,512,128]{2,1,0:T(8,128)(2,1)}, u32[]{:S(2)}, u32[]{:S(2)}) collective-permute-start(bf16[2,512,128]{2,1,0:T(8,128)(2,1)} %collective-permute-done.9.refs_4_), channel_id=1, source_target_pairs={{0,16},{16,0},{1,17},{17,1},{2,18},{18,2},{3,19},{19,3},{4,20},{20... | collective-permute-start | bytes 786440 | tf_op jit(solution)/shard_map/ppermute | solution.py:35
  53.6 16.9 %copy-start.11 = (bf16[2,512,128]{2,1,0:T(8,128)(2,1)}, bf16[2,512,128]{2,1,0:T(8,128)(2,1)S(1)}, u32[]{:S(2)}) copy-start(bf16[2,512,128]{2,1,0:T(8,128)(2,1)S(1)} %collective-permute-done.18.refs_13_) | copy-start | bytes 786436
  53.7 11.1 %collective-permute-start.10 = (bf16[2,512,128]{2,1,0:T(8,128)(2,1)}, bf16[2,512,128]{2,1,0:T(8,128)(2,1)S(1)}, u32[]{:S(2)}, u32[]{:S(2)}) collective-permute-start(bf16[2,512,128]{2,1,0:T(8,128)(2,1)} %collective-permute-done.9.refs_4_), channel_id=1, source_target_pairs={{0,8},{8,0},{1,9},{9,1},{2,10},{10,2},{3,11},{11,3},{4,12},{12,4},... | collective-permute-start | bytes 786440 | tf_op jit(solution)/shard_map/ppermute | solution.py:35
  53.8 11.7 %collective-permute-start.8 = (bf16[2,512,128]{2,1,0:T(8,128)(2,1)}, bf16[2,512,128]{2,1,0:T(8,128)(2,1)S(1)}, u32[]{:S(2)}, u32[]{:S(2)}) collective-permute-start(bf16[2,512,128]{2,1,0:T(8,128)(2,1)} %collective-permute-done.7.refs_2_), channel_id=1, source_target_pairs={{0,8},{8,0},{1,9},{9,1},{2,10},{10,2},{3,11},{11,3},{4,12},{12,4},... | collective-permute-start | bytes 786440 | tf_op jit(solution)/shard_map/ppermute | solution.py:35
  54.9 22.9 %collective-permute-start.3 = (bf16[2,256,512]{2,1,0:T(8,128)(2,1)S(1)}, bf16[2,256,512]{2,1,0:T(8,128)(2,1)S(1)}, u32[]{:S(2)}, u32[]{:S(2)}) collective-permute-start(bf16[2,256,512]{2,1,0:T(8,128)(2,1)S(1)} %pad_maximum_fusion.cot0), channel_id=1, source_target_pairs={{0,2},{1,3},{2,0},{3,1},{4,6},{5,7},{6,4},{7,5},{8,10},{9,11},{10,... | collective-permute-start | bytes 1572872 | tf_op jit(solution)/shard_map/ppermute | solution.py:345
  63.3 18.5 %collective-permute-start.2 = (bf16[2,256,512]{2,1,0:T(8,128)(2,1)S(1)}, bf16[2,256,512]{2,1,0:T(8,128)(2,1)}, u32[]{:S(2)}, u32[]{:S(2)}) collective-permute-start(bf16[2,256,512]{2,1,0:T(8,128)(2,1)S(1)} %pad_maximum_fusion.cot0), channel_id=1, source_target_pairs={{0,1},{1,2},{2,3},{3,0},{4,5},{5,6},{6,7},{7,4},{8,9},{9,10},{10,1... | collective-permute-start | bytes 1572872 | tf_op jit(solution)/shard_map/ppermute | solution.py:345
  65.5 16.3 %collective-permute-start.20 = (bf16[2,512,128]{2,1,0:T(8,128)(2,1)}, bf16[2,512,128]{2,1,0:T(8,128)(2,1)}, u32[]{:S(2)}, u32[]{:S(2)}) collective-permute-start(bf16[2,512,128]{2,1,0:T(8,128)(2,1)} %collective-permute-done.19.refs_14_), channel_id=1, source_target_pairs={{0,8},{8,0},{1,9},{9,1},{2,10},{10,2},{3,11},{11,3},{4,12},{12,4},... | collective-permute-start | bytes 786440 | tf_op jit(solution)/shard_map/ppermute | solution.py:35
  66.2 15.6 %collective-permute-start.16 = (bf16[2,512,128]{2,1,0:T(8,128)(2,1)}, bf16[2,512,128]{2,1,0:T(8,128)(2,1)}, u32[]{:S(2)}, u32[]{:S(2)}) collective-permute-start(bf16[2,512,128]{2,1,0:T(8,128)(2,1)} %collective-permute-done.15.refs_10_), channel_id=1, source_target_pairs={{0,8},{8,0},{1,9},{9,1},{2,10},{10,2},{3,11},{11,3},{4,12},{12,4},... | collective-permute-start | bytes 786440 | tf_op jit(solution)/shard_map/ppermute | solution.py:35
  66.7 15.0 %collective-permute-start.12 = (bf16[2,512,128]{2,1,0:T(8,128)(2,1)}, bf16[2,512,128]{2,1,0:T(8,128)(2,1)}, u32[]{:S(2)}, u32[]{:S(2)}) collective-permute-start(bf16[2,512,128]{2,1,0:T(8,128)(2,1)} %collective-permute-done.11.refs_6_), channel_id=1, source_target_pairs={{0,8},{8,0},{1,9},{9,1},{2,10},{10,2},{3,11},{11,3},{4,12},{12,4},... | collective-permute-start | bytes 786440 | tf_op jit(solution)/shard_map/ppermute | solution.py:35
  70.6 21.0 %all-to-all-start.1 = ((bf16[32,16,256]{2,1,0:T(8,128)(2,1)}), bf16[32,16,256]{2,1,0:T(8,128)(2,1)S(1)}, u32[]{:S(2)}, u32[]{:S(2)}) async-start(bf16[32,16,256]{2,1,0:T(8,128)(2,1)} %conv_forward.1), calls=%async_computation.1 | async-start | bytes 524288 | tf_op jit(solution)/shard_map/all_to_all | solution.py:438
  81.8 1.0 copy-start.6
  82.7 0.9 copy-start.9
  83.7 0.9 copy-start.12
  84.6 0.9 copy-start.15
  85.6 0.9 copy-start.18
  86.5 0.9 copy-start.21
  91.5 7.6 %copy-start.7 = (bf16[2,512,128]{2,1,0:T(8,128)(2,1)S(1)}, bf16[2,512,128]{2,1,0:T(8,128)(2,1)}, u32[]{:S(2)}) copy-start(bf16[2,512,128]{2,1,0:T(8,128)(2,1)} %copy-done.5) | copy-start | bytes 786436
  91.5 7.6 %copy-start.10 = (bf16[2,512,128]{2,1,0:T(8,128)(2,1)S(1)}, bf16[2,512,128]{2,1,0:T(8,128)(2,1)}, u32[]{:S(2)}) copy-start(bf16[2,512,128]{2,1,0:T(8,128)(2,1)} %copy-done.8) | copy-start | bytes 786436
  91.5 24.2 %all-to-all-start.2 = ((bf16[32,16,256]{2,1,0:T(8,128)(2,1)}), bf16[32,16,256]{2,1,0:T(8,128)(2,1)S(1)}, u32[]{:S(2)}, u32[]{:S(2)}) async-start(bf16[32,16,256]{2,1,0:T(8,128)(2,1)} %bitcast.40), calls=%async_computation.2 | async-start | bytes 524288 | tf_op jit(solution)/shard_map/all_to_all | solution.py:434
  99.8 0.9 copy-start.13
  103.6 1.0 copy-start.24
  111.0 20.2 %collective-permute-start.21 = (bf16[2,256,512]{2,1,0:T(8,128)(2,1)}, bf16[2,256,512]{2,1,0:T(8,128)(2,1)S(1)}, u32[]{:S(2)}, u32[]{:S(2)}) collective-permute-start(bf16[2,256,512]{2,1,0:T(8,128)(2,1)} %get-tuple-element.18), channel_id=1, source_target_pairs={{0,1},{1,2},{2,3},{3,0},{4,5},{5,6},{6,7},{7,4},{8,9},{9,10},{10,1... | collective-permute-start | bytes 1572872 | tf_op jit(solution)/shard_map/ppermute | solution.py:345
  112.4 18.8 %collective-permute-start.22 = (bf16[2,256,512]{2,1,0:T(8,128)(2,1)}, bf16[2,256,512]{2,1,0:T(8,128)(2,1)S(1)}, u32[]{:S(2)}, u32[]{:S(2)}) collective-permute-start(bf16[2,256,512]{2,1,0:T(8,128)(2,1)} %get-tuple-element.19), channel_id=1, source_target_pairs={{0,2},{1,3},{2,0},{3,1},{4,6},{5,7},{6,4},{7,5},{8,10},{9,11},{10,... | collective-permute-start | bytes 1572872 | tf_op jit(solution)/shard_map/ppermute | solution.py:345
  115.7 23.6 %collective-permute-start.23 = (bf16[2,256,512]{2,1,0:T(8,128)(2,1)}, bf16[2,256,512]{2,1,0:T(8,128)(2,1)}, u32[]{:S(2)}, u32[]{:S(2)}) collective-permute-start(bf16[2,256,512]{2,1,0:T(8,128)(2,1)} %get-tuple-element.20), channel_id=1, source_target_pairs={{0,3},{1,0},{2,1},{3,2},{4,7},{5,4},{6,5},{7,6},{8,11},{9,8},{10,9... | collective-permute-start | bytes 1572872 | tf_op jit(solution)/shard_map/ppermute | solution.py:345
  122.7 16.6 %copy-start.25 = (bf16[2,256,512]{2,1,0:T(8,128)(2,1)S(1)}, bf16[2,256,512]{2,1,0:T(8,128)(2,1)}, u32[]{:S(2)}) copy-start(bf16[2,256,512]{2,1,0:T(8,128)(2,1)} %get-tuple-element.17) | copy-start | bytes 1572868
  122.7 22.1 %all-to-all-start.3 = ((bf16[32,16,256]{2,1,0:T(8,128)(2,1)}), bf16[32,16,256]{2,1,0:T(8,128)(2,1)S(1)}, u32[]{:S(2)}, u32[]{:S(2)}) async-start(bf16[32,16,256]{2,1,0:T(8,128)(2,1)} %get-tuple-element.22), calls=%async_computation.3 | async-start | bytes 524288 | tf_op jit(solution)/shard_map/all_to_all | solution.py:438
  139.4 5.4 %copy-start.1 = (f32[256,512]{1,0:T(8,128)S(1)}, f32[256,512]{1,0:T(8,128)}, u32[]{:S(2)}) copy-start(f32[256,512]{1,0:T(8,128)} %get-tuple-element.24.query_grad_ref) | copy-start | bytes 1572868
  139.4 5.4 %copy-start.2 = (bf16[256,512]{1,0:T(8,128)(2,1)S(1)}, bf16[256,512]{1,0:T(8,128)(2,1)}, u32[]{:S(2)}) copy-start(bf16[256,512]{1,0:T(8,128)(2,1)} %get-tuple-element.23.mixed_ref) | copy-start | bytes 786436
  141.2 10.0 %collective-permute-start.24 = (bf16[256,512]{1,0:T(8,128)(2,1)}, bf16[256,512]{1,0:T(8,128)(2,1)}, u32[]{:S(2)}, u32[]{:S(2)}) collective-permute-start(bf16[256,512]{1,0:T(8,128)(2,1)} %fusion.1), channel_id=1, source_target_pairs={{0,4},{4,0},{1,5},{5,1},{2,6},{6,2},{3,7},{7,3},{8,12},{12,8},{9,1... | collective-permute-start | bytes 786440 | tf_op jit(solution)/shard_map/ppermute | solution.py:35
  147.0 6.2 %collective-permute-start.25 = (f32[3,8,512]{2,1,0:T(8,128)}, f32[3,8,512]{2,1,0:T(8,128)S(1)}, u32[]{:S(2)}, u32[]{:S(2)}) collective-permute-start(f32[3,8,512]{2,1,0:T(8,128)} %get-tuple-element.26), channel_id=1, source_target_pairs={{8,0},{16,8},{24,16},{32,24},{40,32},{48,40},{56,48},{64,56},{72,6... | collective-permute-start | bytes 147464 | tf_op jit(solution)/shard_map/ppermute | solution.py:31
  (8 other events, 6.4 us)

commit v5 on v4

--- a/solution.py
+++ b/solution.py
@@ -221,9 +221,21 @@
             yield (sign * ((chan & 3) - at_ref[3])) & 3, (chan >> 2) ^ at_ref[2]
 
 
-def whole_columns(at_ref, place, refs):
+def outside(array):
+    return pltpu.with_memory_space_constraint(array, pltpu.HBM)
+
+
+def piece_copy(source, target, sems, n):
+    return pltpu.make_async_copy(source, target, sems.at[n])
+
+
+def weight_copies(refs, buffer_ref, sems):
+    return [piece_copy(ref, buffer_ref.at[n], sems, n) for n, ref in enumerate(refs)]
+
+
+def whole_columns(at_ref, place, buffer_ref):
     first = at_ref[1] == 0
-    own, own_c, side, side_c = (ref[place % 2] for ref in refs[place // 2 * 4 : place // 2 * 4 + 4])
+    own, own_c, side, side_c = (buffer_ref[place // 2 * 4 + n, place % 2] for n in range(4))
     parts = []
     for mine, other in ((own, own_c), (side, side_c)):
         parts += [jnp.where(first, mine, other), jnp.where(first, other, mine)]
@@ -248,34 +260,43 @@
 
 
 def grad_mm_kernel(at_ref, proj_ref, before_ref, taps_ref, cot0, cot1, cot2, cot3, *refs):
-    *w_refs, out_ref, mixed_ref, sent_ref = refs
+    *w_refs, out_ref, mixed_ref, sent_ref, cots_ref, buffer_ref, cot_sems, sems = refs
+    copies = weight_copies(w_refs, buffer_ref, sems)
+    arrivals = [
+        piece_copy(ref, cots_ref.at[n], cot_sems, n) for n, ref in enumerate((cot0, cot1, cot2, cot3))
+    ]
+    for copy in arrivals + copies:
+        copy.start()
+    query = short_side(0, proj_ref, before_ref, taps_ref)
+    for copy in arrivals:
+        copy.wait()
     yl = at_ref[0]
     width = cot0.shape[2] // 2
-    for step, (k, e) in enumerate(met_places(at_ref, -1)):
-        halves = []
-        for at in (yl, 1 - yl):
-            c0, c1, c2, c3 = (
-                cot_ref[e, :, side_columns(at, width)] for cot_ref in (cot0, cot1, cot2, cot3)
-            )
-            halves.append(jnp.where(k < 2, jnp.where(k == 0, c0, c1), jnp.where(k == 2, c2, c3)))
-        lhs = jnp.concatenate(halves, axis=1)
+    for place, (k, e) in enumerate(met_places(at_ref, -1)):
+        if place % 2 == 0:
+            for copy in copies[place * 2 : place * 2 + 4]:
+                copy.wait()
+        lhs = jnp.concatenate(
+            [cots_ref[k, e, :, side_columns(at, width)] for at in (yl, 1 - yl)], axis=1
+        )
         part = lax.dot_general(
             lhs,
-            whole_columns(at_ref, step, w_refs),
+            whole_columns(at_ref, place, buffer_ref),
             (((1,), (1,)), ((), ())),
             preferred_element_type=F32,
         )
-        if step == 0:
+        if place == 0:
             out_ref[...] = part
         else:
             out_ref[...] += part
-    mixed = (out_ref[...] * short_side(0, proj_ref, before_ref, taps_ref)).astype(BF16)
+    mixed = (out_ref[...] * query).astype(BF16)
     mixed_ref[...] = mixed
     sent_ref[...] = mixed.astype(F32).T.astype(BF16)
 
 
 SCALARS = pl.BlockSpec(memory_space=pltpu.SMEM)
 WHOLE = pl.BlockSpec(memory_space=pltpu.VMEM)
+LEFT = pl.BlockSpec(memory_space=pl.ANY)
 
 
 def grad_matmul(at, side_args, cots, ws):
@@ -288,32 +309,47 @@
             OUTSIDE((tok, rows), BF16),
             OUTSIDE((rows, tok), BF16),
         ),
-        in_specs=[SCALARS] + [WHOLE] * (len(side_args) + len(cots) + len(ws)),
+        in_specs=[SCALARS] + [WHOLE] * len(side_args) + [LEFT] * (len(cots) + len(ws)),
         out_specs=(WHOLE,) * 3,
+        scratch_shapes=[
+            pltpu.VMEM((len(cots),) + cots[0].shape, BF16),
+            pltpu.VMEM((len(ws),) + ws[0].shape, BF16),
+            pltpu.SemaphoreType.DMA((len(cots),)),
+            pltpu.SemaphoreType.DMA((len(ws),)),
+        ],
         compiler_params=SCRATCH,
         cost_estimate=pl.CostEstimate(flops=4000000000, bytes_accessed=6500000, transcendentals=0),
     )(at, *side_args, *cots, *ws)
 
 
 def mix_mm_kernel(at_ref, conv_ref, proj_ref, before_ref, taps_ref, skip_ref, grad_ref, *refs):
-    *w_refs, out0, out1, out2, out3, query_grad_ref = refs
+    *w_refs, out0, out1, out2, out3, query_grad_ref, parts_ref, buffer_ref, out_sems, sems = refs
+    copies = weight_copies(w_refs, buffer_ref, sems)
+    for copy in copies:
+        copy.start()
     yl = at_ref[0]
     conv = conv_ref[...].astype(F32).T
     query, key, value = (short_side(i, proj_ref, before_ref, taps_ref) for i in range(3))
     mixed_in = conv + skip_ref[...] * (key * value).astype(BF16).astype(F32)
     query_grad_ref[...] = grad_ref[...] * mixed_in
     gated = (query * mixed_in).astype(BF16)
-    width = out0.shape[2] // 2
-    for step, (k, e) in enumerate(met_places(at_ref, 1)):
+    width = parts_ref.shape[3] // 2
+    for place, (k, e) in enumerate(met_places(at_ref, 1)):
+        if place % 2 == 0:
+            for copy in copies[place * 2 : place * 2 + 4]:
+                copy.wait()
         part = jnp.dot(
-            gated, whole_columns(at_ref, step, w_refs), preferred_element_type=F32
+            gated, whole_columns(at_ref, place, buffer_ref), preferred_element_type=F32
         ).astype(BF16)
-        for turn, out_ref in enumerate((out0, out1, out2, out3)):
-
-            @pl.when(k == turn)
-            def _(out_ref=out_ref, part=part, e=e):
-                out_ref[e, :, side_columns(yl, width)] = part[:, :width]
-                out_ref[e, :, side_columns(1 - yl, width)] = part[:, width:]
+        parts_ref[k, e, :, side_columns(yl, width)] = part[:, :width]
+        parts_ref[k, e, :, side_columns(1 - yl, width)] = part[:, width:]
+    leaving = [
+        piece_copy(parts_ref.at[n], ref, out_sems, n) for n, ref in enumerate((out0, out1, out2, out3))
+    ]
+    for copy in leaving:
+        copy.start()
+    for copy in leaving:
+        copy.wait()
 
 
 def mix_matmul(at, conv, side_args, skip, grad, ws):
@@ -323,11 +359,17 @@
         mix_mm_kernel,
         name="mix_matmul",
         out_shape=(OUTSIDE((2, tok, cols), BF16),) * 4 + (OUTSIDE((tok, rows), F32),),
-        in_specs=[SCALARS] + [WHOLE] * (3 + len(side_args) + len(ws)),
-        out_specs=(WHOLE,) * 5,
+        in_specs=[SCALARS] + [WHOLE] * (3 + len(side_args)) + [LEFT] * len(ws),
+        out_specs=(LEFT,) * 4 + (WHOLE,),
+        scratch_shapes=[
+            pltpu.VMEM((4, 2, tok, cols), BF16),
+            pltpu.VMEM((len(ws),) + ws[0].shape, BF16),
+            pltpu.SemaphoreType.DMA((4,)),
+            pltpu.SemaphoreType.DMA((len(ws),)),
+        ],
         compiler_params=SCRATCH,
         cost_estimate=pl.CostEstimate(flops=4000000000, bytes_accessed=6500000, transcendentals=0),
-    )(at, conv, *side_args, skip, grad, *ws)
+    )(at, conv, *side_args, outside(skip), outside(grad), *ws)
     return parts, query_grad
 
 
@@ -391,7 +433,7 @@
         ),
         compiler_params=SCRATCH,
         cost_estimate=pl.CostEstimate(flops=5000000, bytes_accessed=3500000, transcendentals=0),
-    )(back, mixed_grad, query_grad, *side_args, skip)
+    )(back, outside(mixed_grad), outside(query_grad), *side_args, skip)
 
 
 def edge_kernel(tail_ref, after_ref, taps_ref, whole_ref, out_ref):
@@ -461,7 +503,7 @@
     ws = tuple(w for group in zip(pairs, pairs_c, sides, sides_c) for w in group)
 
     side_args = (projected.transpose(1, 0, 2), before.transpose(1, 0, 2), short_weight)
-    carried_sent = carried_columns(side_args)
+    carried_sent = carried_columns((outside(side_args[0]), side_args[1], outside(side_args[2])))
     carried_seq = channel_major(carried_sent)
     conv_seq = conv_forward(carried_seq, filters)
     conv = token_major(conv_seq)
@@ -472,8 +514,10 @@
     parts, query_grad = mix_matmul(at, conv, side_args, skip[None, :], gated_grad, ws)
     shares = [parts[0]] + [shift_x(parts[k], k) for k in range(1, wide)]
     theirs = sum(p[1].astype(F32) for p in shares).astype(BF16)
+    mine = sum(p[0].astype(F32) for p in shares)
+    theirs, mine = lax.optimization_barrier((theirs, mine))
     got = swap(theirs, "yh")
-    mixed = (sum(p[0].astype(F32) for p in shares) + got.astype(F32)).astype(BF16)
+    mixed = (mine + got.astype(F32)).astype(BF16)
 
     back_seq, filter_grad = conv_backward(grad_seq, carried_seq, filters)
     back = token_major(back_seq)

time: 156 us -> 158 us (1.013)
  the two profiles are of different devices: /device:TPU:2 before, /device:TPU:1 now
where the time goes in v5:
time: 158 us; the launch traced here: 157 us
  starting transfers between devices  84.2 us (53%)
  Pallas kernels  27.7 us (18%)
  waiting for transfers between devices  25.5 us (16%)
  local copies, waits for them, and re-layouts  14.6 us (9%)
  other arithmetic  3.79 us (2%)
    all_to_all x2, starting transfers between devices, channel_major(): return lax.all_to_all(sent, SEQ, split_axis=0, concat_axis=0, tiled=True)  23.9 us
    all_to_all x2, starting transfers between devices, token_major(): got = lax.all_to_all(block, SEQ, split_axis=0, concat_axis=0, tiled=True)  16 us
    unnamed x49, local copies, waits for them, and re-layouts  13.7 us
    ppermute x14, starting transfers between devices, swap(): return lax.ppermute(shard, axis, [(0, 1), (1, 0)])  13.7 us
    ppermute x2, starting transfers between devices, cross_z(): lax.ppermute(shard, 'z', [(i, i ^ by) for i in range(lax.axis_size('z'))])  12.7 us
    ppermute x6, waiting for transfers between devices, shift_x(): lax.ppermute(shard, 'x', [(i, (i + by) % count) for i in range(count)])  12.7 us
    ppermute x14, waiting for transfers between devices, swap(): return lax.ppermute(shard, axis, [(0, 1), (1, 0)])  9.87 us
    ppermute x2, starting transfers between devices, from_behind(): return lax.ppermute(shard, SEQ, pairs)  9.4 us
  transfers between devices with their start and end apart: 30, of which 8 were waited for; matrix products, arithmetic and copies ran while one was open for 3% of the time, Pallas kernels for 17%

profile of v5, /device:TPU:1, one launch (start us, length us, event | category | flops | bytes accessed | tf_op | source)
XLA Modules:
  0.0 156.6 jit_solution(9868921245880459793)
XLA Ops:
  0.6 7.8 %collective-permute-start.5 = (bf16[512,128]{1,0:T(8,128)(2,1)}, bf16[512,128]{1,0:T(8,128)(2,1)S(1)}, u32[]{:S(2)}, u32[]{:S(2)}) collective-permute-start(bf16[512,128]{1,0:T(8,128)(2,1)} %param.10), channel_id=1, source_target_pairs={{0,128},{32,160},{64,192},{96,224},{128,0},{160,32},{192,64},{224,... | collective-permute-start | bytes 393224 | tf_op jit(solution)/shard_map/ppermute | solution.py:382
  8.4 2.9 %collective-permute-start.1 = (bf16[256,512]{1,0:T(8,128)(2,1)}, bf16[256,512]{1,0:T(8,128)(2,1)S(1)}, u32[]{:S(2)}, u32[]{:S(2)}) collective-permute-start(bf16[256,512]{1,0:T(8,128)(2,1)} %param.11), channel_id=1, source_target_pairs={{0,4},{4,0},{1,5},{5,1},{2,6},{6,2},{3,7},{7,3},{8,12},{12,8},{9,1... | collective-permute-start | bytes 786440 | tf_op jit(solution)/shard_map/ppermute | solution.py:35
  11.4 1.0 pad_maximum_fusion.1.refs_0_
  12.4 4.9 %collective-permute-start.17 = (bf16[2,512,128]{2,1,0:T(8,128)(2,1)S(1)}, bf16[2,512,128]{2,1,0:T(8,128)(2,1)S(1)}, u32[]{:S(2)}, u32[]{:S(2)}) collective-permute-start(bf16[2,512,128]{2,1,0:T(8,128)(2,1)S(1)} %pad_maximum_fusion.1.refs_0_), channel_id=1, source_target_pairs={{0,64},{32,96},{64,0},{96,32},{128,192},{160,224},{192,128},{224,1... | collective-permute-start | bytes 786440 | tf_op jit(solution)/shard_map/ppermute | solution.py:382
  17.3 2.7 %collective-permute-start.9 = (bf16[2,512,128]{2,1,0:T(8,128)(2,1)S(1)}, bf16[2,512,128]{2,1,0:T(8,128)(2,1)}, u32[]{:S(2)}, u32[]{:S(2)}) collective-permute-start(bf16[2,512,128]{2,1,0:T(8,128)(2,1)S(1)} %pad_maximum_fusion.1.refs_0_), channel_id=1, source_target_pairs={{0,224},{32,0},{64,32},{96,64},{128,96},{160,128},{192,160},{224,1... | collective-permute-start | bytes 786440 | tf_op jit(solution)/shard_map/ppermute | solution.py:378
  20.0 0.7 slice.27
  20.7 5.9 %collective-permute-start = (bf16[2,3,512]{2,0,1:T(2,128)(2,1)S(1)}, bf16[2,3,512]{2,0,1:T(2,128)(2,1)S(1)}, u32[]{:S(2)}, u32[]{:S(2)}) collective-permute-start(bf16[2,3,512]{2,0,1:T(2,128)(2,1)S(1)} %slice.27), channel_id=1, source_target_pairs={{0,8},{8,16},{16,24},{24,32},{32,40},{40,48},{48,56},{56,64},{64,7... | collective-permute-start | bytes 18440 | tf_op jit(solution)/shard_map/ppermute | solution.py:31
  26.6 0.8 collective-permute-done
  27.4 1.5 collective-permute-start.7
  28.8 1.2 collective-permute-start.6
  30.8 1.3 collective-permute-start.15
  32.1 2.6 %collective-permute-done.7.refs_2_ = bf16[2,512,128]{2,1,0:T(8,128)(2,1)} collective-permute-done((bf16[2,512,128]{2,1,0:T(8,128)(2,1)S(1)}, bf16[2,512,128]{2,1,0:T(8,128)(2,1)}, u32[]{:S(2)}, u32[]{:S(2)}) %collective-permute-start.7) | collective-permute-done | bytes 262176 | tf_op jit(solution)/shard_map/ppermute | solution.py:35
  34.7 2.5 %collective-permute-start.4 = (bf16[2,256,512]{2,1,0:T(8,128)(2,1)S(1)}, bf16[2,256,512]{2,1,0:T(8,128)(2,1)S(1)}, u32[]{:S(2)}, u32[]{:S(2)}) collective-permute-start(bf16[2,256,512]{2,1,0:T(8,128)(2,1)S(1)} %pad_maximum_fusion.cot0), channel_id=1, source_target_pairs={{0,3},{1,0},{2,1},{3,2},{4,7},{5,4},{6,5},{7,6},{8,11},{9,8},{10,9... | collective-permute-start | bytes 1572872 | tf_op jit(solution)/shard_map/ppermute | solution.py:387
  37.2 2.3 %carried_columns.1 = bf16[512,256]{1,0:T(8,128)(2,1)} custom-call(bf16[3,256,512]{2,1,0:T(8,128)(2,1)} %bitcast.23, bf16[3,2,512]{2,1,0:T(2,128)(2,1)S(1)} %bitcast.30, f32[3,3,512]{2,1,0:T(4,128)} %taps_ref.9), custom_call_target="tpu_custom_call" | custom-call | flops 5000000 | bytes 1500000 | tf_op jit(solution)/shard_map/carried_columns/pallas_call | solution.py:397
  39.5 16.1 %all-to-all-start = ((bf16[32,16,256]{2,1,0:T(8,128)(2,1)}), bf16[32,16,256]{2,1,0:T(8,128)(2,1)S(1)}, u32[]{:S(2)}, u32[]{:S(2)}) async-start(bf16[32,16,256]{2,1,0:T(8,128)(2,1)} %bitcast.36), calls=%async_computation | async-start | bytes 524288 | tf_op jit(solution)/shard_map/all_to_all | solution.py:476
  55.6 0.7 copy-done.6
  56.6 1.5 collective-permute-start.11
  58.6 0.7 copy-done.12
  59.9 7.2 %collective-permute-done.11.refs_6_ = bf16[2,512,128]{2,1,0:T(8,128)(2,1)} collective-permute-done((bf16[2,512,128]{2,1,0:T(8,128)(2,1)}, bf16[2,512,128]{2,1,0:T(8,128)(2,1)}, u32[]{:S(2)}, u32[]{:S(2)}) %collective-permute-start.11) | collective-permute-done | bytes 262176 | tf_op jit(solution)/shard_map/ppermute | solution.py:35
  67.1 0.7 copy-done.15
  67.8 1.0 collective-permute-start.20
  70.1 3.8 %conv_forward.1 = bf16[32,16,256]{2,1,0:T(8,128)(2,1)} custom-call(bf16[32,16,256]{2,1,0:T(8,128)(2,1)S(1)} %all-to-all-done.x_ref, f32[2,8192]{1,0:T(2,128)S(1)} %copy-done.21), custom_call_target="tpu_custom_call" | custom-call | flops 6000000000 | bytes 600000 | tf_op jit(solution)/shard_map/conv_forward/pallas_call | solution.py:180
  73.9 6.9 %all-to-all-start.1 = ((bf16[32,16,256]{2,1,0:T(8,128)(2,1)}), bf16[32,16,256]{2,1,0:T(8,128)(2,1)S(1)}, u32[]{:S(2)}, u32[]{:S(2)}) async-start(bf16[32,16,256]{2,1,0:T(8,128)(2,1)} %conv_forward.1), calls=%async_computation.1 | async-start | bytes 524288 | tf_op jit(solution)/shard_map/all_to_all | solution.py:480
  80.9 5.1 %collective-permute-done.2.cot1 = bf16[2,256,512]{2,1,0:T(8,128)(2,1)} collective-permute-done((bf16[2,256,512]{2,1,0:T(8,128)(2,1)S(1)}, bf16[2,256,512]{2,1,0:T(8,128)(2,1)}, u32[]{:S(2)}, u32[]{:S(2)}) %collective-permute-start.2) | collective-permute-done | bytes 524320 | tf_op jit(solution)/shard_map/ppermute | solution.py:387
  86.1 0.9 copy-done.4
  87.0 0.9 copy-done.7
  88.0 0.9 copy-done.10
  88.9 0.9 copy-done.13
  89.9 0.9 copy-done.16
  90.8 0.9 copy-done.19
  91.8 4.5 %grad_matmul.1 = (f32[256,512]{1,0:T(8,128)}, bf16[256,512]{1,0:T(8,128)(2,1)}, bf16[512,256]{1,0:T(8,128)(2,1)}) custom-call(s32[5]{0:T(128)S(1)} %stack.41.at_ref, bf16[3,256,512]{2,1,0:T(8,128)(2,1)S(1)} %bitcast.24, bf16[3,2,512]{2,1,0:T(2,128)(2,1)S(1)} %bitcast.31, f32[3,3,512]{2,1,0:T(4,128)S(1)} %copy-done.1, ...), custom_call_target="tpu_custom_call" | custom-call | flops 4000000000 | bytes 6500000 | tf_op jit(solution)/shard_map/grad_matmul/pallas_call | solution.py:304
  96.3 7.8 %all-to-all-start.2 = ((bf16[32,16,256]{2,1,0:T(8,128)(2,1)}), bf16[32,16,256]{2,1,0:T(8,128)(2,1)S(1)}, u32[]{:S(2)}, u32[]{:S(2)}) async-start(bf16[32,16,256]{2,1,0:T(8,128)(2,1)} %bitcast.38), calls=%async_computation.2 | async-start | bytes 524288 | tf_op jit(solution)/shard_map/all_to_all | solution.py:476
  104.1 0.9 copy-done.11
  105.0 0.9 copy-done.14
  106.0 0.9 copy-done.17
  106.9 0.9 copy-done.20
  107.9 6.2 %mix_matmul.1 = (bf16[2,256,512]{2,1,0:T(8,128)(2,1)}, bf16[2,256,512]{2,1,0:T(8,128)(2,1)}, bf16[2,256,512]{2,1,0:T(8,128)(2,1)}, bf16[2,256,512]{2,1,0:T(8,128)(2,1)}, f32[256,512]{1,0:T(8,128)}) custom-call(s32[5]{0:T(128)S(1)} %stack.41.at_ref, bf16[512,256]{1,0:T(8,128)(2,1)S(1)} %bitcast.28, bf16[3,256,512]{2,1,0:T(8,128)(2,1)S(1)} %bitcast.25, ...), custom_call_target="tpu_custom_call" | custom-call | flops 4000000000 | bytes 6500000 | tf_op jit(solution)/shard_map/mix_matmul/pallas_call | solution.py:358
  114.2 1.5 collective-permute-start.22
  115.7 1.2 collective-permute-start.23
  116.8 7.0 %conv_backward.1 = (bf16[32,16,256]{2,1,0:T(8,128)(2,1)}, f32[2,32,256]{2,1,0:T(8,128)S(1)}) custom-call(bf16[32,16,256]{2,1,0:T(8,128)(2,1)S(1)} %all-to-all-done.2.m_ref, bf16[32,16,256]{2,1,0:T(8,128)(2,1)S(1)} %all-to-all-done.x_ref, f32[2,8192]{1,0:T(2,128)S(1)} %copy-done.21), custom_call_target="tpu_custom_call" | custom-call | flops 10000000000 | bytes 1000000 | tf_op jit(solution)/shard_map/conv_backward/pallas_call | solution.py:198
  123.8 9.2 %all-to-all-start.3 = ((bf16[32,16,256]{2,1,0:T(8,128)(2,1)}), bf16[32,16,256]{2,1,0:T(8,128)(2,1)S(1)}, u32[]{:S(2)}, u32[]{:S(2)}) async-start(bf16[32,16,256]{2,1,0:T(8,128)(2,1)} %get-tuple-element.26), calls=%async_computation.3 | async-start | bytes 524288 | tf_op jit(solution)/shard_map/all_to_all | solution.py:480
  133.0 7.1 %collective-permute-done.21 = bf16[2,256,512]{2,1,0:T(8,128)(2,1)S(1)} collective-permute-done((bf16[2,256,512]{2,1,0:T(8,128)(2,1)}, bf16[2,256,512]{2,1,0:T(8,128)(2,1)S(1)}, u32[]{:S(2)}, u32[]{:S(2)}) %collective-permute-start.21) | collective-permute-done | bytes 524320 | tf_op jit(solution)/shard_map/ppermute | solution.py:387
  140.5 2.0 %add_bitcast_fusion = (f32[256,512]{1,0:T(8,128)S(1)}, bf16[256,512]{1,0:T(8,128)(2,1)}) fusion(bf16[2,256,512]{2,1,0:T(8,128)(2,1)} %collective-permute-done.23, bf16[2,256,512]{2,1,0:T(8,128)(2,1)S(1)} %collective-permute-done.22, bf16[2,256,512]{2,1,0:T(8,128)(2,1)S(1)} %collective-permute-done.21, bf16[2,256,512]{2,1,0:T(8,128)(2,1)S(1)} %copy-done.22), kind=kLoop, calls=%fused_computation.2 | loop fusion | flops 1966080 | bytes 2883584 | tf_op jit(solution)/shard_map/add | solution.py:517
  142.5 2.6 %collective-permute-start.24 = (bf16[256,512]{1,0:T(8,128)(2,1)}, bf16[256,512]{1,0:T(8,128)(2,1)S(1)}, u32[]{:S(2)}, u32[]{:S(2)}) collective-permute-start(bf16[256,512]{1,0:T(8,128)(2,1)} %get-tuple-element.24), channel_id=1, source_target_pairs={{0,4},{4,0},{1,5},{5,1},{2,6},{6,2},{3,7},{7,3},{8,12},{12,8},{9,1... | collective-permute-start | bytes 786440 | tf_op jit(solution)/shard_map/ppermute | solution.py:35
  146.5 3.3 %final_short.1 = (bf16[3,256,512]{2,1,0:T(8,128)(2,1)}, f32[3,8,512]{2,1,0:T(8,128)}, f32[3,16,512]{2,1,0:T(8,128)S(1)}) custom-call(bf16[512,256]{1,0:T(8,128)(2,1)S(1)} %bitcast.27, bf16[256,512]{1,0:T(8,128)(2,1)} %get-tuple-element.27.mixed_ref, f32[256,512]{1,0:T(8,128)} %get-tuple-element.28.query_grad_ref, bf16[3,256,512]{2,1,0:T(8,128)(2,1)S(1)} %bitcast.26, ...), custom_call_target="tpu_custom_call" | custom-call | flops 5000000 | bytes 3500000 | tf_op jit(solution)/shard_map/final_short/pallas_call | solution.py:426
  149.8 3.5 %collective-permute-start.25 = (f32[3,8,512]{2,1,0:T(8,128)}, f32[3,8,512]{2,1,0:T(8,128)S(1)}, u32[]{:S(2)}, u32[]{:S(2)}) collective-permute-start(f32[3,8,512]{2,1,0:T(8,128)} %get-tuple-element.30), channel_id=1, source_target_pairs={{8,0},{16,8},{24,16},{32,24},{40,32},{48,40},{56,48},{64,56},{72,6... | collective-permute-start | bytes 147464 | tf_op jit(solution)/shard_map/ppermute | solution.py:31
  153.3 0.8 add_convert_fusion
  154.1 1.8 %collective-permute-done.25.after_ref = f32[3,8,512]{2,1,0:T(8,128)S(1)} collective-permute-done((f32[3,8,512]{2,1,0:T(8,128)}, f32[3,8,512]{2,1,0:T(8,128)S(1)}, u32[]{:S(2)}, u32[]{:S(2)}) %collective-permute-start.25) | collective-permute-done | bytes 49184 | tf_op jit(solution)/shard_map/ppermute | solution.py:31
  (74 shorter events, 6.0 us)
Async XLA Ops:
  0.6 10.8 %collective-permute-start.5 = (bf16[512,128]{1,0:T(8,128)(2,1)}, bf16[512,128]{1,0:T(8,128)(2,1)S(1)}, u32[]{:S(2)}, u32[]{:S(2)}) collective-permute-start(bf16[512,128]{1,0:T(8,128)(2,1)} %param.10), channel_id=1, source_target_pairs={{0,128},{32,160},{64,192},{96,224},{128,0},{160,32},{192,64},{224,... | collective-permute-start | bytes 393224 | tf_op jit(solution)/shard_map/ppermute | solution.py:382
  8.4 20.4 %collective-permute-start.1 = (bf16[256,512]{1,0:T(8,128)(2,1)}, bf16[256,512]{1,0:T(8,128)(2,1)S(1)}, u32[]{:S(2)}, u32[]{:S(2)}) collective-permute-start(bf16[256,512]{1,0:T(8,128)(2,1)} %param.11), channel_id=1, source_target_pairs={{0,4},{4,0},{1,5},{5,1},{2,6},{6,2},{3,7},{7,3},{8,12},{12,8},{9,1... | collective-permute-start | bytes 786440 | tf_op jit(solution)/shard_map/ppermute | solution.py:35
  11.4 20.6 %copy-start.23 = (bf16[256,512]{1,0:T(8,128)(2,1)S(1)}, bf16[256,512]{1,0:T(8,128)(2,1)}, u32[]{:S(2)}) copy-start(bf16[256,512]{1,0:T(8,128)(2,1)} %param.11) | copy-start | bytes 786436
  12.4 17.6 %collective-permute-start.17 = (bf16[2,512,128]{2,1,0:T(8,128)(2,1)S(1)}, bf16[2,512,128]{2,1,0:T(8,128)(2,1)S(1)}, u32[]{:S(2)}, u32[]{:S(2)}) collective-permute-start(bf16[2,512,128]{2,1,0:T(8,128)(2,1)S(1)} %pad_maximum_fusion.1.refs_0_), channel_id=1, source_target_pairs={{0,64},{32,96},{64,0},{96,32},{128,192},{160,224},{192,128},{224,1... | collective-permute-start | bytes 786440 | tf_op jit(solution)/shard_map/ppermute | solution.py:382
  17.3 12.7 %collective-permute-start.13 = (bf16[2,512,128]{2,1,0:T(8,128)(2,1)S(1)}, bf16[2,512,128]{2,1,0:T(8,128)(2,1)S(1)}, u32[]{:S(2)}, u32[]{:S(2)}) collective-permute-start(bf16[2,512,128]{2,1,0:T(8,128)(2,1)S(1)} %pad_maximum_fusion.1.refs_0_), channel_id=1, source_target_pairs={{0,32},{32,64},{64,96},{96,128},{128,160},{160,192},{192,224},{224... | collective-permute-start | bytes 786440 | tf_op jit(solution)/shard_map/ppermute | solution.py:378
  17.3 13.4 %collective-permute-start.9 = (bf16[2,512,128]{2,1,0:T(8,128)(2,1)S(1)}, bf16[2,512,128]{2,1,0:T(8,128)(2,1)}, u32[]{:S(2)}, u32[]{:S(2)}) collective-permute-start(bf16[2,512,128]{2,1,0:T(8,128)(2,1)S(1)} %pad_maximum_fusion.1.refs_0_), channel_id=1, source_target_pairs={{0,224},{32,0},{64,32},{96,64},{128,96},{160,128},{192,160},{224,1... | collective-permute-start | bytes 786440 | tf_op jit(solution)/shard_map/ppermute | solution.py:378
  20.7 6.6 %collective-permute-start = (bf16[2,3,512]{2,0,1:T(2,128)(2,1)S(1)}, bf16[2,3,512]{2,0,1:T(2,128)(2,1)S(1)}, u32[]{:S(2)}, u32[]{:S(2)}) collective-permute-start(bf16[2,3,512]{2,0,1:T(2,128)(2,1)S(1)} %slice.27), channel_id=1, source_target_pairs={{0,8},{8,16},{16,24},{24,32},{32,40},{40,48},{48,56},{56,64},{64,7... | collective-permute-start | bytes 18440 | tf_op jit(solution)/shard_map/ppermute | solution.py:31
  27.4 7.4 %collective-permute-start.7 = (bf16[2,512,128]{2,1,0:T(8,128)(2,1)S(1)}, bf16[2,512,128]{2,1,0:T(8,128)(2,1)}, u32[]{:S(2)}, u32[]{:S(2)}) collective-permute-start(bf16[2,512,128]{2,1,0:T(8,128)(2,1)S(1)} %pad_maximum_fusion.1.refs_0_), channel_id=1, source_target_pairs={{0,16},{16,0},{1,17},{17,1},{2,18},{18,2},{3,19},{19,3},{4,20},{20... | collective-permute-start | bytes 786440 | tf_op jit(solution)/shard_map/ppermute | solution.py:35
  28.8 26.8 %collective-permute-start.6 = (bf16[2,512,128]{2,1,0:T(8,128)(2,1)S(1)}, bf16[2,512,128]{2,1,0:T(8,128)(2,1)S(1)}, u32[]{:S(2)}, u32[]{:S(2)}) collective-permute-start(bf16[2,512,128]{2,1,0:T(8,128)(2,1)S(1)} %pad_maximum_fusion.1.refs_0_), channel_id=1, source_target_pairs={{0,8},{8,0},{1,9},{9,1},{2,10},{10,2},{3,11},{11,3},{4,12},{12,4},... | collective-permute-start | bytes 786440 | tf_op jit(solution)/shard_map/ppermute | solution.py:35
  30.0 26.5 %collective-permute-start.19 = (bf16[2,512,128]{2,1,0:T(8,128)(2,1)S(1)}, bf16[2,512,128]{2,1,0:T(8,128)(2,1)}, u32[]{:S(2)}, u32[]{:S(2)}) collective-permute-start(bf16[2,512,128]{2,1,0:T(8,128)(2,1)S(1)} %collective-permute-done.17.refs_12_), channel_id=1, source_target_pairs={{0,16},{16,0},{1,17},{17,1},{2,18},{18,2},{3,19},{19,3},{4,20},{20... | collective-permute-start | bytes 786440 | tf_op jit(solution)/shard_map/ppermute | solution.py:35
  30.0 25.6 %copy-start.3 = (bf16[2,512,128]{2,1,0:T(8,128)(2,1)}, bf16[2,512,128]{2,1,0:T(8,128)(2,1)S(1)}, u32[]{:S(2)}) copy-start(bf16[2,512,128]{2,1,0:T(8,128)(2,1)S(1)} %collective-permute-done.13.refs_8_) | copy-start | bytes 786436
  30.1 28.0 %collective-permute-start.18 = (bf16[2,512,128]{2,1,0:T(8,128)(2,1)S(1)}, bf16[2,512,128]{2,1,0:T(8,128)(2,1)S(1)}, u32[]{:S(2)}, u32[]{:S(2)}) collective-permute-start(bf16[2,512,128]{2,1,0:T(8,128)(2,1)S(1)} %collective-permute-done.17.refs_12_), channel_id=1, source_target_pairs={{0,8},{8,0},{1,9},{9,1},{2,10},{10,2},{3,11},{11,3},{4,12},{12,4},... | collective-permute-start | bytes 786440 | tf_op jit(solution)/shard_map/ppermute | solution.py:35
  30.8 27.7 %collective-permute-start.15 = (bf16[2,512,128]{2,1,0:T(8,128)(2,1)S(1)}, bf16[2,512,128]{2,1,0:T(8,128)(2,1)}, u32[]{:S(2)}, u32[]{:S(2)}) collective-permute-start(bf16[2,512,128]{2,1,0:T(8,128)(2,1)S(1)} %collective-permute-done.13.refs_8_), channel_id=1, source_target_pairs={{0,16},{16,0},{1,17},{17,1},{2,18},{18,2},{3,19},{19,3},{4,20},{20... | collective-permute-start | bytes 786440 | tf_op jit(solution)/shard_map/ppermute | solution.py:35
  34.7 34.8 %collective-permute-start.4 = (bf16[2,256,512]{2,1,0:T(8,128)(2,1)S(1)}, bf16[2,256,512]{2,1,0:T(8,128)(2,1)S(1)}, u32[]{:S(2)}, u32[]{:S(2)}) collective-permute-start(bf16[2,256,512]{2,1,0:T(8,128)(2,1)S(1)} %pad_maximum_fusion.cot0), channel_id=1, source_target_pairs={{0,3},{1,0},{2,1},{3,2},{4,7},{5,4},{6,5},{7,6},{8,11},{9,8},{10,9... | collective-permute-start | bytes 1572872 | tf_op jit(solution)/shard_map/ppermute | solution.py:387
  39.5 30.5 %copy-start.21 = (f32[2,8192]{1,0:T(2,128)S(1)}, f32[2,8192]{1,0:T(2,128)}, u32[]{:S(2)}) copy-start(f32[2,8192]{1,0:T(2,128)} %h_ref.3) | copy-start | bytes 196612
  39.5 30.5 %all-to-all-start = ((bf16[32,16,256]{2,1,0:T(8,128)(2,1)}), bf16[32,16,256]{2,1,0:T(8,128)(2,1)S(1)}, u32[]{:S(2)}, u32[]{:S(2)}) async-start(bf16[32,16,256]{2,1,0:T(8,128)(2,1)} %bitcast.36), calls=%async_computation | async-start | bytes 524288 | tf_op jit(solution)/shard_map/all_to_all | solution.py:476
  55.6 30.5 %copy-start = (bf16[256,3,512]{2,0,1:T(8,128)(2,1)S(1)}, bf16[256,3,512]{2,0,1:T(8,128)(2,1)}, u32[]{:S(2)}) copy-start(bf16[256,3,512]{2,0,1:T(8,128)(2,1)} %param.6) | copy-start | bytes 2359300
  56.3 2.3 %collective-permute-start.14 = (bf16[2,512,128]{2,1,0:T(8,128)(2,1)S(1)}, bf16[2,512,128]{2,1,0:T(8,128)(2,1)S(1)}, u32[]{:S(2)}, u32[]{:S(2)}) collective-permute-start(bf16[2,512,128]{2,1,0:T(8,128)(2,1)S(1)} %collective-permute-done.13.refs_8_), channel_id=1, source_target_pairs={{0,8},{8,0},{1,9},{9,1},{2,10},{10,2},{3,11},{11,3},{4,12},{12,4},... | collective-permute-start | bytes 786440 | tf_op jit(solution)/shard_map/ppermute | solution.py:35
  56.6 10.5 %collective-permute-start.11 = (bf16[2,512,128]{2,1,0:T(8,128)(2,1)}, bf16[2,512,128]{2,1,0:T(8,128)(2,1)}, u32[]{:S(2)}, u32[]{:S(2)}) collective-permute-start(bf16[2,512,128]{2,1,0:T(8,128)(2,1)} %collective-permute-done.9.refs_4_), channel_id=1, source_target_pairs={{0,16},{16,0},{1,17},{17,1},{2,18},{18,2},{3,19},{19,3},{4,20},{20... | collective-permute-start | bytes 786440 | tf_op jit(solution)/shard_map/ppermute | solution.py:35
  58.1 15.8 %copy-start.9 = (bf16[2,512,128]{2,1,0:T(8,128)(2,1)}, bf16[2,512,128]{2,1,0:T(8,128)(2,1)S(1)}, u32[]{:S(2)}) copy-start(bf16[2,512,128]{2,1,0:T(8,128)(2,1)S(1)} %collective-permute-done.18.refs_13_) | copy-start | bytes 786436
  58.1 9.0 %collective-permute-start.10 = (bf16[2,512,128]{2,1,0:T(8,128)(2,1)}, bf16[2,512,128]{2,1,0:T(8,128)(2,1)S(1)}, u32[]{:S(2)}, u32[]{:S(2)}) collective-permute-start(bf16[2,512,128]{2,1,0:T(8,128)(2,1)} %collective-permute-done.9.refs_4_), channel_id=1, source_target_pairs={{0,8},{8,0},{1,9},{9,1},{2,10},{10,2},{3,11},{11,3},{4,12},{12,4},... | collective-permute-start | bytes 786440 | tf_op jit(solution)/shard_map/ppermute | solution.py:35
  58.5 10.3 %collective-permute-start.8 = (bf16[2,512,128]{2,1,0:T(8,128)(2,1)}, bf16[2,512,128]{2,1,0:T(8,128)(2,1)S(1)}, u32[]{:S(2)}, u32[]{:S(2)}) collective-permute-start(bf16[2,512,128]{2,1,0:T(8,128)(2,1)} %collective-permute-done.7.refs_2_), channel_id=1, source_target_pairs={{0,8},{8,0},{1,9},{9,1},{2,10},{10,2},{3,11},{11,3},{4,12},{12,4},... | collective-permute-start | bytes 786440 | tf_op jit(solution)/shard_map/ppermute | solution.py:35
  59.3 21.5 %collective-permute-start.3 = (bf16[2,256,512]{2,1,0:T(8,128)(2,1)S(1)}, bf16[2,256,512]{2,1,0:T(8,128)(2,1)S(1)}, u32[]{:S(2)}, u32[]{:S(2)}) collective-permute-start(bf16[2,256,512]{2,1,0:T(8,128)(2,1)S(1)} %pad_maximum_fusion.cot0), channel_id=1, source_target_pairs={{0,2},{1,3},{2,0},{3,1},{4,6},{5,7},{6,4},{7,5},{8,10},{9,11},{10,... | collective-permute-start | bytes 1572872 | tf_op jit(solution)/shard_map/ppermute | solution.py:387
  67.1 18.9 %collective-permute-start.2 = (bf16[2,256,512]{2,1,0:T(8,128)(2,1)S(1)}, bf16[2,256,512]{2,1,0:T(8,128)(2,1)}, u32[]{:S(2)}, u32[]{:S(2)}) collective-permute-start(bf16[2,256,512]{2,1,0:T(8,128)(2,1)S(1)} %pad_maximum_fusion.cot0), channel_id=1, source_target_pairs={{0,1},{1,2},{2,3},{3,0},{4,5},{5,6},{6,7},{7,4},{8,9},{9,10},{10,1... | collective-permute-start | bytes 1572872 | tf_op jit(solution)/shard_map/ppermute | solution.py:387
  67.8 18.2 %collective-permute-start.20 = (bf16[2,512,128]{2,1,0:T(8,128)(2,1)}, bf16[2,512,128]{2,1,0:T(8,128)(2,1)}, u32[]{:S(2)}, u32[]{:S(2)}) collective-permute-start(bf16[2,512,128]{2,1,0:T(8,128)(2,1)} %collective-permute-done.19.refs_14_), channel_id=1, source_target_pairs={{0,8},{8,0},{1,9},{9,1},{2,10},{10,2},{3,11},{11,3},{4,12},{12,4},... | collective-permute-start | bytes 786440 | tf_op jit(solution)/shard_map/ppermute | solution.py:35
  69.5 16.5 %collective-permute-start.16 = (bf16[2,512,128]{2,1,0:T(8,128)(2,1)}, bf16[2,512,128]{2,1,0:T(8,128)(2,1)}, u32[]{:S(2)}, u32[]{:S(2)}) collective-permute-start(bf16[2,512,128]{2,1,0:T(8,128)(2,1)} %collective-permute-done.15.refs_10_), channel_id=1, source_target_pairs={{0,8},{8,0},{1,9},{9,1},{2,10},{10,2},{3,11},{11,3},{4,12},{12,4},... | collective-permute-start | bytes 786440 | tf_op jit(solution)/shard_map/ppermute | solution.py:35
  69.5 16.5 %collective-permute-start.12 = (bf16[2,512,128]{2,1,0:T(8,128)(2,1)}, bf16[2,512,128]{2,1,0:T(8,128)(2,1)}, u32[]{:S(2)}, u32[]{:S(2)}) collective-permute-start(bf16[2,512,128]{2,1,0:T(8,128)(2,1)} %collective-permute-done.11.refs_6_), channel_id=1, source_target_pairs={{0,8},{8,0},{1,9},{9,1},{2,10},{10,2},{3,11},{11,3},{4,12},{12,4},... | collective-permute-start | bytes 786440 | tf_op jit(solution)/shard_map/ppermute | solution.py:35
  73.9 22.3 %all-to-all-start.1 = ((bf16[32,16,256]{2,1,0:T(8,128)(2,1)}), bf16[32,16,256]{2,1,0:T(8,128)(2,1)S(1)}, u32[]{:S(2)}, u32[]{:S(2)}) async-start(bf16[32,16,256]{2,1,0:T(8,128)(2,1)} %conv_forward.1), calls=%async_computation.1 | async-start | bytes 524288 | tf_op jit(solution)/shard_map/all_to_all | solution.py:480
  80.8 5.3 %copy-start.1 = (f32[3,3,512]{2,1,0:T(4,128)S(1)}, f32[3,3,512]{2,1,0:T(4,128)}, u32[]{:S(2)}) copy-start(f32[3,3,512]{2,1,0:T(4,128)} %taps_ref.9) | copy-start | bytes 55300
  86.1 1.0 copy-start.4
  87.0 0.9 copy-start.7
  88.0 0.9 copy-start.10
  88.9 0.9 copy-start.13
  89.9 0.9 copy-start.16
  90.8 0.9 copy-start.19
  96.2 7.8 %copy-start.5 = (bf16[2,512,128]{2,1,0:T(8,128)(2,1)S(1)}, bf16[2,512,128]{2,1,0:T(8,128)(2,1)}, u32[]{:S(2)}) copy-start(bf16[2,512,128]{2,1,0:T(8,128)(2,1)} %copy-done.3) | copy-start | bytes 786436
  96.2 7.8 %copy-start.8 = (bf16[2,512,128]{2,1,0:T(8,128)(2,1)S(1)}, bf16[2,512,128]{2,1,0:T(8,128)(2,1)}, u32[]{:S(2)}) copy-start(bf16[2,512,128]{2,1,0:T(8,128)(2,1)} %copy-done.6) | copy-start | bytes 786436
  96.3 20.6 %all-to-all-start.2 = ((bf16[32,16,256]{2,1,0:T(8,128)(2,1)}), bf16[32,16,256]{2,1,0:T(8,128)(2,1)S(1)}, u32[]{:S(2)}, u32[]{:S(2)}) async-start(bf16[32,16,256]{2,1,0:T(8,128)(2,1)} %bitcast.38), calls=%async_computation.2 | async-start | bytes 524288 | tf_op jit(solution)/shard_map/all_to_all | solution.py:476
  104.1 1.0 copy-start.11
  105.0 0.9 copy-start.14
  106.0 0.9 copy-start.17
  114.1 26.0 %collective-permute-start.21 = (bf16[2,256,512]{2,1,0:T(8,128)(2,1)}, bf16[2,256,512]{2,1,0:T(8,128)(2,1)S(1)}, u32[]{:S(2)}, u32[]{:S(2)}) collective-permute-start(bf16[2,256,512]{2,1,0:T(8,128)(2,1)} %get-tuple-element.20), channel_id=1, source_target_pairs={{0,1},{1,2},{2,3},{3,0},{4,5},{5,6},{6,7},{7,4},{8,9},{9,10},{10,1... | collective-permute-start | bytes 1572872 | tf_op jit(solution)/shard_map/ppermute | solution.py:387
  114.2 25.9 %collective-permute-start.22 = (bf16[2,256,512]{2,1,0:T(8,128)(2,1)}, bf16[2,256,512]{2,1,0:T(8,128)(2,1)S(1)}, u32[]{:S(2)}, u32[]{:S(2)}) collective-permute-start(bf16[2,256,512]{2,1,0:T(8,128)(2,1)} %get-tuple-element.21), channel_id=1, source_target_pairs={{0,2},{1,3},{2,0},{3,1},{4,6},{5,7},{6,4},{7,5},{8,10},{9,11},{10,... | collective-permute-start | bytes 1572872 | tf_op jit(solution)/shard_map/ppermute | solution.py:387
  115.7 24.9 %collective-permute-start.23 = (bf16[2,256,512]{2,1,0:T(8,128)(2,1)}, bf16[2,256,512]{2,1,0:T(8,128)(2,1)}, u32[]{:S(2)}, u32[]{:S(2)}) collective-permute-start(bf16[2,256,512]{2,1,0:T(8,128)(2,1)} %get-tuple-element.22), channel_id=1, source_target_pairs={{0,3},{1,0},{2,1},{3,2},{4,7},{5,4},{6,5},{7,6},{8,11},{9,8},{10,9... | collective-permute-start | bytes 1572872 | tf_op jit(solution)/shard_map/ppermute | solution.py:387
  123.8 16.7 %copy-start.22 = (bf16[2,256,512]{2,1,0:T(8,128)(2,1)S(1)}, bf16[2,256,512]{2,1,0:T(8,128)(2,1)}, u32[]{:S(2)}) copy-start(bf16[2,256,512]{2,1,0:T(8,128)(2,1)} %get-tuple-element.19) | copy-start | bytes 1572868
  123.8 22.0 %all-to-all-start.3 = ((bf16[32,16,256]{2,1,0:T(8,128)(2,1)}), bf16[32,16,256]{2,1,0:T(8,128)(2,1)S(1)}, u32[]{:S(2)}, u32[]{:S(2)}) async-start(bf16[32,16,256]{2,1,0:T(8,128)(2,1)} %get-tuple-element.26), calls=%async_computation.3 | async-start | bytes 524288 | tf_op jit(solution)/shard_map/all_to_all | solution.py:480
  142.5 10.8 %collective-permute-start.24 = (bf16[256,512]{1,0:T(8,128)(2,1)}, bf16[256,512]{1,0:T(8,128)(2,1)S(1)}, u32[]{:S(2)}, u32[]{:S(2)}) collective-permute-start(bf16[256,512]{1,0:T(8,128)(2,1)} %get-tuple-element.24), channel_id=1, source_target_pairs={{0,4},{4,0},{1,5},{5,1},{2,6},{6,2},{3,7},{7,3},{8,12},{12,8},{9,1... | collective-permute-start | bytes 786440 | tf_op jit(solution)/shard_map/ppermute | solution.py:35
  149.8 6.1 %collective-permute-start.25 = (f32[3,8,512]{2,1,0:T(8,128)}, f32[3,8,512]{2,1,0:T(8,128)S(1)}, u32[]{:S(2)}, u32[]{:S(2)}) collective-permute-start(f32[3,8,512]{2,1,0:T(8,128)} %get-tuple-element.30), channel_id=1, source_target_pairs={{8,0},{16,8},{24,16},{32,24},{40,32},{48,40},{56,48},{64,56},{72,6... | collective-permute-start | bytes 147464 | tf_op jit(solution)/shard_map/ppermute | solution.py:31
  (6 other events, 4.5 us)

commit v6 on v5

--- a/solution.py
+++ b/solution.py
@@ -170,7 +170,9 @@
                 low_ref[d + k] = jnp.concatenate([fold(low0), fold(low1)], axis=1)
                 high_ref[d + k] = jnp.concatenate([fold(high0), fold(high1)], axis=1)
         parts.append(acc_ref[...].reshape(blocks, GROUP, BLOCK))
-        f_ref[g] = (low_ref[...] + high_ref[pl.ds(1, blocks)]).sum(axis=1) * scale
+        rows = (low_ref[...] + high_ref[pl.ds(1, blocks)]).sum(axis=1) * scale
+        for d in range(blocks):
+            f_ref[g : g + 1, d * BLOCK : (d + 1) * BLOCK] = rows[d : d + 1]
     y_ref[...] = jnp.concatenate(parts, axis=1).astype(BF16)
 
 
@@ -200,7 +202,7 @@
         name="conv_backward",
         out_shape=(
             jax.ShapeDtypeStruct(x.shape, BF16),
-            jax.ShapeDtypeStruct((chans // GROUP, blocks, BLOCK), F32),
+            jax.ShapeDtypeStruct((chans // GROUP, blocks * BLOCK), F32),
         ),
         scratch_shapes=[
             pltpu.VMEM((h.shape[0], h.shape[1] // HALF + 1, HALF, HALF), BF16),
@@ -233,13 +235,22 @@
     return [piece_copy(ref, buffer_ref.at[n], sems, n) for n, ref in enumerate(refs)]
 
 
-def whole_columns(at_ref, place, buffer_ref):
+def all_columns(at_ref, pair, half, buffer_ref):
     first = at_ref[1] == 0
-    own, own_c, side, side_c = (buffer_ref[place // 2 * 4 + n, place % 2] for n in range(4))
+    own, own_c, side, side_c = (buffer_ref[pair * 4 + n, half] for n in range(4))
     parts = []
     for mine, other in ((own, own_c), (side, side_c)):
         parts += [jnp.where(first, mine, other), jnp.where(first, other, mine)]
     return jnp.concatenate(parts, axis=1)
+
+
+def met_columns(at_ref, k, e, buffer_ref):
+    z = at_ref[4]
+    chan = ((at_ref[2] + e) & 1) * 4 + ((at_ref[3] + k) & 3)
+    apart = (chan - z) & 3
+    pair = jnp.where(apart == 0, 0, jnp.where(apart == 1, 1, jnp.where(apart == 3, 2, 3)))
+    start = jnp.where(pair == 3, z ^ 2, (z + jnp.where(pair == 2, 7, pair)) & 7)
+    return all_columns(at_ref, pair, jnp.where(chan == start, 0, 1), buffer_ref)
 
 
 def side_columns(side, width):
@@ -281,7 +292,7 @@
         )
         part = lax.dot_general(
             lhs,
-            whole_columns(at_ref, place, buffer_ref),
+            all_columns(at_ref, place // 2, place % 2, buffer_ref),
             (((1,), (1,)), ((), ())),
             preferred_element_type=F32,
         )
@@ -334,20 +345,18 @@
     query_grad_ref[...] = grad_ref[...] * mixed_in
     gated = (query * mixed_in).astype(BF16)
     width = parts_ref.shape[3] // 2
-    for place, (k, e) in enumerate(met_places(at_ref, 1)):
-        if place % 2 == 0:
-            for copy in copies[place * 2 : place * 2 + 4]:
-                copy.wait()
-        part = jnp.dot(
-            gated, whole_columns(at_ref, place, buffer_ref), preferred_element_type=F32
-        ).astype(BF16)
-        parts_ref[k, e, :, side_columns(yl, width)] = part[:, :width]
-        parts_ref[k, e, :, side_columns(1 - yl, width)] = part[:, width:]
-    leaving = [
-        piece_copy(parts_ref.at[n], ref, out_sems, n) for n, ref in enumerate((out0, out1, out2, out3))
-    ]
-    for copy in leaving:
-        copy.start()
+    for copy in copies:
+        copy.wait()
+    leaving = []
+    for k, ref in enumerate((out0, out1, out2, out3)):
+        for e in range(2):
+            part = jnp.dot(
+                gated, met_columns(at_ref, k, e, buffer_ref), preferred_element_type=F32
+            ).astype(BF16)
+            parts_ref[k, e, :, side_columns(yl, width)] = part[:, :width]
+            parts_ref[k, e, :, side_columns(1 - yl, width)] = part[:, width:]
+        leaving.append(piece_copy(parts_ref.at[k], ref, out_sems, k))
+        leaving[-1].start()
     for copy in leaving:
         copy.wait()
 
@@ -433,7 +442,7 @@
         ),
         compiler_params=SCRATCH,
         cost_estimate=pl.CostEstimate(flops=5000000, bytes_accessed=3500000, transcendentals=0),
-    )(back, outside(mixed_grad), outside(query_grad), *side_args, skip)
+    )(back, mixed_grad, query_grad, *side_args, outside(skip))
 
 
 def edge_kernel(tail_ref, after_ref, taps_ref, whole_ref, out_ref):
@@ -483,7 +492,6 @@
 
 def on_device(projected, short_weight, filters, skip, out_weight, cotangent):
     tok_rows, _ = cotangent.shape
-    groups_dev, seq_length = filters.shape
     rim = SHORT - 1
     wide, deep = lax.axis_size("x"), lax.axis_size("z")
     yl, core = lax.axis_index("yl"), lax.axis_index("core")
@@ -527,7 +535,7 @@
     return (
         mixed,
         projected_grad.transpose(1, 0, 2),
-        filter_grad.reshape(groups_dev, seq_length),
+        filter_grad,
     )
 
 

time: 158 us -> 156 us (0.987)
    unnamed x49 -> x52, local copies, waits for them, and re-layouts: 13.7 us -> 12.8 us
where the time goes in v6:
time: 156 us; the launch traced here: 155 us
  starting transfers between devices  83.9 us (54%)
  Pallas kernels  26.8 us (17%)
  waiting for transfers between devices  25.4 us (16%)
  local copies, waits for them, and re-layouts  13.6 us (9%)
  other arithmetic  4.03 us (3%)
    all_to_all x2, starting transfers between devices, channel_major(): return lax.all_to_all(sent, SEQ, split_axis=0, concat_axis=0, tiled=True)  23.9 us
    all_to_all x2, starting transfers between devices, token_major(): got = lax.all_to_all(block, SEQ, split_axis=0, concat_axis=0, tiled=True)  16 us
    ppermute x14, starting transfers between devices, swap(): return lax.ppermute(shard, axis, [(0, 1), (1, 0)])  13.7 us
    unnamed x52, local copies, waits for them, and re-layouts  12.8 us
    ppermute x2, starting transfers between devices, cross_z(): lax.ppermute(shard, 'z', [(i, i ^ by) for i in range(lax.axis_size('z'))])  12.7 us
    ppermute x6, waiting for transfers between devices, shift_x(): lax.ppermute(shard, 'x', [(i, (i + by) % count) for i in range(count)])  12.6 us
    ppermute x14, waiting for transfers between devices, swap(): return lax.ppermute(shard, axis, [(0, 1), (1, 0)])  9.84 us
    ppermute x2, starting transfers between devices, from_behind(): return lax.ppermute(shard, SEQ, pairs)  9.13 us
  transfers between devices with their start and end apart: 30, of which 8 were waited for; matrix products, arithmetic and copies ran while one was open for 3% of the time, Pallas kernels for 17%

profile of v6, /device:TPU:1, one launch (start us, length us, event | category | flops | bytes accessed | tf_op | source)
XLA Modules:
  0.0 154.6 jit_solution(6750295044357134518)
XLA Ops:
  0.6 7.8 %collective-permute-start.5 = (bf16[512,128]{1,0:T(8,128)(2,1)}, bf16[512,128]{1,0:T(8,128)(2,1)S(1)}, u32[]{:S(2)}, u32[]{:S(2)}) collective-permute-start(bf16[512,128]{1,0:T(8,128)(2,1)} %param.10), channel_id=1, source_target_pairs={{0,128},{32,160},{64,192},{96,224},{128,0},{160,32},{192,64},{224,... | collective-permute-start | bytes 393224 | tf_op jit(solution)/shard_map/ppermute | solution.py:391
  8.4 2.9 %collective-permute-start.1 = (bf16[256,512]{1,0:T(8,128)(2,1)}, bf16[256,512]{1,0:T(8,128)(2,1)S(1)}, u32[]{:S(2)}, u32[]{:S(2)}) collective-permute-start(bf16[256,512]{1,0:T(8,128)(2,1)} %param.11), channel_id=1, source_target_pairs={{0,4},{4,0},{1,5},{5,1},{2,6},{6,2},{3,7},{7,3},{8,12},{12,8},{9,1... | collective-permute-start | bytes 786440 | tf_op jit(solution)/shard_map/ppermute | solution.py:35
  11.4 1.0 pad_maximum_fusion.1.refs_0_
  12.4 4.9 %collective-permute-start.17 = (bf16[2,512,128]{2,1,0:T(8,128)(2,1)S(1)}, bf16[2,512,128]{2,1,0:T(8,128)(2,1)S(1)}, u32[]{:S(2)}, u32[]{:S(2)}) collective-permute-start(bf16[2,512,128]{2,1,0:T(8,128)(2,1)S(1)} %pad_maximum_fusion.1.refs_0_), channel_id=1, source_target_pairs={{0,64},{32,96},{64,0},{96,32},{128,192},{160,224},{192,128},{224,1... | collective-permute-start | bytes 786440 | tf_op jit(solution)/shard_map/ppermute | solution.py:391
  17.3 2.7 %collective-permute-start.9 = (bf16[2,512,128]{2,1,0:T(8,128)(2,1)S(1)}, bf16[2,512,128]{2,1,0:T(8,128)(2,1)}, u32[]{:S(2)}, u32[]{:S(2)}) collective-permute-start(bf16[2,512,128]{2,1,0:T(8,128)(2,1)S(1)} %pad_maximum_fusion.1.refs_0_), channel_id=1, source_target_pairs={{0,224},{32,0},{64,32},{96,64},{128,96},{160,128},{192,160},{224,1... | collective-permute-start | bytes 786440 | tf_op jit(solution)/shard_map/ppermute | solution.py:387
  20.0 0.7 slice.27
  20.7 5.9 %collective-permute-start = (bf16[2,3,512]{2,0,1:T(2,128)(2,1)S(1)}, bf16[2,3,512]{2,0,1:T(2,128)(2,1)S(1)}, u32[]{:S(2)}, u32[]{:S(2)}) collective-permute-start(bf16[2,3,512]{2,0,1:T(2,128)(2,1)S(1)} %slice.27), channel_id=1, source_target_pairs={{0,8},{8,16},{16,24},{24,32},{32,40},{40,48},{48,56},{56,64},{64,7... | collective-permute-start | bytes 18440 | tf_op jit(solution)/shard_map/ppermute | solution.py:31
  26.6 0.8 collective-permute-done
  27.4 1.5 collective-permute-start.7
  28.8 1.2 collective-permute-start.6
  30.8 1.3 collective-permute-start.15
  32.1 2.6 %collective-permute-done.7.refs_2_ = bf16[2,512,128]{2,1,0:T(8,128)(2,1)} collective-permute-done((bf16[2,512,128]{2,1,0:T(8,128)(2,1)S(1)}, bf16[2,512,128]{2,1,0:T(8,128)(2,1)}, u32[]{:S(2)}, u32[]{:S(2)}) %collective-permute-start.7) | collective-permute-done | bytes 262176 | tf_op jit(solution)/shard_map/ppermute | solution.py:35
  34.7 2.5 %collective-permute-start.4 = (bf16[2,256,512]{2,1,0:T(8,128)(2,1)S(1)}, bf16[2,256,512]{2,1,0:T(8,128)(2,1)S(1)}, u32[]{:S(2)}, u32[]{:S(2)}) collective-permute-start(bf16[2,256,512]{2,1,0:T(8,128)(2,1)S(1)} %pad_maximum_fusion.cot0), channel_id=1, source_target_pairs={{0,3},{1,0},{2,1},{3,2},{4,7},{5,4},{6,5},{7,6},{8,11},{9,8},{10,9... | collective-permute-start | bytes 1572872 | tf_op jit(solution)/shard_map/ppermute | solution.py:396
  37.2 2.3 %carried_columns.1 = bf16[512,256]{1,0:T(8,128)(2,1)} custom-call(bf16[3,256,512]{2,1,0:T(8,128)(2,1)} %bitcast.21, bf16[3,2,512]{2,1,0:T(2,128)(2,1)S(1)} %bitcast.27, f32[3,3,512]{2,1,0:T(4,128)} %taps_ref.9), custom_call_target="tpu_custom_call" | custom-call | flops 5000000 | bytes 1500000 | tf_op jit(solution)/shard_map/carried_columns/pallas_call | solution.py:406
  39.5 16.1 %all-to-all-start = ((bf16[32,16,256]{2,1,0:T(8,128)(2,1)}), bf16[32,16,256]{2,1,0:T(8,128)(2,1)S(1)}, u32[]{:S(2)}, u32[]{:S(2)}) async-start(bf16[32,16,256]{2,1,0:T(8,128)(2,1)} %bitcast.31), calls=%async_computation | async-start | bytes 524288 | tf_op jit(solution)/shard_map/all_to_all | solution.py:485
  56.6 1.5 collective-permute-start.11
  58.6 0.7 copy-done.13
  59.9 7.2 %collective-permute-done.11.refs_6_ = bf16[2,512,128]{2,1,0:T(8,128)(2,1)} collective-permute-done((bf16[2,512,128]{2,1,0:T(8,128)(2,1)}, bf16[2,512,128]{2,1,0:T(8,128)(2,1)}, u32[]{:S(2)}, u32[]{:S(2)}) %collective-permute-start.11) | collective-permute-done | bytes 262176 | tf_op jit(solution)/shard_map/ppermute | solution.py:35
  67.1 0.7 copy-done.16
  67.8 1.0 collective-permute-start.20
  68.8 0.7 copy-done.19
  70.1 3.8 %conv_forward.1 = bf16[32,16,256]{2,1,0:T(8,128)(2,1)} custom-call(bf16[32,16,256]{2,1,0:T(8,128)(2,1)S(1)} %all-to-all-done.x_ref, f32[2,8192]{1,0:T(2,128)S(1)} %copy-done.22), custom_call_target="tpu_custom_call" | custom-call | flops 6000000000 | bytes 600000 | tf_op jit(solution)/shard_map/conv_forward/pallas_call | solution.py:182
  73.9 6.9 %all-to-all-start.1 = ((bf16[32,16,256]{2,1,0:T(8,128)(2,1)}), bf16[32,16,256]{2,1,0:T(8,128)(2,1)S(1)}, u32[]{:S(2)}, u32[]{:S(2)}) async-start(bf16[32,16,256]{2,1,0:T(8,128)(2,1)} %conv_forward.1), calls=%async_computation.1 | async-start | bytes 524288 | tf_op jit(solution)/shard_map/all_to_all | solution.py:489
  80.9 5.1 %collective-permute-done.2.cot1 = bf16[2,256,512]{2,1,0:T(8,128)(2,1)} collective-permute-done((bf16[2,256,512]{2,1,0:T(8,128)(2,1)S(1)}, bf16[2,256,512]{2,1,0:T(8,128)(2,1)}, u32[]{:S(2)}, u32[]{:S(2)}) %collective-permute-start.2) | collective-permute-done | bytes 524320 | tf_op jit(solution)/shard_map/ppermute | solution.py:396
  86.1 0.9 copy-done.5
  87.0 0.9 copy-done.8
  88.0 0.9 copy-done.11
  88.9 0.9 copy-done.14
  89.9 0.9 copy-done.17
  90.8 0.9 copy-done.20
  91.8 4.5 %grad_matmul.1 = (f32[256,512]{1,0:T(8,128)}, bf16[256,512]{1,0:T(8,128)(2,1)}, bf16[512,256]{1,0:T(8,128)(2,1)}) custom-call(s32[5]{0:T(128)S(1)} %stack.41.at_ref, bf16[3,256,512]{2,1,0:T(8,128)(2,1)S(1)} %bitcast.22, bf16[3,2,512]{2,1,0:T(2,128)(2,1)S(1)} %bitcast.28, f32[3,3,512]{2,1,0:T(4,128)S(1)} %copy-done.3, ...), custom_call_target="tpu_custom_call" | custom-call | flops 4000000000 | bytes 6500000 | tf_op jit(solution)/shard_map/grad_matmul/pallas_call | solution.py:315
  96.3 7.8 %all-to-all-start.2 = ((bf16[32,16,256]{2,1,0:T(8,128)(2,1)}), bf16[32,16,256]{2,1,0:T(8,128)(2,1)S(1)}, u32[]{:S(2)}, u32[]{:S(2)}) async-start(bf16[32,16,256]{2,1,0:T(8,128)(2,1)} %bitcast.33), calls=%async_computation.2 | async-start | bytes 524288 | tf_op jit(solution)/shard_map/all_to_all | solution.py:485
  104.1 0.9 copy-done.12
  105.1 0.9 copy-done.15
  106.0 0.9 copy-done.18
  107.0 0.9 copy-done.21
  107.9 5.7 %mix_matmul.1 = (bf16[2,256,512]{2,1,0:T(8,128)(2,1)}, bf16[2,256,512]{2,1,0:T(8,128)(2,1)}, bf16[2,256,512]{2,1,0:T(8,128)(2,1)}, bf16[2,256,512]{2,1,0:T(8,128)(2,1)}, f32[256,512]{1,0:T(8,128)}) custom-call(s32[5]{0:T(128)S(1)} %stack.41.at_ref, bf16[512,256]{1,0:T(8,128)(2,1)S(1)} %bitcast.26, bf16[3,256,512]{2,1,0:T(8,128)(2,1)S(1)} %bitcast.23, ...), custom_call_target="tpu_custom_call" | custom-call | flops 4000000000 | bytes 6500000 | tf_op jit(solution)/shard_map/mix_matmul/pallas_call | solution.py:367
  113.7 1.5 collective-permute-start.22
  115.2 1.2 collective-permute-start.23
  116.4 7.0 %conv_backward.1 = (bf16[32,16,256]{2,1,0:T(8,128)(2,1)}, f32[2,8192]{1,0:T(2,128)}) custom-call(bf16[32,16,256]{2,1,0:T(8,128)(2,1)S(1)} %all-to-all-done.2.m_ref, bf16[32,16,256]{2,1,0:T(8,128)(2,1)S(1)} %all-to-all-done.x_ref, f32[2,8192]{1,0:T(2,128)S(1)} %copy-done.22), custom_call_target="tpu_custom_call" | custom-call | flops 10000000000 | bytes 1000000 | tf_op jit(solution)/shard_map/conv_backward/pallas_call | solution.py:200
  123.4 9.1 %all-to-all-start.3 = ((bf16[32,16,256]{2,1,0:T(8,128)(2,1)}), bf16[32,16,256]{2,1,0:T(8,128)(2,1)S(1)}, u32[]{:S(2)}, u32[]{:S(2)}) async-start(bf16[32,16,256]{2,1,0:T(8,128)(2,1)} %get-tuple-element.26), calls=%async_computation.3 | async-start | bytes 524288 | tf_op jit(solution)/shard_map/all_to_all | solution.py:489
  132.5 7.1 %collective-permute-done.21 = bf16[2,256,512]{2,1,0:T(8,128)(2,1)S(1)} collective-permute-done((bf16[2,256,512]{2,1,0:T(8,128)(2,1)}, bf16[2,256,512]{2,1,0:T(8,128)(2,1)S(1)}, u32[]{:S(2)}, u32[]{:S(2)}) %collective-permute-start.21) | collective-permute-done | bytes 524320 | tf_op jit(solution)/shard_map/ppermute | solution.py:396
  140.4 2.2 %add_bitcast_fusion = (f32[256,512]{1,0:T(8,128)S(1)}, bf16[256,512]{1,0:T(8,128)(2,1)}) fusion(bf16[2,256,512]{2,1,0:T(8,128)(2,1)} %collective-permute-done.23, bf16[2,256,512]{2,1,0:T(8,128)(2,1)} %copy-done.24, bf16[2,256,512]{2,1,0:T(8,128)(2,1)S(1)} %collective-permute-done.21, bf16[2,256,512]{2,1,0:T(8,128)(2,1)S(1)} %copy-done.23), kind=kLoop, calls=%fused_computation.2 | loop fusion | flops 1966080 | bytes 2883584 | tf_op jit(solution)/shard_map/add | solution.py:525
  142.6 2.6 %collective-permute-start.24 = (bf16[256,512]{1,0:T(8,128)(2,1)}, bf16[256,512]{1,0:T(8,128)(2,1)S(1)}, u32[]{:S(2)}, u32[]{:S(2)}) collective-permute-start(bf16[256,512]{1,0:T(8,128)(2,1)} %get-tuple-element.24), channel_id=1, source_target_pairs={{0,4},{4,0},{1,5},{5,1},{2,6},{6,2},{3,7},{7,3},{8,12},{12,8},{9,1... | collective-permute-start | bytes 786440 | tf_op jit(solution)/shard_map/ppermute | solution.py:35
  145.3 2.9 %final_short.1 = (bf16[3,256,512]{2,1,0:T(8,128)(2,1)}, f32[3,8,512]{2,1,0:T(8,128)}, f32[3,16,512]{2,1,0:T(8,128)S(1)}) custom-call(bf16[512,256]{1,0:T(8,128)(2,1)S(1)} %bitcast.25, bf16[256,512]{1,0:T(8,128)(2,1)S(1)} %copy-done.2, f32[256,512]{1,0:T(8,128)S(1)} %copy-done.1, bf16[3,256,512]{2,1,0:T(8,128)(2,1)S(1)} %bitcast.24, ...), custom_call_target="tpu_custom_call" | custom-call | flops 5000000 | bytes 3500000 | tf_op jit(solution)/shard_map/final_short/pallas_call | solution.py:435
  148.1 3.3 %collective-permute-start.25 = (f32[3,8,512]{2,1,0:T(8,128)}, f32[3,8,512]{2,1,0:T(8,128)S(1)}, u32[]{:S(2)}, u32[]{:S(2)}) collective-permute-start(f32[3,8,512]{2,1,0:T(8,128)} %get-tuple-element.30), channel_id=1, source_target_pairs={{8,0},{16,8},{24,16},{32,24},{40,32},{48,40},{56,48},{64,56},{72,6... | collective-permute-start | bytes 147464 | tf_op jit(solution)/shard_map/ppermute | solution.py:31
  151.4 0.8 add_convert_fusion
  152.2 1.8 %collective-permute-done.25.after_ref = f32[3,8,512]{2,1,0:T(8,128)S(1)} collective-permute-done((f32[3,8,512]{2,1,0:T(8,128)}, f32[3,8,512]{2,1,0:T(8,128)S(1)}, u32[]{:S(2)}, u32[]{:S(2)}) %collective-permute-start.25) | collective-permute-done | bytes 49184 | tf_op jit(solution)/shard_map/ppermute | solution.py:31
  (77 shorter events, 5.0 us)
Async XLA Ops:
  0.6 10.8 %collective-permute-start.5 = (bf16[512,128]{1,0:T(8,128)(2,1)}, bf16[512,128]{1,0:T(8,128)(2,1)S(1)}, u32[]{:S(2)}, u32[]{:S(2)}) collective-permute-start(bf16[512,128]{1,0:T(8,128)(2,1)} %param.10), channel_id=1, source_target_pairs={{0,128},{32,160},{64,192},{96,224},{128,0},{160,32},{192,64},{224,... | collective-permute-start | bytes 393224 | tf_op jit(solution)/shard_map/ppermute | solution.py:391
  8.4 20.4 %collective-permute-start.1 = (bf16[256,512]{1,0:T(8,128)(2,1)}, bf16[256,512]{1,0:T(8,128)(2,1)S(1)}, u32[]{:S(2)}, u32[]{:S(2)}) collective-permute-start(bf16[256,512]{1,0:T(8,128)(2,1)} %param.11), channel_id=1, source_target_pairs={{0,4},{4,0},{1,5},{5,1},{2,6},{6,2},{3,7},{7,3},{8,12},{12,8},{9,1... | collective-permute-start | bytes 786440 | tf_op jit(solution)/shard_map/ppermute | solution.py:35
  11.4 20.6 %copy-start.25 = (bf16[256,512]{1,0:T(8,128)(2,1)S(1)}, bf16[256,512]{1,0:T(8,128)(2,1)}, u32[]{:S(2)}) copy-start(bf16[256,512]{1,0:T(8,128)(2,1)} %param.11) | copy-start | bytes 786436
  12.4 17.6 %collective-permute-start.17 = (bf16[2,512,128]{2,1,0:T(8,128)(2,1)S(1)}, bf16[2,512,128]{2,1,0:T(8,128)(2,1)S(1)}, u32[]{:S(2)}, u32[]{:S(2)}) collective-permute-start(bf16[2,512,128]{2,1,0:T(8,128)(2,1)S(1)} %pad_maximum_fusion.1.refs_0_), channel_id=1, source_target_pairs={{0,64},{32,96},{64,0},{96,32},{128,192},{160,224},{192,128},{224,1... | collective-permute-start | bytes 786440 | tf_op jit(solution)/shard_map/ppermute | solution.py:391
  17.3 12.7 %collective-permute-start.13 = (bf16[2,512,128]{2,1,0:T(8,128)(2,1)S(1)}, bf16[2,512,128]{2,1,0:T(8,128)(2,1)S(1)}, u32[]{:S(2)}, u32[]{:S(2)}) collective-permute-start(bf16[2,512,128]{2,1,0:T(8,128)(2,1)S(1)} %pad_maximum_fusion.1.refs_0_), channel_id=1, source_target_pairs={{0,32},{32,64},{64,96},{96,128},{128,160},{160,192},{192,224},{224... | collective-permute-start | bytes 786440 | tf_op jit(solution)/shard_map/ppermute | solution.py:387
  17.3 13.4 %collective-permute-start.9 = (bf16[2,512,128]{2,1,0:T(8,128)(2,1)S(1)}, bf16[2,512,128]{2,1,0:T(8,128)(2,1)}, u32[]{:S(2)}, u32[]{:S(2)}) collective-permute-start(bf16[2,512,128]{2,1,0:T(8,128)(2,1)S(1)} %pad_maximum_fusion.1.refs_0_), channel_id=1, source_target_pairs={{0,224},{32,0},{64,32},{96,64},{128,96},{160,128},{192,160},{224,1... | collective-permute-start | bytes 786440 | tf_op jit(solution)/shard_map/ppermute | solution.py:387
  20.7 6.6 %collective-permute-start = (bf16[2,3,512]{2,0,1:T(2,128)(2,1)S(1)}, bf16[2,3,512]{2,0,1:T(2,128)(2,1)S(1)}, u32[]{:S(2)}, u32[]{:S(2)}) collective-permute-start(bf16[2,3,512]{2,0,1:T(2,128)(2,1)S(1)} %slice.27), channel_id=1, source_target_pairs={{0,8},{8,16},{16,24},{24,32},{32,40},{40,48},{48,56},{56,64},{64,7... | collective-permute-start | bytes 18440 | tf_op jit(solution)/shard_map/ppermute | solution.py:31
  27.4 7.4 %collective-permute-start.7 = (bf16[2,512,128]{2,1,0:T(8,128)(2,1)S(1)}, bf16[2,512,128]{2,1,0:T(8,128)(2,1)}, u32[]{:S(2)}, u32[]{:S(2)}) collective-permute-start(bf16[2,512,128]{2,1,0:T(8,128)(2,1)S(1)} %pad_maximum_fusion.1.refs_0_), channel_id=1, source_target_pairs={{0,16},{16,0},{1,17},{17,1},{2,18},{18,2},{3,19},{19,3},{4,20},{20... | collective-permute-start | bytes 786440 | tf_op jit(solution)/shard_map/ppermute | solution.py:35
  28.8 26.8 %collective-permute-start.6 = (bf16[2,512,128]{2,1,0:T(8,128)(2,1)S(1)}, bf16[2,512,128]{2,1,0:T(8,128)(2,1)S(1)}, u32[]{:S(2)}, u32[]{:S(2)}) collective-permute-start(bf16[2,512,128]{2,1,0:T(8,128)(2,1)S(1)} %pad_maximum_fusion.1.refs_0_), channel_id=1, source_target_pairs={{0,8},{8,0},{1,9},{9,1},{2,10},{10,2},{3,11},{11,3},{4,12},{12,4},... | collective-permute-start | bytes 786440 | tf_op jit(solution)/shard_map/ppermute | solution.py:35
  30.0 26.5 %collective-permute-start.19 = (bf16[2,512,128]{2,1,0:T(8,128)(2,1)S(1)}, bf16[2,512,128]{2,1,0:T(8,128)(2,1)}, u32[]{:S(2)}, u32[]{:S(2)}) collective-permute-start(bf16[2,512,128]{2,1,0:T(8,128)(2,1)S(1)} %collective-permute-done.17.refs_12_), channel_id=1, source_target_pairs={{0,16},{16,0},{1,17},{17,1},{2,18},{18,2},{3,19},{19,3},{4,20},{20... | collective-permute-start | bytes 786440 | tf_op jit(solution)/shard_map/ppermute | solution.py:35
  30.0 25.6 %copy-start.4 = (bf16[2,512,128]{2,1,0:T(8,128)(2,1)}, bf16[2,512,128]{2,1,0:T(8,128)(2,1)S(1)}, u32[]{:S(2)}) copy-start(bf16[2,512,128]{2,1,0:T(8,128)(2,1)S(1)} %collective-permute-done.13.refs_8_) | copy-start | bytes 786436
  30.1 28.0 %collective-permute-start.18 = (bf16[2,512,128]{2,1,0:T(8,128)(2,1)S(1)}, bf16[2,512,128]{2,1,0:T(8,128)(2,1)S(1)}, u32[]{:S(2)}, u32[]{:S(2)}) collective-permute-start(bf16[2,512,128]{2,1,0:T(8,128)(2,1)S(1)} %collective-permute-done.17.refs_12_), channel_id=1, source_target_pairs={{0,8},{8,0},{1,9},{9,1},{2,10},{10,2},{3,11},{11,3},{4,12},{12,4},... | collective-permute-start | bytes 786440 | tf_op jit(solution)/shard_map/ppermute | solution.py:35
  30.8 27.7 %collective-permute-start.15 = (bf16[2,512,128]{2,1,0:T(8,128)(2,1)S(1)}, bf16[2,512,128]{2,1,0:T(8,128)(2,1)}, u32[]{:S(2)}, u32[]{:S(2)}) collective-permute-start(bf16[2,512,128]{2,1,0:T(8,128)(2,1)S(1)} %collective-permute-done.13.refs_8_), channel_id=1, source_target_pairs={{0,16},{16,0},{1,17},{17,1},{2,18},{18,2},{3,19},{19,3},{4,20},{20... | collective-permute-start | bytes 786440 | tf_op jit(solution)/shard_map/ppermute | solution.py:35
  34.7 34.9 %collective-permute-start.4 = (bf16[2,256,512]{2,1,0:T(8,128)(2,1)S(1)}, bf16[2,256,512]{2,1,0:T(8,128)(2,1)S(1)}, u32[]{:S(2)}, u32[]{:S(2)}) collective-permute-start(bf16[2,256,512]{2,1,0:T(8,128)(2,1)S(1)} %pad_maximum_fusion.cot0), channel_id=1, source_target_pairs={{0,3},{1,0},{2,1},{3,2},{4,7},{5,4},{6,5},{7,6},{8,11},{9,8},{10,9... | collective-permute-start | bytes 1572872 | tf_op jit(solution)/shard_map/ppermute | solution.py:396
  39.5 30.6 %copy-start.22 = (f32[2,8192]{1,0:T(2,128)S(1)}, f32[2,8192]{1,0:T(2,128)}, u32[]{:S(2)}) copy-start(f32[2,8192]{1,0:T(2,128)} %h_ref.3) | copy-start | bytes 196612
  39.5 30.6 %all-to-all-start = ((bf16[32,16,256]{2,1,0:T(8,128)(2,1)}), bf16[32,16,256]{2,1,0:T(8,128)(2,1)S(1)}, u32[]{:S(2)}, u32[]{:S(2)}) async-start(bf16[32,16,256]{2,1,0:T(8,128)(2,1)} %bitcast.31), calls=%async_computation | async-start | bytes 524288 | tf_op jit(solution)/shard_map/all_to_all | solution.py:485
  55.6 30.5 %copy-start = (bf16[256,3,512]{2,0,1:T(8,128)(2,1)S(1)}, bf16[256,3,512]{2,0,1:T(8,128)(2,1)}, u32[]{:S(2)}) copy-start(bf16[256,3,512]{2,0,1:T(8,128)(2,1)} %param.6) | copy-start | bytes 2359300
  56.3 2.3 %collective-permute-start.14 = (bf16[2,512,128]{2,1,0:T(8,128)(2,1)S(1)}, bf16[2,512,128]{2,1,0:T(8,128)(2,1)S(1)}, u32[]{:S(2)}, u32[]{:S(2)}) collective-permute-start(bf16[2,512,128]{2,1,0:T(8,128)(2,1)S(1)} %collective-permute-done.13.refs_8_), channel_id=1, source_target_pairs={{0,8},{8,0},{1,9},{9,1},{2,10},{10,2},{3,11},{11,3},{4,12},{12,4},... | collective-permute-start | bytes 786440 | tf_op jit(solution)/shard_map/ppermute | solution.py:35
  56.6 10.5 %collective-permute-start.11 = (bf16[2,512,128]{2,1,0:T(8,128)(2,1)}, bf16[2,512,128]{2,1,0:T(8,128)(2,1)}, u32[]{:S(2)}, u32[]{:S(2)}) collective-permute-start(bf16[2,512,128]{2,1,0:T(8,128)(2,1)} %collective-permute-done.9.refs_4_), channel_id=1, source_target_pairs={{0,16},{16,0},{1,17},{17,1},{2,18},{18,2},{3,19},{19,3},{4,20},{20... | collective-permute-start | bytes 786440 | tf_op jit(solution)/shard_map/ppermute | solution.py:35
  58.1 15.8 %copy-start.10 = (bf16[2,512,128]{2,1,0:T(8,128)(2,1)}, bf16[2,512,128]{2,1,0:T(8,128)(2,1)S(1)}, u32[]{:S(2)}) copy-start(bf16[2,512,128]{2,1,0:T(8,128)(2,1)S(1)} %collective-permute-done.18.refs_13_) | copy-start | bytes 786436
  58.1 9.0 %collective-permute-start.10 = (bf16[2,512,128]{2,1,0:T(8,128)(2,1)}, bf16[2,512,128]{2,1,0:T(8,128)(2,1)S(1)}, u32[]{:S(2)}, u32[]{:S(2)}) collective-permute-start(bf16[2,512,128]{2,1,0:T(8,128)(2,1)} %collective-permute-done.9.refs_4_), channel_id=1, source_target_pairs={{0,8},{8,0},{1,9},{9,1},{2,10},{10,2},{3,11},{11,3},{4,12},{12,4},... | collective-permute-start | bytes 786440 | tf_op jit(solution)/shard_map/ppermute | solution.py:35
  58.5 10.4 %collective-permute-start.8 = (bf16[2,512,128]{2,1,0:T(8,128)(2,1)}, bf16[2,512,128]{2,1,0:T(8,128)(2,1)S(1)}, u32[]{:S(2)}, u32[]{:S(2)}) collective-permute-start(bf16[2,512,128]{2,1,0:T(8,128)(2,1)} %collective-permute-done.7.refs_2_), channel_id=1, source_target_pairs={{0,8},{8,0},{1,9},{9,1},{2,10},{10,2},{3,11},{11,3},{4,12},{12,4},... | collective-permute-start | bytes 786440 | tf_op jit(solution)/shard_map/ppermute | solution.py:35
  59.3 21.6 %collective-permute-start.3 = (bf16[2,256,512]{2,1,0:T(8,128)(2,1)S(1)}, bf16[2,256,512]{2,1,0:T(8,128)(2,1)S(1)}, u32[]{:S(2)}, u32[]{:S(2)}) collective-permute-start(bf16[2,256,512]{2,1,0:T(8,128)(2,1)S(1)} %pad_maximum_fusion.cot0), channel_id=1, source_target_pairs={{0,2},{1,3},{2,0},{3,1},{4,6},{5,7},{6,4},{7,5},{8,10},{9,11},{10,... | collective-permute-start | bytes 1572872 | tf_op jit(solution)/shard_map/ppermute | solution.py:396
  67.1 19.0 %collective-permute-start.2 = (bf16[2,256,512]{2,1,0:T(8,128)(2,1)S(1)}, bf16[2,256,512]{2,1,0:T(8,128)(2,1)}, u32[]{:S(2)}, u32[]{:S(2)}) collective-permute-start(bf16[2,256,512]{2,1,0:T(8,128)(2,1)S(1)} %pad_maximum_fusion.cot0), channel_id=1, source_target_pairs={{0,1},{1,2},{2,3},{3,0},{4,5},{5,6},{6,7},{7,4},{8,9},{9,10},{10,1... | collective-permute-start | bytes 1572872 | tf_op jit(solution)/shard_map/ppermute | solution.py:396
  67.8 18.2 %collective-permute-start.20 = (bf16[2,512,128]{2,1,0:T(8,128)(2,1)}, bf16[2,512,128]{2,1,0:T(8,128)(2,1)}, u32[]{:S(2)}, u32[]{:S(2)}) collective-permute-start(bf16[2,512,128]{2,1,0:T(8,128)(2,1)} %collective-permute-done.19.refs_14_), channel_id=1, source_target_pairs={{0,8},{8,0},{1,9},{9,1},{2,10},{10,2},{3,11},{11,3},{4,12},{12,4},... | collective-permute-start | bytes 786440 | tf_op jit(solution)/shard_map/ppermute | solution.py:35
  69.6 16.5 %collective-permute-start.16 = (bf16[2,512,128]{2,1,0:T(8,128)(2,1)}, bf16[2,512,128]{2,1,0:T(8,128)(2,1)}, u32[]{:S(2)}, u32[]{:S(2)}) collective-permute-start(bf16[2,512,128]{2,1,0:T(8,128)(2,1)} %collective-permute-done.15.refs_10_), channel_id=1, source_target_pairs={{0,8},{8,0},{1,9},{9,1},{2,10},{10,2},{3,11},{11,3},{4,12},{12,4},... | collective-permute-start | bytes 786440 | tf_op jit(solution)/shard_map/ppermute | solution.py:35
  69.6 16.5 %collective-permute-start.12 = (bf16[2,512,128]{2,1,0:T(8,128)(2,1)}, bf16[2,512,128]{2,1,0:T(8,128)(2,1)}, u32[]{:S(2)}, u32[]{:S(2)}) collective-permute-start(bf16[2,512,128]{2,1,0:T(8,128)(2,1)} %collective-permute-done.11.refs_6_), channel_id=1, source_target_pairs={{0,8},{8,0},{1,9},{9,1},{2,10},{10,2},{3,11},{11,3},{4,12},{12,4},... | collective-permute-start | bytes 786440 | tf_op jit(solution)/shard_map/ppermute | solution.py:35
  73.9 22.3 %all-to-all-start.1 = ((bf16[32,16,256]{2,1,0:T(8,128)(2,1)}), bf16[32,16,256]{2,1,0:T(8,128)(2,1)S(1)}, u32[]{:S(2)}, u32[]{:S(2)}) async-start(bf16[32,16,256]{2,1,0:T(8,128)(2,1)} %conv_forward.1), calls=%async_computation.1 | async-start | bytes 524288 | tf_op jit(solution)/shard_map/all_to_all | solution.py:489
  80.8 5.2 %copy-start.3 = (f32[3,3,512]{2,1,0:T(4,128)S(1)}, f32[3,3,512]{2,1,0:T(4,128)}, u32[]{:S(2)}) copy-start(f32[3,3,512]{2,1,0:T(4,128)} %taps_ref.9) | copy-start | bytes 55300
  86.1 1.0 copy-start.5
  87.0 0.9 copy-start.8
  88.0 0.9 copy-start.11
  88.9 0.9 copy-start.14
  89.9 0.9 copy-start.17
  90.8 0.9 copy-start.20
  96.3 7.8 %copy-start.6 = (bf16[2,512,128]{2,1,0:T(8,128)(2,1)S(1)}, bf16[2,512,128]{2,1,0:T(8,128)(2,1)}, u32[]{:S(2)}) copy-start(bf16[2,512,128]{2,1,0:T(8,128)(2,1)} %copy-done.4) | copy-start | bytes 786436
  96.3 7.8 %copy-start.9 = (bf16[2,512,128]{2,1,0:T(8,128)(2,1)S(1)}, bf16[2,512,128]{2,1,0:T(8,128)(2,1)}, u32[]{:S(2)}) copy-start(bf16[2,512,128]{2,1,0:T(8,128)(2,1)} %copy-done.7) | copy-start | bytes 786436
  96.3 20.1 %all-to-all-start.2 = ((bf16[32,16,256]{2,1,0:T(8,128)(2,1)}), bf16[32,16,256]{2,1,0:T(8,128)(2,1)S(1)}, u32[]{:S(2)}, u32[]{:S(2)}) async-start(bf16[32,16,256]{2,1,0:T(8,128)(2,1)} %bitcast.33), calls=%async_computation.2 | async-start | bytes 524288 | tf_op jit(solution)/shard_map/all_to_all | solution.py:485
  104.1 1.0 copy-start.12
  113.6 26.0 %collective-permute-start.21 = (bf16[2,256,512]{2,1,0:T(8,128)(2,1)}, bf16[2,256,512]{2,1,0:T(8,128)(2,1)S(1)}, u32[]{:S(2)}, u32[]{:S(2)}) collective-permute-start(bf16[2,256,512]{2,1,0:T(8,128)(2,1)} %get-tuple-element.20), channel_id=1, source_target_pairs={{0,1},{1,2},{2,3},{3,0},{4,5},{5,6},{6,7},{7,4},{8,9},{9,10},{10,1... | collective-permute-start | bytes 1572872 | tf_op jit(solution)/shard_map/ppermute | solution.py:396
  113.7 25.9 %collective-permute-start.22 = (bf16[2,256,512]{2,1,0:T(8,128)(2,1)}, bf16[2,256,512]{2,1,0:T(8,128)(2,1)S(1)}, u32[]{:S(2)}, u32[]{:S(2)}) collective-permute-start(bf16[2,256,512]{2,1,0:T(8,128)(2,1)} %get-tuple-element.21), channel_id=1, source_target_pairs={{0,2},{1,3},{2,0},{3,1},{4,6},{5,7},{6,4},{7,5},{8,10},{9,11},{10,... | collective-permute-start | bytes 1572872 | tf_op jit(solution)/shard_map/ppermute | solution.py:396
  115.2 24.9 %collective-permute-start.23 = (bf16[2,256,512]{2,1,0:T(8,128)(2,1)}, bf16[2,256,512]{2,1,0:T(8,128)(2,1)}, u32[]{:S(2)}, u32[]{:S(2)}) collective-permute-start(bf16[2,256,512]{2,1,0:T(8,128)(2,1)} %get-tuple-element.22), channel_id=1, source_target_pairs={{0,3},{1,0},{2,1},{3,2},{4,7},{5,4},{6,5},{7,6},{8,11},{9,8},{10,9... | collective-permute-start | bytes 1572872 | tf_op jit(solution)/shard_map/ppermute | solution.py:396
  123.4 17.0 %copy-start.23 = (bf16[2,256,512]{2,1,0:T(8,128)(2,1)S(1)}, bf16[2,256,512]{2,1,0:T(8,128)(2,1)}, u32[]{:S(2)}) copy-start(bf16[2,256,512]{2,1,0:T(8,128)(2,1)} %get-tuple-element.19) | copy-start | bytes 1572868
  123.4 21.9 %all-to-all-start.3 = ((bf16[32,16,256]{2,1,0:T(8,128)(2,1)}), bf16[32,16,256]{2,1,0:T(8,128)(2,1)S(1)}, u32[]{:S(2)}, u32[]{:S(2)}) async-start(bf16[32,16,256]{2,1,0:T(8,128)(2,1)} %get-tuple-element.26), calls=%async_computation.3 | async-start | bytes 524288 | tf_op jit(solution)/shard_map/all_to_all | solution.py:489
  140.4 4.8 %copy-start.1 = (f32[256,512]{1,0:T(8,128)S(1)}, f32[256,512]{1,0:T(8,128)}, u32[]{:S(2)}) copy-start(f32[256,512]{1,0:T(8,128)} %get-tuple-element.28.query_grad_ref) | copy-start | bytes 1572868
  140.4 4.8 %copy-start.2 = (bf16[256,512]{1,0:T(8,128)(2,1)S(1)}, bf16[256,512]{1,0:T(8,128)(2,1)}, u32[]{:S(2)}) copy-start(bf16[256,512]{1,0:T(8,128)(2,1)} %get-tuple-element.27.mixed_ref) | copy-start | bytes 786436
  142.6 8.8 %collective-permute-start.24 = (bf16[256,512]{1,0:T(8,128)(2,1)}, bf16[256,512]{1,0:T(8,128)(2,1)S(1)}, u32[]{:S(2)}, u32[]{:S(2)}) collective-permute-start(bf16[256,512]{1,0:T(8,128)(2,1)} %get-tuple-element.24), channel_id=1, source_target_pairs={{0,4},{4,0},{1,5},{5,1},{2,6},{6,2},{3,7},{7,3},{8,12},{12,8},{9,1... | collective-permute-start | bytes 786440 | tf_op jit(solution)/shard_map/ppermute | solution.py:35
  148.1 5.9 %collective-permute-start.25 = (f32[3,8,512]{2,1,0:T(8,128)}, f32[3,8,512]{2,1,0:T(8,128)S(1)}, u32[]{:S(2)}, u32[]{:S(2)}) collective-permute-start(f32[3,8,512]{2,1,0:T(8,128)} %get-tuple-element.30), channel_id=1, source_target_pairs={{8,0},{16,8},{24,16},{32,24},{40,32},{48,40},{56,48},{64,56},{72,6... | collective-permute-start | bytes 147464 | tf_op jit(solution)/shard_map/ppermute | solution.py:31
  (8 other events, 6.5 us)

commit v7 on v6

--- a/solution.py
+++ b/solution.py
@@ -520,11 +520,12 @@
     grad_seq = channel_major(grad_sent)
 
     parts, query_grad = mix_matmul(at, conv, side_args, skip[None, :], gated_grad, ws)
-    shares = [parts[0]] + [shift_x(parts[k], k) for k in range(1, wide)]
+    shares = [parts[0]]
+    for k in range(1, wide):
+        shares.append(shift_x(parts[k], k))
     theirs = sum(p[1].astype(F32) for p in shares).astype(BF16)
+    got = swap(theirs, "yh")
     mine = sum(p[0].astype(F32) for p in shares)
-    theirs, mine = lax.optimization_barrier((theirs, mine))
-    got = swap(theirs, "yh")
     mixed = (mine + got.astype(F32)).astype(BF16)
 
     back_seq, filter_grad = conv_backward(grad_seq, carried_seq, filters)

time: 156 us -> 155 us (level)
  the two profiles are of different devices: /device:TPU:1 before, /device:TPU:2 now
where the time goes in v7:
time: 155 us; the launch traced here: 152 us
  starting transfers between devices  79.9 us (52%)
  waiting for transfers between devices  27.4 us (18%)
  Pallas kernels  26.8 us (17%)
  local copies, waits for them, and re-layouts  13.2 us (9%)
  other arithmetic  4.16 us (3%)
    all_to_all x2, starting transfers between devices, channel_major(): return lax.all_to_all(sent, SEQ, split_axis=0, concat_axis=0, tiled=True)  21 us
    ppermute x14, starting transfers between devices, swap(): return lax.ppermute(shard, axis, [(0, 1), (1, 0)])  15.7 us
    all_to_all x2, starting transfers between devices, token_major(): got = lax.all_to_all(block, SEQ, split_axis=0, concat_axis=0, tiled=True)  15.5 us
    ppermute x14, waiting for transfers between devices, swap(): return lax.ppermute(shard, axis, [(0, 1), (1, 0)])  12.9 us
    unnamed x50, local copies, waits for them, and re-layouts  12.4 us
    ppermute x6, waiting for transfers between devices, shift_x(): lax.ppermute(shard, 'x', [(i, (i + by) % count) for i in range(count)])  12.2 us
    ppermute x2, starting transfers between devices, cross_z(): lax.ppermute(shard, 'z', [(i, i ^ by) for i in range(lax.axis_size('z'))])  11.9 us
    ppermute x6, starting transfers between devices, shift_x(): lax.ppermute(shard, 'x', [(i, (i + by) % count) for i in range(count)])  9.28 us
  transfers between devices with their start and end apart: 30, of which 8 were waited for; matrix products, arithmetic and copies ran while one was open for 3% of the time, Pallas kernels for 17%

profile of v7, /device:TPU:2, one launch (start us, length us, event | category | flops | bytes accessed | tf_op | source)
XLA Modules:
  0.0 152.4 jit_solution(12343827211821594913)
XLA Ops:
  0.6 7.3 %collective-permute-start.5 = (bf16[512,128]{1,0:T(8,128)(2,1)}, bf16[512,128]{1,0:T(8,128)(2,1)S(1)}, u32[]{:S(2)}, u32[]{:S(2)}) collective-permute-start(bf16[512,128]{1,0:T(8,128)(2,1)} %param.10), channel_id=1, source_target_pairs={{0,128},{32,160},{64,192},{96,224},{128,0},{160,32},{192,64},{224,... | collective-permute-start | bytes 393224 | tf_op jit(solution)/shard_map/ppermute | solution.py:391
  7.9 3.2 %collective-permute-start.1 = (bf16[256,512]{1,0:T(8,128)(2,1)}, bf16[256,512]{1,0:T(8,128)(2,1)S(1)}, u32[]{:S(2)}, u32[]{:S(2)}) collective-permute-start(bf16[256,512]{1,0:T(8,128)(2,1)} %param.11), channel_id=1, source_target_pairs={{0,4},{4,0},{1,5},{5,1},{2,6},{6,2},{3,7},{7,3},{8,12},{12,8},{9,1... | collective-permute-start | bytes 786440 | tf_op jit(solution)/shard_map/ppermute | solution.py:35
  11.7 1.0 pad_maximum_fusion.1.refs_0_
  12.7 4.7 %collective-permute-start.17 = (bf16[2,512,128]{2,1,0:T(8,128)(2,1)S(1)}, bf16[2,512,128]{2,1,0:T(8,128)(2,1)S(1)}, u32[]{:S(2)}, u32[]{:S(2)}) collective-permute-start(bf16[2,512,128]{2,1,0:T(8,128)(2,1)S(1)} %pad_maximum_fusion.1.refs_0_), channel_id=1, source_target_pairs={{0,64},{32,96},{64,0},{96,32},{128,192},{160,224},{192,128},{224,1... | collective-permute-start | bytes 786440 | tf_op jit(solution)/shard_map/ppermute | solution.py:391
  17.4 3.9 %collective-permute-start.9 = (bf16[2,512,128]{2,1,0:T(8,128)(2,1)S(1)}, bf16[2,512,128]{2,1,0:T(8,128)(2,1)}, u32[]{:S(2)}, u32[]{:S(2)}) collective-permute-start(bf16[2,512,128]{2,1,0:T(8,128)(2,1)S(1)} %pad_maximum_fusion.1.refs_0_), channel_id=1, source_target_pairs={{0,224},{32,0},{64,32},{96,64},{128,96},{160,128},{192,160},{224,1... | collective-permute-start | bytes 786440 | tf_op jit(solution)/shard_map/ppermute | solution.py:387
  21.3 0.7 slice.27
  22.0 1.3 collective-permute-start
  23.3 0.8 collective-permute-done
  24.1 4.4 %collective-permute-start.7 = (bf16[2,512,128]{2,1,0:T(8,128)(2,1)S(1)}, bf16[2,512,128]{2,1,0:T(8,128)(2,1)}, u32[]{:S(2)}, u32[]{:S(2)}) collective-permute-start(bf16[2,512,128]{2,1,0:T(8,128)(2,1)S(1)} %pad_maximum_fusion.1.refs_0_), channel_id=1, source_target_pairs={{0,16},{16,0},{1,17},{17,1},{2,18},{18,2},{3,19},{19,3},{4,20},{20... | collective-permute-start | bytes 786440 | tf_op jit(solution)/shard_map/ppermute | solution.py:35
  29.2 0.9 collective-permute-done.9.refs_4_
  30.0 1.6 %collective-permute-start.15 = (bf16[2,512,128]{2,1,0:T(8,128)(2,1)S(1)}, bf16[2,512,128]{2,1,0:T(8,128)(2,1)}, u32[]{:S(2)}, u32[]{:S(2)}) collective-permute-start(bf16[2,512,128]{2,1,0:T(8,128)(2,1)S(1)} %collective-permute-done.13.refs_8_), channel_id=1, source_target_pairs={{0,16},{16,0},{1,17},{17,1},{2,18},{18,2},{3,19},{19,3},{4,20},{20... | collective-permute-start | bytes 786440 | tf_op jit(solution)/shard_map/ppermute | solution.py:35
  31.7 4.1 %collective-permute-done.7.refs_2_ = bf16[2,512,128]{2,1,0:T(8,128)(2,1)} collective-permute-done((bf16[2,512,128]{2,1,0:T(8,128)(2,1)S(1)}, bf16[2,512,128]{2,1,0:T(8,128)(2,1)}, u32[]{:S(2)}, u32[]{:S(2)}) %collective-permute-start.7) | collective-permute-done | bytes 262176 | tf_op jit(solution)/shard_map/ppermute | solution.py:35
  36.3 2.3 %carried_columns.1 = bf16[512,256]{1,0:T(8,128)(2,1)} custom-call(bf16[3,256,512]{2,1,0:T(8,128)(2,1)} %bitcast.23, bf16[3,2,512]{2,1,0:T(2,128)(2,1)S(1)} %bitcast.29, f32[3,3,512]{2,1,0:T(4,128)} %taps_ref.9), custom_call_target="tpu_custom_call" | custom-call | flops 5000000 | bytes 1500000 | tf_op jit(solution)/shard_map/carried_columns/pallas_call | solution.py:406
  38.7 13.4 %all-to-all-start = ((bf16[32,16,256]{2,1,0:T(8,128)(2,1)}), bf16[32,16,256]{2,1,0:T(8,128)(2,1)S(1)}, u32[]{:S(2)}, u32[]{:S(2)}) async-start(bf16[32,16,256]{2,1,0:T(8,128)(2,1)} %bitcast.33), calls=%async_computation | async-start | bytes 524288 | tf_op jit(solution)/shard_map/all_to_all | solution.py:485
  52.1 0.7 copy-done.7
  53.1 1.6 %collective-permute-start.11 = (bf16[2,512,128]{2,1,0:T(8,128)(2,1)}, bf16[2,512,128]{2,1,0:T(8,128)(2,1)}, u32[]{:S(2)}, u32[]{:S(2)}) collective-permute-start(bf16[2,512,128]{2,1,0:T(8,128)(2,1)} %collective-permute-done.9.refs_4_), channel_id=1, source_target_pairs={{0,16},{16,0},{1,17},{17,1},{2,18},{18,2},{3,19},{19,3},{4,20},{20... | collective-permute-start | bytes 786440 | tf_op jit(solution)/shard_map/ppermute | solution.py:35
  55.3 0.7 copy-done.13
  56.0 2.4 %collective-permute-start.3 = (bf16[2,256,512]{2,1,0:T(8,128)(2,1)S(1)}, bf16[2,256,512]{2,1,0:T(8,128)(2,1)S(1)}, u32[]{:S(2)}, u32[]{:S(2)}) collective-permute-start(bf16[2,256,512]{2,1,0:T(8,128)(2,1)S(1)} %pad_maximum_fusion.cot0), channel_id=1, source_target_pairs={{0,2},{1,3},{2,0},{3,1},{4,6},{5,7},{6,4},{7,5},{8,10},{9,11},{10,... | collective-permute-start | bytes 1572872 | tf_op jit(solution)/shard_map/ppermute | solution.py:396
  58.4 6.0 %collective-permute-done.11.refs_6_ = bf16[2,512,128]{2,1,0:T(8,128)(2,1)} collective-permute-done((bf16[2,512,128]{2,1,0:T(8,128)(2,1)}, bf16[2,512,128]{2,1,0:T(8,128)(2,1)}, u32[]{:S(2)}, u32[]{:S(2)}) %collective-permute-start.11) | collective-permute-done | bytes 262176 | tf_op jit(solution)/shard_map/ppermute | solution.py:35
  64.4 1.5 collective-permute-start.2
  65.9 0.7 copy-done.16
  67.8 3.8 %conv_forward.1 = bf16[32,16,256]{2,1,0:T(8,128)(2,1)} custom-call(bf16[32,16,256]{2,1,0:T(8,128)(2,1)S(1)} %all-to-all-done.x_ref, f32[2,8192]{1,0:T(2,128)S(1)} %copy-done.22), custom_call_target="tpu_custom_call" | custom-call | flops 6000000000 | bytes 600000 | tf_op jit(solution)/shard_map/conv_forward/pallas_call | solution.py:182
  71.7 7.1 %all-to-all-start.1 = ((bf16[32,16,256]{2,1,0:T(8,128)(2,1)}), bf16[32,16,256]{2,1,0:T(8,128)(2,1)S(1)}, u32[]{:S(2)}, u32[]{:S(2)}) async-start(bf16[32,16,256]{2,1,0:T(8,128)(2,1)} %conv_forward.1), calls=%async_computation.1 | async-start | bytes 524288 | tf_op jit(solution)/shard_map/all_to_all | solution.py:489
  78.9 4.0 %collective-permute-done.2.cot1 = bf16[2,256,512]{2,1,0:T(8,128)(2,1)} collective-permute-done((bf16[2,256,512]{2,1,0:T(8,128)(2,1)S(1)}, bf16[2,256,512]{2,1,0:T(8,128)(2,1)}, u32[]{:S(2)}, u32[]{:S(2)}) %collective-permute-start.2) | collective-permute-done | bytes 524320 | tf_op jit(solution)/shard_map/ppermute | solution.py:396
  82.9 0.9 copy-done.5
  83.9 0.9 copy-done.8
  84.8 0.9 copy-done.11
  85.8 0.9 copy-done.14
  86.7 0.9 copy-done.17
  87.7 0.9 copy-done.20
  88.6 4.5 %grad_matmul.1 = (f32[256,512]{1,0:T(8,128)}, bf16[256,512]{1,0:T(8,128)(2,1)}, bf16[512,256]{1,0:T(8,128)(2,1)}) custom-call(s32[5]{0:T(128)S(1)} %stack.41.at_ref, bf16[3,256,512]{2,1,0:T(8,128)(2,1)S(1)} %bitcast.24, bf16[3,2,512]{2,1,0:T(2,128)(2,1)S(1)} %bitcast.30, f32[3,3,512]{2,1,0:T(4,128)S(1)} %copy-done.3, ...), custom_call_target="tpu_custom_call" | custom-call | flops 4000000000 | bytes 6500000 | tf_op jit(solution)/shard_map/grad_matmul/pallas_call | solution.py:315
  93.1 7.6 %all-to-all-start.2 = ((bf16[32,16,256]{2,1,0:T(8,128)(2,1)}), bf16[32,16,256]{2,1,0:T(8,128)(2,1)S(1)}, u32[]{:S(2)}, u32[]{:S(2)}) async-start(bf16[32,16,256]{2,1,0:T(8,128)(2,1)} %bitcast.35), calls=%async_computation.2 | async-start | bytes 524288 | tf_op jit(solution)/shard_map/all_to_all | solution.py:485
  100.7 0.9 copy-done.12
  101.6 0.9 copy-done.15
  102.6 0.9 copy-done.18
  103.5 0.9 copy-done.21
  104.5 5.7 %mix_matmul.1 = (bf16[2,256,512]{2,1,0:T(8,128)(2,1)}, bf16[2,256,512]{2,1,0:T(8,128)(2,1)}, bf16[2,256,512]{2,1,0:T(8,128)(2,1)}, bf16[2,256,512]{2,1,0:T(8,128)(2,1)}, f32[256,512]{1,0:T(8,128)}) custom-call(s32[5]{0:T(128)S(1)} %stack.41.at_ref, bf16[512,256]{1,0:T(8,128)(2,1)S(1)} %bitcast.28, bf16[3,256,512]{2,1,0:T(8,128)(2,1)S(1)} %bitcast.25, ...), custom_call_target="tpu_custom_call" | custom-call | flops 4000000000 | bytes 6500000 | tf_op jit(solution)/shard_map/mix_matmul/pallas_call | solution.py:367
  110.2 1.5 collective-permute-start.21
  111.7 3.3 %collective-permute-start.22 = (bf16[2,256,512]{2,1,0:T(8,128)(2,1)}, bf16[2,256,512]{2,1,0:T(8,128)(2,1)}, u32[]{:S(2)}, u32[]{:S(2)}) collective-permute-start(bf16[2,256,512]{2,1,0:T(8,128)(2,1)} %get-tuple-element.19), channel_id=1, source_target_pairs={{0,2},{1,3},{2,0},{3,1},{4,6},{5,7},{6,4},{7,5},{8,10},{9,11},{10,... | collective-permute-start | bytes 1572872 | tf_op jit(solution)/shard_map/ppermute | solution.py:396
  115.0 7.0 %conv_backward.1 = (bf16[32,16,256]{2,1,0:T(8,128)(2,1)}, f32[2,8192]{1,0:T(2,128)}) custom-call(bf16[32,16,256]{2,1,0:T(8,128)(2,1)S(1)} %all-to-all-done.2.m_ref, bf16[32,16,256]{2,1,0:T(8,128)(2,1)S(1)} %all-to-all-done.x_ref, f32[2,8192]{1,0:T(2,128)S(1)} %copy-done.22), custom_call_target="tpu_custom_call" | custom-call | flops 10000000000 | bytes 1000000 | tf_op jit(solution)/shard_map/conv_backward/pallas_call | solution.py:200
  122.0 8.4 %all-to-all-start.3 = ((bf16[32,16,256]{2,1,0:T(8,128)(2,1)}), bf16[32,16,256]{2,1,0:T(8,128)(2,1)S(1)}, u32[]{:S(2)}, u32[]{:S(2)}) async-start(bf16[32,16,256]{2,1,0:T(8,128)(2,1)} %get-tuple-element.22), calls=%async_computation.3 | async-start | bytes 524288 | tf_op jit(solution)/shard_map/all_to_all | solution.py:489
  130.5 8.2 %collective-permute-done.23 = bf16[2,256,512]{2,1,0:T(8,128)(2,1)} collective-permute-done((bf16[2,256,512]{2,1,0:T(8,128)(2,1)}, bf16[2,256,512]{2,1,0:T(8,128)(2,1)}, u32[]{:S(2)}, u32[]{:S(2)}) %collective-permute-start.23) | collective-permute-done | bytes 524320 | tf_op jit(solution)/shard_map/ppermute | solution.py:396
  138.7 1.2 fusion.1
  139.9 3.0 %collective-permute-start.24 = (bf16[256,512]{1,0:T(8,128)(2,1)S(1)}, bf16[256,512]{1,0:T(8,128)(2,1)S(1)}, u32[]{:S(2)}, u32[]{:S(2)}) collective-permute-start(bf16[256,512]{1,0:T(8,128)(2,1)S(1)} %fusion.1), channel_id=1, source_target_pairs={{0,4},{4,0},{1,5},{5,1},{2,6},{6,2},{3,7},{7,3},{8,12},{12,8},{9,1... | collective-permute-start | bytes 786440 | tf_op jit(solution)/shard_map/ppermute | solution.py:35
  142.9 2.9 %final_short.1 = (bf16[3,256,512]{2,1,0:T(8,128)(2,1)}, f32[3,8,512]{2,1,0:T(8,128)}, f32[3,16,512]{2,1,0:T(8,128)S(1)}) custom-call(bf16[512,256]{1,0:T(8,128)(2,1)S(1)} %bitcast.27, bf16[256,512]{1,0:T(8,128)(2,1)S(1)} %copy-done.2, f32[256,512]{1,0:T(8,128)S(1)} %copy-done.1, bf16[3,256,512]{2,1,0:T(8,128)(2,1)S(1)} %bitcast.26, ...), custom_call_target="tpu_custom_call" | custom-call | flops 5000000 | bytes 3500000 | tf_op jit(solution)/shard_map/final_short/pallas_call | solution.py:435
  145.8 1.3 collective-permute-start.25
  147.0 2.8 %collective-permute-done.24 = bf16[256,512]{1,0:T(8,128)(2,1)S(1)} collective-permute-done((bf16[256,512]{1,0:T(8,128)(2,1)S(1)}, bf16[256,512]{1,0:T(8,128)(2,1)S(1)}, u32[]{:S(2)}, u32[]{:S(2)}) %collective-permute-start.24) | collective-permute-done | bytes 262176 | tf_op jit(solution)/shard_map/ppermute | solution.py:35
  149.8 1.9 %fusion = bf16[256,512]{1,0:T(8,128)(2,1)} fusion(bf16[256,512]{1,0:T(8,128)(2,1)S(1)} %collective-permute-done.24, bf16[2,256,512]{2,1,0:T(8,128)(2,1)} %collective-permute-done.23, bf16[2,256,512]{2,1,0:T(8,128)(2,1)} %collective-permute-done.22, bf16[2,256,512]{2,1,0:T(8,128)(2,1)S(1)} %collective-permute-done.21, bf16[2,256,512]{2,1,0:T(8,128)(2,1)S(1)} %copy-done.23), kind=kLoop, calls=%fused_computation.2 | loop fusion | flops 1310720 | bytes 1572864 | tf_op jit(solution)/shard_map/convert_element_type | solution.py:529
  (75 shorter events, 4.7 us)
Async XLA Ops:
  0.6 11.1 %collective-permute-start.5 = (bf16[512,128]{1,0:T(8,128)(2,1)}, bf16[512,128]{1,0:T(8,128)(2,1)S(1)}, u32[]{:S(2)}, u32[]{:S(2)}) collective-permute-start(bf16[512,128]{1,0:T(8,128)(2,1)} %param.10), channel_id=1, source_target_pairs={{0,128},{32,160},{64,192},{96,224},{128,0},{160,32},{192,64},{224,... | collective-permute-start | bytes 393224 | tf_op jit(solution)/shard_map/ppermute | solution.py:391
  7.9 20.6 %collective-permute-start.1 = (bf16[256,512]{1,0:T(8,128)(2,1)}, bf16[256,512]{1,0:T(8,128)(2,1)S(1)}, u32[]{:S(2)}, u32[]{:S(2)}) collective-permute-start(bf16[256,512]{1,0:T(8,128)(2,1)} %param.11), channel_id=1, source_target_pairs={{0,4},{4,0},{1,5},{5,1},{2,6},{6,2},{3,7},{7,3},{8,12},{12,8},{9,1... | collective-permute-start | bytes 786440 | tf_op jit(solution)/shard_map/ppermute | solution.py:35
  11.7 19.9 %copy-start.24 = (bf16[256,512]{1,0:T(8,128)(2,1)S(1)}, bf16[256,512]{1,0:T(8,128)(2,1)}, u32[]{:S(2)}) copy-start(bf16[256,512]{1,0:T(8,128)(2,1)} %param.11) | copy-start | bytes 786436
  12.7 15.8 %collective-permute-start.17 = (bf16[2,512,128]{2,1,0:T(8,128)(2,1)S(1)}, bf16[2,512,128]{2,1,0:T(8,128)(2,1)S(1)}, u32[]{:S(2)}, u32[]{:S(2)}) collective-permute-start(bf16[2,512,128]{2,1,0:T(8,128)(2,1)S(1)} %pad_maximum_fusion.1.refs_0_), channel_id=1, source_target_pairs={{0,64},{32,96},{64,0},{96,32},{128,192},{160,224},{192,128},{224,1... | collective-permute-start | bytes 786440 | tf_op jit(solution)/shard_map/ppermute | solution.py:391
  17.4 11.6 %collective-permute-start.13 = (bf16[2,512,128]{2,1,0:T(8,128)(2,1)S(1)}, bf16[2,512,128]{2,1,0:T(8,128)(2,1)S(1)}, u32[]{:S(2)}, u32[]{:S(2)}) collective-permute-start(bf16[2,512,128]{2,1,0:T(8,128)(2,1)S(1)} %pad_maximum_fusion.1.refs_0_), channel_id=1, source_target_pairs={{0,32},{32,64},{64,96},{96,128},{128,160},{160,192},{192,224},{224... | collective-permute-start | bytes 786440 | tf_op jit(solution)/shard_map/ppermute | solution.py:387
  17.4 12.7 %collective-permute-start.9 = (bf16[2,512,128]{2,1,0:T(8,128)(2,1)S(1)}, bf16[2,512,128]{2,1,0:T(8,128)(2,1)}, u32[]{:S(2)}, u32[]{:S(2)}) collective-permute-start(bf16[2,512,128]{2,1,0:T(8,128)(2,1)S(1)} %pad_maximum_fusion.1.refs_0_), channel_id=1, source_target_pairs={{0,224},{32,0},{64,32},{96,64},{128,96},{160,128},{192,160},{224,1... | collective-permute-start | bytes 786440 | tf_op jit(solution)/shard_map/ppermute | solution.py:387
  22.0 2.1 %collective-permute-start = (bf16[2,3,512]{2,0,1:T(2,128)(2,1)S(1)}, bf16[2,3,512]{2,0,1:T(2,128)(2,1)S(1)}, u32[]{:S(2)}, u32[]{:S(2)}) collective-permute-start(bf16[2,3,512]{2,0,1:T(2,128)(2,1)S(1)} %slice.27), channel_id=1, source_target_pairs={{0,8},{8,16},{16,24},{24,32},{32,40},{40,48},{48,56},{56,64},{64,7... | collective-permute-start | bytes 18440 | tf_op jit(solution)/shard_map/ppermute | solution.py:31
  24.1 11.7 %collective-permute-start.7 = (bf16[2,512,128]{2,1,0:T(8,128)(2,1)S(1)}, bf16[2,512,128]{2,1,0:T(8,128)(2,1)}, u32[]{:S(2)}, u32[]{:S(2)}) collective-permute-start(bf16[2,512,128]{2,1,0:T(8,128)(2,1)S(1)} %pad_maximum_fusion.1.refs_0_), channel_id=1, source_target_pairs={{0,16},{16,0},{1,17},{17,1},{2,18},{18,2},{3,19},{19,3},{4,20},{20... | collective-permute-start | bytes 786440 | tf_op jit(solution)/shard_map/ppermute | solution.py:35
  28.5 23.6 %collective-permute-start.6 = (bf16[2,512,128]{2,1,0:T(8,128)(2,1)S(1)}, bf16[2,512,128]{2,1,0:T(8,128)(2,1)S(1)}, u32[]{:S(2)}, u32[]{:S(2)}) collective-permute-start(bf16[2,512,128]{2,1,0:T(8,128)(2,1)S(1)} %pad_maximum_fusion.1.refs_0_), channel_id=1, source_target_pairs={{0,8},{8,0},{1,9},{9,1},{2,10},{10,2},{3,11},{11,3},{4,12},{12,4},... | collective-permute-start | bytes 786440 | tf_op jit(solution)/shard_map/ppermute | solution.py:35
  28.5 24.6 %collective-permute-start.19 = (bf16[2,512,128]{2,1,0:T(8,128)(2,1)S(1)}, bf16[2,512,128]{2,1,0:T(8,128)(2,1)}, u32[]{:S(2)}, u32[]{:S(2)}) collective-permute-start(bf16[2,512,128]{2,1,0:T(8,128)(2,1)S(1)} %collective-permute-done.17.refs_12_), channel_id=1, source_target_pairs={{0,16},{16,0},{1,17},{17,1},{2,18},{18,2},{3,19},{19,3},{4,20},{20... | collective-permute-start | bytes 786440 | tf_op jit(solution)/shard_map/ppermute | solution.py:35
  29.0 23.2 %copy-start.4 = (bf16[2,512,128]{2,1,0:T(8,128)(2,1)}, bf16[2,512,128]{2,1,0:T(8,128)(2,1)S(1)}, u32[]{:S(2)}) copy-start(bf16[2,512,128]{2,1,0:T(8,128)(2,1)S(1)} %collective-permute-done.13.refs_8_) | copy-start | bytes 786436
  29.0 25.8 %collective-permute-start.18 = (bf16[2,512,128]{2,1,0:T(8,128)(2,1)S(1)}, bf16[2,512,128]{2,1,0:T(8,128)(2,1)S(1)}, u32[]{:S(2)}, u32[]{:S(2)}) collective-permute-start(bf16[2,512,128]{2,1,0:T(8,128)(2,1)S(1)} %collective-permute-done.17.refs_12_), channel_id=1, source_target_pairs={{0,8},{8,0},{1,9},{9,1},{2,10},{10,2},{3,11},{11,3},{4,12},{12,4},... | collective-permute-start | bytes 786440 | tf_op jit(solution)/shard_map/ppermute | solution.py:35
  30.0 24.8 %collective-permute-start.15 = (bf16[2,512,128]{2,1,0:T(8,128)(2,1)S(1)}, bf16[2,512,128]{2,1,0:T(8,128)(2,1)}, u32[]{:S(2)}, u32[]{:S(2)}) collective-permute-start(bf16[2,512,128]{2,1,0:T(8,128)(2,1)S(1)} %collective-permute-done.13.refs_8_), channel_id=1, source_target_pairs={{0,16},{16,0},{1,17},{17,1},{2,18},{18,2},{3,19},{19,3},{4,20},{20... | collective-permute-start | bytes 786440 | tf_op jit(solution)/shard_map/ppermute | solution.py:35
  35.8 32.0 %collective-permute-start.4 = (bf16[2,256,512]{2,1,0:T(8,128)(2,1)S(1)}, bf16[2,256,512]{2,1,0:T(8,128)(2,1)S(1)}, u32[]{:S(2)}, u32[]{:S(2)}) collective-permute-start(bf16[2,256,512]{2,1,0:T(8,128)(2,1)S(1)} %pad_maximum_fusion.cot0), channel_id=1, source_target_pairs={{0,3},{1,0},{2,1},{3,2},{4,7},{5,4},{6,5},{7,6},{8,11},{9,8},{10,9... | collective-permute-start | bytes 1572872 | tf_op jit(solution)/shard_map/ppermute | solution.py:396
  38.7 29.2 %copy-start.22 = (f32[2,8192]{1,0:T(2,128)S(1)}, f32[2,8192]{1,0:T(2,128)}, u32[]{:S(2)}) copy-start(f32[2,8192]{1,0:T(2,128)} %h_ref.3) | copy-start | bytes 196612
  38.7 29.2 %all-to-all-start = ((bf16[32,16,256]{2,1,0:T(8,128)(2,1)}), bf16[32,16,256]{2,1,0:T(8,128)(2,1)S(1)}, u32[]{:S(2)}, u32[]{:S(2)}) async-start(bf16[32,16,256]{2,1,0:T(8,128)(2,1)} %bitcast.33), calls=%async_computation | async-start | bytes 524288 | tf_op jit(solution)/shard_map/all_to_all | solution.py:485
  52.1 30.8 %copy-start = (bf16[256,3,512]{2,0,1:T(8,128)(2,1)S(1)}, bf16[256,3,512]{2,0,1:T(8,128)(2,1)}, u32[]{:S(2)}) copy-start(bf16[256,3,512]{2,0,1:T(8,128)(2,1)} %param.6) | copy-start | bytes 2359300
  52.9 2.4 %collective-permute-start.14 = (bf16[2,512,128]{2,1,0:T(8,128)(2,1)S(1)}, bf16[2,512,128]{2,1,0:T(8,128)(2,1)S(1)}, u32[]{:S(2)}, u32[]{:S(2)}) collective-permute-start(bf16[2,512,128]{2,1,0:T(8,128)(2,1)S(1)} %collective-permute-done.13.refs_8_), channel_id=1, source_target_pairs={{0,8},{8,0},{1,9},{9,1},{2,10},{10,2},{3,11},{11,3},{4,12},{12,4},... | collective-permute-start | bytes 786440 | tf_op jit(solution)/shard_map/ppermute | solution.py:35
  53.1 11.3 %collective-permute-start.11 = (bf16[2,512,128]{2,1,0:T(8,128)(2,1)}, bf16[2,512,128]{2,1,0:T(8,128)(2,1)}, u32[]{:S(2)}, u32[]{:S(2)}) collective-permute-start(bf16[2,512,128]{2,1,0:T(8,128)(2,1)} %collective-permute-done.9.refs_4_), channel_id=1, source_target_pairs={{0,16},{16,0},{1,17},{17,1},{2,18},{18,2},{3,19},{19,3},{4,20},{20... | collective-permute-start | bytes 786440 | tf_op jit(solution)/shard_map/ppermute | solution.py:35
  54.8 16.9 %copy-start.10 = (bf16[2,512,128]{2,1,0:T(8,128)(2,1)}, bf16[2,512,128]{2,1,0:T(8,128)(2,1)S(1)}, u32[]{:S(2)}) copy-start(bf16[2,512,128]{2,1,0:T(8,128)(2,1)S(1)} %collective-permute-done.18.refs_13_) | copy-start | bytes 786436
  54.8 11.1 %collective-permute-start.10 = (bf16[2,512,128]{2,1,0:T(8,128)(2,1)}, bf16[2,512,128]{2,1,0:T(8,128)(2,1)S(1)}, u32[]{:S(2)}, u32[]{:S(2)}) collective-permute-start(bf16[2,512,128]{2,1,0:T(8,128)(2,1)} %collective-permute-done.9.refs_4_), channel_id=1, source_target_pairs={{0,8},{8,0},{1,9},{9,1},{2,10},{10,2},{3,11},{11,3},{4,12},{12,4},... | collective-permute-start | bytes 786440 | tf_op jit(solution)/shard_map/ppermute | solution.py:35
  54.9 11.7 %collective-permute-start.8 = (bf16[2,512,128]{2,1,0:T(8,128)(2,1)}, bf16[2,512,128]{2,1,0:T(8,128)(2,1)S(1)}, u32[]{:S(2)}, u32[]{:S(2)}) collective-permute-start(bf16[2,512,128]{2,1,0:T(8,128)(2,1)} %collective-permute-done.7.refs_2_), channel_id=1, source_target_pairs={{0,8},{8,0},{1,9},{9,1},{2,10},{10,2},{3,11},{11,3},{4,12},{12,4},... | collective-permute-start | bytes 786440 | tf_op jit(solution)/shard_map/ppermute | solution.py:35
  56.0 22.9 %collective-permute-start.3 = (bf16[2,256,512]{2,1,0:T(8,128)(2,1)S(1)}, bf16[2,256,512]{2,1,0:T(8,128)(2,1)S(1)}, u32[]{:S(2)}, u32[]{:S(2)}) collective-permute-start(bf16[2,256,512]{2,1,0:T(8,128)(2,1)S(1)} %pad_maximum_fusion.cot0), channel_id=1, source_target_pairs={{0,2},{1,3},{2,0},{3,1},{4,6},{5,7},{6,4},{7,5},{8,10},{9,11},{10,... | collective-permute-start | bytes 1572872 | tf_op jit(solution)/shard_map/ppermute | solution.py:396
  64.4 18.5 %collective-permute-start.2 = (bf16[2,256,512]{2,1,0:T(8,128)(2,1)S(1)}, bf16[2,256,512]{2,1,0:T(8,128)(2,1)}, u32[]{:S(2)}, u32[]{:S(2)}) collective-permute-start(bf16[2,256,512]{2,1,0:T(8,128)(2,1)S(1)} %pad_maximum_fusion.cot0), channel_id=1, source_target_pairs={{0,1},{1,2},{2,3},{3,0},{4,5},{5,6},{6,7},{7,4},{8,9},{9,10},{10,1... | collective-permute-start | bytes 1572872 | tf_op jit(solution)/shard_map/ppermute | solution.py:396
  66.6 16.3 %collective-permute-start.20 = (bf16[2,512,128]{2,1,0:T(8,128)(2,1)}, bf16[2,512,128]{2,1,0:T(8,128)(2,1)}, u32[]{:S(2)}, u32[]{:S(2)}) collective-permute-start(bf16[2,512,128]{2,1,0:T(8,128)(2,1)} %collective-permute-done.19.refs_14_), channel_id=1, source_target_pairs={{0,8},{8,0},{1,9},{9,1},{2,10},{10,2},{3,11},{11,3},{4,12},{12,4},... | collective-permute-start | bytes 786440 | tf_op jit(solution)/shard_map/ppermute | solution.py:35
  67.3 15.6 %collective-permute-start.16 = (bf16[2,512,128]{2,1,0:T(8,128)(2,1)}, bf16[2,512,128]{2,1,0:T(8,128)(2,1)}, u32[]{:S(2)}, u32[]{:S(2)}) collective-permute-start(bf16[2,512,128]{2,1,0:T(8,128)(2,1)} %collective-permute-done.15.refs_10_), channel_id=1, source_target_pairs={{0,8},{8,0},{1,9},{9,1},{2,10},{10,2},{3,11},{11,3},{4,12},{12,4},... | collective-permute-start | bytes 786440 | tf_op jit(solution)/shard_map/ppermute | solution.py:35
  67.8 15.1 %collective-permute-start.12 = (bf16[2,512,128]{2,1,0:T(8,128)(2,1)}, bf16[2,512,128]{2,1,0:T(8,128)(2,1)}, u32[]{:S(2)}, u32[]{:S(2)}) collective-permute-start(bf16[2,512,128]{2,1,0:T(8,128)(2,1)} %collective-permute-done.11.refs_6_), channel_id=1, source_target_pairs={{0,8},{8,0},{1,9},{9,1},{2,10},{10,2},{3,11},{11,3},{4,12},{12,4},... | collective-permute-start | bytes 786440 | tf_op jit(solution)/shard_map/ppermute | solution.py:35
  71.7 21.4 %all-to-all-start.1 = ((bf16[32,16,256]{2,1,0:T(8,128)(2,1)}), bf16[32,16,256]{2,1,0:T(8,128)(2,1)S(1)}, u32[]{:S(2)}, u32[]{:S(2)}) async-start(bf16[32,16,256]{2,1,0:T(8,128)(2,1)} %conv_forward.1), calls=%async_computation.1 | async-start | bytes 524288 | tf_op jit(solution)/shard_map/all_to_all | solution.py:489
  78.8 4.1 %copy-start.3 = (f32[3,3,512]{2,1,0:T(4,128)S(1)}, f32[3,3,512]{2,1,0:T(4,128)}, u32[]{:S(2)}) copy-start(f32[3,3,512]{2,1,0:T(4,128)} %taps_ref.9) | copy-start | bytes 55300
  82.9 1.0 copy-start.5
  83.9 0.9 copy-start.8
  84.8 0.9 copy-start.11
  85.8 0.9 copy-start.14
  86.7 0.9 copy-start.17
  87.7 0.9 copy-start.20
  93.1 7.6 %copy-start.6 = (bf16[2,512,128]{2,1,0:T(8,128)(2,1)S(1)}, bf16[2,512,128]{2,1,0:T(8,128)(2,1)}, u32[]{:S(2)}) copy-start(bf16[2,512,128]{2,1,0:T(8,128)(2,1)} %copy-done.4) | copy-start | bytes 786436
  93.1 7.6 %copy-start.9 = (bf16[2,512,128]{2,1,0:T(8,128)(2,1)S(1)}, bf16[2,512,128]{2,1,0:T(8,128)(2,1)}, u32[]{:S(2)}) copy-start(bf16[2,512,128]{2,1,0:T(8,128)(2,1)} %copy-done.7) | copy-start | bytes 786436
  93.1 21.9 %all-to-all-start.2 = ((bf16[32,16,256]{2,1,0:T(8,128)(2,1)}), bf16[32,16,256]{2,1,0:T(8,128)(2,1)S(1)}, u32[]{:S(2)}, u32[]{:S(2)}) async-start(bf16[32,16,256]{2,1,0:T(8,128)(2,1)} %bitcast.35), calls=%async_computation.2 | async-start | bytes 524288 | tf_op jit(solution)/shard_map/all_to_all | solution.py:485
  100.7 1.0 copy-start.12
  110.2 20.3 %collective-permute-start.21 = (bf16[2,256,512]{2,1,0:T(8,128)(2,1)}, bf16[2,256,512]{2,1,0:T(8,128)(2,1)S(1)}, u32[]{:S(2)}, u32[]{:S(2)}) collective-permute-start(bf16[2,256,512]{2,1,0:T(8,128)(2,1)} %get-tuple-element.18), channel_id=1, source_target_pairs={{0,1},{1,2},{2,3},{3,0},{4,5},{5,6},{6,7},{7,4},{8,9},{9,10},{10,1... | collective-permute-start | bytes 1572872 | tf_op jit(solution)/shard_map/ppermute | solution.py:396
  111.7 18.8 %collective-permute-start.22 = (bf16[2,256,512]{2,1,0:T(8,128)(2,1)}, bf16[2,256,512]{2,1,0:T(8,128)(2,1)}, u32[]{:S(2)}, u32[]{:S(2)}) collective-permute-start(bf16[2,256,512]{2,1,0:T(8,128)(2,1)} %get-tuple-element.19), channel_id=1, source_target_pairs={{0,2},{1,3},{2,0},{3,1},{4,6},{5,7},{6,4},{7,5},{8,10},{9,11},{10,... | collective-permute-start | bytes 1572872 | tf_op jit(solution)/shard_map/ppermute | solution.py:396
  115.0 23.6 %collective-permute-start.23 = (bf16[2,256,512]{2,1,0:T(8,128)(2,1)}, bf16[2,256,512]{2,1,0:T(8,128)(2,1)}, u32[]{:S(2)}, u32[]{:S(2)}) collective-permute-start(bf16[2,256,512]{2,1,0:T(8,128)(2,1)} %get-tuple-element.20), channel_id=1, source_target_pairs={{0,3},{1,0},{2,1},{3,2},{4,7},{5,4},{6,5},{7,6},{8,11},{9,8},{10,9... | collective-permute-start | bytes 1572872 | tf_op jit(solution)/shard_map/ppermute | solution.py:396
  122.0 16.6 %copy-start.23 = (bf16[2,256,512]{2,1,0:T(8,128)(2,1)S(1)}, bf16[2,256,512]{2,1,0:T(8,128)(2,1)}, u32[]{:S(2)}) copy-start(bf16[2,256,512]{2,1,0:T(8,128)(2,1)} %get-tuple-element.17) | copy-start | bytes 1572868
  122.0 20.9 %all-to-all-start.3 = ((bf16[32,16,256]{2,1,0:T(8,128)(2,1)}), bf16[32,16,256]{2,1,0:T(8,128)(2,1)S(1)}, u32[]{:S(2)}, u32[]{:S(2)}) async-start(bf16[32,16,256]{2,1,0:T(8,128)(2,1)} %get-tuple-element.22), calls=%async_computation.3 | async-start | bytes 524288 | tf_op jit(solution)/shard_map/all_to_all | solution.py:489
  138.7 4.2 %copy-start.1 = (f32[256,512]{1,0:T(8,128)S(1)}, f32[256,512]{1,0:T(8,128)}, u32[]{:S(2)}) copy-start(f32[256,512]{1,0:T(8,128)} %get-tuple-element.24.query_grad_ref) | copy-start | bytes 1572868
  138.7 4.2 %copy-start.2 = (bf16[256,512]{1,0:T(8,128)(2,1)S(1)}, bf16[256,512]{1,0:T(8,128)(2,1)}, u32[]{:S(2)}) copy-start(bf16[256,512]{1,0:T(8,128)(2,1)} %get-tuple-element.23.mixed_ref) | copy-start | bytes 786436
  139.9 9.9 %collective-permute-start.24 = (bf16[256,512]{1,0:T(8,128)(2,1)S(1)}, bf16[256,512]{1,0:T(8,128)(2,1)S(1)}, u32[]{:S(2)}, u32[]{:S(2)}) collective-permute-start(bf16[256,512]{1,0:T(8,128)(2,1)S(1)} %fusion.1), channel_id=1, source_target_pairs={{0,4},{4,0},{1,5},{5,1},{2,6},{6,2},{3,7},{7,3},{8,12},{12,8},{9,1... | collective-permute-start | bytes 786440 | tf_op jit(solution)/shard_map/ppermute | solution.py:35
  145.8 6.0 %collective-permute-start.25 = (f32[3,8,512]{2,1,0:T(8,128)}, f32[3,8,512]{2,1,0:T(8,128)S(1)}, u32[]{:S(2)}, u32[]{:S(2)}) collective-permute-start(f32[3,8,512]{2,1,0:T(8,128)} %get-tuple-element.26), channel_id=1, source_target_pairs={{8,0},{16,8},{24,16},{32,24},{40,32},{48,40},{56,48},{64,56},{72,6... | collective-permute-start | bytes 147464 | tf_op jit(solution)/shard_map/ppermute | solution.py:31
  (7 other events, 5.7 us)
